TPU v7x, 128 devices: a whole 4x4x4 slice. The times are simulated.
128 devices in a mesh: ch: 16 (over z, y), sx: 4 (over x_lo, core), sy: 2 (over x_hi).
Axes of the slice: x: 4 (x_hi: 2, x_lo: 2; x = x_hi * 2 + x_lo), y: 4, z: 4, core: 2. Of those that a mesh axis runs over, the one named last changes fastest.
Arguments:
- inputs: bfloat16 [768, 16, 4, 64], P('ch', 'sx', 'sy'), may hold values from -6 to 6
- pre_act: bfloat16 [768, 16, 4, 64], P('ch', 'sx', 'sy'), may hold values from -6 to 6
- out_grad: bfloat16 [768, 16, 4, 64], P('ch', 'sx', 'sy'), may hold values from -6 to 6
- weight_one: bfloat16 [27, 768, 768], P(None, 'ch'), may hold values from -0.0390625 to 0.0390625
- weight_two: bfloat16 [27, 768, 768], P(None, 'ch'), may hold values from -0.0390625 to 0.0390625
Outputs:
- input_grad: bfloat16 [768, 16, 4, 64], P('ch', 'sx', 'sy')
- filter_one_grad: float32 [27, 768, 768], P(None, 'ch')
- filter_two_grad: float32 [27, 768, 768], P(None, 'ch')
All inputs are finite; a program needn't handle non-finite values.
Results may differ from a plain program's by a relative error of at most 0.0049.
Values may be sent and summed in bfloat16 or wider, within the bound.
No kernel may reach another device: no remote copies, remote signals or barrier semaphores. Data moves between devices by JAX's collectives and lax.ppermute only.
A program may use at most 192 MiB of HBM per device.

v0:
```python
import functools

import jax
import jax.numpy as jnp
from jax import lax
from jax.experimental import pallas as pl
from jax.experimental.pallas import tpu as pltpu
from jax.sharding import PartitionSpec as P

BF = jnp.bfloat16
F32 = jnp.float32
LINE = ("sx", "sy")
OFF = 27
OFFP = 28
C = 48
CH = 768
SLAB = 128
NXL = 4
ROWS = OFF * C
ROWSP = OFFP * C
HALF = CH // 2


def place(chip, core):
    return ((chip % 2) * 2 + core) * 2 + chip // 2


SAME_CORE = [[place(chip, core) for chip in range(4)] for core in range(2)]
OTHER_CORE = [(place(x, c), place(x, 1 - c)) for x in range(4) for c in range(2)]


def vmem():
    return pl.BlockSpec(memory_space=pltpu.VMEM)


def smem():
    return pl.BlockSpec(memory_space=pltpu.SMEM)


def call(body, outs, scratch, n_in, limit=48):
    return pl.pallas_call(
        body,
        out_shape=outs,
        in_specs=[smem()] + [vmem()] * n_in,
        out_specs=jax.tree.map(lambda _: vmem(), outs),
        scratch_shapes=scratch,
        compiler_params=pltpu.CompilerParams(vmem_limit_bytes=limit << 20),
    )


def lanes():
    return lax.broadcasted_iota(jnp.int32, (C, SLAB), 1)


def shift_z(part, c, lane):
    if c == 1:
        return part
    z = lane % 64
    if c == 0:
        return jnp.where(z >= 1, pltpu.roll(part, 1, 1), 0.0)
    return jnp.where(z <= 62, pltpu.roll(part, SLAB - 1, 1), 0.0)


def fill_windows(line_ref, stack_ref, sx, sy, mirror, act):
    lane = lanes()
    low = lane < 64
    for xp in range(NXL + 2):
        peer_x = sx + (-1 if xp == 0 else 1 if xp == NXL + 1 else 0)
        valid = jnp.logical_and(peer_x >= 0, peer_x <= 3)
        peer_x = jnp.clip(peer_x, 0, 3)
        at = ((xp - 1) % NXL) * SLAB
        own = line_ref[peer_x * 2 + sy, :, at : at + SLAB].astype(F32)
        oth = line_ref[peer_x * 2 + 1 - sy, :, at : at + SLAB].astype(F32)
        if act:
            own, oth = jnp.maximum(own, 0.0), jnp.maximum(oth, 0.0)
        if xp in (0, NXL + 1):
            own, oth = jnp.where(valid, own, 0.0), jnp.where(valid, oth, 0.0)
        r_own, r_oth = pltpu.roll(own, 64, 1), pltpu.roll(oth, 64, 1)
        rows = (
            jnp.where(low, jnp.where(sy == 1, r_oth, 0.0), r_own),
            own,
            jnp.where(low, r_own, jnp.where(sy == 0, r_oth, 0.0)),
        )
        for b in range(3):
            for c in range(3):
                part = shift_z(rows[b], c, lane).astype(BF)
                for a in range(3):
                    xl = xp - a
                    if 0 <= xl < NXL:
                        o = 9 * a + 3 * b + c
                        o = 26 - o if mirror else o
                        stack_ref[o * C : (o + 1) * C, xl * SLAB : (xl + 1) * SLAB] = part


def nt(left, right):
    return lax.dot_general(left, right, (((1,), (1,)), ((), ())), preferred_element_type=F32)


def act_grad_body(ids, w_ref, g_ref, own_ref, send_ref, u_ref):
    sy = ids[1]
    grad = g_ref[...]
    u_ref[...] = jnp.zeros_like(u_ref)
    for a in range(3):
        for b in range(3):
            o = 9 * a + 3 * b
            y = jnp.dot(w_ref[o * C : (o + 3) * C, :], grad, preferred_element_type=F32)
            u_ref[b, :, a * SLAB : (a + NXL) * SLAB] += y
    lane = lanes()
    low = lane < 64
    for xp in range(NXL + 2):
        at = slice(xp * SLAB, (xp + 1) * SLAB)
        v = [
            sum(shift_z(u_ref[b, c * C : (c + 1) * C, at], 2 - c, lane) for c in range(3))
            for b in range(3)
        ]
        r0, r2 = pltpu.roll(v[0], 64, 1), pltpu.roll(v[2], 64, 1)
        own_ref[:, at] = v[1] + jnp.where(low, r0, r2)
        send_ref[:, at] = jnp.where(
            sy == 0, jnp.where(low, r2, 0.0), jnp.where(low, 0.0, r0)
        )


def filter_body(act, mirror, ids, line_ref, full_ref, keep_ref, send_ref, stack_ref):
    sx, sy, core = ids[0], ids[1], ids[2]
    fill_windows(line_ref, stack_ref, sx, sy, mirror, act)
    mine = full_ref[pl.ds(pl.multiple_of(core * HALF, HALF), HALF), :]
    other = full_ref[pl.ds(pl.multiple_of((1 - core) * HALF, HALF), HALF), :]
    step = 3 * C
    for i in range(9):
        rows = stack_ref[i * step : (i + 1) * step, :]
        send_ref[i * step : (i + 1) * step, :] = nt(rows, other).astype(BF)
        keep_ref[i * step : (i + 1) * step, :] = nt(rows, mine)
    keep_ref[ROWS:ROWSP, :] = jnp.zeros((ROWSP - ROWS, HALF), F32)
    send_ref[ROWS:ROWSP, :] = jnp.zeros((ROWSP - ROWS, HALF), BF)


def data_body(ids, line_ref, w_ref, out_ref, stack_ref):
    fill_windows(line_ref, stack_ref, ids[0], ids[1], True, False)
    for i in range(3):
        out_ref[i * 256 : (i + 1) * 256, :] = jnp.dot(
            w_ref[i * 256 : (i + 1) * 256, :], stack_ref[...], preferred_element_type=F32
        ).astype(BF)


def to_all(x, axis, count, groups=None):
    many = jnp.broadcast_to(x[None], (count,) + x.shape)
    return lax.all_to_all(many, axis, 0, 0, tiled=True, axis_index_groups=groups)


def chip_sum(keep, send):
    got = lax.ppermute(send, LINE, OTHER_CORE)
    return (keep + got.astype(F32)).astype(BF).reshape(4, ROWSP // 4, HALF)


def line_sum(part, factor):
    got = lax.all_to_all(part, LINE, 0, 0, tiled=True, axis_index_groups=SAME_CORE)
    return (got.astype(F32).sum(axis=0) * factor).astype(BF)


def spread(block, core):
    mine = to_all(block, LINE, 4, SAME_CORE).reshape(ROWSP, HALF)[:ROWS]
    other = lax.ppermute(mine, LINE, OTHER_CORE)
    first = jnp.where(core == 0, mine, other)
    second = jnp.where(core == 0, other, mine)
    both = jnp.concatenate([first, second], axis=1).astype(F32)
    return both.reshape(OFF, C, CH)


def shards(inputs, pre_act, out_grad, weight_one, weight_two):
    shape = pre_act.shape
    sx, sy = lax.axis_index("sx"), lax.axis_index("sy")
    core = sx % 2
    ids = jnp.stack([sx, sy, core]).astype(jnp.int32)
    n_pos = NXL * SLAB
    factor = 1.0 / 64.0

    grad = to_all(out_grad.reshape(C, n_pos), "ch", 16).reshape(CH, n_pos)
    pre = pre_act.reshape(C, n_pos)
    pre_line = to_all(pre, LINE, 8)
    full_in = to_all(inputs.reshape(C, n_pos), "ch", 16).reshape(CH, n_pos)
    w_two = weight_two.reshape(ROWS, CH)
    w_one = weight_one.reshape(ROWS, CH).T

    wide = (NXL + 2) * SLAB
    own, over = call(
        act_grad_body,
        (jax.ShapeDtypeStruct((C, wide), F32), jax.ShapeDtypeStruct((C, wide), F32)),
        [pltpu.VMEM((3, 3 * C, wide), F32)],
        2,
    )(ids, w_two, grad)
    own = own + lax.ppermute(over, "sy", [(0, 1), (1, 0)])
    to_left = lax.ppermute(own[:, :SLAB], "sx", [(i + 1, i) for i in range(3)])
    to_right = lax.ppermute(own[:, wide - SLAB :], "sx", [(i, i + 1) for i in range(3)])

    filter_outs = (
        jax.ShapeDtypeStruct((ROWSP, HALF), F32),
        jax.ShapeDtypeStruct((ROWSP, HALF), BF),
    )
    stack = pltpu.VMEM((ROWS, n_pos), BF)
    keep2, send2 = call(functools.partial(filter_body, True, False), filter_outs, [stack], 2)(
        ids, pre_line, grad
    )
    chip2 = chip_sum(keep2, send2)

    mid = own[:, SLAB : wide - SLAB]
    mid = jnp.concatenate(
        [mid[:, :SLAB] + to_right, mid[:, SLAB:-SLAB], mid[:, -SLAB:] + to_left], axis=1
    )
    delta = jnp.where(pre > 0, mid, 0.0).astype(BF)
    delta_line = to_all(delta, LINE, 8)
    block2 = line_sum(chip2, factor)

    keep1, send1 = call(functools.partial(filter_body, False, True), filter_outs, [stack], 2)(
        ids, delta_line, full_in
    )
    chip1 = chip_sum(keep1, send1)
    terms = call(data_body, jax.ShapeDtypeStruct((CH, n_pos), BF), [stack], 2)(
        ids, delta_line, w_one
    )
    filter_two = spread(block2, core)
    block1 = line_sum(chip1, factor)
    got = lax.all_to_all(terms.reshape(16, C, n_pos), "ch", 0, 0, tiled=True)
    input_grad = got.astype(F32).sum(axis=0).astype(BF).reshape(shape)
    filter_one = spread(block1, core)
    return input_grad, filter_one, filter_two


def solution(mesh):
    field = P("ch", "sx", "sy", None)
    filt = P(None, "ch", None)
    return jax.shard_map(
        shards,
        mesh=mesh,
        in_specs=(field, field, field, filt, filt),
        out_specs=(field, filt, filt),
        check_vma=False,
    )
```

profile of v0, /device:TPU:1, one launch (start us, length us, event | category | flops | bytes accessed | tf_op | source)
XLA Modules:
  0.0 184.0 jit_solution(2310033447121641550)
XLA Ops:
  2.8 8.6 %all-to-all-start = ((bf16[16,48,512]{2,1,0:T(8,128)(2,1)}), bf16[16,48,512]{2,1,0:T(8,128)(2,1)S(1)}, u32[]{:S(2)}, u32[]{:S(2)}) async-start(bf16[16,48,512]{2,1,0:T(8,128)(2,1)} %broadcast_in_dim.21), calls=%async_computation | async-start | bytes 1572864 | tf_op jit(solution)/shard_map/all_to_all | solution.py:147
  11.5 13.0 %all-to-all-done = bf16[16,48,512]{2,1,0:T(8,128)(2,1)S(1)} async-done(((bf16[16,48,512]{2,1,0:T(8,128)(2,1)}), bf16[16,48,512]{2,1,0:T(8,128)(2,1)S(1)}, u32[]{:S(2)}, u32[]{:S(2)}) %all-to-all-start) | async-done | bytes 786464 | tf_op jit(solution)/shard_map/all_to_all | solution.py:147
  25.3 6.6 %all-to-all-start.6 = ((bf16[8,48,512]{2,1,0:T(8,128)(2,1)}), bf16[8,48,512]{2,1,0:T(8,128)(2,1)S(1)}, u32[]{:S(2)}, u32[]{:S(2)}) async-start(bf16[8,48,512]{2,1,0:T(8,128)(2,1)} %broadcast_in_dim.48), calls=%async_computation.6 | async-start | bytes 786432 | tf_op jit(solution)/shard_map/all_to_all | solution.py:147
  32.0 2.0 %shard_map.76 = (f32[48,768]{1,0:T(8,128)S(1)}, f32[48,768]{1,0:T(8,128)S(1)}) custom-call(s32[3]{0:T(128)S(1)} %pad_add_fusion.ids, bf16[1296,768]{1,0:T(8,128)(2,1)S(1)} %bitcast.21, bf16[768,512]{1,0:T(8,128)(2,1)S(1)} %bitcast.18), custom_call_target="tpu_custom_call" | custom-call | tf_op jit(solution)/shard_map/pallas_call | solution.py:185
  34.0 3.0 %collective-permute-start = (f32[48,768]{1,0:T(8,128)S(1)}, f32[48,768]{1,0:T(8,128)S(1)}, u32[]{:S(2)}, u32[]{:S(2)}) collective-permute-start(f32[48,768]{1,0:T(8,128)S(1)} %get-tuple-element.10), channel_id=1, source_target_pairs={{0,1},{1,0},{2,3},{3,2},{4,5},{5,4},{6,7},{7,6},{8,9},{9,8},{10,11... | collective-permute-start | bytes 442376 | tf_op jit(solution)/shard_map/ppermute | solution.py:191
  38.0 2.1 %all-to-all-done.6.line_ref = bf16[8,48,512]{2,1,0:T(8,128)(2,1)S(1)} async-done(((bf16[8,48,512]{2,1,0:T(8,128)(2,1)}), bf16[8,48,512]{2,1,0:T(8,128)(2,1)S(1)}, u32[]{:S(2)}, u32[]{:S(2)}) %all-to-all-start.6) | async-done | bytes 393248 | tf_op jit(solution)/shard_map/all_to_all | solution.py:147
  41.0 3.6 %all-to-all-start.3 = ((bf16[16,48,512]{2,1,0:T(8,128)(2,1)}), bf16[16,48,512]{2,1,0:T(8,128)(2,1)S(1)}, u32[]{:S(2)}, u32[]{:S(2)}) async-start(bf16[16,48,512]{2,1,0:T(8,128)(2,1)} %broadcast_in_dim.46), calls=%async_computation.3 | async-start | bytes 1572864 | tf_op jit(solution)/shard_map/all_to_all | solution.py:147
  44.7 1.9 %collective-permute-start.1 = (f32[48,128]{1,0:T(8,128)S(1)}, f32[48,128]{1,0:T(8,128)S(1)}, u32[]{:S(2)}, u32[]{:S(2)}) collective-permute-start(f32[48,128]{1,0:T(8,128)S(1)} %get-tuple-element.21), channel_id=1, source_target_pairs={{0,2},{2,4},{4,6},{1,3},{3,5},{5,7},{8,10},{10,12},{12,14},{9,11},... | collective-permute-start | bytes 73736 | tf_op jit(solution)/shard_map/ppermute | solution.py:193
  46.6 2.4 %collective-permute-start.2 = (f32[48,128]{1,0:T(8,128)S(1)}, f32[48,128]{1,0:T(8,128)S(1)}, u32[]{:S(2)}, u32[]{:S(2)}) collective-permute-start(f32[48,128]{1,0:T(8,128)S(1)} %get-tuple-element.22), channel_id=1, source_target_pairs={{2,0},{4,2},{6,4},{3,1},{5,3},{7,5},{10,8},{12,10},{14,12},{11,9},... | collective-permute-start | bytes 73736 | tf_op jit(solution)/shard_map/ppermute | solution.py:192
  49.0 3.9 %shard_map.79 = (f32[1344,384]{1,0:T(8,128)S(1)}, bf16[1344,384]{1,0:T(8,128)(2,1)}) custom-call(s32[3]{0:T(128)S(1)} %pad_add_fusion.ids, bf16[8,48,512]{2,1,0:T(8,128)(2,1)S(1)} %all-to-all-done.6.line_ref, bf16[768,512]{1,0:T(8,128)(2,1)S(1)} %bitcast.19), custom_call_target="tpu_custom_call" | custom-call | tf_op jit(solution)/shard_map/pallas_call | solution.py:200
  54.3 4.5 %all-to-all-done.3 = bf16[16,48,512]{2,1,0:T(8,128)(2,1)S(1)} async-done(((bf16[16,48,512]{2,1,0:T(8,128)(2,1)}), bf16[16,48,512]{2,1,0:T(8,128)(2,1)S(1)}, u32[]{:S(2)}, u32[]{:S(2)}) %all-to-all-start.3) | async-done | bytes 786464 | tf_op jit(solution)/shard_map/all_to_all | solution.py:147
  58.8 11.9 %all_to_all.45.line_ref = bf16[8,48,512]{2,1,0:T(8,128)(2,1)S(1)} all-to-all(bf16[8,48,512]{2,1,0:T(8,128)(2,1)S(1)} %broadcast_in_dim.44), channel_id=1, replica_groups=mesh['ch'=16,'sx'=4,'sy'=2] {'sx','sy'}, dimensions={0} | all-to-all | bytes 786432 | tf_op jit(solution)/shard_map/all_to_all | solution.py:147
  70.7 3.9 %shard_map.78 = (f32[1344,384]{1,0:T(8,128)S(1)}, bf16[1344,384]{1,0:T(8,128)(2,1)}) custom-call(s32[3]{0:T(128)S(1)} %pad_add_fusion.ids, bf16[8,48,512]{2,1,0:T(8,128)(2,1)S(1)} %all_to_all.45.line_ref, bf16[768,512]{1,0:T(8,128)(2,1)S(1)} %bitcast.20), custom_call_target="tpu_custom_call" | custom-call | tf_op jit(solution)/shard_map/pallas_call | solution.py:213
  76.2 4.4 %all-to-all-start.7 = ((bf16[4,336,384]{2,1,0:T(8,128)(2,1)}), bf16[4,336,384]{2,1,0:T(8,128)(2,1)}, u32[]{:S(2)}, u32[]{:S(2)}) async-start(bf16[4,336,384]{2,1,0:T(8,128)(2,1)} %bitcast.13), calls=%async_computation.7 | async-start | bytes 2064384 | tf_op jit(solution)/shard_map/all_to_all | solution.py:156
  80.6 2.5 %add_convert_fusion.1 = bf16[1344,384]{1,0:T(8,128)(2,1)} fusion(f32[1344,384]{1,0:T(8,128)S(1)} %copy-done.3, bf16[1344,384]{1,0:T(8,128)(2,1)} %collective-permute-done.3), kind=kLoop, calls=%fused_computation.3 | loop fusion | flops 1548288 | bytes 4128768 | tf_op jit(solution)/shard_map/convert_element_type | solution.py:152
  83.1 12.3 %all-to-all-done.7 = bf16[4,336,384]{2,1,0:T(8,128)(2,1)} async-done(((bf16[4,336,384]{2,1,0:T(8,128)(2,1)}), bf16[4,336,384]{2,1,0:T(8,128)(2,1)}, u32[]{:S(2)}, u32[]{:S(2)}) %all-to-all-start.7) | async-done | bytes 1032224 | tf_op jit(solution)/shard_map/all_to_all | solution.py:156
  95.4 3.5 %all-to-all-start.4 = ((bf16[4,336,384]{2,1,0:T(8,128)(2,1)}), bf16[4,336,384]{2,1,0:T(8,128)(2,1)S(1)}, u32[]{:S(2)}, u32[]{:S(2)}) async-start(bf16[4,336,384]{2,1,0:T(8,128)(2,1)} %bitcast.9), calls=%async_computation.4 | async-start | bytes 2064384 | tf_op jit(solution)/shard_map/all_to_all | solution.py:156
  98.9 1.4 convert_reduce_fusion
  100.4 12.3 %all-to-all-done.4 = bf16[4,336,384]{2,1,0:T(8,128)(2,1)S(1)} async-done(((bf16[4,336,384]{2,1,0:T(8,128)(2,1)}), bf16[4,336,384]{2,1,0:T(8,128)(2,1)S(1)}, u32[]{:S(2)}, u32[]{:S(2)}) %all-to-all-start.4) | async-done | bytes 1032224 | tf_op jit(solution)/shard_map/all_to_all | solution.py:156
  113.8 3.5 %all-to-all-start.8 = ((bf16[4,336,384]{2,1,0:T(8,128)(2,1)}), bf16[4,336,384]{2,1,0:T(8,128)(2,1)S(1)}, u32[]{:S(2)}, u32[]{:S(2)}) async-start(bf16[4,336,384]{2,1,0:T(8,128)(2,1)} %broadcast_in_dim.49), calls=%async_computation.8 | async-start | bytes 2064384 | tf_op jit(solution)/shard_map/all_to_all | solution.py:147
  117.5 12.7 %all-to-all-done.8 = bf16[4,336,384]{2,1,0:T(8,128)(2,1)S(1)} async-done(((bf16[4,336,384]{2,1,0:T(8,128)(2,1)}), bf16[4,336,384]{2,1,0:T(8,128)(2,1)S(1)}, u32[]{:S(2)}, u32[]{:S(2)}) %all-to-all-start.8) | async-done | bytes 1032224 | tf_op jit(solution)/shard_map/all_to_all | solution.py:147
  131.3 3.5 %all-to-all-start.5 = ((bf16[4,336,384]{2,1,0:T(8,128)(2,1)}), bf16[4,336,384]{2,1,0:T(8,128)(2,1)S(1)}, u32[]{:S(2)}, u32[]{:S(2)}) async-start(bf16[4,336,384]{2,1,0:T(8,128)(2,1)} %broadcast_in_dim.47), calls=%async_computation.5 | async-start | bytes 2064384 | tf_op jit(solution)/shard_map/all_to_all | solution.py:147
  135.9 3.0 %collective-permute-start.6 = (bf16[1296,384]{1,0:T(8,128)(2,1)}, bf16[1296,384]{1,0:T(8,128)(2,1)}, u32[]{:S(2)}, u32[]{:S(2)}) collective-permute-start(bf16[1296,384]{1,0:T(8,128)(2,1)} %slice.38), channel_id=1, source_target_pairs={{0,2},{2,0},{4,6},{6,4},{1,3},{3,1},{5,7},{7,5},{8,10},{10,8},{12,... | collective-permute-start | bytes 2985992 | tf_op jit(solution)/shard_map/ppermute | solution.py:162
  138.9 7.7 %all-to-all-done.5 = bf16[4,336,384]{2,1,0:T(8,128)(2,1)S(1)} async-done(((bf16[4,336,384]{2,1,0:T(8,128)(2,1)}), bf16[4,336,384]{2,1,0:T(8,128)(2,1)S(1)}, u32[]{:S(2)}, u32[]{:S(2)}) %all-to-all-start.5) | async-done | bytes 1032224 | tf_op jit(solution)/shard_map/all_to_all | solution.py:147
  147.7 4.2 %collective-permute-start.4 = (bf16[1296,384]{1,0:T(8,128)(2,1)}, bf16[1296,384]{1,0:T(8,128)(2,1)}, u32[]{:S(2)}, u32[]{:S(2)}) collective-permute-start(bf16[1296,384]{1,0:T(8,128)(2,1)} %slice.37), channel_id=1, source_target_pairs={{0,2},{2,0},{4,6},{6,4},{1,3},{3,1},{5,7},{7,5},{8,10},{10,8},{12,... | collective-permute-start | bytes 2985992 | tf_op jit(solution)/shard_map/ppermute | solution.py:162
  151.9 2.9 %copy.9 = bf16[1296,768]{0,1:T(8,128)(2,1)S(1)} copy(bf16[1296,768]{1,0:T(8,128)(2,1)} %bitcast.30) | data formatting | bytes 3981312 | tf_op jit(solution)/shard_map/reshape | solution.py:182
  154.8 3.1 %shard_map.77 = bf16[768,512]{1,0:T(8,128)(2,1)} custom-call(s32[3]{0:T(128)S(1)} %pad_add_fusion.ids, bf16[8,48,512]{2,1,0:T(8,128)(2,1)S(1)} %all_to_all.45.line_ref, bf16[768,1296]{1,0:T(8,128)(2,1)S(1)} %bitcast.17), custom_call_target="tpu_custom_call" | custom-call | tf_op jit(solution)/shard_map/pallas_call | solution.py:217
  157.9 3.7 %all-to-all-start.2 = ((bf16[16,48,512]{2,1,0:T(8,128)(2,1)}), bf16[16,48,512]{2,1,0:T(8,128)(2,1)S(1)}, u32[]{:S(2)}, u32[]{:S(2)}) async-start(bf16[16,48,512]{2,1,0:T(8,128)(2,1)} %bitcast.7), calls=%async_computation.2 | async-start | bytes 1572864 | tf_op jit(solution)/shard_map/all_to_all | solution.py:222
  161.6 14.7 %all-to-all-done.2 = bf16[16,48,512]{2,1,0:T(8,128)(2,1)S(1)} async-done(((bf16[16,48,512]{2,1,0:T(8,128)(2,1)}), bf16[16,48,512]{2,1,0:T(8,128)(2,1)S(1)}, u32[]{:S(2)}, u32[]{:S(2)}) %all-to-all-start.2) | async-done | bytes 786464 | tf_op jit(solution)/shard_map/all_to_all | solution.py:222
  177.2 1.9 %broadcast_select_fusion.1 = (bf16[1296,384]{1,0:T(8,128)(2,1)S(1)}, bf16[1296,384]{1,0:T(8,128)(2,1)S(1)}, bf16[1296,384]{1,0:T(8,128)(2,1)S(1)}, bf16[1296,384]{1,0:T(8,128)(2,1)S(1)}) fusion(bf16[1296,384]{1,0:T(8,128)(2,1)} %collective-permute-done.6, pred[]{:T(512)S(6)} %eq.4, bf16[1344,384]{1,0:T(8,128)(2,1)S(1)} %bitcast.23, ...), kind=kLoop, calls=%fused_computation.7 | loop fusion | flops 1990656 | bytes 7962625 | tf_op jit(solution)/shard_map/jit(_where)/select_n | solution.py:163
  179.1 2.4 %maximum_convert_fusion.1 = f32[27,48,768]{2,1,0:T(8,128)} fusion(bf16[27,48,384]{2,1,0:T(8,128)(2,1)S(1)} %bitcast.29, bf16[27,48,384]{2,1,0:T(8,128)(2,1)S(1)} %bitcast.28), kind=kLoop, calls=%fused_computation.5 | loop fusion | flops 3981312 | bytes 5971968 | tf_op jit(solution)/shard_map/convert_element_type | solution.py:165
  181.5 2.4 %maximum_convert_fusion = f32[27,48,768]{2,1,0:T(8,128)} fusion(bf16[27,48,384]{2,1,0:T(8,128)(2,1)S(1)} %bitcast.26, bf16[27,48,384]{2,1,0:T(8,128)(2,1)S(1)} %bitcast.27), kind=kLoop, calls=%fused_computation.4 | loop fusion | flops 3981312 | bytes 5971968 | tf_op jit(solution)/shard_map/convert_element_type | solution.py:165
  (52 shorter events, 13.7 us)
Async XLA Ops:
  0.6 10.8 %copy-start.9 = (bf16[48,4,2,64]{3,2,1,0:T(2,128)(2,1)S(1)}, bf16[48,4,2,64]{3,2,1,0:T(2,128)(2,1)}, u32[]{:S(2)}) copy-start(bf16[48,4,2,64]{3,2,1,0:T(2,128)(2,1)} %param.6) | copy-start | bytes 147460
  0.6 31.4 %copy-start.4 = (bf16[27,48,768]{2,1,0:T(8,128)(2,1)S(1)}, bf16[27,48,768]{2,1,0:T(8,128)(2,1)}, u32[]{:S(2)}) copy-start(bf16[27,48,768]{2,1,0:T(8,128)(2,1)} %param.9) | copy-start | bytes 5971972
  2.8 21.8 %all-to-all-start = ((bf16[16,48,512]{2,1,0:T(8,128)(2,1)}), bf16[16,48,512]{2,1,0:T(8,128)(2,1)S(1)}, u32[]{:S(2)}, u32[]{:S(2)}) async-start(bf16[16,48,512]{2,1,0:T(8,128)(2,1)} %broadcast_in_dim.21), calls=%async_computation | async-start | bytes 1572864 | tf_op jit(solution)/shard_map/all_to_all | solution.py:147
  25.3 14.7 %all-to-all-start.6 = ((bf16[8,48,512]{2,1,0:T(8,128)(2,1)}), bf16[8,48,512]{2,1,0:T(8,128)(2,1)S(1)}, u32[]{:S(2)}, u32[]{:S(2)}) async-start(bf16[8,48,512]{2,1,0:T(8,128)(2,1)} %broadcast_in_dim.48), calls=%async_computation.6 | async-start | bytes 786432 | tf_op jit(solution)/shard_map/all_to_all | solution.py:147
  34.0 10.7 %collective-permute-start = (f32[48,768]{1,0:T(8,128)S(1)}, f32[48,768]{1,0:T(8,128)S(1)}, u32[]{:S(2)}, u32[]{:S(2)}) collective-permute-start(f32[48,768]{1,0:T(8,128)S(1)} %get-tuple-element.10), channel_id=1, source_target_pairs={{0,1},{1,0},{2,3},{3,2},{4,5},{5,4},{6,7},{7,6},{8,9},{9,8},{10,11... | collective-permute-start | bytes 442376 | tf_op jit(solution)/shard_map/ppermute | solution.py:191
  41.0 17.8 %all-to-all-start.3 = ((bf16[16,48,512]{2,1,0:T(8,128)(2,1)}), bf16[16,48,512]{2,1,0:T(8,128)(2,1)S(1)}, u32[]{:S(2)}, u32[]{:S(2)}) async-start(bf16[16,48,512]{2,1,0:T(8,128)(2,1)} %broadcast_in_dim.46), calls=%async_computation.3 | async-start | bytes 1572864 | tf_op jit(solution)/shard_map/all_to_all | solution.py:147
  44.7 9.5 %collective-permute-start.1 = (f32[48,128]{1,0:T(8,128)S(1)}, f32[48,128]{1,0:T(8,128)S(1)}, u32[]{:S(2)}, u32[]{:S(2)}) collective-permute-start(f32[48,128]{1,0:T(8,128)S(1)} %get-tuple-element.21), channel_id=1, source_target_pairs={{0,2},{2,4},{4,6},{1,3},{3,5},{5,7},{8,10},{10,12},{12,14},{9,11},... | collective-permute-start | bytes 73736 | tf_op jit(solution)/shard_map/ppermute | solution.py:193
  46.6 7.6 %collective-permute-start.2 = (f32[48,128]{1,0:T(8,128)S(1)}, f32[48,128]{1,0:T(8,128)S(1)}, u32[]{:S(2)}, u32[]{:S(2)}) collective-permute-start(f32[48,128]{1,0:T(8,128)S(1)} %get-tuple-element.22), channel_id=1, source_target_pairs={{2,0},{4,2},{6,4},{3,1},{5,3},{7,5},{10,8},{12,10},{14,12},{11,9},... | collective-permute-start | bytes 73736 | tf_op jit(solution)/shard_map/ppermute | solution.py:192
  52.9 1.3 copy-start
  54.2 20.7 %collective-permute-start.5 = (bf16[1344,384]{1,0:T(8,128)(2,1)}, bf16[1344,384]{1,0:T(8,128)(2,1)S(1)}, u32[]{:S(2)}, u32[]{:S(2)}) collective-permute-start(bf16[1344,384]{1,0:T(8,128)(2,1)} %get-tuple-element.14), channel_id=1, source_target_pairs={{0,2},{2,0},{4,6},{6,4},{1,3},{3,1},{5,7},{7,5},{8,10},{10,8},{12,... | collective-permute-start | bytes 3096584 | tf_op jit(solution)/shard_map/ppermute | solution.py:151
  58.8 16.0 %copy-start.1 = (f32[1344,384]{1,0:T(8,128)S(1)}, f32[1344,384]{1,0:T(8,128)}, u32[]{:S(2)}) copy-start(f32[1344,384]{1,0:T(8,128)} %copy-done) | copy-start | bytes 6193156
  74.6 1.6 copy-start.2
  74.6 6.0 %collective-permute-start.3 = (bf16[1344,384]{1,0:T(8,128)(2,1)}, bf16[1344,384]{1,0:T(8,128)(2,1)}, u32[]{:S(2)}, u32[]{:S(2)}) collective-permute-start(bf16[1344,384]{1,0:T(8,128)(2,1)} %get-tuple-element.12), channel_id=1, source_target_pairs={{0,2},{2,0},{4,6},{6,4},{1,3},{3,1},{5,7},{7,5},{8,10},{10,8},{12,... | collective-permute-start | bytes 3096584 | tf_op jit(solution)/shard_map/ppermute | solution.py:151
  76.2 4.4 %copy-start.3 = (f32[1344,384]{1,0:T(8,128)S(1)}, f32[1344,384]{1,0:T(8,128)}, u32[]{:S(2)}) copy-start(f32[1344,384]{1,0:T(8,128)} %copy-done.2) | copy-start | bytes 6193156
  76.2 19.2 %all-to-all-start.7 = ((bf16[4,336,384]{2,1,0:T(8,128)(2,1)}), bf16[4,336,384]{2,1,0:T(8,128)(2,1)}, u32[]{:S(2)}, u32[]{:S(2)}) async-start(bf16[4,336,384]{2,1,0:T(8,128)(2,1)} %bitcast.13), calls=%async_computation.7 | async-start | bytes 2064384 | tf_op jit(solution)/shard_map/all_to_all | solution.py:156
  95.4 17.3 %all-to-all-start.4 = ((bf16[4,336,384]{2,1,0:T(8,128)(2,1)}), bf16[4,336,384]{2,1,0:T(8,128)(2,1)S(1)}, u32[]{:S(2)}, u32[]{:S(2)}) async-start(bf16[4,336,384]{2,1,0:T(8,128)(2,1)} %bitcast.9), calls=%async_computation.4 | async-start | bytes 2064384 | tf_op jit(solution)/shard_map/all_to_all | solution.py:156
  113.8 16.4 %all-to-all-start.8 = ((bf16[4,336,384]{2,1,0:T(8,128)(2,1)}), bf16[4,336,384]{2,1,0:T(8,128)(2,1)S(1)}, u32[]{:S(2)}, u32[]{:S(2)}) async-start(bf16[4,336,384]{2,1,0:T(8,128)(2,1)} %broadcast_in_dim.49), calls=%async_computation.8 | async-start | bytes 2064384 | tf_op jit(solution)/shard_map/all_to_all | solution.py:147
  130.2 5.7 %copy-start.5 = (bf16[4,336,384]{2,1,0:T(8,128)(2,1)}, bf16[4,336,384]{2,1,0:T(8,128)(2,1)S(1)}, u32[]{:S(2)}) copy-start(bf16[4,336,384]{2,1,0:T(8,128)(2,1)S(1)} %all-to-all-done.8) | copy-start | bytes 3096580
  131.3 15.2 %all-to-all-start.5 = ((bf16[4,336,384]{2,1,0:T(8,128)(2,1)}), bf16[4,336,384]{2,1,0:T(8,128)(2,1)S(1)}, u32[]{:S(2)}, u32[]{:S(2)}) async-start(bf16[4,336,384]{2,1,0:T(8,128)(2,1)} %broadcast_in_dim.47), calls=%async_computation.5 | async-start | bytes 2064384 | tf_op jit(solution)/shard_map/all_to_all | solution.py:147
  135.9 41.3 %collective-permute-start.6 = (bf16[1296,384]{1,0:T(8,128)(2,1)}, bf16[1296,384]{1,0:T(8,128)(2,1)}, u32[]{:S(2)}, u32[]{:S(2)}) collective-permute-start(bf16[1296,384]{1,0:T(8,128)(2,1)} %slice.38), channel_id=1, source_target_pairs={{0,2},{2,0},{4,6},{6,4},{1,3},{3,1},{5,7},{7,5},{8,10},{10,8},{12,... | collective-permute-start | bytes 2985992 | tf_op jit(solution)/shard_map/ppermute | solution.py:162
  146.5 5.3 %copy-start.7 = (bf16[4,336,384]{2,1,0:T(8,128)(2,1)}, bf16[4,336,384]{2,1,0:T(8,128)(2,1)S(1)}, u32[]{:S(2)}) copy-start(bf16[4,336,384]{2,1,0:T(8,128)(2,1)S(1)} %all-to-all-done.5) | copy-start | bytes 3096580
  147.7 29.5 %collective-permute-start.4 = (bf16[1296,384]{1,0:T(8,128)(2,1)}, bf16[1296,384]{1,0:T(8,128)(2,1)}, u32[]{:S(2)}, u32[]{:S(2)}) collective-permute-start(bf16[1296,384]{1,0:T(8,128)(2,1)} %slice.37), channel_id=1, source_target_pairs={{0,2},{2,0},{4,6},{6,4},{1,3},{3,1},{5,7},{7,5},{8,10},{10,8},{12,... | collective-permute-start | bytes 2985992 | tf_op jit(solution)/shard_map/ppermute | solution.py:162
  157.9 19.4 %copy-start.6 = (bf16[4,336,384]{2,1,0:T(8,128)(2,1)S(1)}, bf16[4,336,384]{2,1,0:T(8,128)(2,1)}, u32[]{:S(2)}) copy-start(bf16[4,336,384]{2,1,0:T(8,128)(2,1)} %copy-done.5) | copy-start | bytes 3096580
  157.9 19.4 %copy-start.8 = (bf16[4,336,384]{2,1,0:T(8,128)(2,1)S(1)}, bf16[4,336,384]{2,1,0:T(8,128)(2,1)}, u32[]{:S(2)}) copy-start(bf16[4,336,384]{2,1,0:T(8,128)(2,1)} %copy-done.7) | copy-start | bytes 3096580
  157.9 18.5 %all-to-all-start.2 = ((bf16[16,48,512]{2,1,0:T(8,128)(2,1)}), bf16[16,48,512]{2,1,0:T(8,128)(2,1)S(1)}, u32[]{:S(2)}, u32[]{:S(2)}) async-start(bf16[16,48,512]{2,1,0:T(8,128)(2,1)} %bitcast.7), calls=%async_computation.2 | async-start | bytes 1572864 | tf_op jit(solution)/shard_map/all_to_all | solution.py:222
where the time goes:
time: 185 us; the launch traced here: 184 us
  waiting for transfers between devices  79.5 us (43%)
  starting transfers between devices  52.2 us (28%)
  local copies, waits for them, and re-layouts  14.4 us (8%)
  Pallas kernels  12.8 us (7%)
  other arithmetic  12.4 us (7%)
  blocking collectives  11.9 us (6%)
    all_to_all x5, waiting for transfers between devices, to_all(): lax.all_to_all(many, axis, 0, 0, tiled=True, axis_index_groups=groups)  40 us
    all_to_all x5, starting transfers between devices, to_all(): lax.all_to_all(many, axis, 0, 0, tiled=True, axis_index_groups=groups)  25.8 us
    all_to_all x2, waiting for transfers between devices, line_sum(): lax.all_to_all(part, LINE, 0, 0, tiled=True, axis_index_groups=SAME_CORE)  24.7 us
    all_to_all x1, waiting for transfers between devices, shards(): got = lax.all_to_all(terms.reshape(16, C, n_pos), 'ch', 0, 0, tiled=True)  14.7 us
    all_to_all x1, blocking collectives, to_all(): lax.all_to_all(many, axis, 0, 0, tiled=True, axis_index_groups=groups)  11.9 us
    all_to_all x2, starting transfers between devices, line_sum(): lax.all_to_all(part, LINE, 0, 0, tiled=True, axis_index_groups=SAME_CORE)  7.89 us
    ppermute x2, starting transfers between devices, spread(): other = lax.ppermute(mine, LINE, OTHER_CORE)  7.12 us
    broadcast_in_dim x8, local copies, waits for them, and re-layouts, to_all(): many = jnp.broadcast_to(x[None], (count,) + x.shape)  7.08 us
  transfers between devices with their start and end apart: 15, of which 8 were waited for; matrix products, arithmetic and copies ran while one was open for 7% of the time, Pallas kernels for 7%

commit v1 on v0

--- a/solution.py
+++ b/solution.py
@@ -19,13 +19,13 @@
 ROWS = OFF * C
 ROWSP = OFFP * C
 HALF = CH // 2
+BLOCK = ROWSP // 4
 
 
 def place(chip, core):
     return ((chip % 2) * 2 + core) * 2 + chip // 2
 
 
-SAME_CORE = [[place(chip, core) for chip in range(4)] for core in range(2)]
 OTHER_CORE = [(place(x, c), place(x, 1 - c)) for x in range(4) for c in range(2)]
 
 
@@ -96,9 +96,15 @@
     return lax.dot_general(left, right, (((1,), (1,)), ((), ())), preferred_element_type=F32)
 
 
-def act_grad_body(ids, w_ref, g_ref, own_ref, send_ref, u_ref):
+def take(both_ref, first, field_ref):
+    for k in range(16):
+        field_ref[k * C : (k + 1) * C, :] = both_ref[k, first : first + C, :]
+
+
+def act_grad_body(ids, w_ref, both_ref, own_ref, send_ref, field_ref, u_ref):
     sy = ids[1]
-    grad = g_ref[...]
+    take(both_ref, 0, field_ref)
+    grad = field_ref[...]
     u_ref[...] = jnp.zeros_like(u_ref)
     for a in range(3):
         for b in range(3):
@@ -120,8 +126,11 @@
         )
 
 
-def filter_body(act, mirror, ids, line_ref, full_ref, keep_ref, send_ref, stack_ref):
+def filter_body(
+    act, mirror, first, ids, line_ref, both_ref, keep_ref, send_ref, full_ref, stack_ref
+):
     sx, sy, core = ids[0], ids[1], ids[2]
+    take(both_ref, first, full_ref)
     fill_windows(line_ref, stack_ref, sx, sy, mirror, act)
     mine = full_ref[pl.ds(pl.multiple_of(core * HALF, HALF), HALF), :]
     other = full_ref[pl.ds(pl.multiple_of((1 - core) * HALF, HALF), HALF), :]
@@ -142,53 +151,97 @@
         ).astype(BF)
 
 
-def to_all(x, axis, count, groups=None):
+def to_all(x, axis, count):
     many = jnp.broadcast_to(x[None], (count,) + x.shape)
-    return lax.all_to_all(many, axis, 0, 0, tiled=True, axis_index_groups=groups)
-
-
-def chip_sum(keep, send):
-    got = lax.ppermute(send, LINE, OTHER_CORE)
-    return (keep + got.astype(F32)).astype(BF).reshape(4, ROWSP // 4, HALF)
-
-
-def line_sum(part, factor):
-    got = lax.all_to_all(part, LINE, 0, 0, tiled=True, axis_index_groups=SAME_CORE)
-    return (got.astype(F32).sum(axis=0) * factor).astype(BF)
-
-
-def spread(block, core):
-    mine = to_all(block, LINE, 4, SAME_CORE).reshape(ROWSP, HALF)[:ROWS]
-    other = lax.ppermute(mine, LINE, OTHER_CORE)
-    first = jnp.where(core == 0, mine, other)
-    second = jnp.where(core == 0, other, mine)
-    both = jnp.concatenate([first, second], axis=1).astype(F32)
-    return both.reshape(OFF, C, CH)
+    return lax.all_to_all(many, axis, 0, 0, tiled=True)
+
+
+def split_body(ids, keep_ref, got_ref, own_ref, *send_refs):
+    chip = ids[3]
+    for k in range(4):
+        at = pl.ds(pl.multiple_of(((chip + k) % 4) * BLOCK, BLOCK), BLOCK)
+        total = keep_ref[at, :] + got_ref[at, :].astype(F32)
+        if k == 0:
+            own_ref[...] = total
+        else:
+            send_refs[k - 1][...] = total.astype(BF)
+
+
+def along(shift):
+    return [(place(x, c), place((x + shift) % 4, c)) for x in range(4) for c in range(2)]
+
+
+def chip_split(ids, keep, got):
+    outs = [jax.ShapeDtypeStruct((BLOCK, HALF), F32)]
+    outs += [jax.ShapeDtypeStruct((BLOCK, HALF), BF)] * 3
+    return call(split_body, tuple(outs), [], 2)(ids, keep, got)
+
+
+def line_sum(own, one, two, three, factor):
+    got = [lax.ppermute(v, LINE, along(k)) for k, v in ((1, one), (3, three), (2, two))]
+    total = own
+    for v in got:
+        total = total + v.astype(F32)
+    return (total * factor).astype(BF)
+
+
+def line_spread(block):
+    got = {k: lax.ppermute(block, LINE, along(k)) for k in (1, 3, 2)}
+    mine = jnp.concatenate([block, got[1], got[2], got[3]], axis=0)
+    return mine, lax.ppermute(mine, LINE, OTHER_CORE)
+
+
+def write_body(ids, mine_ref, other_ref, out_ref):
+    core = ids[2]
+    mine = mine_ref[0].astype(F32)
+    other = other_ref[0].astype(F32)
+    out_ref[:, :, :HALF] = jnp.where(core == 0, mine, other)
+    out_ref[:, :, HALF:] = jnp.where(core == 0, other, mine)
+
+
+def write(ids, mine, other):
+    shape = (4, OFFP // 4, C, HALF)
+    spec = pl.BlockSpec((1,) + shape[1:], lambda i, ids: ((ids[3] + 4 - i) % 4, 0, 0, 0))
+    return pl.pallas_call(
+        write_body,
+        out_shape=jax.ShapeDtypeStruct((OFF, C, CH), F32),
+        grid_spec=pltpu.PrefetchScalarGridSpec(
+            num_scalar_prefetch=1,
+            grid=(4,),
+            in_specs=[spec, spec],
+            out_specs=pl.BlockSpec((OFFP // 4, C, CH), lambda i, ids: (i, 0, 0)),
+        ),
+        compiler_params=pltpu.CompilerParams(vmem_limit_bytes=32 << 20),
+    )(ids, mine.reshape(shape), other.reshape(shape))
 
 
 def shards(inputs, pre_act, out_grad, weight_one, weight_two):
     shape = pre_act.shape
     sx, sy = lax.axis_index("sx"), lax.axis_index("sy")
     core = sx % 2
-    ids = jnp.stack([sx, sy, core]).astype(jnp.int32)
+    chip = sx // 2 + 2 * sy
+    ids = jnp.stack([sx, sy, core, chip]).astype(jnp.int32)
     n_pos = NXL * SLAB
     factor = 1.0 / 64.0
 
-    grad = to_all(out_grad.reshape(C, n_pos), "ch", 16).reshape(CH, n_pos)
+    both = jnp.concatenate([out_grad.reshape(C, n_pos), inputs.reshape(C, n_pos)], axis=0)
+    both = to_all(both, "ch", 16)
     pre = pre_act.reshape(C, n_pos)
-    pre_line = to_all(pre, LINE, 8)
-    full_in = to_all(inputs.reshape(C, n_pos), "ch", 16).reshape(CH, n_pos)
     w_two = weight_two.reshape(ROWS, CH)
     w_one = weight_one.reshape(ROWS, CH).T
+    both, w_one, pre = lax.optimization_barrier((both, w_one, pre))
+    pre_line = to_all(pre, LINE, 8)
 
     wide = (NXL + 2) * SLAB
+    field = pltpu.VMEM((CH, n_pos), BF)
     own, over = call(
         act_grad_body,
         (jax.ShapeDtypeStruct((C, wide), F32), jax.ShapeDtypeStruct((C, wide), F32)),
-        [pltpu.VMEM((3, 3 * C, wide), F32)],
+        [field, pltpu.VMEM((3, 3 * C, wide), F32)],
         2,
-    )(ids, w_two, grad)
+    )(ids, w_two, both)
     own = own + lax.ppermute(over, "sy", [(0, 1), (1, 0)])
+    own, pre_line = lax.optimization_barrier((own, pre_line))
     to_left = lax.ppermute(own[:, :SLAB], "sx", [(i + 1, i) for i in range(3)])
     to_right = lax.ppermute(own[:, wide - SLAB :], "sx", [(i, i + 1) for i in range(3)])
 
@@ -197,10 +250,10 @@
         jax.ShapeDtypeStruct((ROWSP, HALF), BF),
     )
     stack = pltpu.VMEM((ROWS, n_pos), BF)
-    keep2, send2 = call(functools.partial(filter_body, True, False), filter_outs, [stack], 2)(
-        ids, pre_line, grad
-    )
-    chip2 = chip_sum(keep2, send2)
+    keep2, send2 = call(
+        functools.partial(filter_body, True, False, 0), filter_outs, [field, stack], 2
+    )(ids, pre_line, both)
+    split2 = chip_split(ids, keep2, lax.ppermute(send2, LINE, OTHER_CORE))
 
     mid = own[:, SLAB : wide - SLAB]
     mid = jnp.concatenate(
@@ -208,20 +261,24 @@
     )
     delta = jnp.where(pre > 0, mid, 0.0).astype(BF)
     delta_line = to_all(delta, LINE, 8)
-    block2 = line_sum(chip2, factor)
-
-    keep1, send1 = call(functools.partial(filter_body, False, True), filter_outs, [stack], 2)(
-        ids, delta_line, full_in
-    )
-    chip1 = chip_sum(keep1, send1)
+    block2 = line_sum(*split2, factor)
+
+    keep1, send1 = call(
+        functools.partial(filter_body, False, True, C), filter_outs, [field, stack], 2
+    )(ids, delta_line, both)
+    got1 = lax.ppermute(send1, LINE, OTHER_CORE)
     terms = call(data_body, jax.ShapeDtypeStruct((CH, n_pos), BF), [stack], 2)(
         ids, delta_line, w_one
     )
-    filter_two = spread(block2, core)
-    block1 = line_sum(chip1, factor)
+    terms, got1 = lax.optimization_barrier((terms, got1))
     got = lax.all_to_all(terms.reshape(16, C, n_pos), "ch", 0, 0, tiled=True)
+    split1 = chip_split(ids, keep1, got1)
+    block1 = line_sum(*split1, factor)
+    pair2 = line_spread(block2)
     input_grad = got.astype(F32).sum(axis=0).astype(BF).reshape(shape)
-    filter_one = spread(block1, core)
+    input_grad, block1 = lax.optimization_barrier((input_grad, block1))
+    filter_two = write(ids, *pair2)
+    filter_one = write(ids, *line_spread(block1))
     return input_grad, filter_one, filter_two
 
 

time: 185 us -> 144 us (0.78)
  waiting for transfers between devices: 79.5 us -> 53 us
  blocking collectives: 11.9 us -> 0 us
  other arithmetic: 12.4 us -> 1.72 us
  Pallas kernels: 12.8 us -> 19.9 us
  local copies, waits for them, and re-layouts: 14.4 us -> 17.4 us
  starting transfers between devices: 52.2 us -> 50 us
    all_to_all x7 -> x3, waiting for transfers between devices: 64.7 us -> 21.5 us  [to_all(): return lax.all_to_all(many, axis, 0, 0, tiled=True)]
    ppermute x4 -> x16, waiting for transfers between devices: 0.01 us -> 23.6 us  [the longest x6 17.1 us: line_spread(): got = {k: lax.ppermute(block, LINE, along(k)) for k in (1, 3, 2)}]
    all_to_all x1, waiting for transfers between devices: 14.7 us -> 0.01 us  [shards(): got = lax.all_to_all(terms.reshape(16, C, n_pos), 'ch', 0, 0, tiled=True)]
    all_to_all x7 -> x3, starting transfers between devices: 33.7 us -> 19.5 us  [to_all(): return lax.all_to_all(many, axis, 0, 0, tiled=True)]
    all_to_all x1 -> x0, blocking collectives: 11.9 us -> none  [to_all(): lax.all_to_all(many, axis, 0, 0, tiled=True, axis_index_groups=groups)]
    ppermute x4 -> x16, starting transfers between devices: 7.41 us -> 18.7 us  [the longest x6 7.64 us: line_spread(): got = {k: lax.ppermute(block, LINE, along(k)) for k in (1, 3, 2)}]
    convert_element_type x6 -> x2, other arithmetic: 8.71 us -> 1.36 us  [line_sum(): return (total * factor).astype(BF)]
    pallas_call x2 -> x6, Pallas kernels: 7.71 us -> 14.9 us  [the longest x2 6.05 us: write(): pl.pallas_call(write_body, out_shape=jax.ShapeDtypeStruct((OFF, C, CH), F...]
  transfers between devices with their start and end apart: 15 -> 23, of which waited for: 8 -> 11; matrix products, arithmetic and copies ran while one was open for 7% -> 5% of each run, Pallas kernels for 7% -> 12%
where the time goes in v1:
time: 144 us; the launch traced here: 143 us
  waiting for transfers between devices  53 us (37%)
  starting transfers between devices  50 us (35%)
  Pallas kernels  19.9 us (14%)
  local copies, waits for them, and re-layouts  17.4 us (12%)
  other arithmetic  1.72 us (1%)
    all_to_all x3, waiting for transfers between devices, to_all(): return lax.all_to_all(many, axis, 0, 0, tiled=True)  21.5 us
    all_to_all x3, starting transfers between devices, to_all(): return lax.all_to_all(many, axis, 0, 0, tiled=True)  19.5 us
    ppermute x6, waiting for transfers between devices, line_spread(): got = {k: lax.ppermute(block, LINE, along(k)) for k in (1, 3, 2)}  17.1 us
    ppermute x6, starting transfers between devices, line_spread(): got = {k: lax.ppermute(block, LINE, along(k)) for k in (1, 3, 2)}  7.64 us
    unnamed x17, local copies, waits for them, and re-layouts  7.46 us
    ppermute x6, starting transfers between devices, line_sum(): lax.ppermute(v, LINE, along(k))  7.18 us
    ppermute x6, waiting for transfers between devices, line_sum(): lax.ppermute(v, LINE, along(k))  6.5 us
    pallas_call x2, Pallas kernels, write(): pl.pallas_call(write_body, out_shape=jax.ShapeDtypeStruct((OFF, C, CH), F...  6.05 us
  transfers between devices with their start and end apart: 23, of which 11 were waited for; matrix products, arithmetic and copies ran while one was open for 5% of the time, Pallas kernels for 12%

profile of v1, /device:TPU:1, one launch (start us, length us, event | category | flops | bytes accessed | tf_op | source)
XLA Modules:
  0.0 142.9 jit_solution(4147036583623507683)
XLA Ops:
  4.0 8.6 %all-to-all-start = ((bf16[16,96,512]{2,1,0:T(8,128)(2,1)}), bf16[16,96,512]{2,1,0:T(8,128)(2,1)S(1)}, u32[]{:S(2)}, u32[]{:S(2)}) async-start(bf16[16,96,512]{2,1,0:T(8,128)(2,1)} %broadcast_in_dim.10), calls=%async_computation | async-start | bytes 3145728 | tf_op jit(solution)/shard_map/all_to_all | solution.py:156
  12.8 4.1 %copy.9 = bf16[1296,768]{0,1:T(8,128)(2,1)} copy(bf16[1296,768]{1,0:T(8,128)(2,1)} %bitcast.18) | data formatting | bytes 3981312 | tf_op jit(solution)/shard_map/reshape | solution.py:231
  16.8 18.6 %all-to-all-done.both_ref = bf16[16,96,512]{2,1,0:T(8,128)(2,1)S(1)} async-done(((bf16[16,96,512]{2,1,0:T(8,128)(2,1)}), bf16[16,96,512]{2,1,0:T(8,128)(2,1)S(1)}, u32[]{:S(2)}, u32[]{:S(2)}) %all-to-all-start) | async-done | bytes 1572896 | tf_op jit(solution)/shard_map/all_to_all | solution.py:156
  36.3 6.8 %all-to-all-start.1 = ((bf16[8,48,512]{2,1,0:T(8,128)(2,1)}), bf16[8,48,512]{2,1,0:T(8,128)(2,1)S(1)}, u32[]{:S(2)}, u32[]{:S(2)}) async-start(bf16[8,48,512]{2,1,0:T(8,128)(2,1)} %broadcast_in_dim.11), calls=%async_computation.1 | async-start | bytes 786432 | tf_op jit(solution)/shard_map/all_to_all | solution.py:156
  43.2 1.6 %copy-done.5 = bf16[27,48,768]{2,1,0:T(8,128)(2,1)S(1)} copy-done((bf16[27,48,768]{2,1,0:T(8,128)(2,1)S(1)}, bf16[27,48,768]{2,1,0:T(8,128)(2,1)}, u32[]{:S(2)}) %copy-start.5) | copy-done | bytes 1990680
  44.7 1.9 %shard_map.76 = (f32[48,768]{1,0:T(8,128)S(1)}, f32[48,768]{1,0:T(8,128)S(1)}) custom-call(s32[4]{0:T(128)S(1)} %pad_add_fusion.ids, bf16[1296,768]{1,0:T(8,128)(2,1)S(1)} %bitcast.14, bf16[16,96,512]{2,1,0:T(8,128)(2,1)S(1)} %all-to-all-done.both_ref), custom_call_target="tpu_custom_call" | custom-call | tf_op jit(solution)/shard_map/pallas_call | solution.py:237
  46.7 3.0 %collective-permute-start = (f32[48,768]{1,0:T(8,128)S(1)}, f32[48,768]{1,0:T(8,128)S(1)}, u32[]{:S(2)}, u32[]{:S(2)}) collective-permute-start(f32[48,768]{1,0:T(8,128)S(1)} %get-tuple-element.29), channel_id=1, source_target_pairs={{0,1},{1,0},{2,3},{3,2},{4,5},{5,4},{6,7},{7,6},{8,9},{9,8},{10,11... | collective-permute-start | bytes 442376 | tf_op jit(solution)/shard_map/ppermute | solution.py:243
  49.6 4.7 %collective-permute-done = f32[48,768]{1,0:T(8,128)S(1)} collective-permute-done((f32[48,768]{1,0:T(8,128)S(1)}, f32[48,768]{1,0:T(8,128)S(1)}, u32[]{:S(2)}, u32[]{:S(2)}) %collective-permute-start) | collective-permute-done | bytes 147488 | tf_op jit(solution)/shard_map/ppermute | solution.py:243
  54.4 3.3 %collective-permute-start.1 = (f32[48,128]{1,0:T(8,128)S(1)}, f32[48,128]{1,0:T(8,128)S(1)}, u32[]{:S(2)}, u32[]{:S(2)}) collective-permute-start(f32[48,128]{1,0:T(8,128)S(1)} %get-tuple-element.51), channel_id=1, source_target_pairs={{0,2},{2,4},{4,6},{1,3},{3,5},{5,7},{8,10},{10,12},{12,14},{9,11},... | collective-permute-start | bytes 73736 | tf_op jit(solution)/shard_map/ppermute | solution.py:246
  57.7 1.9 %collective-permute-start.2 = (f32[48,128]{1,0:T(8,128)S(1)}, f32[48,128]{1,0:T(8,128)S(1)}, u32[]{:S(2)}, u32[]{:S(2)}) collective-permute-start(f32[48,128]{1,0:T(8,128)S(1)} %get-tuple-element.52), channel_id=1, source_target_pairs={{2,0},{4,2},{6,4},{3,1},{5,3},{7,5},{10,8},{12,10},{14,12},{11,9},... | collective-permute-start | bytes 73736 | tf_op jit(solution)/shard_map/ppermute | solution.py:245
  59.7 3.2 %collective-permute-done.2 = f32[48,128]{1,0:T(8,128)S(1)} collective-permute-done((f32[48,128]{1,0:T(8,128)S(1)}, f32[48,128]{1,0:T(8,128)S(1)}, u32[]{:S(2)}, u32[]{:S(2)}) %collective-permute-start.2) | collective-permute-done | bytes 24608 | tf_op jit(solution)/shard_map/ppermute | solution.py:245
  63.7 4.1 %all-to-all-start.2 = ((bf16[8,48,512]{2,1,0:T(8,128)(2,1)}), bf16[8,48,512]{2,1,0:T(8,128)(2,1)S(1)}, u32[]{:S(2)}, u32[]{:S(2)}) async-start(bf16[8,48,512]{2,1,0:T(8,128)(2,1)} %broadcast_in_dim.13), calls=%async_computation.2 | async-start | bytes 786432 | tf_op jit(solution)/shard_map/all_to_all | solution.py:156
  67.8 3.8 %shard_map.81 = (f32[1344,384]{1,0:T(8,128)S(1)}, bf16[1344,384]{1,0:T(8,128)(2,1)}) custom-call(s32[4]{0:T(128)S(1)} %pad_add_fusion.ids, bf16[8,48,512]{2,1,0:T(8,128)(2,1)S(1)} %all-to-all-done.1.line_ref, bf16[16,96,512]{2,1,0:T(8,128)(2,1)S(1)} %all-to-all-done.both_ref), custom_call_target="tpu_custom_call" | custom-call | tf_op jit(solution)/shard_map/pallas_call | solution.py:253
  72.9 2.8 %all-to-all-done.2.line_ref = bf16[8,48,512]{2,1,0:T(8,128)(2,1)S(1)} async-done(((bf16[8,48,512]{2,1,0:T(8,128)(2,1)}), bf16[8,48,512]{2,1,0:T(8,128)(2,1)S(1)}, u32[]{:S(2)}, u32[]{:S(2)}) %all-to-all-start.2) | async-done | bytes 393248 | tf_op jit(solution)/shard_map/all_to_all | solution.py:156
  75.7 2.9 %shard_map.78 = (f32[1344,384]{1,0:T(8,128)S(1)}, bf16[1344,384]{1,0:T(8,128)(2,1)S(1)}) custom-call(s32[4]{0:T(128)S(1)} %pad_add_fusion.ids, bf16[8,48,512]{2,1,0:T(8,128)(2,1)S(1)} %all-to-all-done.2.line_ref, bf16[16,96,512]{2,1,0:T(8,128)(2,1)S(1)} %all-to-all-done.both_ref), custom_call_target="tpu_custom_call" | custom-call | tf_op jit(solution)/shard_map/pallas_call | solution.py:266
  80.3 1.6 %copy-done.4 = f32[1344,384]{1,0:T(8,128)S(1)} copy-done((f32[1344,384]{1,0:T(8,128)S(1)}, f32[1344,384]{1,0:T(8,128)}, u32[]{:S(2)}) %copy-start.4) | copy-done | bytes 2064408
  81.9 1.4 shard_map.82
  83.3 2.7 %collective-permute-start.13 = (bf16[336,384]{1,0:T(8,128)(2,1)S(1)}, bf16[336,384]{1,0:T(8,128)(2,1)}, u32[]{:S(2)}, u32[]{:S(2)}) collective-permute-start(bf16[336,384]{1,0:T(8,128)(2,1)S(1)} %get-tuple-element.47), channel_id=1, source_target_pairs={{0,5},{2,7},{4,0},{6,2},{1,4},{3,6},{5,1},{7,3},{8,13},{10,15},{12... | collective-permute-start | bytes 774152 | tf_op jit(solution)/shard_map/ppermute | solution.py:181
  86.3 3.1 %shard_map.77 = bf16[768,512]{1,0:T(8,128)(2,1)} custom-call(s32[4]{0:T(128)S(1)} %pad_add_fusion.ids, bf16[8,48,512]{2,1,0:T(8,128)(2,1)S(1)} %all-to-all-done.2.line_ref, bf16[768,1296]{1,0:T(8,128)(2,1)S(1)} %bitcast.12), custom_call_target="tpu_custom_call" | custom-call | tf_op jit(solution)/shard_map/pallas_call | solution.py:270
  89.4 3.6 %all-to-all-start.3 = ((bf16[16,48,512]{2,1,0:T(8,128)(2,1)}), bf16[16,48,512]{2,1,0:T(8,128)(2,1)S(1)}, u32[]{:S(2)}, u32[]{:S(2)}) async-start(bf16[16,48,512]{2,1,0:T(8,128)(2,1)} %bitcast.7), calls=%async_computation.3 | async-start | bytes 1572864 | tf_op jit(solution)/shard_map/all_to_all | solution.py:274
  93.0 1.6 %copy-done.2 = f32[1344,384]{1,0:T(8,128)S(1)} copy-done((f32[1344,384]{1,0:T(8,128)S(1)}, f32[1344,384]{1,0:T(8,128)}, u32[]{:S(2)}) %copy-start.2) | copy-done | bytes 2064408
  95.6 2.5 %collective-permute-start.5 = (bf16[336,384]{1,0:T(8,128)(2,1)S(1)}, bf16[336,384]{1,0:T(8,128)(2,1)S(1)}, u32[]{:S(2)}, u32[]{:S(2)}) collective-permute-start(bf16[336,384]{1,0:T(8,128)(2,1)S(1)} %get-tuple-element.38), channel_id=1, source_target_pairs={{0,5},{2,7},{4,0},{6,2},{1,4},{3,6},{5,1},{7,3},{8,13},{10,15},{12... | collective-permute-start | bytes 774152 | tf_op jit(solution)/shard_map/ppermute | solution.py:181
  103.5 5.6 %collective-permute-done.6 = bf16[336,384]{1,0:T(8,128)(2,1)S(1)} collective-permute-done((bf16[336,384]{1,0:T(8,128)(2,1)S(1)}, bf16[336,384]{1,0:T(8,128)(2,1)S(1)}, u32[]{:S(2)}, u32[]{:S(2)}) %collective-permute-start.6) | collective-permute-done | bytes 258080 | tf_op jit(solution)/shard_map/ppermute | solution.py:181
  110.8 1.8 %collective-permute-start.7 = (bf16[336,384]{1,0:T(8,128)(2,1)S(1)}, bf16[336,384]{1,0:T(8,128)(2,1)S(1)}, u32[]{:S(2)}, u32[]{:S(2)}) collective-permute-start(bf16[336,384]{1,0:T(8,128)(2,1)S(1)} %multiply_convert_fusion.1), channel_id=1, source_target_pairs={{0,4},{2,6},{4,1},{6,3},{1,5},{3,7},{5,0},{7,2},{8,12},{10,14},{12... | collective-permute-start | bytes 774152 | tf_op jit(solution)/shard_map/ppermute | solution.py:189
  112.5 1.5 %collective-permute-done.17 = bf16[336,384]{1,0:T(8,128)(2,1)S(1)} collective-permute-done((bf16[336,384]{1,0:T(8,128)(2,1)S(1)}, bf16[336,384]{1,0:T(8,128)(2,1)S(1)}, u32[]{:S(2)}, u32[]{:S(2)}) %collective-permute-start.17) | collective-permute-done | bytes 258080 | tf_op jit(solution)/shard_map/ppermute | solution.py:189
  114.7 9.5 %collective-permute-done.15 = bf16[336,384]{1,0:T(8,128)(2,1)S(1)} collective-permute-done((bf16[336,384]{1,0:T(8,128)(2,1)S(1)}, bf16[336,384]{1,0:T(8,128)(2,1)S(1)}, u32[]{:S(2)}, u32[]{:S(2)}) %collective-permute-start.15) | collective-permute-done | bytes 258080 | tf_op jit(solution)/shard_map/ppermute | solution.py:189
  124.3 2.6 %collective-permute-start.18 = (bf16[1344,384]{1,0:T(8,128)(2,1)S(1)}, bf16[1344,384]{1,0:T(8,128)(2,1)S(1)}, u32[]{:S(2)}, u32[]{:S(2)}) collective-permute-start(bf16[1344,384]{1,0:T(8,128)(2,1)S(1)} %pad_maximum_fusion), channel_id=1, source_target_pairs={{0,2},{2,0},{4,6},{6,4},{1,3},{3,1},{5,7},{7,5},{8,10},{10,8},{12,... | collective-permute-start | bytes 3096584 | tf_op jit(solution)/shard_map/ppermute | solution.py:191
  126.9 3.4 %collective-permute-start.9 = (bf16[336,384]{1,0:T(8,128)(2,1)S(1)}, bf16[336,384]{1,0:T(8,128)(2,1)S(1)}, u32[]{:S(2)}, u32[]{:S(2)}) collective-permute-start(bf16[336,384]{1,0:T(8,128)(2,1)S(1)} %multiply_convert_fusion.1), channel_id=1, source_target_pairs={{0,5},{2,7},{4,0},{6,2},{1,4},{3,6},{5,1},{7,3},{8,13},{10,15},{12... | collective-permute-start | bytes 774152 | tf_op jit(solution)/shard_map/ppermute | solution.py:189
  130.3 2.2 %collective-permute-done.7 = bf16[336,384]{1,0:T(8,128)(2,1)S(1)} collective-permute-done((bf16[336,384]{1,0:T(8,128)(2,1)S(1)}, bf16[336,384]{1,0:T(8,128)(2,1)S(1)}, u32[]{:S(2)}, u32[]{:S(2)}) %collective-permute-start.7) | collective-permute-done | bytes 258080 | tf_op jit(solution)/shard_map/ppermute | solution.py:189
  132.6 3.3 %collective-permute-done.9 = bf16[336,384]{1,0:T(8,128)(2,1)S(1)} collective-permute-done((bf16[336,384]{1,0:T(8,128)(2,1)S(1)}, bf16[336,384]{1,0:T(8,128)(2,1)S(1)}, u32[]{:S(2)}, u32[]{:S(2)}) %collective-permute-start.9) | collective-permute-done | bytes 258080 | tf_op jit(solution)/shard_map/ppermute | solution.py:189
  136.8 3.0 %shard_map.83 = f32[27,48,768]{2,1,0:T(8,128)} custom-call(s32[4]{0:T(128)S(1)} %pad_add_fusion.ids, bf16[4,7,48,384]{3,2,1,0:T(8,128)(2,1)S(1)} %bitcast.13, bf16[4,7,48,384]{3,2,1,0:T(8,128)(2,1)S(1)} %bitcast.16), custom_call_target="tpu_custom_call" | custom-call | tf_op jit(solution)/shard_map/pallas_call | solution.py:205
  139.9 3.0 %shard_map.80 = f32[27,48,768]{2,1,0:T(8,128)} custom-call(s32[4]{0:T(128)S(1)} %pad_add_fusion.ids, bf16[4,7,48,384]{3,2,1,0:T(8,128)(2,1)S(1)} %bitcast.15, bf16[4,7,48,384]{3,2,1,0:T(8,128)(2,1)S(1)} %bitcast.17), custom_call_target="tpu_custom_call" | custom-call | tf_op jit(solution)/shard_map/pallas_call | solution.py:205
  (59 shorter events, 18.4 us)
Async XLA Ops:
  2.7 9.9 %copy-start.6 = (bf16[48,4,2,64]{3,2,1,0:T(2,128)(2,1)S(1)}, bf16[48,4,2,64]{3,2,1,0:T(2,128)(2,1)}, u32[]{:S(2)}) copy-start(bf16[48,4,2,64]{3,2,1,0:T(2,128)(2,1)} %param.6) | copy-start | bytes 147460
  4.0 31.5 %all-to-all-start = ((bf16[16,96,512]{2,1,0:T(8,128)(2,1)}), bf16[16,96,512]{2,1,0:T(8,128)(2,1)S(1)}, u32[]{:S(2)}, u32[]{:S(2)}) async-start(bf16[16,96,512]{2,1,0:T(8,128)(2,1)} %broadcast_in_dim.10), calls=%async_computation | async-start | bytes 3145728 | tf_op jit(solution)/shard_map/all_to_all | solution.py:156
  36.3 18.1 %all-to-all-start.1 = ((bf16[8,48,512]{2,1,0:T(8,128)(2,1)}), bf16[8,48,512]{2,1,0:T(8,128)(2,1)S(1)}, u32[]{:S(2)}, u32[]{:S(2)}) async-start(bf16[8,48,512]{2,1,0:T(8,128)(2,1)} %broadcast_in_dim.11), calls=%async_computation.1 | async-start | bytes 786432 | tf_op jit(solution)/shard_map/all_to_all | solution.py:156
  43.2 1.6 %copy-start.5 = (bf16[27,48,768]{2,1,0:T(8,128)(2,1)S(1)}, bf16[27,48,768]{2,1,0:T(8,128)(2,1)}, u32[]{:S(2)}) copy-start(bf16[27,48,768]{2,1,0:T(8,128)(2,1)} %param.9) | copy-start | bytes 5971972
  46.7 7.7 %collective-permute-start = (f32[48,768]{1,0:T(8,128)S(1)}, f32[48,768]{1,0:T(8,128)S(1)}, u32[]{:S(2)}, u32[]{:S(2)}) collective-permute-start(f32[48,768]{1,0:T(8,128)S(1)} %get-tuple-element.29), channel_id=1, source_target_pairs={{0,1},{1,0},{2,3},{3,2},{4,5},{5,4},{6,7},{7,6},{8,9},{9,8},{10,11... | collective-permute-start | bytes 442376 | tf_op jit(solution)/shard_map/ppermute | solution.py:243
  54.4 5.3 %collective-permute-start.1 = (f32[48,128]{1,0:T(8,128)S(1)}, f32[48,128]{1,0:T(8,128)S(1)}, u32[]{:S(2)}, u32[]{:S(2)}) collective-permute-start(f32[48,128]{1,0:T(8,128)S(1)} %get-tuple-element.51), channel_id=1, source_target_pairs={{0,2},{2,4},{4,6},{1,3},{3,5},{5,7},{8,10},{10,12},{12,14},{9,11},... | collective-permute-start | bytes 73736 | tf_op jit(solution)/shard_map/ppermute | solution.py:246
  57.7 5.1 %collective-permute-start.2 = (f32[48,128]{1,0:T(8,128)S(1)}, f32[48,128]{1,0:T(8,128)S(1)}, u32[]{:S(2)}, u32[]{:S(2)}) collective-permute-start(f32[48,128]{1,0:T(8,128)S(1)} %get-tuple-element.52), channel_id=1, source_target_pairs={{2,0},{4,2},{6,4},{3,1},{5,3},{7,5},{10,8},{12,10},{14,12},{11,9},... | collective-permute-start | bytes 73736 | tf_op jit(solution)/shard_map/ppermute | solution.py:245
  63.7 12.0 %all-to-all-start.2 = ((bf16[8,48,512]{2,1,0:T(8,128)(2,1)}), bf16[8,48,512]{2,1,0:T(8,128)(2,1)S(1)}, u32[]{:S(2)}, u32[]{:S(2)}) async-start(bf16[8,48,512]{2,1,0:T(8,128)(2,1)} %broadcast_in_dim.13), calls=%async_computation.2 | async-start | bytes 786432 | tf_op jit(solution)/shard_map/all_to_all | solution.py:156
  71.6 1.3 copy-start.3
  72.9 7.4 %collective-permute-start.11 = (bf16[1344,384]{1,0:T(8,128)(2,1)}, bf16[1344,384]{1,0:T(8,128)(2,1)S(1)}, u32[]{:S(2)}, u32[]{:S(2)}) collective-permute-start(bf16[1344,384]{1,0:T(8,128)(2,1)} %get-tuple-element.44), channel_id=1, source_target_pairs={{0,2},{2,0},{4,6},{6,4},{1,3},{3,1},{5,7},{7,5},{8,10},{10,8},{12,... | collective-permute-start | bytes 3096584 | tf_op jit(solution)/shard_map/ppermute | solution.py:256
  75.7 10.6 %copy-start = (bf16[1296,768]{0,1:T(8,128)(2,1)S(1)}, bf16[1296,768]{0,1:T(8,128)(2,1)}, u32[]{:S(2)}) copy-start(bf16[1296,768]{0,1:T(8,128)(2,1)} %copy.9) | copy-start | bytes 5971972
  78.7 1.3 copy-start.1
  80.0 9.4 %collective-permute-start.3 = (bf16[1344,384]{1,0:T(8,128)(2,1)S(1)}, bf16[1344,384]{1,0:T(8,128)(2,1)S(1)}, u32[]{:S(2)}, u32[]{:S(2)}) collective-permute-start(bf16[1344,384]{1,0:T(8,128)(2,1)S(1)} %get-tuple-element.32), channel_id=1, source_target_pairs={{0,2},{2,0},{4,6},{6,4},{1,3},{3,1},{5,7},{7,5},{8,10},{10,8},{12,... | collective-permute-start | bytes 3096584 | tf_op jit(solution)/shard_map/ppermute | solution.py:269
  80.3 1.6 %copy-start.4 = (f32[1344,384]{1,0:T(8,128)S(1)}, f32[1344,384]{1,0:T(8,128)}, u32[]{:S(2)}) copy-start(f32[1344,384]{1,0:T(8,128)} %copy-done.3) | copy-start | bytes 6193156
  83.3 14.8 %collective-permute-start.12 = (bf16[336,384]{1,0:T(8,128)(2,1)}, bf16[336,384]{1,0:T(8,128)(2,1)S(1)}, u32[]{:S(2)}, u32[]{:S(2)}) collective-permute-start(bf16[336,384]{1,0:T(8,128)(2,1)} %get-tuple-element.46), channel_id=1, source_target_pairs={{0,4},{2,6},{4,1},{6,3},{1,5},{3,7},{5,0},{7,2},{8,12},{10,14},{12... | collective-permute-start | bytes 774152 | tf_op jit(solution)/shard_map/ppermute | solution.py:181
  83.3 16.2 %collective-permute-start.13 = (bf16[336,384]{1,0:T(8,128)(2,1)S(1)}, bf16[336,384]{1,0:T(8,128)(2,1)}, u32[]{:S(2)}, u32[]{:S(2)}) collective-permute-start(bf16[336,384]{1,0:T(8,128)(2,1)S(1)} %get-tuple-element.47), channel_id=1, source_target_pairs={{0,5},{2,7},{4,0},{6,2},{1,4},{3,6},{5,1},{7,3},{8,13},{10,15},{12... | collective-permute-start | bytes 774152 | tf_op jit(solution)/shard_map/ppermute | solution.py:181
  85.9 13.6 %collective-permute-start.14 = (bf16[336,384]{1,0:T(8,128)(2,1)S(1)}, bf16[336,384]{1,0:T(8,128)(2,1)}, u32[]{:S(2)}, u32[]{:S(2)}) collective-permute-start(bf16[336,384]{1,0:T(8,128)(2,1)S(1)} %get-tuple-element.48), channel_id=1, source_target_pairs={{0,1},{2,3},{4,5},{6,7},{1,0},{3,2},{5,4},{7,6},{8,9},{10,11},{12,... | collective-permute-start | bytes 774152 | tf_op jit(solution)/shard_map/ppermute | solution.py:181
  89.4 19.9 %all-to-all-start.3 = ((bf16[16,48,512]{2,1,0:T(8,128)(2,1)}), bf16[16,48,512]{2,1,0:T(8,128)(2,1)S(1)}, u32[]{:S(2)}, u32[]{:S(2)}) async-start(bf16[16,48,512]{2,1,0:T(8,128)(2,1)} %bitcast.7), calls=%async_computation.3 | async-start | bytes 1572864 | tf_op jit(solution)/shard_map/all_to_all | solution.py:274
  93.0 1.6 %copy-start.2 = (f32[1344,384]{1,0:T(8,128)S(1)}, f32[1344,384]{1,0:T(8,128)}, u32[]{:S(2)}) copy-start(f32[1344,384]{1,0:T(8,128)} %copy-done.1) | copy-start | bytes 6193156
  95.4 8.2 %collective-permute-start.4 = (bf16[336,384]{1,0:T(8,128)(2,1)S(1)}, bf16[336,384]{1,0:T(8,128)(2,1)S(1)}, u32[]{:S(2)}, u32[]{:S(2)}) collective-permute-start(bf16[336,384]{1,0:T(8,128)(2,1)S(1)} %get-tuple-element.37), channel_id=1, source_target_pairs={{0,4},{2,6},{4,1},{6,3},{1,5},{3,7},{5,0},{7,2},{8,12},{10,14},{12... | collective-permute-start | bytes 774152 | tf_op jit(solution)/shard_map/ppermute | solution.py:181
  95.6 7.9 %collective-permute-start.5 = (bf16[336,384]{1,0:T(8,128)(2,1)S(1)}, bf16[336,384]{1,0:T(8,128)(2,1)S(1)}, u32[]{:S(2)}, u32[]{:S(2)}) collective-permute-start(bf16[336,384]{1,0:T(8,128)(2,1)S(1)} %get-tuple-element.38), channel_id=1, source_target_pairs={{0,5},{2,7},{4,0},{6,2},{1,4},{3,6},{5,1},{7,3},{8,13},{10,15},{12... | collective-permute-start | bytes 774152 | tf_op jit(solution)/shard_map/ppermute | solution.py:181
  98.1 11.0 %collective-permute-start.6 = (bf16[336,384]{1,0:T(8,128)(2,1)S(1)}, bf16[336,384]{1,0:T(8,128)(2,1)S(1)}, u32[]{:S(2)}, u32[]{:S(2)}) collective-permute-start(bf16[336,384]{1,0:T(8,128)(2,1)S(1)} %get-tuple-element.39), channel_id=1, source_target_pairs={{0,1},{2,3},{4,5},{6,7},{1,0},{3,2},{5,4},{7,6},{8,9},{10,11},{12,... | collective-permute-start | bytes 774152 | tf_op jit(solution)/shard_map/ppermute | solution.py:181
  100.7 13.3 %collective-permute-start.17 = (bf16[336,384]{1,0:T(8,128)(2,1)S(1)}, bf16[336,384]{1,0:T(8,128)(2,1)S(1)}, u32[]{:S(2)}, u32[]{:S(2)}) collective-permute-start(bf16[336,384]{1,0:T(8,128)(2,1)S(1)} %multiply_convert_fusion), channel_id=1, source_target_pairs={{0,5},{2,7},{4,0},{6,2},{1,4},{3,6},{5,1},{7,3},{8,13},{10,15},{12... | collective-permute-start | bytes 774152 | tf_op jit(solution)/shard_map/ppermute | solution.py:189
  101.6 13.1 %collective-permute-start.16 = (bf16[336,384]{1,0:T(8,128)(2,1)S(1)}, bf16[336,384]{1,0:T(8,128)(2,1)S(1)}, u32[]{:S(2)}, u32[]{:S(2)}) collective-permute-start(bf16[336,384]{1,0:T(8,128)(2,1)S(1)} %multiply_convert_fusion), channel_id=1, source_target_pairs={{0,1},{2,3},{4,5},{6,7},{1,0},{3,2},{5,4},{7,6},{8,9},{10,11},{12,... | collective-permute-start | bytes 774152 | tf_op jit(solution)/shard_map/ppermute | solution.py:189
  103.5 20.7 %collective-permute-start.15 = (bf16[336,384]{1,0:T(8,128)(2,1)S(1)}, bf16[336,384]{1,0:T(8,128)(2,1)S(1)}, u32[]{:S(2)}, u32[]{:S(2)}) collective-permute-start(bf16[336,384]{1,0:T(8,128)(2,1)S(1)} %multiply_convert_fusion), channel_id=1, source_target_pairs={{0,4},{2,6},{4,1},{6,3},{1,5},{3,7},{5,0},{7,2},{8,12},{10,14},{12... | collective-permute-start | bytes 774152 | tf_op jit(solution)/shard_map/ppermute | solution.py:189
  110.2 22.4 %collective-permute-start.8 = (bf16[336,384]{1,0:T(8,128)(2,1)S(1)}, bf16[336,384]{1,0:T(8,128)(2,1)S(1)}, u32[]{:S(2)}, u32[]{:S(2)}) collective-permute-start(bf16[336,384]{1,0:T(8,128)(2,1)S(1)} %multiply_convert_fusion.1), channel_id=1, source_target_pairs={{0,1},{2,3},{4,5},{6,7},{1,0},{3,2},{5,4},{7,6},{8,9},{10,11},{12,... | collective-permute-start | bytes 774152 | tf_op jit(solution)/shard_map/ppermute | solution.py:189
  110.8 21.7 %collective-permute-start.7 = (bf16[336,384]{1,0:T(8,128)(2,1)S(1)}, bf16[336,384]{1,0:T(8,128)(2,1)S(1)}, u32[]{:S(2)}, u32[]{:S(2)}) collective-permute-start(bf16[336,384]{1,0:T(8,128)(2,1)S(1)} %multiply_convert_fusion.1), channel_id=1, source_target_pairs={{0,4},{2,6},{4,1},{6,3},{1,5},{3,7},{5,0},{7,2},{8,12},{10,14},{12... | collective-permute-start | bytes 774152 | tf_op jit(solution)/shard_map/ppermute | solution.py:189
  124.3 12.5 %collective-permute-start.18 = (bf16[1344,384]{1,0:T(8,128)(2,1)S(1)}, bf16[1344,384]{1,0:T(8,128)(2,1)S(1)}, u32[]{:S(2)}, u32[]{:S(2)}) collective-permute-start(bf16[1344,384]{1,0:T(8,128)(2,1)S(1)} %pad_maximum_fusion), channel_id=1, source_target_pairs={{0,2},{2,0},{4,6},{6,4},{1,3},{3,1},{5,7},{7,5},{8,10},{10,8},{12,... | collective-permute-start | bytes 3096584 | tf_op jit(solution)/shard_map/ppermute | solution.py:191
  126.9 9.0 %collective-permute-start.9 = (bf16[336,384]{1,0:T(8,128)(2,1)S(1)}, bf16[336,384]{1,0:T(8,128)(2,1)S(1)}, u32[]{:S(2)}, u32[]{:S(2)}) collective-permute-start(bf16[336,384]{1,0:T(8,128)(2,1)S(1)} %multiply_convert_fusion.1), channel_id=1, source_target_pairs={{0,5},{2,7},{4,0},{6,2},{1,4},{3,6},{5,1},{7,3},{8,13},{10,15},{12... | collective-permute-start | bytes 774152 | tf_op jit(solution)/shard_map/ppermute | solution.py:189
  135.9 4.0 %collective-permute-start.10 = (bf16[1344,384]{1,0:T(8,128)(2,1)S(1)}, bf16[1344,384]{1,0:T(8,128)(2,1)S(1)}, u32[]{:S(2)}, u32[]{:S(2)}) collective-permute-start(bf16[1344,384]{1,0:T(8,128)(2,1)S(1)} %constant_dynamic-update-slice_fusion), channel_id=1, source_target_pairs={{0,2},{2,0},{4,6},{6,4},{1,3},{3,1},{5,7},{7,5},{8,10},{10,8},{12,... | collective-permute-start | bytes 3096584 | tf_op jit(solution)/shard_map/ppermute | solution.py:191

commit v2 on v1

--- a/solution.py
+++ b/solution.py
@@ -37,7 +37,7 @@
     return pl.BlockSpec(memory_space=pltpu.SMEM)
 
 
-def call(body, outs, scratch, n_in, limit=48):
+def call(body, outs, scratch, n_in, limit=16):
     return pl.pallas_call(
         body,
         out_shape=outs,
@@ -61,20 +61,21 @@
     return jnp.where(z <= 62, pltpu.roll(part, SLAB - 1, 1), 0.0)
 
 
-def fill_windows(line_ref, stack_ref, sx, sy, mirror, act):
+def fill_windows(halo_refs, stack_ref, sy, mirror, act):
+    own_ref, left_ref, right_ref, y_ref, y_left_ref, y_right_ref = halo_refs
     lane = lanes()
     low = lane < 64
     for xp in range(NXL + 2):
-        peer_x = sx + (-1 if xp == 0 else 1 if xp == NXL + 1 else 0)
-        valid = jnp.logical_and(peer_x >= 0, peer_x <= 3)
-        peer_x = jnp.clip(peer_x, 0, 3)
-        at = ((xp - 1) % NXL) * SLAB
-        own = line_ref[peer_x * 2 + sy, :, at : at + SLAB].astype(F32)
-        oth = line_ref[peer_x * 2 + 1 - sy, :, at : at + SLAB].astype(F32)
+        at = slice((xp - 1) * SLAB, xp * SLAB)
+        if xp == 0:
+            own, oth = left_ref[...], y_left_ref[...]
+        elif xp == NXL + 1:
+            own, oth = right_ref[...], y_right_ref[...]
+        else:
+            own, oth = own_ref[:, at], y_ref[:, at]
+        own, oth = own.astype(F32), oth.astype(F32)
         if act:
             own, oth = jnp.maximum(own, 0.0), jnp.maximum(oth, 0.0)
-        if xp in (0, NXL + 1):
-            own, oth = jnp.where(valid, own, 0.0), jnp.where(valid, oth, 0.0)
         r_own, r_oth = pltpu.roll(own, 64, 1), pltpu.roll(oth, 64, 1)
         rows = (
             jnp.where(low, jnp.where(sy == 1, r_oth, 0.0), r_own),
@@ -96,15 +97,11 @@
     return lax.dot_general(left, right, (((1,), (1,)), ((), ())), preferred_element_type=F32)
 
 
-def take(both_ref, first, field_ref):
-    for k in range(16):
-        field_ref[k * C : (k + 1) * C, :] = both_ref[k, first : first + C, :]
-
-
-def act_grad_body(ids, w_ref, both_ref, own_ref, send_ref, field_ref, u_ref):
+def act_grad_body(
+    ids, w_ref, grad_ref, mid_ref, left_ref, right_ref, y_ref, y_left_ref, y_right_ref, u_ref
+):
     sy = ids[1]
-    take(both_ref, 0, field_ref)
-    grad = field_ref[...]
+    grad = grad_ref[...]
     u_ref[...] = jnp.zeros_like(u_ref)
     for a in range(3):
         for b in range(3):
@@ -120,18 +117,38 @@
             for b in range(3)
         ]
         r0, r2 = pltpu.roll(v[0], 64, 1), pltpu.roll(v[2], 64, 1)
-        own_ref[:, at] = v[1] + jnp.where(low, r0, r2)
-        send_ref[:, at] = jnp.where(
-            sy == 0, jnp.where(low, r2, 0.0), jnp.where(low, 0.0, r0)
-        )
-
-
-def filter_body(
-    act, mirror, first, ids, line_ref, both_ref, keep_ref, send_ref, full_ref, stack_ref
-):
-    sx, sy, core = ids[0], ids[1], ids[2]
-    take(both_ref, first, full_ref)
-    fill_windows(line_ref, stack_ref, sx, sy, mirror, act)
+        own = v[1] + jnp.where(low, r0, r2)
+        over = jnp.where(sy == 0, jnp.where(low, r2, 0.0), jnp.where(low, 0.0, r0))
+        if xp == 0:
+            left_ref[...], y_left_ref[...] = own, over
+        elif xp == NXL + 1:
+            right_ref[...], y_right_ref[...] = own, over
+        else:
+            at = slice((xp - 1) * SLAB, xp * SLAB)
+            mid_ref[:, at], y_ref[:, at] = own, over
+
+
+def delta_body(ids, pre_ref, mid_ref, *refs):
+    left_ref, right_ref, y_ref, y_left_ref, y_right_ref, out_ref, first_ref, last_ref = refs
+    for xl in range(NXL):
+        at = slice(xl * SLAB, (xl + 1) * SLAB)
+        grad = mid_ref[:, at] + y_ref[:, at]
+        if xl == 0:
+            grad = grad + left_ref[...] + y_left_ref[...]
+        if xl == NXL - 1:
+            grad = grad + right_ref[...] + y_right_ref[...]
+        delta = jnp.where(pre_ref[:, at].astype(F32) > 0, grad, 0.0).astype(BF)
+        out_ref[:, at] = delta
+        if xl == 0:
+            first_ref[...] = delta
+        if xl == NXL - 1:
+            last_ref[...] = delta
+
+
+def filter_body(act, mirror, ids, *refs):
+    halo_refs, (full_ref, keep_ref, send_ref, stack_ref) = refs[:6], refs[6:]
+    sy, core = ids[1], ids[2]
+    fill_windows(halo_refs, stack_ref, sy, mirror, act)
     mine = full_ref[pl.ds(pl.multiple_of(core * HALF, HALF), HALF), :]
     other = full_ref[pl.ds(pl.multiple_of((1 - core) * HALF, HALF), HALF), :]
     step = 3 * C
@@ -143,12 +160,32 @@
     send_ref[ROWS:ROWSP, :] = jnp.zeros((ROWSP - ROWS, HALF), BF)
 
 
-def data_body(ids, line_ref, w_ref, out_ref, stack_ref):
-    fill_windows(line_ref, stack_ref, ids[0], ids[1], True, False)
+def data_body(ids, *refs):
+    halo_refs, (w_ref, out_ref, stack_ref) = refs[:6], refs[6:]
+    fill_windows(halo_refs, stack_ref, ids[1], True, False)
     for i in range(3):
         out_ref[i * 256 : (i + 1) * 256, :] = jnp.dot(
             w_ref[i * 256 : (i + 1) * 256, :], stack_ref[...], preferred_element_type=F32
         ).astype(BF)
+
+
+def to_side(dx, flip):
+    return [
+        (sx * 2 + sy, (sx + dx) * 2 + (1 - sy if flip else sy))
+        for sx in range(4)
+        for sy in range(2)
+        if 0 <= sx + dx < 4
+    ]
+
+
+def swap(to_left, to_right, whole, y_to_left, y_to_right):
+    send = functools.partial(lax.ppermute, axis_name=LINE)
+    whole = send(whole, perm=to_side(0, True))
+    y_left = send(y_to_right, perm=to_side(1, True))
+    y_right = send(y_to_left, perm=to_side(-1, True))
+    left = send(to_right, perm=to_side(1, False))
+    right = send(to_left, perm=to_side(-1, False))
+    return left, right, whole, y_left, y_right
 
 
 def to_all(x, axis, count):
@@ -223,55 +260,54 @@
     ids = jnp.stack([sx, sy, core, chip]).astype(jnp.int32)
     n_pos = NXL * SLAB
     factor = 1.0 / 64.0
-
-    both = jnp.concatenate([out_grad.reshape(C, n_pos), inputs.reshape(C, n_pos)], axis=0)
-    both = to_all(both, "ch", 16)
+    edge_f = jax.ShapeDtypeStruct((C, SLAB), F32)
+    edge_b = jax.ShapeDtypeStruct((C, SLAB), BF)
+    mid_f = jax.ShapeDtypeStruct((C, n_pos), F32)
+    mid_b = jax.ShapeDtypeStruct((C, n_pos), BF)
+
+    grad = to_all(out_grad.reshape(C, n_pos), "ch", 16).reshape(CH, n_pos)
     pre = pre_act.reshape(C, n_pos)
+    first, last = pre[:, :SLAB], pre[:, n_pos - SLAB :]
+    pre_halo = swap(first, last, pre, first, last)
     w_two = weight_two.reshape(ROWS, CH)
     w_one = weight_one.reshape(ROWS, CH).T
-    both, w_one, pre = lax.optimization_barrier((both, w_one, pre))
-    pre_line = to_all(pre, LINE, 8)
-
-    wide = (NXL + 2) * SLAB
-    field = pltpu.VMEM((CH, n_pos), BF)
-    own, over = call(
+    mine_in = inputs.reshape(C, n_pos)
+    grad, w_one, mine_in, pre_halo = lax.optimization_barrier((grad, w_one, mine_in, pre_halo))
+    full_in = to_all(mine_in, "ch", 16).reshape(CH, n_pos)
+
+    mid, left, right, y_mid, y_left, y_right = call(
         act_grad_body,
-        (jax.ShapeDtypeStruct((C, wide), F32), jax.ShapeDtypeStruct((C, wide), F32)),
-        [field, pltpu.VMEM((3, 3 * C, wide), F32)],
+        (mid_f, edge_f, edge_f, mid_f, edge_f, edge_f),
+        [pltpu.VMEM((3, 3 * C, n_pos + 2 * SLAB), F32)],
         2,
-    )(ids, w_two, both)
-    own = own + lax.ppermute(over, "sy", [(0, 1), (1, 0)])
-    own, pre_line = lax.optimization_barrier((own, pre_line))
-    to_left = lax.ppermute(own[:, :SLAB], "sx", [(i + 1, i) for i in range(3)])
-    to_right = lax.ppermute(own[:, wide - SLAB :], "sx", [(i, i + 1) for i in range(3)])
+    )(ids, w_two, grad)
+    sums = swap(left, right, y_mid, y_left, y_right)
 
     filter_outs = (
         jax.ShapeDtypeStruct((ROWSP, HALF), F32),
         jax.ShapeDtypeStruct((ROWSP, HALF), BF),
     )
     stack = pltpu.VMEM((ROWS, n_pos), BF)
-    keep2, send2 = call(
-        functools.partial(filter_body, True, False, 0), filter_outs, [field, stack], 2
-    )(ids, pre_line, both)
-    split2 = chip_split(ids, keep2, lax.ppermute(send2, LINE, OTHER_CORE))
-
-    mid = own[:, SLAB : wide - SLAB]
-    mid = jnp.concatenate(
-        [mid[:, :SLAB] + to_right, mid[:, SLAB:-SLAB], mid[:, -SLAB:] + to_left], axis=1
-    )
-    delta = jnp.where(pre > 0, mid, 0.0).astype(BF)
-    delta_line = to_all(delta, LINE, 8)
-    block2 = line_sum(*split2, factor)
-
-    keep1, send1 = call(
-        functools.partial(filter_body, False, True, C), filter_outs, [field, stack], 2
-    )(ids, delta_line, both)
+    keep2, send2 = call(functools.partial(filter_body, True, False), filter_outs, [stack], 7)(
+        ids, pre, *pre_halo, grad
+    )
+    sums, send2 = lax.optimization_barrier((sums, send2))
+    got2 = lax.ppermute(send2, LINE, OTHER_CORE)
+    delta, first, last = call(delta_body, (mid_b, edge_b, edge_b), [], 7)(ids, pre, mid, *sums)
+    halo = swap(first, last, delta, first, last)
+    split2 = chip_split(ids, keep2, got2)
+    halo, _ = lax.optimization_barrier((halo, split2))
+
+    keep1, send1 = call(functools.partial(filter_body, False, True), filter_outs, [stack], 7)(
+        ids, delta, *halo, full_in
+    )
     got1 = lax.ppermute(send1, LINE, OTHER_CORE)
-    terms = call(data_body, jax.ShapeDtypeStruct((CH, n_pos), BF), [stack], 2)(
-        ids, delta_line, w_one
+    terms = call(data_body, jax.ShapeDtypeStruct((CH, n_pos), BF), [stack], 7)(
+        ids, delta, *halo, w_one
     )
     terms, got1 = lax.optimization_barrier((terms, got1))
     got = lax.all_to_all(terms.reshape(16, C, n_pos), "ch", 0, 0, tiled=True)
+    block2 = line_sum(*split2, factor)
     split1 = chip_split(ids, keep1, got1)
     block1 = line_sum(*split1, factor)
     pair2 = line_spread(block2)

time: 144 us -> 149 us (1.035)
  starting transfers between devices: 50 us -> 89.2 us
  waiting for transfers between devices: 53 us -> 20.5 us
  local copies, waits for them, and re-layouts: 17.4 us -> 14.7 us
    ppermute x4 -> x16, starting transfers between devices: 8.24 us -> 41.4 us  [the longest x3 12.2 us: swap(): y_right = send(y_to_left, perm=to_side(-1, True))]
    all_to_all x3 -> x2, waiting for transfers between devices: 21.5 us -> 0.01 us  [to_all(): return lax.all_to_all(many, axis, 0, 0, tiled=True)]
    ppermute x2, starting transfers between devices: 3.52 us -> 12.5 us  [line_spread(): return (mine, lax.ppermute(mine, LINE, OTHER_CORE))]
    ppermute x4 -> x16, waiting for transfers between devices: 7.91 us -> 0.37 us  [the longest x3 0.34 us: swap(): whole = send(whole, perm=to_side(0, True))]
    all_to_all x3 -> x2, starting transfers between devices: 19.5 us -> 15.5 us  [to_all(): return lax.all_to_all(many, axis, 0, 0, tiled=True)]
    all_to_all x1, starting transfers between devices: 3.62 us -> 7.08 us  [shards(): got = lax.all_to_all(terms.reshape(16, C, n_pos), 'ch', 0, 0, tiled=True)]
    ppermute x6, waiting for transfers between devices: 17.1 us -> 14.6 us  [line_spread(): got = {k: lax.ppermute(block, LINE, along(k)) for k in (1, 3, 2)}]
    ppermute x6, starting transfers between devices: 7.64 us -> 5.65 us  [line_spread(): got = {k: lax.ppermute(block, LINE, along(k)) for k in (1, 3, 2)}]
  transfers between devices with their start and end apart: 23 -> 34, of which waited for: 11 -> 6; matrix products, arithmetic and copies ran while one was open for 5% -> 5% of each run, Pallas kernels for 12% -> 9%
where the time goes in v2:
time: 149 us; the launch traced here: 148 us
  starting transfers between devices  89.2 us (60%)
  waiting for transfers between devices  20.5 us (14%)
  Pallas kernels  20.5 us (14%)
  local copies, waits for them, and re-layouts  14.7 us (10%)
  other arithmetic  1.78 us (1%)
    all_to_all x2, starting transfers between devices, to_all(): return lax.all_to_all(many, axis, 0, 0, tiled=True)  15.5 us
    ppermute x6, waiting for transfers between devices, line_spread(): got = {k: lax.ppermute(block, LINE, along(k)) for k in (1, 3, 2)}  14.6 us
    ppermute x2, starting transfers between devices, line_spread(): return (mine, lax.ppermute(mine, LINE, OTHER_CORE))  12.5 us
    ppermute x3, starting transfers between devices, swap(): y_right = send(y_to_left, perm=to_side(-1, True))  12.2 us
    ppermute x3, starting transfers between devices, swap(): y_left = send(y_to_right, perm=to_side(1, True))  10.2 us
    unnamed x27, local copies, waits for them, and re-layouts  7.76 us
    ppermute x3, starting transfers between devices, swap(): left = send(to_right, perm=to_side(1, False))  7.71 us
    all_to_all x1, starting transfers between devices, shards(): got = lax.all_to_all(terms.reshape(16, C, n_pos), 'ch', 0, 0, tiled=True)  7.08 us
  transfers between devices with their start and end apart: 34, of which 6 were waited for; matrix products, arithmetic and copies ran while one was open for 5% of the time, Pallas kernels for 9%

profile of v2, /device:TPU:1, one launch (start us, length us, event | category | flops | bytes accessed | tf_op | source)
XLA Modules:
  0.0 147.7 jit_solution(2039617029495631483)
XLA Ops:
  2.7 8.6 %all-to-all-start = ((bf16[16,48,512]{2,1,0:T(8,128)(2,1)}), bf16[16,48,512]{2,1,0:T(8,128)(2,1)S(1)}, u32[]{:S(2)}, u32[]{:S(2)}) async-start(bf16[16,48,512]{2,1,0:T(8,128)(2,1)} %broadcast_in_dim.14), calls=%async_computation | async-start | bytes 1572864 | tf_op jit(solution)/shard_map/all_to_all | solution.py:193
  11.4 5.5 %collective-permute-start.4 = (bf16[48,128]{1,0:T(8,128)(2,1)S(1)}, bf16[48,128]{1,0:T(8,128)(2,1)S(1)}, u32[]{:S(2)}, u32[]{:S(2)}) collective-permute-start(bf16[48,128]{1,0:T(8,128)(2,1)S(1)} %get-tuple-element.91), channel_id=1, source_target_pairs={{2,1},{3,0},{4,3},{5,2},{6,5},{7,4},{10,9},{11,8},{12,11},{13,10},... | collective-permute-start | bytes 36872 | tf_op jit(solution)/shard_map/ppermute | solution.py:185
  16.9 1.9 %collective-permute-start.1 = (bf16[48,128]{1,0:T(8,128)(2,1)S(1)}, bf16[48,128]{1,0:T(8,128)(2,1)S(1)}, u32[]{:S(2)}, u32[]{:S(2)}) collective-permute-start(bf16[48,128]{1,0:T(8,128)(2,1)S(1)} %get-tuple-element.91), channel_id=1, source_target_pairs={{2,0},{3,1},{4,2},{5,3},{6,4},{7,5},{10,8},{11,9},{12,10},{13,11},... | collective-permute-start | bytes 36872 | tf_op jit(solution)/shard_map/ppermute | solution.py:187
  18.9 2.7 %collective-permute-start.3 = (bf16[48,128]{1,0:T(8,128)(2,1)S(1)}, bf16[48,128]{1,0:T(8,128)(2,1)S(1)}, u32[]{:S(2)}, u32[]{:S(2)}) collective-permute-start(bf16[48,128]{1,0:T(8,128)(2,1)S(1)} %get-tuple-element.92), channel_id=1, source_target_pairs={{0,3},{1,2},{2,5},{3,4},{4,7},{5,6},{8,11},{9,10},{10,13},{11,12},... | collective-permute-start | bytes 36872 | tf_op jit(solution)/shard_map/ppermute | solution.py:184
  21.6 2.9 %collective-permute-start = (bf16[48,128]{1,0:T(8,128)(2,1)S(1)}, bf16[48,128]{1,0:T(8,128)(2,1)S(1)}, u32[]{:S(2)}, u32[]{:S(2)}) collective-permute-start(bf16[48,128]{1,0:T(8,128)(2,1)S(1)} %get-tuple-element.92), channel_id=1, source_target_pairs={{0,2},{1,3},{2,4},{3,5},{4,6},{5,7},{8,10},{9,11},{10,12},{11,13},... | collective-permute-start | bytes 36872 | tf_op jit(solution)/shard_map/ppermute | solution.py:186
  24.4 1.9 %collective-permute-start.2 = (bf16[48,512]{1,0:T(8,128)(2,1)S(1)}, bf16[48,512]{1,0:T(8,128)(2,1)S(1)}, u32[]{:S(2)}, u32[]{:S(2)}) collective-permute-start(bf16[48,512]{1,0:T(8,128)(2,1)S(1)} %reshape.44.refs_0_.pre_ref), channel_id=1, source_target_pairs={{0,1},{1,0},{2,3},{3,2},{4,5},{5,4},{6,7},{7,6},{8,9},{9,8},{10,11... | collective-permute-start | bytes 147464 | tf_op jit(solution)/shard_map/ppermute | solution.py:183
  26.5 2.9 %copy.9 = bf16[1296,768]{0,1:T(8,128)(2,1)S(1)} copy(bf16[1296,768]{1,0:T(8,128)(2,1)} %bitcast.23) | data formatting | bytes 3981312 | tf_op jit(solution)/shard_map/reshape | solution.py:273
  31.3 1.9 %shard_map.76 = (f32[48,512]{1,0:T(8,128)S(1)}, f32[48,128]{1,0:T(8,128)S(1)}, f32[48,128]{1,0:T(8,128)S(1)}, f32[48,512]{1,0:T(8,128)S(1)}, f32[48,128]{1,0:T(8,128)S(1)}, /*index=5*/f32[48,128]{1,0:T(8,128)S(1)}) custom-call(s32[4]{0:T(128)S(1)} %pad_add_fusion.ids, bf16[1296,768]{1,0:T(8,128)(2,1)S(1)} %bitcast.19, bf16[768,512]{1,0:T(8,128)(2,1)S(1)} %bitcast.15), custom_call_target="tpu_custom_call" | custom-call | tf_op jit(solution)/shard_map/pallas_call | solution.py:278
  34.3 2.7 %collective-permute-start.5 = (f32[48,128]{1,0:T(8,128)S(1)}, f32[48,128]{1,0:T(8,128)S(1)}, u32[]{:S(2)}, u32[]{:S(2)}) collective-permute-start(f32[48,128]{1,0:T(8,128)S(1)} %get-tuple-element.49), channel_id=1, source_target_pairs={{0,2},{1,3},{2,4},{3,5},{4,6},{5,7},{8,10},{9,11},{10,12},{11,13},... | collective-permute-start | bytes 73736 | tf_op jit(solution)/shard_map/ppermute | solution.py:186
  37.1 2.4 %collective-permute-start.6 = (f32[48,128]{1,0:T(8,128)S(1)}, f32[48,128]{1,0:T(8,128)S(1)}, u32[]{:S(2)}, u32[]{:S(2)}) collective-permute-start(f32[48,128]{1,0:T(8,128)S(1)} %get-tuple-element.50), channel_id=1, source_target_pairs={{2,0},{3,1},{4,2},{5,3},{6,4},{7,5},{10,8},{11,9},{12,10},{13,11},... | collective-permute-start | bytes 73736 | tf_op jit(solution)/shard_map/ppermute | solution.py:187
  39.4 4.4 %collective-permute-start.8 = (f32[48,128]{1,0:T(8,128)S(1)}, f32[48,128]{1,0:T(8,128)S(1)}, u32[]{:S(2)}, u32[]{:S(2)}) collective-permute-start(f32[48,128]{1,0:T(8,128)S(1)} %get-tuple-element.52), channel_id=1, source_target_pairs={{0,3},{1,2},{2,5},{3,4},{4,7},{5,6},{8,11},{9,10},{10,13},{11,12},... | collective-permute-start | bytes 73736 | tf_op jit(solution)/shard_map/ppermute | solution.py:184
  43.8 2.7 %collective-permute-start.9 = (f32[48,128]{1,0:T(8,128)S(1)}, f32[48,128]{1,0:T(8,128)S(1)}, u32[]{:S(2)}, u32[]{:S(2)}) collective-permute-start(f32[48,128]{1,0:T(8,128)S(1)} %get-tuple-element.53), channel_id=1, source_target_pairs={{2,1},{3,0},{4,3},{5,2},{6,5},{7,4},{10,9},{11,8},{12,11},{13,10},... | collective-permute-start | bytes 73736 | tf_op jit(solution)/shard_map/ppermute | solution.py:185
  46.5 3.8 %shard_map.77 = (f32[1344,384]{1,0:T(8,128)S(1)}, bf16[1344,384]{1,0:T(8,128)(2,1)}) custom-call(s32[4]{0:T(128)S(1)} %pad_add_fusion.ids, bf16[48,512]{1,0:T(8,128)(2,1)S(1)} %reshape.44.refs_0_.pre_ref, bf16[48,128]{1,0:T(8,128)(2,1)S(1)} %collective-permute-done.refs_1_, bf16[48,128]{1,0:T(8,128)(2,1)S(1)} %collective-permute-done.1.refs_2_, ...), custom_call_target="tpu_custom_call" | custom-call | tf_op jit(solution)/shard_map/pallas_call | solution.py:291
  52.7 6.9 %all-to-all-start.1 = ((bf16[16,48,512]{2,1,0:T(8,128)(2,1)}), bf16[16,48,512]{2,1,0:T(8,128)(2,1)S(1)}, u32[]{:S(2)}, u32[]{:S(2)}) async-start(bf16[16,48,512]{2,1,0:T(8,128)(2,1)} %broadcast_in_dim.15), calls=%async_computation.1 | async-start | bytes 1572864 | tf_op jit(solution)/shard_map/all_to_all | solution.py:193
  60.2 2.0 %collective-permute-start.12 = (bf16[48,512]{1,0:T(8,128)(2,1)S(1)}, bf16[48,512]{1,0:T(8,128)(2,1)S(1)}, u32[]{:S(2)}, u32[]{:S(2)}) collective-permute-start(bf16[48,512]{1,0:T(8,128)(2,1)S(1)} %get-tuple-element.65.refs_0_), channel_id=1, source_target_pairs={{0,1},{1,0},{2,3},{3,2},{4,5},{5,4},{6,7},{7,6},{8,9},{9,8},{10,11... | collective-permute-start | bytes 147464 | tf_op jit(solution)/shard_map/ppermute | solution.py:183
  62.2 3.1 %collective-permute-start.13 = (bf16[48,128]{1,0:T(8,128)(2,1)S(1)}, bf16[48,128]{1,0:T(8,128)(2,1)S(1)}, u32[]{:S(2)}, u32[]{:S(2)}) collective-permute-start(bf16[48,128]{1,0:T(8,128)(2,1)S(1)} %get-tuple-element.66), channel_id=1, source_target_pairs={{0,3},{1,2},{2,5},{3,4},{4,7},{5,6},{8,11},{9,10},{10,13},{11,12},... | collective-permute-start | bytes 36872 | tf_op jit(solution)/shard_map/ppermute | solution.py:184
  65.4 2.1 %collective-permute-start.10 = (bf16[48,128]{1,0:T(8,128)(2,1)S(1)}, bf16[48,128]{1,0:T(8,128)(2,1)S(1)}, u32[]{:S(2)}, u32[]{:S(2)}) collective-permute-start(bf16[48,128]{1,0:T(8,128)(2,1)S(1)} %get-tuple-element.66), channel_id=1, source_target_pairs={{0,2},{1,3},{2,4},{3,5},{4,6},{5,7},{8,10},{9,11},{10,12},{11,13},... | collective-permute-start | bytes 36872 | tf_op jit(solution)/shard_map/ppermute | solution.py:186
  67.5 4.1 %collective-permute-start.14 = (bf16[48,128]{1,0:T(8,128)(2,1)S(1)}, bf16[48,128]{1,0:T(8,128)(2,1)S(1)}, u32[]{:S(2)}, u32[]{:S(2)}) collective-permute-start(bf16[48,128]{1,0:T(8,128)(2,1)S(1)} %get-tuple-element.67), channel_id=1, source_target_pairs={{2,1},{3,0},{4,3},{5,2},{6,5},{7,4},{10,9},{11,8},{12,11},{13,10},... | collective-permute-start | bytes 36872 | tf_op jit(solution)/shard_map/ppermute | solution.py:185
  71.6 1.9 %collective-permute-start.11 = (bf16[48,128]{1,0:T(8,128)(2,1)S(1)}, bf16[48,128]{1,0:T(8,128)(2,1)S(1)}, u32[]{:S(2)}, u32[]{:S(2)}) collective-permute-start(bf16[48,128]{1,0:T(8,128)(2,1)S(1)} %get-tuple-element.67), channel_id=1, source_target_pairs={{2,0},{3,1},{4,2},{5,3},{6,4},{7,5},{10,8},{11,9},{12,10},{13,11},... | collective-permute-start | bytes 36872 | tf_op jit(solution)/shard_map/ppermute | solution.py:187
  78.2 2.9 %shard_map.81 = (f32[1344,384]{1,0:T(8,128)S(1)}, bf16[1344,384]{1,0:T(8,128)(2,1)S(1)}) custom-call(s32[4]{0:T(128)S(1)} %pad_add_fusion.ids, bf16[48,512]{1,0:T(8,128)(2,1)S(1)} %get-tuple-element.65.refs_0_, bf16[48,128]{1,0:T(8,128)(2,1)S(1)} %collective-permute-done.10.refs_1_, bf16[48,128]{1,0:T(8,128)(2,1)S(1)} %collective-permute-done.11.refs_2_, ...), custom_call_target="tpu_custom_call" | custom-call | tf_op jit(solution)/shard_map/pallas_call | solution.py:301
  81.2 1.8 %collective-permute-start.24 = (bf16[336,384]{1,0:T(8,128)(2,1)}, bf16[336,384]{1,0:T(8,128)(2,1)}, u32[]{:S(2)}, u32[]{:S(2)}) collective-permute-start(bf16[336,384]{1,0:T(8,128)(2,1)} %copy-done.9), channel_id=1, source_target_pairs={{0,4},{2,6},{4,1},{6,3},{1,5},{3,7},{5,0},{7,2},{8,12},{10,14},{12... | collective-permute-start | bytes 774152 | tf_op jit(solution)/shard_map/ppermute | solution.py:218
  85.4 3.0 %shard_map.80 = bf16[768,512]{1,0:T(8,128)(2,1)} custom-call(s32[4]{0:T(128)S(1)} %pad_add_fusion.ids, bf16[48,512]{1,0:T(8,128)(2,1)S(1)} %get-tuple-element.65.refs_0_, bf16[48,128]{1,0:T(8,128)(2,1)S(1)} %collective-permute-done.10.refs_1_, bf16[48,128]{1,0:T(8,128)(2,1)S(1)} %collective-permute-done.11.refs_2_, ...), custom_call_target="tpu_custom_call" | custom-call | tf_op jit(solution)/shard_map/pallas_call | solution.py:305
  88.5 7.1 %all-to-all-start.2 = ((bf16[16,48,512]{2,1,0:T(8,128)(2,1)}), bf16[16,48,512]{2,1,0:T(8,128)(2,1)S(1)}, u32[]{:S(2)}, u32[]{:S(2)}) async-start(bf16[16,48,512]{2,1,0:T(8,128)(2,1)} %bitcast.9), calls=%async_computation.2 | async-start | bytes 1572864 | tf_op jit(solution)/shard_map/all_to_all | solution.py:309
  98.1 2.6 %collective-permute-start.18 = (bf16[336,384]{1,0:T(8,128)(2,1)S(1)}, bf16[336,384]{1,0:T(8,128)(2,1)S(1)}, u32[]{:S(2)}, u32[]{:S(2)}) collective-permute-start(bf16[336,384]{1,0:T(8,128)(2,1)S(1)} %get-tuple-element.87), channel_id=1, source_target_pairs={{0,5},{2,7},{4,0},{6,2},{1,4},{3,6},{5,1},{7,3},{8,13},{10,15},{12... | collective-permute-start | bytes 774152 | tf_op jit(solution)/shard_map/ppermute | solution.py:218
  103.5 1.6 %collective-permute-start.28 = (bf16[336,384]{1,0:T(8,128)(2,1)S(1)}, bf16[336,384]{1,0:T(8,128)(2,1)S(1)}, u32[]{:S(2)}, u32[]{:S(2)}) collective-permute-start(bf16[336,384]{1,0:T(8,128)(2,1)S(1)} %multiply_convert_fusion), channel_id=1, source_target_pairs={{0,1},{2,3},{4,5},{6,7},{1,0},{3,2},{5,4},{7,6},{8,9},{10,11},{12,... | collective-permute-start | bytes 774152 | tf_op jit(solution)/shard_map/ppermute | solution.py:226
  106.7 4.0 %collective-permute-done.19 = bf16[336,384]{1,0:T(8,128)(2,1)S(1)} collective-permute-done((bf16[336,384]{1,0:T(8,128)(2,1)S(1)}, bf16[336,384]{1,0:T(8,128)(2,1)S(1)}, u32[]{:S(2)}, u32[]{:S(2)}) %collective-permute-start.19) | collective-permute-done | bytes 258080 | tf_op jit(solution)/shard_map/ppermute | solution.py:218
  114.2 2.4 %collective-permute-done.29 = bf16[336,384]{1,0:T(8,128)(2,1)S(1)} collective-permute-done((bf16[336,384]{1,0:T(8,128)(2,1)S(1)}, bf16[336,384]{1,0:T(8,128)(2,1)S(1)}, u32[]{:S(2)}, u32[]{:S(2)}) %collective-permute-start.29) | collective-permute-done | bytes 258080 | tf_op jit(solution)/shard_map/ppermute | solution.py:226
  116.6 4.6 %collective-permute-done.27 = bf16[336,384]{1,0:T(8,128)(2,1)S(1)} collective-permute-done((bf16[336,384]{1,0:T(8,128)(2,1)S(1)}, bf16[336,384]{1,0:T(8,128)(2,1)S(1)}, u32[]{:S(2)}, u32[]{:S(2)}) %collective-permute-start.27) | collective-permute-done | bytes 258080 | tf_op jit(solution)/shard_map/ppermute | solution.py:226
  121.3 11.6 %collective-permute-start.30 = (bf16[1344,384]{1,0:T(8,128)(2,1)S(1)}, bf16[1344,384]{1,0:T(8,128)(2,1)S(1)}, u32[]{:S(2)}, u32[]{:S(2)}) collective-permute-start(bf16[1344,384]{1,0:T(8,128)(2,1)S(1)} %pad_maximum_fusion), channel_id=1, source_target_pairs={{0,2},{2,0},{4,6},{6,4},{1,3},{3,1},{5,7},{7,5},{8,10},{10,8},{12,... | collective-permute-start | bytes 3096584 | tf_op jit(solution)/shard_map/ppermute | solution.py:228
  133.0 7.6 %collective-permute-done.22 = bf16[336,384]{1,0:T(8,128)(2,1)S(1)} collective-permute-done((bf16[336,384]{1,0:T(8,128)(2,1)S(1)}, bf16[336,384]{1,0:T(8,128)(2,1)S(1)}, u32[]{:S(2)}, u32[]{:S(2)}) %collective-permute-start.22) | collective-permute-done | bytes 258080 | tf_op jit(solution)/shard_map/ppermute | solution.py:226
  141.7 3.0 %shard_map.84 = f32[27,48,768]{2,1,0:T(8,128)} custom-call(s32[4]{0:T(128)S(1)} %pad_add_fusion.ids, bf16[4,7,48,384]{3,2,1,0:T(8,128)(2,1)S(1)} %bitcast.17, bf16[4,7,48,384]{3,2,1,0:T(8,128)(2,1)S(1)} %bitcast.21), custom_call_target="tpu_custom_call" | custom-call | tf_op jit(solution)/shard_map/pallas_call | solution.py:242
  144.7 3.0 %shard_map.83 = f32[27,48,768]{2,1,0:T(8,128)} custom-call(s32[4]{0:T(128)S(1)} %pad_add_fusion.ids, bf16[4,7,48,384]{3,2,1,0:T(8,128)(2,1)S(1)} %bitcast.20, bf16[4,7,48,384]{3,2,1,0:T(8,128)(2,1)S(1)} %bitcast.22), custom_call_target="tpu_custom_call" | custom-call | tf_op jit(solution)/shard_map/pallas_call | solution.py:242
  (86 shorter events, 27.0 us)
Async XLA Ops:
  2.7 27.1 %all-to-all-start = ((bf16[16,48,512]{2,1,0:T(8,128)(2,1)}), bf16[16,48,512]{2,1,0:T(8,128)(2,1)S(1)}, u32[]{:S(2)}, u32[]{:S(2)}) async-start(bf16[16,48,512]{2,1,0:T(8,128)(2,1)} %broadcast_in_dim.14), calls=%async_computation | async-start | bytes 1572864 | tf_op jit(solution)/shard_map/all_to_all | solution.py:193
  11.4 18.0 %collective-permute-start.4 = (bf16[48,128]{1,0:T(8,128)(2,1)S(1)}, bf16[48,128]{1,0:T(8,128)(2,1)S(1)}, u32[]{:S(2)}, u32[]{:S(2)}) collective-permute-start(bf16[48,128]{1,0:T(8,128)(2,1)S(1)} %get-tuple-element.91), channel_id=1, source_target_pairs={{2,1},{3,0},{4,3},{5,2},{6,5},{7,4},{10,9},{11,8},{12,11},{13,10},... | collective-permute-start | bytes 36872 | tf_op jit(solution)/shard_map/ppermute | solution.py:185
  16.9 12.5 %collective-permute-start.1 = (bf16[48,128]{1,0:T(8,128)(2,1)S(1)}, bf16[48,128]{1,0:T(8,128)(2,1)S(1)}, u32[]{:S(2)}, u32[]{:S(2)}) collective-permute-start(bf16[48,128]{1,0:T(8,128)(2,1)S(1)} %get-tuple-element.91), channel_id=1, source_target_pairs={{2,0},{3,1},{4,2},{5,3},{6,4},{7,5},{10,8},{11,9},{12,10},{13,11},... | collective-permute-start | bytes 36872 | tf_op jit(solution)/shard_map/ppermute | solution.py:187
  18.9 10.6 %collective-permute-start.3 = (bf16[48,128]{1,0:T(8,128)(2,1)S(1)}, bf16[48,128]{1,0:T(8,128)(2,1)S(1)}, u32[]{:S(2)}, u32[]{:S(2)}) collective-permute-start(bf16[48,128]{1,0:T(8,128)(2,1)S(1)} %get-tuple-element.92), channel_id=1, source_target_pairs={{0,3},{1,2},{2,5},{3,4},{4,7},{5,6},{8,11},{9,10},{10,13},{11,12},... | collective-permute-start | bytes 36872 | tf_op jit(solution)/shard_map/ppermute | solution.py:184
  21.6 7.9 %collective-permute-start = (bf16[48,128]{1,0:T(8,128)(2,1)S(1)}, bf16[48,128]{1,0:T(8,128)(2,1)S(1)}, u32[]{:S(2)}, u32[]{:S(2)}) collective-permute-start(bf16[48,128]{1,0:T(8,128)(2,1)S(1)} %get-tuple-element.92), channel_id=1, source_target_pairs={{0,2},{1,3},{2,4},{3,5},{4,6},{5,7},{8,10},{9,11},{10,12},{11,13},... | collective-permute-start | bytes 36872 | tf_op jit(solution)/shard_map/ppermute | solution.py:186
  33.3 18.4 %collective-permute-start.7 = (f32[48,512]{1,0:T(8,128)S(1)}, f32[48,512]{1,0:T(8,128)S(1)}, u32[]{:S(2)}, u32[]{:S(2)}) collective-permute-start(f32[48,512]{1,0:T(8,128)S(1)} %get-tuple-element.51), channel_id=1, source_target_pairs={{0,1},{1,0},{2,3},{3,2},{4,5},{5,4},{6,7},{7,6},{8,9},{9,8},{10,11... | collective-permute-start | bytes 294920 | tf_op jit(solution)/shard_map/ppermute | solution.py:183
  34.3 17.3 %collective-permute-start.5 = (f32[48,128]{1,0:T(8,128)S(1)}, f32[48,128]{1,0:T(8,128)S(1)}, u32[]{:S(2)}, u32[]{:S(2)}) collective-permute-start(f32[48,128]{1,0:T(8,128)S(1)} %get-tuple-element.49), channel_id=1, source_target_pairs={{0,2},{1,3},{2,4},{3,5},{4,6},{5,7},{8,10},{9,11},{10,12},{11,13},... | collective-permute-start | bytes 73736 | tf_op jit(solution)/shard_map/ppermute | solution.py:186
  37.1 14.6 %collective-permute-start.6 = (f32[48,128]{1,0:T(8,128)S(1)}, f32[48,128]{1,0:T(8,128)S(1)}, u32[]{:S(2)}, u32[]{:S(2)}) collective-permute-start(f32[48,128]{1,0:T(8,128)S(1)} %get-tuple-element.50), channel_id=1, source_target_pairs={{2,0},{3,1},{4,2},{5,3},{6,4},{7,5},{10,8},{11,9},{12,10},{13,11},... | collective-permute-start | bytes 73736 | tf_op jit(solution)/shard_map/ppermute | solution.py:187
  39.4 12.2 %collective-permute-start.8 = (f32[48,128]{1,0:T(8,128)S(1)}, f32[48,128]{1,0:T(8,128)S(1)}, u32[]{:S(2)}, u32[]{:S(2)}) collective-permute-start(f32[48,128]{1,0:T(8,128)S(1)} %get-tuple-element.52), channel_id=1, source_target_pairs={{0,3},{1,2},{2,5},{3,4},{4,7},{5,6},{8,11},{9,10},{10,13},{11,12},... | collective-permute-start | bytes 73736 | tf_op jit(solution)/shard_map/ppermute | solution.py:184
  43.8 7.8 %collective-permute-start.9 = (f32[48,128]{1,0:T(8,128)S(1)}, f32[48,128]{1,0:T(8,128)S(1)}, u32[]{:S(2)}, u32[]{:S(2)}) collective-permute-start(f32[48,128]{1,0:T(8,128)S(1)} %get-tuple-element.53), channel_id=1, source_target_pairs={{2,1},{3,0},{4,3},{5,2},{6,5},{7,4},{10,9},{11,8},{12,11},{13,10},... | collective-permute-start | bytes 73736 | tf_op jit(solution)/shard_map/ppermute | solution.py:185
  51.7 19.9 %collective-permute-start.15 = (bf16[1344,384]{1,0:T(8,128)(2,1)}, bf16[1344,384]{1,0:T(8,128)(2,1)}, u32[]{:S(2)}, u32[]{:S(2)}) collective-permute-start(bf16[1344,384]{1,0:T(8,128)(2,1)} %get-tuple-element.69), channel_id=1, source_target_pairs={{0,2},{2,0},{4,6},{6,4},{1,3},{3,1},{5,7},{7,5},{8,10},{10,8},{12,... | collective-permute-start | bytes 3096584 | tf_op jit(solution)/shard_map/ppermute | solution.py:295
  52.7 25.5 %all-to-all-start.1 = ((bf16[16,48,512]{2,1,0:T(8,128)(2,1)}), bf16[16,48,512]{2,1,0:T(8,128)(2,1)S(1)}, u32[]{:S(2)}, u32[]{:S(2)}) async-start(bf16[16,48,512]{2,1,0:T(8,128)(2,1)} %broadcast_in_dim.15), calls=%async_computation.1 | async-start | bytes 1572864 | tf_op jit(solution)/shard_map/all_to_all | solution.py:193
  60.2 17.1 %collective-permute-start.12 = (bf16[48,512]{1,0:T(8,128)(2,1)S(1)}, bf16[48,512]{1,0:T(8,128)(2,1)S(1)}, u32[]{:S(2)}, u32[]{:S(2)}) collective-permute-start(bf16[48,512]{1,0:T(8,128)(2,1)S(1)} %get-tuple-element.65.refs_0_), channel_id=1, source_target_pairs={{0,1},{1,0},{2,3},{3,2},{4,5},{5,4},{6,7},{7,6},{8,9},{9,8},{10,11... | collective-permute-start | bytes 147464 | tf_op jit(solution)/shard_map/ppermute | solution.py:183
  62.2 15.1 %collective-permute-start.13 = (bf16[48,128]{1,0:T(8,128)(2,1)S(1)}, bf16[48,128]{1,0:T(8,128)(2,1)S(1)}, u32[]{:S(2)}, u32[]{:S(2)}) collective-permute-start(bf16[48,128]{1,0:T(8,128)(2,1)S(1)} %get-tuple-element.66), channel_id=1, source_target_pairs={{0,3},{1,2},{2,5},{3,4},{4,7},{5,6},{8,11},{9,10},{10,13},{11,12},... | collective-permute-start | bytes 36872 | tf_op jit(solution)/shard_map/ppermute | solution.py:184
  65.4 12.0 %collective-permute-start.10 = (bf16[48,128]{1,0:T(8,128)(2,1)S(1)}, bf16[48,128]{1,0:T(8,128)(2,1)S(1)}, u32[]{:S(2)}, u32[]{:S(2)}) collective-permute-start(bf16[48,128]{1,0:T(8,128)(2,1)S(1)} %get-tuple-element.66), channel_id=1, source_target_pairs={{0,2},{1,3},{2,4},{3,5},{4,6},{5,7},{8,10},{9,11},{10,12},{11,13},... | collective-permute-start | bytes 36872 | tf_op jit(solution)/shard_map/ppermute | solution.py:186
  67.5 9.9 %collective-permute-start.14 = (bf16[48,128]{1,0:T(8,128)(2,1)S(1)}, bf16[48,128]{1,0:T(8,128)(2,1)S(1)}, u32[]{:S(2)}, u32[]{:S(2)}) collective-permute-start(bf16[48,128]{1,0:T(8,128)(2,1)S(1)} %get-tuple-element.67), channel_id=1, source_target_pairs={{2,1},{3,0},{4,3},{5,2},{6,5},{7,4},{10,9},{11,8},{12,11},{13,10},... | collective-permute-start | bytes 36872 | tf_op jit(solution)/shard_map/ppermute | solution.py:185
  71.6 5.8 %collective-permute-start.11 = (bf16[48,128]{1,0:T(8,128)(2,1)S(1)}, bf16[48,128]{1,0:T(8,128)(2,1)S(1)}, u32[]{:S(2)}, u32[]{:S(2)}) collective-permute-start(bf16[48,128]{1,0:T(8,128)(2,1)S(1)} %get-tuple-element.67), channel_id=1, source_target_pairs={{2,0},{3,1},{4,2},{5,3},{6,4},{7,5},{10,8},{11,9},{12,10},{13,11},... | collective-permute-start | bytes 36872 | tf_op jit(solution)/shard_map/ppermute | solution.py:187
  81.1 7.3 %collective-permute-start.16 = (bf16[1344,384]{1,0:T(8,128)(2,1)S(1)}, bf16[1344,384]{1,0:T(8,128)(2,1)S(1)}, u32[]{:S(2)}, u32[]{:S(2)}) collective-permute-start(bf16[1344,384]{1,0:T(8,128)(2,1)S(1)} %get-tuple-element.81), channel_id=1, source_target_pairs={{0,2},{2,0},{4,6},{6,4},{1,3},{3,1},{5,7},{7,5},{8,10},{10,8},{12,... | collective-permute-start | bytes 3096584 | tf_op jit(solution)/shard_map/ppermute | solution.py:304
  81.2 19.4 %collective-permute-start.24 = (bf16[336,384]{1,0:T(8,128)(2,1)}, bf16[336,384]{1,0:T(8,128)(2,1)}, u32[]{:S(2)}, u32[]{:S(2)}) collective-permute-start(bf16[336,384]{1,0:T(8,128)(2,1)} %copy-done.9), channel_id=1, source_target_pairs={{0,4},{2,6},{4,1},{6,3},{1,5},{3,7},{5,0},{7,2},{8,12},{10,14},{12... | collective-permute-start | bytes 774152 | tf_op jit(solution)/shard_map/ppermute | solution.py:218
  83.1 17.6 %collective-permute-start.26 = (bf16[336,384]{1,0:T(8,128)(2,1)}, bf16[336,384]{1,0:T(8,128)(2,1)}, u32[]{:S(2)}, u32[]{:S(2)}) collective-permute-start(bf16[336,384]{1,0:T(8,128)(2,1)} %copy-done.8), channel_id=1, source_target_pairs={{0,1},{2,3},{4,5},{6,7},{1,0},{3,2},{5,4},{7,6},{8,9},{10,11},{12,... | collective-permute-start | bytes 774152 | tf_op jit(solution)/shard_map/ppermute | solution.py:218
  84.3 16.4 %collective-permute-start.25 = (bf16[336,384]{1,0:T(8,128)(2,1)}, bf16[336,384]{1,0:T(8,128)(2,1)}, u32[]{:S(2)}, u32[]{:S(2)}) collective-permute-start(bf16[336,384]{1,0:T(8,128)(2,1)} %copy-done.7), channel_id=1, source_target_pairs={{0,5},{2,7},{4,0},{6,2},{1,4},{3,6},{5,1},{7,3},{8,13},{10,15},{12... | collective-permute-start | bytes 774152 | tf_op jit(solution)/shard_map/ppermute | solution.py:218
  88.5 22.3 %all-to-all-start.2 = ((bf16[16,48,512]{2,1,0:T(8,128)(2,1)}), bf16[16,48,512]{2,1,0:T(8,128)(2,1)S(1)}, u32[]{:S(2)}, u32[]{:S(2)}) async-start(bf16[16,48,512]{2,1,0:T(8,128)(2,1)} %bitcast.9), calls=%async_computation.2 | async-start | bytes 1572864 | tf_op jit(solution)/shard_map/all_to_all | solution.py:309
  97.9 8.8 %collective-permute-start.17 = (bf16[336,384]{1,0:T(8,128)(2,1)S(1)}, bf16[336,384]{1,0:T(8,128)(2,1)S(1)}, u32[]{:S(2)}, u32[]{:S(2)}) collective-permute-start(bf16[336,384]{1,0:T(8,128)(2,1)S(1)} %get-tuple-element.86), channel_id=1, source_target_pairs={{0,4},{2,6},{4,1},{6,3},{1,5},{3,7},{5,0},{7,2},{8,12},{10,14},{12... | collective-permute-start | bytes 774152 | tf_op jit(solution)/shard_map/ppermute | solution.py:218
  98.1 8.6 %collective-permute-start.18 = (bf16[336,384]{1,0:T(8,128)(2,1)S(1)}, bf16[336,384]{1,0:T(8,128)(2,1)S(1)}, u32[]{:S(2)}, u32[]{:S(2)}) collective-permute-start(bf16[336,384]{1,0:T(8,128)(2,1)S(1)} %get-tuple-element.87), channel_id=1, source_target_pairs={{0,5},{2,7},{4,0},{6,2},{1,4},{3,6},{5,1},{7,3},{8,13},{10,15},{12... | collective-permute-start | bytes 774152 | tf_op jit(solution)/shard_map/ppermute | solution.py:218
  100.6 10.0 %collective-permute-start.19 = (bf16[336,384]{1,0:T(8,128)(2,1)S(1)}, bf16[336,384]{1,0:T(8,128)(2,1)S(1)}, u32[]{:S(2)}, u32[]{:S(2)}) collective-permute-start(bf16[336,384]{1,0:T(8,128)(2,1)S(1)} %get-tuple-element.88), channel_id=1, source_target_pairs={{0,1},{2,3},{4,5},{6,7},{1,0},{3,2},{5,4},{7,6},{8,9},{10,11},{12,... | collective-permute-start | bytes 774152 | tf_op jit(solution)/shard_map/ppermute | solution.py:218
  102.0 14.6 %collective-permute-start.29 = (bf16[336,384]{1,0:T(8,128)(2,1)S(1)}, bf16[336,384]{1,0:T(8,128)(2,1)S(1)}, u32[]{:S(2)}, u32[]{:S(2)}) collective-permute-start(bf16[336,384]{1,0:T(8,128)(2,1)S(1)} %multiply_convert_fusion), channel_id=1, source_target_pairs={{0,5},{2,7},{4,0},{6,2},{1,4},{3,6},{5,1},{7,3},{8,13},{10,15},{12... | collective-permute-start | bytes 774152 | tf_op jit(solution)/shard_map/ppermute | solution.py:226
  103.5 13.1 %collective-permute-start.28 = (bf16[336,384]{1,0:T(8,128)(2,1)S(1)}, bf16[336,384]{1,0:T(8,128)(2,1)S(1)}, u32[]{:S(2)}, u32[]{:S(2)}) collective-permute-start(bf16[336,384]{1,0:T(8,128)(2,1)S(1)} %multiply_convert_fusion), channel_id=1, source_target_pairs={{0,1},{2,3},{4,5},{6,7},{1,0},{3,2},{5,4},{7,6},{8,9},{10,11},{12,... | collective-permute-start | bytes 774152 | tf_op jit(solution)/shard_map/ppermute | solution.py:226
  106.7 14.5 %collective-permute-start.27 = (bf16[336,384]{1,0:T(8,128)(2,1)S(1)}, bf16[336,384]{1,0:T(8,128)(2,1)S(1)}, u32[]{:S(2)}, u32[]{:S(2)}) collective-permute-start(bf16[336,384]{1,0:T(8,128)(2,1)S(1)} %multiply_convert_fusion), channel_id=1, source_target_pairs={{0,4},{2,6},{4,1},{6,3},{1,5},{3,7},{5,0},{7,2},{8,12},{10,14},{12... | collective-permute-start | bytes 774152 | tf_op jit(solution)/shard_map/ppermute | solution.py:226
  111.7 21.3 %collective-permute-start.21 = (bf16[336,384]{1,0:T(8,128)(2,1)S(1)}, bf16[336,384]{1,0:T(8,128)(2,1)S(1)}, u32[]{:S(2)}, u32[]{:S(2)}) collective-permute-start(bf16[336,384]{1,0:T(8,128)(2,1)S(1)} %multiply_convert_fusion.1), channel_id=1, source_target_pairs={{0,1},{2,3},{4,5},{6,7},{1,0},{3,2},{5,4},{7,6},{8,9},{10,11},{12,... | collective-permute-start | bytes 774152 | tf_op jit(solution)/shard_map/ppermute | solution.py:226
  112.7 20.2 %collective-permute-start.20 = (bf16[336,384]{1,0:T(8,128)(2,1)S(1)}, bf16[336,384]{1,0:T(8,128)(2,1)S(1)}, u32[]{:S(2)}, u32[]{:S(2)}) collective-permute-start(bf16[336,384]{1,0:T(8,128)(2,1)S(1)} %multiply_convert_fusion.1), channel_id=1, source_target_pairs={{0,4},{2,6},{4,1},{6,3},{1,5},{3,7},{5,0},{7,2},{8,12},{10,14},{12... | collective-permute-start | bytes 774152 | tf_op jit(solution)/shard_map/ppermute | solution.py:226
  121.3 20.4 %collective-permute-start.30 = (bf16[1344,384]{1,0:T(8,128)(2,1)S(1)}, bf16[1344,384]{1,0:T(8,128)(2,1)S(1)}, u32[]{:S(2)}, u32[]{:S(2)}) collective-permute-start(bf16[1344,384]{1,0:T(8,128)(2,1)S(1)} %pad_maximum_fusion), channel_id=1, source_target_pairs={{0,2},{2,0},{4,6},{6,4},{1,3},{3,1},{5,7},{7,5},{8,10},{10,8},{12,... | collective-permute-start | bytes 3096584 | tf_op jit(solution)/shard_map/ppermute | solution.py:228
  132.9 7.8 %collective-permute-start.22 = (bf16[336,384]{1,0:T(8,128)(2,1)S(1)}, bf16[336,384]{1,0:T(8,128)(2,1)S(1)}, u32[]{:S(2)}, u32[]{:S(2)}) collective-permute-start(bf16[336,384]{1,0:T(8,128)(2,1)S(1)} %multiply_convert_fusion.1), channel_id=1, source_target_pairs={{0,5},{2,7},{4,0},{6,2},{1,4},{3,6},{5,1},{7,3},{8,13},{10,15},{12... | collective-permute-start | bytes 774152 | tf_op jit(solution)/shard_map/ppermute | solution.py:226
  (14 other events, 74.5 us)

commit v3 on v2

--- a/solution.py
+++ b/solution.py
@@ -61,19 +61,12 @@
     return jnp.where(z <= 62, pltpu.roll(part, SLAB - 1, 1), 0.0)
 
 
-def fill_windows(halo_refs, stack_ref, sy, mirror, act):
-    own_ref, left_ref, right_ref, y_ref, y_left_ref, y_right_ref = halo_refs
+def fill_windows(own_ref, oth_ref, stack_ref, sy, mirror, act):
     lane = lanes()
     low = lane < 64
     for xp in range(NXL + 2):
-        at = slice((xp - 1) * SLAB, xp * SLAB)
-        if xp == 0:
-            own, oth = left_ref[...], y_left_ref[...]
-        elif xp == NXL + 1:
-            own, oth = right_ref[...], y_right_ref[...]
-        else:
-            own, oth = own_ref[:, at], y_ref[:, at]
-        own, oth = own.astype(F32), oth.astype(F32)
+        at = slice(xp * SLAB, (xp + 1) * SLAB)
+        own, oth = own_ref[:, at].astype(F32), oth_ref[:, at].astype(F32)
         if act:
             own, oth = jnp.maximum(own, 0.0), jnp.maximum(oth, 0.0)
         r_own, r_oth = pltpu.roll(own, 64, 1), pltpu.roll(oth, 64, 1)
@@ -97,9 +90,7 @@
     return lax.dot_general(left, right, (((1,), (1,)), ((), ())), preferred_element_type=F32)
 
 
-def act_grad_body(
-    ids, w_ref, grad_ref, mid_ref, left_ref, right_ref, y_ref, y_left_ref, y_right_ref, u_ref
-):
+def act_grad_body(ids, w_ref, grad_ref, own_ref, over_ref, pack_ref, u_ref):
     sy = ids[1]
     grad = grad_ref[...]
     u_ref[...] = jnp.zeros_like(u_ref)
@@ -119,36 +110,48 @@
         r0, r2 = pltpu.roll(v[0], 64, 1), pltpu.roll(v[2], 64, 1)
         own = v[1] + jnp.where(low, r0, r2)
         over = jnp.where(sy == 0, jnp.where(low, r2, 0.0), jnp.where(low, 0.0, r0))
-        if xp == 0:
-            left_ref[...], y_left_ref[...] = own, over
-        elif xp == NXL + 1:
-            right_ref[...], y_right_ref[...] = own, over
-        else:
-            at = slice((xp - 1) * SLAB, xp * SLAB)
-            mid_ref[:, at], y_ref[:, at] = own, over
-
-
-def delta_body(ids, pre_ref, mid_ref, *refs):
-    left_ref, right_ref, y_ref, y_left_ref, y_right_ref, out_ref, first_ref, last_ref = refs
-    for xl in range(NXL):
-        at = slice(xl * SLAB, (xl + 1) * SLAB)
-        grad = mid_ref[:, at] + y_ref[:, at]
-        if xl == 0:
-            grad = grad + left_ref[...] + y_left_ref[...]
-        if xl == NXL - 1:
-            grad = grad + right_ref[...] + y_right_ref[...]
-        delta = jnp.where(pre_ref[:, at].astype(F32) > 0, grad, 0.0).astype(BF)
-        out_ref[:, at] = delta
-        if xl == 0:
-            first_ref[...] = delta
-        if xl == NXL - 1:
-            last_ref[...] = delta
+        own_ref[:, at], over_ref[:, at] = own, over
+        pack_ref[:, at] = jnp.where(low, jnp.where(sy == 0, over, own), jnp.where(sy == 0, own, over))
+
+
+def join_y_body(ids, own_ref, over_ref, pack_ref, own_out, oth_out, left_out, right_out):
+    sy = ids[1]
+    low = lanes() < 64
+    for xp in range(NXL + 2):
+        at = slice(xp * SLAB, (xp + 1) * SLAB)
+        pack = pack_ref[:, at]
+        lower, upper = jnp.where(low, pack, 0.0), jnp.where(low, 0.0, pack)
+        own = own_ref[:, at] + jnp.where(sy == 0, upper, lower)
+        oth = over_ref[:, at] + jnp.where(sy == 0, lower, upper)
+        own_out[:, at], oth_out[:, at] = own, oth
+        for out, first in ((left_out, 0), (right_out, NXL)):
+            if first <= xp < first + 2:
+                k = (xp - first) * SLAB
+                out[:, k : k + SLAB] = own
+                out[:, k + 2 * SLAB : k + 3 * SLAB] = oth
+
+
+def delta_body(ids, own_ref, oth_ref, left_ref, right_ref, pre_own_ref, pre_oth_ref, own_out, oth_out):
+    for xp in range(NXL + 2):
+        at = slice(xp * SLAB, (xp + 1) * SLAB)
+        for grad_ref, pre_ref, out, half in (
+            (own_ref, pre_own_ref, own_out, 0),
+            (oth_ref, pre_oth_ref, oth_out, 2 * SLAB),
+        ):
+            grad = grad_ref[:, at]
+            if xp < 2:
+                k = half + xp * SLAB
+                grad = grad + left_ref[:, k : k + SLAB]
+            if xp >= NXL:
+                k = half + (xp - NXL) * SLAB
+                grad = grad + right_ref[:, k : k + SLAB]
+            out[:, at] = jnp.where(pre_ref[:, at].astype(F32) > 0, grad, 0.0).astype(BF)
 
 
 def filter_body(act, mirror, ids, *refs):
-    halo_refs, (full_ref, keep_ref, send_ref, stack_ref) = refs[:6], refs[6:]
+    own_ref, oth_ref, full_ref, keep_ref, send_ref, stack_ref = refs
     sy, core = ids[1], ids[2]
-    fill_windows(halo_refs, stack_ref, sy, mirror, act)
+    fill_windows(own_ref, oth_ref, stack_ref, sy, mirror, act)
     mine = full_ref[pl.ds(pl.multiple_of(core * HALF, HALF), HALF), :]
     other = full_ref[pl.ds(pl.multiple_of((1 - core) * HALF, HALF), HALF), :]
     step = 3 * C
@@ -161,8 +164,8 @@
 
 
 def data_body(ids, *refs):
-    halo_refs, (w_ref, out_ref, stack_ref) = refs[:6], refs[6:]
-    fill_windows(halo_refs, stack_ref, ids[1], True, False)
+    own_ref, oth_ref, w_ref, out_ref, stack_ref = refs
+    fill_windows(own_ref, oth_ref, stack_ref, ids[1], True, False)
     for i in range(3):
         out_ref[i * 256 : (i + 1) * 256, :] = jnp.dot(
             w_ref[i * 256 : (i + 1) * 256, :], stack_ref[...], preferred_element_type=F32
@@ -178,14 +181,15 @@
     ]
 
 
-def swap(to_left, to_right, whole, y_to_left, y_to_right):
+def halo(whole):
     send = functools.partial(lax.ppermute, axis_name=LINE)
-    whole = send(whole, perm=to_side(0, True))
-    y_left = send(y_to_right, perm=to_side(1, True))
-    y_right = send(y_to_left, perm=to_side(-1, True))
-    left = send(to_right, perm=to_side(1, False))
-    right = send(to_left, perm=to_side(-1, False))
-    return left, right, whole, y_left, y_right
+    first, last = whole[:, :SLAB], whole[:, whole.shape[1] - SLAB :]
+    sides = []
+    for flip, mid in ((False, whole), (True, send(whole, perm=to_side(0, True)))):
+        left = send(last, perm=to_side(1, flip))
+        right = send(first, perm=to_side(-1, flip))
+        sides.append(jnp.concatenate([left, mid, right], axis=1))
+    return tuple(sides)
 
 
 def to_all(x, axis, count):
@@ -260,55 +264,61 @@
     ids = jnp.stack([sx, sy, core, chip]).astype(jnp.int32)
     n_pos = NXL * SLAB
     factor = 1.0 / 64.0
-    edge_f = jax.ShapeDtypeStruct((C, SLAB), F32)
-    edge_b = jax.ShapeDtypeStruct((C, SLAB), BF)
+    wide = n_pos + 2 * SLAB
+    wide_f = jax.ShapeDtypeStruct((C, wide), F32)
+    wide_b = jax.ShapeDtypeStruct((C, wide), BF)
     mid_f = jax.ShapeDtypeStruct((C, n_pos), F32)
-    mid_b = jax.ShapeDtypeStruct((C, n_pos), BF)
 
     grad = to_all(out_grad.reshape(C, n_pos), "ch", 16).reshape(CH, n_pos)
-    pre = pre_act.reshape(C, n_pos)
-    first, last = pre[:, :SLAB], pre[:, n_pos - SLAB :]
-    pre_halo = swap(first, last, pre, first, last)
+    pre = halo(pre_act.reshape(C, n_pos))
     w_two = weight_two.reshape(ROWS, CH)
     w_one = weight_one.reshape(ROWS, CH).T
     mine_in = inputs.reshape(C, n_pos)
-    grad, w_one, mine_in, pre_halo = lax.optimization_barrier((grad, w_one, mine_in, pre_halo))
+    grad, w_one, mine_in, pre = lax.optimization_barrier((grad, w_one, mine_in, pre))
     full_in = to_all(mine_in, "ch", 16).reshape(CH, n_pos)
 
-    mid, left, right, y_mid, y_left, y_right = call(
+    own, over, pack = call(
         act_grad_body,
-        (mid_f, edge_f, edge_f, mid_f, edge_f, edge_f),
-        [pltpu.VMEM((3, 3 * C, n_pos + 2 * SLAB), F32)],
+        (wide_f, wide_f, wide_f),
+        [pltpu.VMEM((3, 3 * C, wide), F32)],
         2,
     )(ids, w_two, grad)
-    sums = swap(left, right, y_mid, y_left, y_right)
+    pack = lax.ppermute(pack, LINE, to_side(0, True))
 
     filter_outs = (
         jax.ShapeDtypeStruct((ROWSP, HALF), F32),
         jax.ShapeDtypeStruct((ROWSP, HALF), BF),
     )
     stack = pltpu.VMEM((ROWS, n_pos), BF)
-    keep2, send2 = call(functools.partial(filter_body, True, False), filter_outs, [stack], 7)(
-        ids, pre, *pre_halo, grad
-    )
-    sums, send2 = lax.optimization_barrier((sums, send2))
+    keep2, send2 = call(functools.partial(filter_body, True, False), filter_outs, [stack], 3)(
+        ids, *pre, grad
+    )
+    pack, send2 = lax.optimization_barrier((pack, send2))
+    own, oth, left, right = call(join_y_body, (wide_f, wide_f, mid_f, mid_f), [], 3)(
+        ids, own, over, pack
+    )
+    from_left = lax.ppermute(right, LINE, to_side(1, False))
+    from_right = lax.ppermute(left, LINE, to_side(-1, False))
     got2 = lax.ppermute(send2, LINE, OTHER_CORE)
-    delta, first, last = call(delta_body, (mid_b, edge_b, edge_b), [], 7)(ids, pre, mid, *sums)
-    halo = swap(first, last, delta, first, last)
     split2 = chip_split(ids, keep2, got2)
-    halo, _ = lax.optimization_barrier((halo, split2))
-
-    keep1, send1 = call(functools.partial(filter_body, False, True), filter_outs, [stack], 7)(
-        ids, delta, *halo, full_in
+    from_left, from_right, full_in, _ = lax.optimization_barrier(
+        (from_left, from_right, full_in, split2)
+    )
+    delta = call(delta_body, (wide_b, wide_b), [], 6)(
+        ids, own, oth, from_left, from_right, *pre
+    )
+
+    keep1, send1 = call(functools.partial(filter_body, False, True), filter_outs, [stack], 3)(
+        ids, *delta, full_in
     )
     got1 = lax.ppermute(send1, LINE, OTHER_CORE)
-    terms = call(data_body, jax.ShapeDtypeStruct((CH, n_pos), BF), [stack], 7)(
-        ids, delta, *halo, w_one
-    )
-    terms, got1 = lax.optimization_barrier((terms, got1))
+    split1 = chip_split(ids, keep1, got1)
+    delta, _ = lax.optimization_barrier((delta, split1))
+    terms = call(data_body, jax.ShapeDtypeStruct((CH, n_pos), BF), [stack], 3)(
+        ids, *delta, w_one
+    )
     got = lax.all_to_all(terms.reshape(16, C, n_pos), "ch", 0, 0, tiled=True)
     block2 = line_sum(*split2, factor)
-    split1 = chip_split(ids, keep1, got1)
     block1 = line_sum(*split1, factor)
     pair2 = line_spread(block2)
     input_grad = got.astype(F32).sum(axis=0).astype(BF).reshape(shape)

time: 149 us -> 128 us (0.86)
  starting transfers between devices: 89.2 us -> 62 us
  local copies, waits for them, and re-layouts: 14.7 us -> 18.4 us
    ppermute x15 -> x8, starting transfers between devices: 41.3 us -> 20.4 us  [the longest x2 6.79 us: halo(): left = send(last, perm=to_side(1, flip))]
    ppermute x2, starting transfers between devices: 12.5 us -> 1.81 us  [line_spread(): return (mine, lax.ppermute(mine, LINE, OTHER_CORE))]
    ppermute x6, starting transfers between devices: 5.65 us -> 9.87 us  [line_spread(): got = {k: lax.ppermute(block, LINE, along(k)) for k in (1, 3, 2)}]
    unnamed x27 -> x41, local copies, waits for them, and re-layouts: 7.76 us -> 10.8 us
    ppermute x6, waiting for transfers between devices: 5.53 us -> 8.45 us  [line_sum(): lax.ppermute(v, LINE, along(k))]
    ppermute x6, waiting for transfers between devices: 14.6 us -> 12 us  [line_spread(): got = {k: lax.ppermute(block, LINE, along(k)) for k in (1, 3, 2)}]
    all_to_all x1, starting transfers between devices: 7.08 us -> 5.24 us  [shards(): got = lax.all_to_all(terms.reshape(16, C, n_pos), 'ch', 0, 0, tiled=True)]
    pallas_call x5 -> x6, Pallas kernels: 12.2 us -> 12.9 us  [the longest x1 3.82 us: shards(): call(functools.partial(filter_body, True, False), filter_outs, [stack], 3)]
  transfers between devices with their start and end apart: 34 -> 27, of which waited for: 6 -> 9; matrix products, arithmetic and copies ran while one was open for 5% -> 7% of each run, Pallas kernels for 9% -> 10%
where the time goes in v3:
time: 128 us; the launch traced here: 126 us
  starting transfers between devices  62 us (48%)
  Pallas kernels  21.2 us (17%)
  waiting for transfers between devices  21.1 us (16%)
  local copies, waits for them, and re-layouts  18.4 us (14%)
  other arithmetic  2.76 us (2%)
    all_to_all x2, starting transfers between devices, to_all(): return lax.all_to_all(many, axis, 0, 0, tiled=True)  15.5 us
    ppermute x6, waiting for transfers between devices, line_spread(): got = {k: lax.ppermute(block, LINE, along(k)) for k in (1, 3, 2)}  12 us
    unnamed x41, local copies, waits for them, and re-layouts  10.8 us
    ppermute x6, starting transfers between devices, line_spread(): got = {k: lax.ppermute(block, LINE, along(k)) for k in (1, 3, 2)}  9.87 us
    ppermute x6, waiting for transfers between devices, line_sum(): lax.ppermute(v, LINE, along(k))  8.45 us
    ppermute x2, starting transfers between devices, halo(): left = send(last, perm=to_side(1, flip))  6.79 us
    ppermute x2, starting transfers between devices, halo(): right = send(first, perm=to_side(-1, flip))  6.78 us
    ppermute x6, starting transfers between devices, line_sum(): lax.ppermute(v, LINE, along(k))  6.54 us
  transfers between devices with their start and end apart: 27, of which 9 were waited for; matrix products, arithmetic and copies ran while one was open for 7% of the time, Pallas kernels for 10%

profile of v3, /device:TPU:1, one launch (start us, length us, event | category | flops | bytes accessed | tf_op | source)
XLA Modules:
  0.0 126.4 jit_solution(8637986188435184841)
XLA Ops:
  2.7 8.6 %all-to-all-start = ((bf16[16,48,512]{2,1,0:T(8,128)(2,1)}), bf16[16,48,512]{2,1,0:T(8,128)(2,1)S(1)}, u32[]{:S(2)}, u32[]{:S(2)}) async-start(bf16[16,48,512]{2,1,0:T(8,128)(2,1)} %broadcast_in_dim.14), calls=%async_computation | async-start | bytes 1572864 | tf_op jit(solution)/shard_map/all_to_all | solution.py:197
  11.4 2.9 %collective-permute-start.1 = (bf16[48,128]{1,0:T(8,128)(2,1)S(1)}, bf16[48,128]{1,0:T(8,128)(2,1)S(1)}, u32[]{:S(2)}, u32[]{:S(2)}) collective-permute-start(bf16[48,128]{1,0:T(8,128)(2,1)S(1)} %get-tuple-element.74), channel_id=1, source_target_pairs={{2,0},{3,1},{4,2},{5,3},{6,4},{7,5},{10,8},{11,9},{12,10},{13,11},... | collective-permute-start | bytes 36872 | tf_op jit(solution)/shard_map/ppermute | solution.py:190
  14.3 3.9 %collective-permute-start.4 = (bf16[48,128]{1,0:T(8,128)(2,1)S(1)}, bf16[48,128]{1,0:T(8,128)(2,1)S(1)}, u32[]{:S(2)}, u32[]{:S(2)}) collective-permute-start(bf16[48,128]{1,0:T(8,128)(2,1)S(1)} %get-tuple-element.74), channel_id=1, source_target_pairs={{2,1},{3,0},{4,3},{5,2},{6,5},{7,4},{10,9},{11,8},{12,11},{13,10},... | collective-permute-start | bytes 36872 | tf_op jit(solution)/shard_map/ppermute | solution.py:190
  19.0 3.0 %collective-permute-start = (bf16[48,128]{1,0:T(8,128)(2,1)S(1)}, bf16[48,128]{1,0:T(8,128)(2,1)S(1)}, u32[]{:S(2)}, u32[]{:S(2)}) collective-permute-start(bf16[48,128]{1,0:T(8,128)(2,1)S(1)} %get-tuple-element.73), channel_id=1, source_target_pairs={{0,2},{1,3},{2,4},{3,5},{4,6},{5,7},{8,10},{9,11},{10,12},{11,13},... | collective-permute-start | bytes 36872 | tf_op jit(solution)/shard_map/ppermute | solution.py:189
  22.0 3.8 %collective-permute-start.2 = (bf16[48,128]{1,0:T(8,128)(2,1)S(1)}, bf16[48,128]{1,0:T(8,128)(2,1)S(1)}, u32[]{:S(2)}, u32[]{:S(2)}) collective-permute-start(bf16[48,128]{1,0:T(8,128)(2,1)S(1)} %get-tuple-element.73), channel_id=1, source_target_pairs={{0,3},{1,2},{2,5},{3,4},{4,7},{5,6},{8,11},{9,10},{10,13},{11,12},... | collective-permute-start | bytes 36872 | tf_op jit(solution)/shard_map/ppermute | solution.py:189
  25.9 2.9 %copy.9 = bf16[1296,768]{0,1:T(8,128)(2,1)S(1)} copy(bf16[1296,768]{1,0:T(8,128)(2,1)} %bitcast.23) | data formatting | bytes 3981312 | tf_op jit(solution)/shard_map/reshape | solution.py:275
  29.7 1.5 %copy-done.2 = bf16[27,48,768]{2,1,0:T(8,128)(2,1)S(1)} copy-done((bf16[27,48,768]{2,1,0:T(8,128)(2,1)S(1)}, bf16[27,48,768]{2,1,0:T(8,128)(2,1)}, u32[]{:S(2)}) %copy-start.2) | copy-done | bytes 1990680
  31.3 1.9 %shard_map.76 = (f32[48,768]{1,0:T(8,128)S(1)}, f32[48,768]{1,0:T(8,128)S(1)}, f32[48,768]{1,0:T(8,128)S(1)}) custom-call(s32[4]{0:T(128)S(1)} %pad_add_fusion.ids, bf16[1296,768]{1,0:T(8,128)(2,1)S(1)} %bitcast.19, bf16[768,512]{1,0:T(8,128)(2,1)S(1)} %bitcast.15), custom_call_target="tpu_custom_call" | custom-call | tf_op jit(solution)/shard_map/pallas_call | solution.py:280
  33.2 1.7 %collective-permute-start.5 = (f32[48,768]{1,0:T(8,128)S(1)}, f32[48,768]{1,0:T(8,128)S(1)}, u32[]{:S(2)}, u32[]{:S(2)}) collective-permute-start(f32[48,768]{1,0:T(8,128)S(1)} %get-tuple-element.41), channel_id=1, source_target_pairs={{0,1},{1,0},{2,3},{3,2},{4,5},{5,4},{6,7},{7,6},{8,9},{9,8},{10,11... | collective-permute-start | bytes 442376 | tf_op jit(solution)/shard_map/ppermute | solution.py:286
  34.9 3.8 %shard_map.77 = (f32[1344,384]{1,0:T(8,128)S(1)}, bf16[1344,384]{1,0:T(8,128)(2,1)}) custom-call(s32[4]{0:T(128)S(1)} %pad_add_fusion.ids, bf16[48,768]{1,0:T(8,128)(2,1)S(1)} %pad_maximum_fusion.1.refs_0_.pre_own_ref, bf16[48,768]{1,0:T(8,128)(2,1)S(1)} %pad_maximum_fusion.2.refs_1_.pre_oth_ref, bf16[768,512]{1,0:T(8,128)(2,1)S(1)} %bitcast.16), custom_call_target="tpu_custom_call" | custom-call | tf_op jit(solution)/shard_map/pallas_call | solution.py:293
  42.1 6.9 %all-to-all-start.1 = ((bf16[16,48,512]{2,1,0:T(8,128)(2,1)}), bf16[16,48,512]{2,1,0:T(8,128)(2,1)S(1)}, u32[]{:S(2)}, u32[]{:S(2)}) async-start(bf16[16,48,512]{2,1,0:T(8,128)(2,1)} %broadcast_in_dim.15), calls=%async_computation.1 | async-start | bytes 1572864 | tf_op jit(solution)/shard_map/all_to_all | solution.py:197
  51.5 1.9 %collective-permute-start.6 = (f32[48,512]{1,0:T(8,128)S(1)}, f32[48,512]{1,0:T(8,128)S(1)}, u32[]{:S(2)}, u32[]{:S(2)}) collective-permute-start(f32[48,512]{1,0:T(8,128)S(1)} %get-tuple-element.48), channel_id=1, source_target_pairs={{0,2},{1,3},{2,4},{3,5},{4,6},{5,7},{8,10},{9,11},{10,12},{11,13},... | collective-permute-start | bytes 294920 | tf_op jit(solution)/shard_map/ppermute | solution.py:300
  53.4 2.4 %collective-permute-start.7 = (f32[48,512]{1,0:T(8,128)S(1)}, f32[48,512]{1,0:T(8,128)S(1)}, u32[]{:S(2)}, u32[]{:S(2)}) collective-permute-start(f32[48,512]{1,0:T(8,128)S(1)} %get-tuple-element.49), channel_id=1, source_target_pairs={{2,0},{3,1},{4,2},{5,3},{6,4},{7,5},{10,8},{11,9},{12,10},{13,11},... | collective-permute-start | bytes 294920 | tf_op jit(solution)/shard_map/ppermute | solution.py:301
  55.9 1.6 %copy-done.1 = f32[1344,384]{1,0:T(8,128)S(1)} copy-done((f32[1344,384]{1,0:T(8,128)S(1)}, f32[1344,384]{1,0:T(8,128)}, u32[]{:S(2)}) %copy-start.1) | copy-done | bytes 2064408
  57.4 1.4 %shard_map.79 = (f32[336,384]{1,0:T(8,128)S(1)}, bf16[336,384]{1,0:T(8,128)(2,1)S(1)}, bf16[336,384]{1,0:T(8,128)(2,1)S(1)}, bf16[336,384]{1,0:T(8,128)(2,1)S(1)}) custom-call(s32[4]{0:T(128)S(1)} %pad_add_fusion.ids, f32[1344,384]{1,0:T(8,128)S(1)} %copy-done.1, bf16[1344,384]{1,0:T(8,128)(2,1)} %collective-permute-done.8.got_ref), custom_call_target="tpu_custom_call" | custom-call | tf_op jit(solution)/shard_map/pallas_call | solution.py:218
  64.4 2.9 %shard_map.81 = (f32[1344,384]{1,0:T(8,128)S(1)}, bf16[1344,384]{1,0:T(8,128)(2,1)S(1)}) custom-call(s32[4]{0:T(128)S(1)} %pad_add_fusion.ids, bf16[48,768]{1,0:T(8,128)(2,1)S(1)} %get-tuple-element.68.refs_0_, bf16[48,768]{1,0:T(8,128)(2,1)S(1)} %get-tuple-element.69.refs_1_, bf16[768,512]{1,0:T(8,128)(2,1)S(1)} %bitcast.18), custom_call_target="tpu_custom_call" | custom-call | tf_op jit(solution)/shard_map/pallas_call | solution.py:311
  67.4 1.5 %collective-permute-start.9 = (bf16[1344,384]{1,0:T(8,128)(2,1)S(1)}, bf16[1344,384]{1,0:T(8,128)(2,1)S(1)}, u32[]{:S(2)}, u32[]{:S(2)}) collective-permute-start(bf16[1344,384]{1,0:T(8,128)(2,1)S(1)} %get-tuple-element.63), channel_id=1, source_target_pairs={{0,2},{2,0},{4,6},{6,4},{1,3},{3,1},{5,7},{7,5},{8,10},{10,8},{12,... | collective-permute-start | bytes 3096584 | tf_op jit(solution)/shard_map/ppermute | solution.py:314
  68.9 1.7 %collective-permute-start.19 = (bf16[336,384]{1,0:T(8,128)(2,1)}, bf16[336,384]{1,0:T(8,128)(2,1)}, u32[]{:S(2)}, u32[]{:S(2)}) collective-permute-start(bf16[336,384]{1,0:T(8,128)(2,1)} %copy-done.13), channel_id=1, source_target_pairs={{0,1},{2,3},{4,5},{6,7},{1,0},{3,2},{5,4},{7,6},{8,9},{10,11},{12,... | collective-permute-start | bytes 774152 | tf_op jit(solution)/shard_map/ppermute | solution.py:222
  70.7 1.4 %collective-permute-start.17 = (bf16[336,384]{1,0:T(8,128)(2,1)}, bf16[336,384]{1,0:T(8,128)(2,1)}, u32[]{:S(2)}, u32[]{:S(2)}) collective-permute-start(bf16[336,384]{1,0:T(8,128)(2,1)} %copy-done.11), channel_id=1, source_target_pairs={{0,4},{2,6},{4,1},{6,3},{1,5},{3,7},{5,0},{7,2},{8,12},{10,14},{12... | collective-permute-start | bytes 774152 | tf_op jit(solution)/shard_map/ppermute | solution.py:222
  72.9 3.1 %shard_map.83 = bf16[768,512]{1,0:T(8,128)(2,1)} custom-call(s32[4]{0:T(128)S(1)} %pad_add_fusion.ids, bf16[48,768]{1,0:T(8,128)(2,1)S(1)} %get-tuple-element.68.refs_0_, bf16[48,768]{1,0:T(8,128)(2,1)S(1)} %get-tuple-element.69.refs_1_, bf16[768,1296]{1,0:T(8,128)(2,1)S(1)} %bitcast.14), custom_call_target="tpu_custom_call" | custom-call | tf_op jit(solution)/shard_map/pallas_call | solution.py:317
  75.9 5.2 %all-to-all-start.2 = ((bf16[16,48,512]{2,1,0:T(8,128)(2,1)}), bf16[16,48,512]{2,1,0:T(8,128)(2,1)S(1)}, u32[]{:S(2)}, u32[]{:S(2)}) async-start(bf16[16,48,512]{2,1,0:T(8,128)(2,1)} %bitcast.9), calls=%async_computation.2 | async-start | bytes 1572864 | tf_op jit(solution)/shard_map/all_to_all | solution.py:320
  82.5 1.6 %collective-permute-start.11 = (bf16[336,384]{1,0:T(8,128)(2,1)}, bf16[336,384]{1,0:T(8,128)(2,1)S(1)}, u32[]{:S(2)}, u32[]{:S(2)}) collective-permute-start(bf16[336,384]{1,0:T(8,128)(2,1)} %copy-done.14), channel_id=1, source_target_pairs={{0,5},{2,7},{4,0},{6,2},{1,4},{3,6},{5,1},{7,3},{8,13},{10,15},{12... | collective-permute-start | bytes 774152 | tf_op jit(solution)/shard_map/ppermute | solution.py:222
  85.9 2.2 %collective-permute-start.22 = (bf16[336,384]{1,0:T(8,128)(2,1)S(1)}, bf16[336,384]{1,0:T(8,128)(2,1)S(1)}, u32[]{:S(2)}, u32[]{:S(2)}) collective-permute-start(bf16[336,384]{1,0:T(8,128)(2,1)S(1)} %multiply_convert_fusion), channel_id=1, source_target_pairs={{0,5},{2,7},{4,0},{6,2},{1,4},{3,6},{5,1},{7,3},{8,13},{10,15},{12... | collective-permute-start | bytes 774152 | tf_op jit(solution)/shard_map/ppermute | solution.py:230
  89.9 5.7 %collective-permute-done.11 = bf16[336,384]{1,0:T(8,128)(2,1)S(1)} collective-permute-done((bf16[336,384]{1,0:T(8,128)(2,1)}, bf16[336,384]{1,0:T(8,128)(2,1)S(1)}, u32[]{:S(2)}, u32[]{:S(2)}) %collective-permute-start.11) | collective-permute-done | bytes 258080 | tf_op jit(solution)/shard_map/ppermute | solution.py:222
  95.6 2.3 %collective-permute-done.10 = bf16[336,384]{1,0:T(8,128)(2,1)S(1)} collective-permute-done((bf16[336,384]{1,0:T(8,128)(2,1)S(1)}, bf16[336,384]{1,0:T(8,128)(2,1)S(1)}, u32[]{:S(2)}, u32[]{:S(2)}) %collective-permute-start.10) | collective-permute-done | bytes 258080 | tf_op jit(solution)/shard_map/ppermute | solution.py:222
  99.0 2.2 %collective-permute-start.14 = (bf16[336,384]{1,0:T(8,128)(2,1)S(1)}, bf16[336,384]{1,0:T(8,128)(2,1)S(1)}, u32[]{:S(2)}, u32[]{:S(2)}) collective-permute-start(bf16[336,384]{1,0:T(8,128)(2,1)S(1)} %multiply_convert_fusion.1), channel_id=1, source_target_pairs={{0,1},{2,3},{4,5},{6,7},{1,0},{3,2},{5,4},{7,6},{8,9},{10,11},{12,... | collective-permute-start | bytes 774152 | tf_op jit(solution)/shard_map/ppermute | solution.py:230
  101.6 6.1 %collective-permute-done.20 = bf16[336,384]{1,0:T(8,128)(2,1)} collective-permute-done((bf16[336,384]{1,0:T(8,128)(2,1)S(1)}, bf16[336,384]{1,0:T(8,128)(2,1)}, u32[]{:S(2)}, u32[]{:S(2)}) %collective-permute-start.20) | collective-permute-done | bytes 258080 | tf_op jit(solution)/shard_map/ppermute | solution.py:230
  109.7 4.1 %collective-permute-start.15 = (bf16[336,384]{1,0:T(8,128)(2,1)S(1)}, bf16[336,384]{1,0:T(8,128)(2,1)S(1)}, u32[]{:S(2)}, u32[]{:S(2)}) collective-permute-start(bf16[336,384]{1,0:T(8,128)(2,1)S(1)} %multiply_convert_fusion.1), channel_id=1, source_target_pairs={{0,5},{2,7},{4,0},{6,2},{1,4},{3,6},{5,1},{7,3},{8,13},{10,15},{12... | collective-permute-start | bytes 774152 | tf_op jit(solution)/shard_map/ppermute | solution.py:230
  114.5 2.8 %collective-permute-done.14 = bf16[336,384]{1,0:T(8,128)(2,1)S(1)} collective-permute-done((bf16[336,384]{1,0:T(8,128)(2,1)S(1)}, bf16[336,384]{1,0:T(8,128)(2,1)S(1)}, u32[]{:S(2)}, u32[]{:S(2)}) %collective-permute-start.14) | collective-permute-done | bytes 258080 | tf_op jit(solution)/shard_map/ppermute | solution.py:230
  117.4 1.9 %collective-permute-done.15 = bf16[336,384]{1,0:T(8,128)(2,1)S(1)} collective-permute-done((bf16[336,384]{1,0:T(8,128)(2,1)S(1)}, bf16[336,384]{1,0:T(8,128)(2,1)S(1)}, u32[]{:S(2)}, u32[]{:S(2)}) %collective-permute-start.15) | collective-permute-done | bytes 258080 | tf_op jit(solution)/shard_map/ppermute | solution.py:230
  120.3 3.0 %shard_map.85 = f32[27,48,768]{2,1,0:T(8,128)} custom-call(s32[4]{0:T(128)S(1)} %pad_add_fusion.ids, bf16[4,7,48,384]{3,2,1,0:T(8,128)(2,1)S(1)} %bitcast.17, bf16[4,7,48,384]{3,2,1,0:T(8,128)(2,1)S(1)} %bitcast.21), custom_call_target="tpu_custom_call" | custom-call | tf_op jit(solution)/shard_map/pallas_call | solution.py:246
  123.4 3.0 %shard_map.84 = f32[27,48,768]{2,1,0:T(8,128)} custom-call(s32[4]{0:T(128)S(1)} %pad_add_fusion.ids, bf16[4,7,48,384]{3,2,1,0:T(8,128)(2,1)S(1)} %bitcast.20, bf16[4,7,48,384]{3,2,1,0:T(8,128)(2,1)S(1)} %bitcast.22), custom_call_target="tpu_custom_call" | custom-call | tf_op jit(solution)/shard_map/pallas_call | solution.py:246
  (89 shorter events, 26.2 us)
Async XLA Ops:
  0.6 10.6 %copy-start.17 = (bf16[48,4,2,64]{3,2,1,0:T(2,128)(2,1)S(1)}, bf16[48,4,2,64]{3,2,1,0:T(2,128)(2,1)}, u32[]{:S(2)}) copy-start(bf16[48,4,2,64]{3,2,1,0:T(2,128)(2,1)} %param.6) | copy-start | bytes 147460
  2.7 27.0 %all-to-all-start = ((bf16[16,48,512]{2,1,0:T(8,128)(2,1)}), bf16[16,48,512]{2,1,0:T(8,128)(2,1)S(1)}, u32[]{:S(2)}, u32[]{:S(2)}) async-start(bf16[16,48,512]{2,1,0:T(8,128)(2,1)} %broadcast_in_dim.14), calls=%async_computation | async-start | bytes 1572864 | tf_op jit(solution)/shard_map/all_to_all | solution.py:197
  11.4 18.2 %collective-permute-start.1 = (bf16[48,128]{1,0:T(8,128)(2,1)S(1)}, bf16[48,128]{1,0:T(8,128)(2,1)S(1)}, u32[]{:S(2)}, u32[]{:S(2)}) collective-permute-start(bf16[48,128]{1,0:T(8,128)(2,1)S(1)} %get-tuple-element.74), channel_id=1, source_target_pairs={{2,0},{3,1},{4,2},{5,3},{6,4},{7,5},{10,8},{11,9},{12,10},{13,11},... | collective-permute-start | bytes 36872 | tf_op jit(solution)/shard_map/ppermute | solution.py:190
  14.3 15.4 %collective-permute-start.4 = (bf16[48,128]{1,0:T(8,128)(2,1)S(1)}, bf16[48,128]{1,0:T(8,128)(2,1)S(1)}, u32[]{:S(2)}, u32[]{:S(2)}) collective-permute-start(bf16[48,128]{1,0:T(8,128)(2,1)S(1)} %get-tuple-element.74), channel_id=1, source_target_pairs={{2,1},{3,0},{4,3},{5,2},{6,5},{7,4},{10,9},{11,8},{12,11},{13,10},... | collective-permute-start | bytes 36872 | tf_op jit(solution)/shard_map/ppermute | solution.py:190
  18.2 11.4 %collective-permute-start.3 = (bf16[48,512]{1,0:T(8,128)(2,1)S(1)}, bf16[48,512]{1,0:T(8,128)(2,1)S(1)}, u32[]{:S(2)}, u32[]{:S(2)}) collective-permute-start(bf16[48,512]{1,0:T(8,128)(2,1)S(1)} %reshape.48), channel_id=1, source_target_pairs={{0,1},{1,0},{2,3},{3,2},{4,5},{5,4},{6,7},{7,6},{8,9},{9,8},{10,11... | collective-permute-start | bytes 147464 | tf_op jit(solution)/shard_map/ppermute | solution.py:188
  19.0 10.6 %collective-permute-start = (bf16[48,128]{1,0:T(8,128)(2,1)S(1)}, bf16[48,128]{1,0:T(8,128)(2,1)S(1)}, u32[]{:S(2)}, u32[]{:S(2)}) collective-permute-start(bf16[48,128]{1,0:T(8,128)(2,1)S(1)} %get-tuple-element.73), channel_id=1, source_target_pairs={{0,2},{1,3},{2,4},{3,5},{4,6},{5,7},{8,10},{9,11},{10,12},{11,13},... | collective-permute-start | bytes 36872 | tf_op jit(solution)/shard_map/ppermute | solution.py:189
  22.0 7.7 %collective-permute-start.2 = (bf16[48,128]{1,0:T(8,128)(2,1)S(1)}, bf16[48,128]{1,0:T(8,128)(2,1)S(1)}, u32[]{:S(2)}, u32[]{:S(2)}) collective-permute-start(bf16[48,128]{1,0:T(8,128)(2,1)S(1)} %get-tuple-element.73), channel_id=1, source_target_pairs={{0,3},{1,2},{2,5},{3,4},{4,7},{5,6},{8,11},{9,10},{10,13},{11,12},... | collective-permute-start | bytes 36872 | tf_op jit(solution)/shard_map/ppermute | solution.py:189
  31.3 9.9 %copy-start.16 = (bf16[48,512]{1,0:T(8,128)(2,1)S(1)}, bf16[48,512]{1,0:T(8,128)(2,1)}, u32[]{:S(2)}) copy-start(bf16[48,512]{1,0:T(8,128)(2,1)} %reshape.47) | copy-start | bytes 147460
  33.2 15.9 %copy-start.5 = (f32[48,768]{1,0:T(8,128)}, f32[48,768]{1,0:T(8,128)S(1)}, u32[]{:S(2)}) copy-start(f32[48,768]{1,0:T(8,128)S(1)} %get-tuple-element.40.over_ref) | copy-start | bytes 442372
  33.2 6.8 %collective-permute-start.5 = (f32[48,768]{1,0:T(8,128)S(1)}, f32[48,768]{1,0:T(8,128)S(1)}, u32[]{:S(2)}, u32[]{:S(2)}) collective-permute-start(f32[48,768]{1,0:T(8,128)S(1)} %get-tuple-element.41), channel_id=1, source_target_pairs={{0,1},{1,0},{2,3},{3,2},{4,5},{5,4},{6,7},{7,6},{8,9},{9,8},{10,11... | collective-permute-start | bytes 442376 | tf_op jit(solution)/shard_map/ppermute | solution.py:286
  40.0 9.1 %copy-start.7 = (f32[48,768]{1,0:T(8,128)}, f32[48,768]{1,0:T(8,128)S(1)}, u32[]{:S(2)}) copy-start(f32[48,768]{1,0:T(8,128)S(1)} %collective-permute-done.5.pack_ref) | copy-start | bytes 442372
  40.0 15.8 %collective-permute-start.8 = (bf16[1344,384]{1,0:T(8,128)(2,1)}, bf16[1344,384]{1,0:T(8,128)(2,1)}, u32[]{:S(2)}, u32[]{:S(2)}) collective-permute-start(bf16[1344,384]{1,0:T(8,128)(2,1)} %get-tuple-element.52), channel_id=1, source_target_pairs={{0,2},{2,0},{4,6},{6,4},{1,3},{3,1},{5,7},{7,5},{8,10},{10,8},{12,... | collective-permute-start | bytes 3096584 | tf_op jit(solution)/shard_map/ppermute | solution.py:302
  42.1 20.8 %all-to-all-start.1 = ((bf16[16,48,512]{2,1,0:T(8,128)(2,1)}), bf16[16,48,512]{2,1,0:T(8,128)(2,1)S(1)}, u32[]{:S(2)}, u32[]{:S(2)}) async-start(bf16[16,48,512]{2,1,0:T(8,128)(2,1)} %broadcast_in_dim.15), calls=%async_computation.1 | async-start | bytes 1572864 | tf_op jit(solution)/shard_map/all_to_all | solution.py:197
  51.5 10.3 %collective-permute-start.6 = (f32[48,512]{1,0:T(8,128)S(1)}, f32[48,512]{1,0:T(8,128)S(1)}, u32[]{:S(2)}, u32[]{:S(2)}) collective-permute-start(f32[48,512]{1,0:T(8,128)S(1)} %get-tuple-element.48), channel_id=1, source_target_pairs={{0,2},{1,3},{2,4},{3,5},{4,6},{5,7},{8,10},{9,11},{10,12},{11,13},... | collective-permute-start | bytes 294920 | tf_op jit(solution)/shard_map/ppermute | solution.py:300
  53.4 8.3 %collective-permute-start.7 = (f32[48,512]{1,0:T(8,128)S(1)}, f32[48,512]{1,0:T(8,128)S(1)}, u32[]{:S(2)}, u32[]{:S(2)}) collective-permute-start(f32[48,512]{1,0:T(8,128)S(1)} %get-tuple-element.49), channel_id=1, source_target_pairs={{2,0},{3,1},{4,2},{5,3},{6,4},{7,5},{10,8},{11,9},{12,10},{13,11},... | collective-permute-start | bytes 294920 | tf_op jit(solution)/shard_map/ppermute | solution.py:301
  67.4 4.7 %collective-permute-start.9 = (bf16[1344,384]{1,0:T(8,128)(2,1)S(1)}, bf16[1344,384]{1,0:T(8,128)(2,1)S(1)}, u32[]{:S(2)}, u32[]{:S(2)}) collective-permute-start(bf16[1344,384]{1,0:T(8,128)(2,1)S(1)} %get-tuple-element.63), channel_id=1, source_target_pairs={{0,2},{2,0},{4,6},{6,4},{1,3},{3,1},{5,7},{7,5},{8,10},{10,8},{12,... | collective-permute-start | bytes 3096584 | tf_op jit(solution)/shard_map/ppermute | solution.py:314
  68.9 15.2 %collective-permute-start.19 = (bf16[336,384]{1,0:T(8,128)(2,1)}, bf16[336,384]{1,0:T(8,128)(2,1)}, u32[]{:S(2)}, u32[]{:S(2)}) collective-permute-start(bf16[336,384]{1,0:T(8,128)(2,1)} %copy-done.13), channel_id=1, source_target_pairs={{0,1},{2,3},{4,5},{6,7},{1,0},{3,2},{5,4},{7,6},{8,9},{10,11},{12,... | collective-permute-start | bytes 774152 | tf_op jit(solution)/shard_map/ppermute | solution.py:222
  70.6 13.9 %collective-permute-start.18 = (bf16[336,384]{1,0:T(8,128)(2,1)}, bf16[336,384]{1,0:T(8,128)(2,1)}, u32[]{:S(2)}, u32[]{:S(2)}) collective-permute-start(bf16[336,384]{1,0:T(8,128)(2,1)} %copy-done.12), channel_id=1, source_target_pairs={{0,5},{2,7},{4,0},{6,2},{1,4},{3,6},{5,1},{7,3},{8,13},{10,15},{12... | collective-permute-start | bytes 774152 | tf_op jit(solution)/shard_map/ppermute | solution.py:222
  70.7 13.9 %collective-permute-start.17 = (bf16[336,384]{1,0:T(8,128)(2,1)}, bf16[336,384]{1,0:T(8,128)(2,1)}, u32[]{:S(2)}, u32[]{:S(2)}) collective-permute-start(bf16[336,384]{1,0:T(8,128)(2,1)} %copy-done.11), channel_id=1, source_target_pairs={{0,4},{2,6},{4,1},{6,3},{1,5},{3,7},{5,0},{7,2},{8,12},{10,14},{12... | collective-permute-start | bytes 774152 | tf_op jit(solution)/shard_map/ppermute | solution.py:222
  72.9 11.7 %copy-start.4 = (f32[336,384]{1,0:T(8,128)S(1)}, f32[336,384]{1,0:T(8,128)}, u32[]{:S(2)}) copy-start(f32[336,384]{1,0:T(8,128)} %copy-done.3) | copy-start | bytes 1548292
  75.9 22.1 %all-to-all-start.2 = ((bf16[16,48,512]{2,1,0:T(8,128)(2,1)}), bf16[16,48,512]{2,1,0:T(8,128)(2,1)S(1)}, u32[]{:S(2)}, u32[]{:S(2)}) async-start(bf16[16,48,512]{2,1,0:T(8,128)(2,1)} %bitcast.9), calls=%async_computation.2 | async-start | bytes 1572864 | tf_op jit(solution)/shard_map/all_to_all | solution.py:320
  81.2 8.5 %collective-permute-start.12 = (bf16[336,384]{1,0:T(8,128)(2,1)}, bf16[336,384]{1,0:T(8,128)(2,1)S(1)}, u32[]{:S(2)}, u32[]{:S(2)}) collective-permute-start(bf16[336,384]{1,0:T(8,128)(2,1)} %copy-done.15), channel_id=1, source_target_pairs={{0,1},{2,3},{4,5},{6,7},{1,0},{3,2},{5,4},{7,6},{8,9},{10,11},{12,... | collective-permute-start | bytes 774152 | tf_op jit(solution)/shard_map/ppermute | solution.py:222
  82.5 13.1 %collective-permute-start.11 = (bf16[336,384]{1,0:T(8,128)(2,1)}, bf16[336,384]{1,0:T(8,128)(2,1)S(1)}, u32[]{:S(2)}, u32[]{:S(2)}) collective-permute-start(bf16[336,384]{1,0:T(8,128)(2,1)} %copy-done.14), channel_id=1, source_target_pairs={{0,5},{2,7},{4,0},{6,2},{1,4},{3,6},{5,1},{7,3},{8,13},{10,15},{12... | collective-permute-start | bytes 774152 | tf_op jit(solution)/shard_map/ppermute | solution.py:222
  84.0 13.9 %collective-permute-start.10 = (bf16[336,384]{1,0:T(8,128)(2,1)S(1)}, bf16[336,384]{1,0:T(8,128)(2,1)S(1)}, u32[]{:S(2)}, u32[]{:S(2)}) collective-permute-start(bf16[336,384]{1,0:T(8,128)(2,1)S(1)} %get-tuple-element.65), channel_id=1, source_target_pairs={{0,4},{2,6},{4,1},{6,3},{1,5},{3,7},{5,0},{7,2},{8,12},{10,14},{12... | collective-permute-start | bytes 774152 | tf_op jit(solution)/shard_map/ppermute | solution.py:222
  85.9 15.8 %collective-permute-start.22 = (bf16[336,384]{1,0:T(8,128)(2,1)S(1)}, bf16[336,384]{1,0:T(8,128)(2,1)S(1)}, u32[]{:S(2)}, u32[]{:S(2)}) collective-permute-start(bf16[336,384]{1,0:T(8,128)(2,1)S(1)} %multiply_convert_fusion), channel_id=1, source_target_pairs={{0,5},{2,7},{4,0},{6,2},{1,4},{3,6},{5,1},{7,3},{8,13},{10,15},{12... | collective-permute-start | bytes 774152 | tf_op jit(solution)/shard_map/ppermute | solution.py:230
  88.1 13.5 %collective-permute-start.21 = (bf16[336,384]{1,0:T(8,128)(2,1)S(1)}, bf16[336,384]{1,0:T(8,128)(2,1)S(1)}, u32[]{:S(2)}, u32[]{:S(2)}) collective-permute-start(bf16[336,384]{1,0:T(8,128)(2,1)S(1)} %multiply_convert_fusion), channel_id=1, source_target_pairs={{0,1},{2,3},{4,5},{6,7},{1,0},{3,2},{5,4},{7,6},{8,9},{10,11},{12,... | collective-permute-start | bytes 774152 | tf_op jit(solution)/shard_map/ppermute | solution.py:230
  89.7 18.1 %collective-permute-start.20 = (bf16[336,384]{1,0:T(8,128)(2,1)S(1)}, bf16[336,384]{1,0:T(8,128)(2,1)}, u32[]{:S(2)}, u32[]{:S(2)}) collective-permute-start(bf16[336,384]{1,0:T(8,128)(2,1)S(1)} %multiply_convert_fusion), channel_id=1, source_target_pairs={{0,4},{2,6},{4,1},{6,3},{1,5},{3,7},{5,0},{7,2},{8,12},{10,14},{12... | collective-permute-start | bytes 774152 | tf_op jit(solution)/shard_map/ppermute | solution.py:230
  99.0 15.5 %collective-permute-start.13 = (bf16[336,384]{1,0:T(8,128)(2,1)S(1)}, bf16[336,384]{1,0:T(8,128)(2,1)S(1)}, u32[]{:S(2)}, u32[]{:S(2)}) collective-permute-start(bf16[336,384]{1,0:T(8,128)(2,1)S(1)} %multiply_convert_fusion.1), channel_id=1, source_target_pairs={{0,4},{2,6},{4,1},{6,3},{1,5},{3,7},{5,0},{7,2},{8,12},{10,14},{12... | collective-permute-start | bytes 774152 | tf_op jit(solution)/shard_map/ppermute | solution.py:230
  99.0 18.4 %collective-permute-start.14 = (bf16[336,384]{1,0:T(8,128)(2,1)S(1)}, bf16[336,384]{1,0:T(8,128)(2,1)S(1)}, u32[]{:S(2)}, u32[]{:S(2)}) collective-permute-start(bf16[336,384]{1,0:T(8,128)(2,1)S(1)} %multiply_convert_fusion.1), channel_id=1, source_target_pairs={{0,1},{2,3},{4,5},{6,7},{1,0},{3,2},{5,4},{7,6},{8,9},{10,11},{12,... | collective-permute-start | bytes 774152 | tf_op jit(solution)/shard_map/ppermute | solution.py:230
  108.8 11.6 %collective-permute-start.23 = (bf16[1344,384]{1,0:T(8,128)(2,1)S(1)}, bf16[1344,384]{1,0:T(8,128)(2,1)S(1)}, u32[]{:S(2)}, u32[]{:S(2)}) collective-permute-start(bf16[1344,384]{1,0:T(8,128)(2,1)S(1)} %pad_maximum_fusion), channel_id=1, source_target_pairs={{0,2},{2,0},{4,6},{6,4},{1,3},{3,1},{5,7},{7,5},{8,10},{10,8},{12,... | collective-permute-start | bytes 3096584 | tf_op jit(solution)/shard_map/ppermute | solution.py:232
  109.7 9.7 %collective-permute-start.15 = (bf16[336,384]{1,0:T(8,128)(2,1)S(1)}, bf16[336,384]{1,0:T(8,128)(2,1)S(1)}, u32[]{:S(2)}, u32[]{:S(2)}) collective-permute-start(bf16[336,384]{1,0:T(8,128)(2,1)S(1)} %multiply_convert_fusion.1), channel_id=1, source_target_pairs={{0,5},{2,7},{4,0},{6,2},{1,4},{3,6},{5,1},{7,3},{8,13},{10,15},{12... | collective-permute-start | bytes 774152 | tf_op jit(solution)/shard_map/ppermute | solution.py:230
  119.4 4.0 %collective-permute-start.16 = (bf16[1344,384]{1,0:T(8,128)(2,1)S(1)}, bf16[1344,384]{1,0:T(8,128)(2,1)S(1)}, u32[]{:S(2)}, u32[]{:S(2)}) collective-permute-start(bf16[1344,384]{1,0:T(8,128)(2,1)S(1)} %constant_dynamic-update-slice_fusion), channel_id=1, source_target_pairs={{0,2},{2,0},{4,6},{6,4},{1,3},{3,1},{5,7},{7,5},{8,10},{10,8},{12,... | collective-permute-start | bytes 3096584 | tf_op jit(solution)/shard_map/ppermute | solution.py:232
  (14 other events, 19.8 us)

commit v4 on v3

--- a/solution.py
+++ b/solution.py
@@ -148,19 +148,33 @@
             out[:, at] = jnp.where(pre_ref[:, at].astype(F32) > 0, grad, 0.0).astype(BF)
 
 
-def filter_body(act, mirror, ids, *refs):
-    own_ref, oth_ref, full_ref, keep_ref, send_ref, stack_ref = refs
+def send_body(act, mirror, ids, own_ref, oth_ref, full_ref, send_ref, stack_ref):
     sy, core = ids[1], ids[2]
     fill_windows(own_ref, oth_ref, stack_ref, sy, mirror, act)
+    other = full_ref[pl.ds(pl.multiple_of((1 - core) * HALF, HALF), HALF), :]
+    for i in range(9):
+        at = slice(i * 3 * C, (i + 1) * 3 * C)
+        send_ref[at, :] = nt(stack_ref[at, :], other).astype(BF)
+    send_ref[ROWS:ROWSP, :] = jnp.zeros((ROWSP - ROWS, HALF), BF)
+
+
+def keep_body(act, mirror, ids, own_ref, oth_ref, full_ref, got_ref, keep_ref, *refs):
+    send_refs, stack_ref = refs[:3], refs[3]
+    sy, core, chip = ids[1], ids[2], ids[3]
+    fill_windows(own_ref, oth_ref, stack_ref, sy, mirror, act)
+    stack_ref[ROWS:ROWSP, :] = jnp.zeros((ROWSP - ROWS, NXL * SLAB), BF)
     mine = full_ref[pl.ds(pl.multiple_of(core * HALF, HALF), HALF), :]
-    other = full_ref[pl.ds(pl.multiple_of((1 - core) * HALF, HALF), HALF), :]
-    step = 3 * C
-    for i in range(9):
-        rows = stack_ref[i * step : (i + 1) * step, :]
-        send_ref[i * step : (i + 1) * step, :] = nt(rows, other).astype(BF)
-        keep_ref[i * step : (i + 1) * step, :] = nt(rows, mine)
-    keep_ref[ROWS:ROWSP, :] = jnp.zeros((ROWSP - ROWS, HALF), F32)
-    send_ref[ROWS:ROWSP, :] = jnp.zeros((ROWSP - ROWS, HALF), BF)
+    for k in (1, 3, 2, 0):
+        for part in range(2):
+            n = BLOCK // 2 - 8 * (1 - 2 * part)
+            first = part * 160
+            at = pl.ds(pl.multiple_of(((chip + k) % 4) * BLOCK + first, 16), n)
+            total = nt(stack_ref[at, :], mine) + got_ref[at, :].astype(F32)
+            to = slice(first, first + n)
+            if k == 0:
+                keep_ref[to, :] = total
+            else:
+                send_refs[k - 1][to, :] = total.astype(BF)
 
 
 def data_body(ids, *refs):
@@ -197,37 +211,47 @@
     return lax.all_to_all(many, axis, 0, 0, tiled=True)
 
 
-def split_body(ids, keep_ref, got_ref, own_ref, *send_refs):
-    chip = ids[3]
-    for k in range(4):
-        at = pl.ds(pl.multiple_of(((chip + k) % 4) * BLOCK, BLOCK), BLOCK)
-        total = keep_ref[at, :] + got_ref[at, :].astype(F32)
-        if k == 0:
-            own_ref[...] = total
-        else:
-            send_refs[k - 1][...] = total.astype(BF)
-
-
 def along(shift):
     return [(place(x, c), place((x + shift) % 4, c)) for x in range(4) for c in range(2)]
 
 
-def chip_split(ids, keep, got):
+def filter_sums(ids, own, oth, full, act, mirror):
+    n_pos = NXL * SLAB
+    sent = jax.ShapeDtypeStruct((ROWSP, HALF), BF)
     outs = [jax.ShapeDtypeStruct((BLOCK, HALF), F32)]
     outs += [jax.ShapeDtypeStruct((BLOCK, HALF), BF)] * 3
-    return call(split_body, tuple(outs), [], 2)(ids, keep, got)
-
-
-def line_sum(own, one, two, three, factor):
-    got = [lax.ppermute(v, LINE, along(k)) for k, v in ((1, one), (3, three), (2, two))]
-    total = own
-    for v in got:
+
+    def send():
+        stack = pltpu.VMEM((ROWS, n_pos), BF)
+        body = functools.partial(send_body, act, mirror)
+        return call(body, sent, [stack], 3)(ids, own, oth, full)
+
+    def keep(got):
+        stack = pltpu.VMEM((ROWSP, n_pos), BF)
+        body = functools.partial(keep_body, act, mirror)
+        return call(body, tuple(outs), [stack], 4)(ids, own, oth, full, got)
+
+    return send, keep
+
+
+def arrive(split):
+    own, one, two, three = split
+    return [own] + [lax.ppermute(v, LINE, along(k)) for k, v in ((1, one), (3, three), (2, two))]
+
+
+def line_sum(parts, factor, after=None):
+    if after is not None:
+        parts, _ = lax.optimization_barrier((parts, after))
+    total = parts[0]
+    for v in parts[1:]:
         total = total + v.astype(F32)
     return (total * factor).astype(BF)
 
 
-def line_spread(block):
+def line_spread(block, after=None):
     got = {k: lax.ppermute(block, LINE, along(k)) for k in (1, 3, 2)}
+    if after is not None:
+        got, _ = lax.optimization_barrier((got, after))
     mine = jnp.concatenate([block, got[1], got[2], got[3]], axis=0)
     return mine, lax.ppermute(mine, LINE, OTHER_CORE)
 
@@ -274,8 +298,9 @@
     w_two = weight_two.reshape(ROWS, CH)
     w_one = weight_one.reshape(ROWS, CH).T
     mine_in = inputs.reshape(C, n_pos)
-    grad, w_one, mine_in, pre = lax.optimization_barrier((grad, w_one, mine_in, pre))
-    full_in = to_all(mine_in, "ch", 16).reshape(CH, n_pos)
+    many_in = jnp.broadcast_to(mine_in[None], (16, C, n_pos))
+    grad, w_one, many_in, pre = lax.optimization_barrier((grad, w_one, many_in, pre))
+    full_in = lax.all_to_all(many_in, "ch", 0, 0, tiled=True).reshape(CH, n_pos)
 
     own, over, pack = call(
         act_grad_body,
@@ -285,46 +310,38 @@
     )(ids, w_two, grad)
     pack = lax.ppermute(pack, LINE, to_side(0, True))
 
-    filter_outs = (
-        jax.ShapeDtypeStruct((ROWSP, HALF), F32),
-        jax.ShapeDtypeStruct((ROWSP, HALF), BF),
-    )
-    stack = pltpu.VMEM((ROWS, n_pos), BF)
-    keep2, send2 = call(functools.partial(filter_body, True, False), filter_outs, [stack], 3)(
-        ids, *pre, grad
-    )
-    pack, send2 = lax.optimization_barrier((pack, send2))
+    send_two, keep_two = filter_sums(ids, *pre, grad, True, False)
+    send2 = send_two()
+    pack, send2, full_in = lax.optimization_barrier((pack, send2, full_in))
+    got2 = lax.ppermute(send2, LINE, OTHER_CORE)
     own, oth, left, right = call(join_y_body, (wide_f, wide_f, mid_f, mid_f), [], 3)(
         ids, own, over, pack
     )
     from_left = lax.ppermute(right, LINE, to_side(1, False))
     from_right = lax.ppermute(left, LINE, to_side(-1, False))
-    got2 = lax.ppermute(send2, LINE, OTHER_CORE)
-    split2 = chip_split(ids, keep2, got2)
-    from_left, from_right, full_in, _ = lax.optimization_barrier(
-        (from_left, from_right, full_in, split2)
-    )
+    split2 = keep_two(got2)
+    from_left, from_right, _ = lax.optimization_barrier((from_left, from_right, split2))
     delta = call(delta_body, (wide_b, wide_b), [], 6)(
         ids, own, oth, from_left, from_right, *pre
     )
 
-    keep1, send1 = call(functools.partial(filter_body, False, True), filter_outs, [stack], 3)(
-        ids, *delta, full_in
-    )
-    got1 = lax.ppermute(send1, LINE, OTHER_CORE)
-    split1 = chip_split(ids, keep1, got1)
+    arrive2 = arrive(split2)
+    send_one, keep_one = filter_sums(ids, *delta, full_in, False, True)
+    got1 = lax.ppermute(send_one(), LINE, OTHER_CORE)
+    split1 = keep_one(got1)
     delta, _ = lax.optimization_barrier((delta, split1))
-    terms = call(data_body, jax.ShapeDtypeStruct((CH, n_pos), BF), [stack], 3)(
-        ids, *delta, w_one
-    )
+    terms = call(
+        data_body,
+        jax.ShapeDtypeStruct((CH, n_pos), BF),
+        [pltpu.VMEM((ROWS, n_pos), BF)],
+        3,
+    )(ids, *delta, w_one)
     got = lax.all_to_all(terms.reshape(16, C, n_pos), "ch", 0, 0, tiled=True)
-    block2 = line_sum(*split2, factor)
-    block1 = line_sum(*split1, factor)
-    pair2 = line_spread(block2)
+    block2 = line_sum(arrive2, factor)
+    block1 = line_sum(arrive(split1), factor, terms)
+    filter_two = write(ids, *line_spread(block2, (block1, got)))
     input_grad = got.astype(F32).sum(axis=0).astype(BF).reshape(shape)
-    input_grad, block1 = lax.optimization_barrier((input_grad, block1))
-    filter_two = write(ids, *pair2)
-    filter_one = write(ids, *line_spread(block1))
+    filter_one = write(ids, *line_spread(block1, (filter_two, input_grad)))
     return input_grad, filter_one, filter_two
 
 

time: 128 us -> 133 us (1.039)
  waiting for transfers between devices: 21.1 us -> 37 us
  local copies, waits for them, and re-layouts: 18.4 us -> 10.2 us
  starting transfers between devices: 62 us -> 58.1 us
    unnamed x41 -> x18, local copies, waits for them, and re-layouts: 10.8 us -> 3.32 us
    all_to_all x0 -> x1, starting transfers between devices: none -> 6.98 us  [shards(): full_in = lax.all_to_all(many_in, 'ch', 0, 0, tiled=True).reshape(CH, n_pos)]
    all_to_all x2 -> x1, starting transfers between devices: 15.5 us -> 8.6 us  [to_all(): return lax.all_to_all(many, axis, 0, 0, tiled=True)]
    ppermute x6, starting transfers between devices: 9.87 us -> 3.11 us  [line_spread(): got = {k: lax.ppermute(block, LINE, along(k)) for k in (1, 3, 2)}]
    ppermute x6, waiting for transfers between devices: 12 us -> 17.9 us  [line_spread(): got = {k: lax.ppermute(block, LINE, along(k)) for k in (1, 3, 2)}]
    all_to_all x0 -> x1, waiting for transfers between devices: none -> 5.28 us  [shards(): full_in = lax.all_to_all(many_in, 'ch', 0, 0, tiled=True).reshape(CH, n_pos)]
    ppermute x2, starting transfers between devices: 1.81 us -> 6.2 us  [line_spread(): return (mine, lax.ppermute(mine, LINE, OTHER_CORE))]
    ppermute x1, waiting for transfers between devices: 0.01 us -> 3.21 us  [shards(): pack = lax.ppermute(pack, LINE, to_side(0, True))]
  transfers between devices with their start and end apart: 27 -> 27, of which waited for: 9 -> 12; matrix products, arithmetic and copies ran while one was open for 7% -> 5% of each run, Pallas kernels for 10% -> 12%
where the time goes in v4:
time: 133 us; the launch traced here: 132 us
  starting transfers between devices  58.1 us (44%)
  waiting for transfers between devices  37 us (28%)
  Pallas kernels  21.5 us (16%)
  local copies, waits for them, and re-layouts  10.2 us (8%)
  other arithmetic  3.99 us (3%)
    ppermute x6, waiting for transfers between devices, line_spread(): got = {k: lax.ppermute(block, LINE, along(k)) for k in (1, 3, 2)}  17.9 us
    ppermute x2, starting transfers between devices, halo(): left = send(last, perm=to_side(1, flip))  8.87 us
    all_to_all x1, starting transfers between devices, to_all(): return lax.all_to_all(many, axis, 0, 0, tiled=True)  8.6 us
    ppermute x6, waiting for transfers between devices, arrive(): lax.ppermute(v, LINE, along(k))  8.04 us
    ppermute x6, starting transfers between devices, arrive(): lax.ppermute(v, LINE, along(k))  7.24 us
    all_to_all x1, starting transfers between devices, shards(): full_in = lax.all_to_all(many_in, 'ch', 0, 0, tiled=True).reshape(CH, n_pos)  6.98 us
    ppermute x2, starting transfers between devices, line_spread(): return (mine, lax.ppermute(mine, LINE, OTHER_CORE))  6.2 us
    pallas_call x2, Pallas kernels, write(): pl.pallas_call(write_body, out_shape=jax.ShapeDtypeStruct((OFF, C, CH), F...  6.05 us
  transfers between devices with their start and end apart: 27, of which 12 were waited for; matrix products, arithmetic and copies ran while one was open for 5% of the time, Pallas kernels for 12%

profile of v4, /device:TPU:1, one launch (start us, length us, event | category | flops | bytes accessed | tf_op | source)
XLA Modules:
  0.0 131.8 jit_solution(15257158226887979288)
XLA Ops:
  2.7 8.6 %all-to-all-start = ((bf16[16,48,512]{2,1,0:T(8,128)(2,1)}), bf16[16,48,512]{2,1,0:T(8,128)(2,1)S(1)}, u32[]{:S(2)}, u32[]{:S(2)}) async-start(bf16[16,48,512]{2,1,0:T(8,128)(2,1)} %broadcast_in_dim.15), calls=%async_computation | async-start | bytes 1572864 | tf_op jit(solution)/shard_map/all_to_all | solution.py:211
  11.4 4.0 %collective-permute-start = (bf16[48,128]{1,0:T(8,128)(2,1)S(1)}, bf16[48,128]{1,0:T(8,128)(2,1)S(1)}, u32[]{:S(2)}, u32[]{:S(2)}) collective-permute-start(bf16[48,128]{1,0:T(8,128)(2,1)S(1)} %get-tuple-element.81), channel_id=1, source_target_pairs={{0,2},{1,3},{2,4},{3,5},{4,6},{5,7},{8,10},{9,11},{10,12},{11,13},... | collective-permute-start | bytes 36872 | tf_op jit(solution)/shard_map/ppermute | solution.py:203
  15.4 1.9 %collective-permute-start.1 = (bf16[48,128]{1,0:T(8,128)(2,1)S(1)}, bf16[48,128]{1,0:T(8,128)(2,1)S(1)}, u32[]{:S(2)}, u32[]{:S(2)}) collective-permute-start(bf16[48,128]{1,0:T(8,128)(2,1)S(1)} %get-tuple-element.82), channel_id=1, source_target_pairs={{2,0},{3,1},{4,2},{5,3},{6,4},{7,5},{10,8},{11,9},{12,10},{13,11},... | collective-permute-start | bytes 36872 | tf_op jit(solution)/shard_map/ppermute | solution.py:204
  17.3 4.9 %collective-permute-start.2 = (bf16[48,128]{1,0:T(8,128)(2,1)S(1)}, bf16[48,128]{1,0:T(8,128)(2,1)S(1)}, u32[]{:S(2)}, u32[]{:S(2)}) collective-permute-start(bf16[48,128]{1,0:T(8,128)(2,1)S(1)} %get-tuple-element.81), channel_id=1, source_target_pairs={{0,3},{1,2},{2,5},{3,4},{4,7},{5,6},{8,11},{9,10},{10,13},{11,12},... | collective-permute-start | bytes 36872 | tf_op jit(solution)/shard_map/ppermute | solution.py:203
  22.2 2.2 %collective-permute-start.4 = (bf16[48,128]{1,0:T(8,128)(2,1)S(1)}, bf16[48,128]{1,0:T(8,128)(2,1)S(1)}, u32[]{:S(2)}, u32[]{:S(2)}) collective-permute-start(bf16[48,128]{1,0:T(8,128)(2,1)S(1)} %get-tuple-element.82), channel_id=1, source_target_pairs={{2,1},{3,0},{4,3},{5,2},{6,5},{7,4},{10,9},{11,8},{12,11},{13,10},... | collective-permute-start | bytes 36872 | tf_op jit(solution)/shard_map/ppermute | solution.py:204
  24.4 2.5 %collective-permute-start.3 = (bf16[48,512]{1,0:T(8,128)(2,1)S(1)}, bf16[48,512]{1,0:T(8,128)(2,1)S(1)}, u32[]{:S(2)}, u32[]{:S(2)}) collective-permute-start(bf16[48,512]{1,0:T(8,128)(2,1)S(1)} %reshape.44), channel_id=1, source_target_pairs={{0,1},{1,0},{2,3},{3,2},{4,5},{5,4},{6,7},{7,6},{8,9},{9,8},{10,11... | collective-permute-start | bytes 147464 | tf_op jit(solution)/shard_map/ppermute | solution.py:202
  27.1 2.9 %copy.9 = bf16[1296,768]{0,1:T(8,128)(2,1)S(1)} copy(bf16[1296,768]{1,0:T(8,128)(2,1)} %bitcast.23) | data formatting | bytes 3981312 | tf_op jit(solution)/shard_map/reshape | solution.py:299
  31.0 7.0 %all-to-all-start.1 = ((bf16[16,48,512]{2,1,0:T(8,128)(2,1)}), bf16[16,48,512]{2,1,0:T(8,128)(2,1)}, u32[]{:S(2)}, u32[]{:S(2)}) async-start(bf16[16,48,512]{2,1,0:T(8,128)(2,1)} %broadcast_in_dim.17), calls=%async_computation.1 | async-start | bytes 1572864 | tf_op jit(solution)/shard_map/all_to_all | solution.py:303
  39.7 1.9 %shard_map.76 = (f32[48,768]{1,0:T(8,128)S(1)}, f32[48,768]{1,0:T(8,128)S(1)}, f32[48,768]{1,0:T(8,128)S(1)}) custom-call(s32[4]{0:T(128)S(1)} %pad_add_fusion.ids, bf16[1296,768]{1,0:T(8,128)(2,1)S(1)} %bitcast.20, bf16[768,512]{1,0:T(8,128)(2,1)S(1)} %bitcast.14), custom_call_target="tpu_custom_call" | custom-call | tf_op jit(solution)/shard_map/pallas_call | solution.py:305
  43.0 1.9 %shard_map.77 = bf16[1344,384]{1,0:T(8,128)(2,1)S(1)} custom-call(s32[4]{0:T(128)S(1)} %pad_add_fusion.ids, bf16[48,768]{1,0:T(8,128)(2,1)S(1)} %pad_maximum_fusion.2.own_ref.pre_own_ref, bf16[48,768]{1,0:T(8,128)(2,1)S(1)} %pad_maximum_fusion.3.oth_ref.pre_oth_ref, bf16[768,512]{1,0:T(8,128)(2,1)S(1)} %bitcast.15), custom_call_target="tpu_custom_call" | custom-call | tf_op jit(solution)/shard_map/pallas_call | solution.py:227
  45.9 3.2 %collective-permute-done.5.pack_ref = f32[48,768]{1,0:T(8,128)S(1)} collective-permute-done((f32[48,768]{1,0:T(8,128)S(1)}, f32[48,768]{1,0:T(8,128)S(1)}, u32[]{:S(2)}, u32[]{:S(2)}) %collective-permute-start.5) | collective-permute-done | bytes 147488 | tf_op jit(solution)/shard_map/ppermute | solution.py:311
  49.1 5.3 %all-to-all-done.1 = bf16[16,48,512]{2,1,0:T(8,128)(2,1)} async-done(((bf16[16,48,512]{2,1,0:T(8,128)(2,1)}), bf16[16,48,512]{2,1,0:T(8,128)(2,1)}, u32[]{:S(2)}, u32[]{:S(2)}) %all-to-all-start.1) | async-done | bytes 786464 | tf_op jit(solution)/shard_map/all_to_all | solution.py:303
  55.3 1.9 %collective-permute-start.6 = (f32[48,512]{1,0:T(8,128)S(1)}, f32[48,512]{1,0:T(8,128)S(1)}, u32[]{:S(2)}, u32[]{:S(2)}) collective-permute-start(f32[48,512]{1,0:T(8,128)S(1)} %get-tuple-element.52), channel_id=1, source_target_pairs={{0,2},{1,3},{2,4},{3,5},{4,6},{5,7},{8,10},{9,11},{10,12},{11,13},... | collective-permute-start | bytes 294920 | tf_op jit(solution)/shard_map/ppermute | solution.py:320
  57.3 2.4 %collective-permute-start.7 = (f32[48,512]{1,0:T(8,128)S(1)}, f32[48,512]{1,0:T(8,128)S(1)}, u32[]{:S(2)}, u32[]{:S(2)}) collective-permute-start(f32[48,512]{1,0:T(8,128)S(1)} %get-tuple-element.53), channel_id=1, source_target_pairs={{2,0},{3,1},{4,2},{5,3},{6,4},{7,5},{10,8},{11,9},{12,10},{13,11},... | collective-permute-start | bytes 294920 | tf_op jit(solution)/shard_map/ppermute | solution.py:321
  59.7 2.4 %shard_map.79 = (f32[336,384]{1,0:T(8,128)S(1)}, bf16[336,384]{1,0:T(8,128)(2,1)}, bf16[336,384]{1,0:T(8,128)(2,1)}, bf16[336,384]{1,0:T(8,128)(2,1)S(1)}) custom-call(s32[4]{0:T(128)S(1)} %pad_add_fusion.ids, bf16[48,768]{1,0:T(8,128)(2,1)S(1)} %pad_maximum_fusion.2.own_ref.pre_own_ref, bf16[48,768]{1,0:T(8,128)(2,1)S(1)} %pad_maximum_fusion.3.oth_ref.pre_oth_ref, ...), custom_call_target="tpu_custom_call" | custom-call | tf_op jit(solution)/shard_map/pallas_call | solution.py:232
  63.8 2.5 %shard_map.81 = bf16[1344,384]{1,0:T(8,128)(2,1)S(1)} custom-call(s32[4]{0:T(128)S(1)} %pad_add_fusion.ids, bf16[48,768]{1,0:T(8,128)(2,1)S(1)} %get-tuple-element.68.own_ref.refs_0_, bf16[48,768]{1,0:T(8,128)(2,1)S(1)} %get-tuple-element.69.oth_ref.refs_1_, bf16[768,512]{1,0:T(8,128)(2,1)} %bitcast.8.full_ref), custom_call_target="tpu_custom_call" | custom-call | tf_op jit(solution)/shard_map/pallas_call | solution.py:227
  67.5 2.4 %collective-permute-start.17 = (bf16[336,384]{1,0:T(8,128)(2,1)S(1)}, bf16[336,384]{1,0:T(8,128)(2,1)}, u32[]{:S(2)}, u32[]{:S(2)}) collective-permute-start(bf16[336,384]{1,0:T(8,128)(2,1)S(1)} %get-tuple-element.58), channel_id=1, source_target_pairs={{0,5},{2,7},{4,0},{6,2},{1,4},{3,6},{5,1},{7,3},{8,13},{10,15},{12... | collective-permute-start | bytes 774152 | tf_op jit(solution)/shard_map/ppermute | solution.py:239
  69.8 2.5 %shard_map.82 = (f32[336,384]{1,0:T(8,128)S(1)}, bf16[336,384]{1,0:T(8,128)(2,1)S(1)}, bf16[336,384]{1,0:T(8,128)(2,1)S(1)}, bf16[336,384]{1,0:T(8,128)(2,1)S(1)}) custom-call(s32[4]{0:T(128)S(1)} %pad_add_fusion.ids, bf16[48,768]{1,0:T(8,128)(2,1)S(1)} %get-tuple-element.68.own_ref.refs_0_, bf16[48,768]{1,0:T(8,128)(2,1)S(1)} %get-tuple-element.69.oth_ref.refs_1_, ...), custom_call_target="tpu_custom_call" | custom-call | tf_op jit(solution)/shard_map/pallas_call | solution.py:232
  72.4 3.0 %shard_map.83 = bf16[768,512]{1,0:T(8,128)(2,1)} custom-call(s32[4]{0:T(128)S(1)} %pad_add_fusion.ids, bf16[48,768]{1,0:T(8,128)(2,1)S(1)} %get-tuple-element.68.own_ref.refs_0_, bf16[48,768]{1,0:T(8,128)(2,1)S(1)} %get-tuple-element.69.oth_ref.refs_1_, bf16[768,1296]{1,0:T(8,128)(2,1)S(1)} %bitcast.17), custom_call_target="tpu_custom_call" | custom-call | tf_op jit(solution)/shard_map/pallas_call | solution.py:333
  75.5 4.3 %all-to-all-start.2 = ((bf16[16,48,512]{2,1,0:T(8,128)(2,1)}), bf16[16,48,512]{2,1,0:T(8,128)(2,1)}, u32[]{:S(2)}, u32[]{:S(2)}) async-start(bf16[16,48,512]{2,1,0:T(8,128)(2,1)} %bitcast.9), calls=%async_computation.2 | async-start | bytes 1572864 | tf_op jit(solution)/shard_map/all_to_all | solution.py:339
  79.9 2.0 %collective-permute-start.12 = (bf16[336,384]{1,0:T(8,128)(2,1)}, bf16[336,384]{1,0:T(8,128)(2,1)S(1)}, u32[]{:S(2)}, u32[]{:S(2)}) collective-permute-start(bf16[336,384]{1,0:T(8,128)(2,1)} %copy-done.5), channel_id=1, source_target_pairs={{0,1},{2,3},{4,5},{6,7},{1,0},{3,2},{5,4},{7,6},{8,9},{10,11},{12,... | collective-permute-start | bytes 774152 | tf_op jit(solution)/shard_map/ppermute | solution.py:239
  81.9 1.7 %collective-permute-start.11 = (bf16[336,384]{1,0:T(8,128)(2,1)}, bf16[336,384]{1,0:T(8,128)(2,1)S(1)}, u32[]{:S(2)}, u32[]{:S(2)}) collective-permute-start(bf16[336,384]{1,0:T(8,128)(2,1)} %copy-done.4), channel_id=1, source_target_pairs={{0,5},{2,7},{4,0},{6,2},{1,4},{3,6},{5,1},{7,3},{8,13},{10,15},{12... | collective-permute-start | bytes 774152 | tf_op jit(solution)/shard_map/ppermute | solution.py:239
  86.6 2.6 %collective-permute-done.10 = bf16[336,384]{1,0:T(8,128)(2,1)S(1)} collective-permute-done((bf16[336,384]{1,0:T(8,128)(2,1)}, bf16[336,384]{1,0:T(8,128)(2,1)S(1)}, u32[]{:S(2)}, u32[]{:S(2)}) %collective-permute-start.10) | collective-permute-done | bytes 258080 | tf_op jit(solution)/shard_map/ppermute | solution.py:239
  89.2 3.8 %collective-permute-done.12 = bf16[336,384]{1,0:T(8,128)(2,1)S(1)} collective-permute-done((bf16[336,384]{1,0:T(8,128)(2,1)}, bf16[336,384]{1,0:T(8,128)(2,1)S(1)}, u32[]{:S(2)}, u32[]{:S(2)}) %collective-permute-start.12) | collective-permute-done | bytes 258080 | tf_op jit(solution)/shard_map/ppermute | solution.py:239
  94.8 6.2 %collective-permute-done.21 = bf16[336,384]{1,0:T(8,128)(2,1)S(1)} collective-permute-done((bf16[336,384]{1,0:T(8,128)(2,1)S(1)}, bf16[336,384]{1,0:T(8,128)(2,1)S(1)}, u32[]{:S(2)}, u32[]{:S(2)}) %collective-permute-start.21) | collective-permute-done | bytes 258080 | tf_op jit(solution)/shard_map/ppermute | solution.py:252
  100.9 2.2 %collective-permute-done.19 = bf16[336,384]{1,0:T(8,128)(2,1)} collective-permute-done((bf16[336,384]{1,0:T(8,128)(2,1)S(1)}, bf16[336,384]{1,0:T(8,128)(2,1)}, u32[]{:S(2)}, u32[]{:S(2)}) %collective-permute-start.19) | collective-permute-done | bytes 258080 | tf_op jit(solution)/shard_map/ppermute | solution.py:252
  104.2 5.6 %collective-permute-start.22 = (bf16[1344,384]{1,0:T(8,128)(2,1)S(1)}, bf16[1344,384]{1,0:T(8,128)(2,1)S(1)}, u32[]{:S(2)}, u32[]{:S(2)}) collective-permute-start(bf16[1344,384]{1,0:T(8,128)(2,1)S(1)} %pad_maximum_fusion), channel_id=1, source_target_pairs={{0,2},{2,0},{4,6},{6,4},{1,3},{3,1},{5,7},{7,5},{8,10},{10,8},{12,... | collective-permute-start | bytes 3096584 | tf_op jit(solution)/shard_map/ppermute | solution.py:256
  113.3 3.0 %shard_map.84 = f32[27,48,768]{2,1,0:T(8,128)} custom-call(s32[4]{0:T(128)S(1)} %pad_add_fusion.ids, bf16[4,7,48,384]{3,2,1,0:T(8,128)(2,1)S(1)} %bitcast.18, bf16[4,7,48,384]{3,2,1,0:T(8,128)(2,1)S(1)} %bitcast.21), custom_call_target="tpu_custom_call" | custom-call | tf_op jit(solution)/shard_map/pallas_call | solution.py:270
  117.6 2.1 %collective-permute-done.14 = bf16[336,384]{1,0:T(8,128)(2,1)S(1)} collective-permute-done((bf16[336,384]{1,0:T(8,128)(2,1)S(1)}, bf16[336,384]{1,0:T(8,128)(2,1)S(1)}, u32[]{:S(2)}, u32[]{:S(2)}) %collective-permute-start.14) | collective-permute-done | bytes 258080 | tf_op jit(solution)/shard_map/ppermute | solution.py:252
  119.7 6.2 %collective-permute-done.13 = bf16[336,384]{1,0:T(8,128)(2,1)S(1)} collective-permute-done((bf16[336,384]{1,0:T(8,128)(2,1)S(1)}, bf16[336,384]{1,0:T(8,128)(2,1)S(1)}, u32[]{:S(2)}, u32[]{:S(2)}) %collective-permute-start.13) | collective-permute-done | bytes 258080 | tf_op jit(solution)/shard_map/ppermute | solution.py:252
  126.5 2.3 %collective-permute-done.23 = bf16[1344,384]{1,0:T(8,128)(2,1)S(1)} collective-permute-done((bf16[1344,384]{1,0:T(8,128)(2,1)S(1)}, bf16[1344,384]{1,0:T(8,128)(2,1)S(1)}, u32[]{:S(2)}, u32[]{:S(2)}) %collective-permute-start.23) | collective-permute-done | bytes 1032224 | tf_op jit(solution)/shard_map/ppermute | solution.py:256
  128.8 3.0 %shard_map.85 = f32[27,48,768]{2,1,0:T(8,128)} custom-call(s32[4]{0:T(128)S(1)} %pad_add_fusion.ids, bf16[4,7,48,384]{3,2,1,0:T(8,128)(2,1)S(1)} %bitcast.19, bf16[4,7,48,384]{3,2,1,0:T(8,128)(2,1)S(1)} %bitcast.22), custom_call_target="tpu_custom_call" | custom-call | tf_op jit(solution)/shard_map/pallas_call | solution.py:270
  (66 shorter events, 22.4 us)
Async XLA Ops:
  0.6 10.6 %copy-start.7 = (bf16[48,4,2,64]{3,2,1,0:T(2,128)(2,1)S(1)}, bf16[48,4,2,64]{3,2,1,0:T(2,128)(2,1)}, u32[]{:S(2)}) copy-start(bf16[48,4,2,64]{3,2,1,0:T(2,128)(2,1)} %param.6) | copy-start | bytes 147460
  0.6 26.3 %copy-start.8 = (bf16[48,4,2,64]{3,2,1,0:T(2,128)(2,1)S(1)}, bf16[48,4,2,64]{3,2,1,0:T(2,128)(2,1)}, u32[]{:S(2)}) copy-start(bf16[48,4,2,64]{3,2,1,0:T(2,128)(2,1)} %param.5) | copy-start | bytes 147460
  2.7 27.4 %all-to-all-start = ((bf16[16,48,512]{2,1,0:T(8,128)(2,1)}), bf16[16,48,512]{2,1,0:T(8,128)(2,1)S(1)}, u32[]{:S(2)}, u32[]{:S(2)}) async-start(bf16[16,48,512]{2,1,0:T(8,128)(2,1)} %broadcast_in_dim.15), calls=%async_computation | async-start | bytes 1572864 | tf_op jit(solution)/shard_map/all_to_all | solution.py:211
  11.4 18.5 %collective-permute-start = (bf16[48,128]{1,0:T(8,128)(2,1)S(1)}, bf16[48,128]{1,0:T(8,128)(2,1)S(1)}, u32[]{:S(2)}, u32[]{:S(2)}) collective-permute-start(bf16[48,128]{1,0:T(8,128)(2,1)S(1)} %get-tuple-element.81), channel_id=1, source_target_pairs={{0,2},{1,3},{2,4},{3,5},{4,6},{5,7},{8,10},{9,11},{10,12},{11,13},... | collective-permute-start | bytes 36872 | tf_op jit(solution)/shard_map/ppermute | solution.py:203
  15.4 14.6 %collective-permute-start.1 = (bf16[48,128]{1,0:T(8,128)(2,1)S(1)}, bf16[48,128]{1,0:T(8,128)(2,1)S(1)}, u32[]{:S(2)}, u32[]{:S(2)}) collective-permute-start(bf16[48,128]{1,0:T(8,128)(2,1)S(1)} %get-tuple-element.82), channel_id=1, source_target_pairs={{2,0},{3,1},{4,2},{5,3},{6,4},{7,5},{10,8},{11,9},{12,10},{13,11},... | collective-permute-start | bytes 36872 | tf_op jit(solution)/shard_map/ppermute | solution.py:204
  17.3 12.7 %collective-permute-start.2 = (bf16[48,128]{1,0:T(8,128)(2,1)S(1)}, bf16[48,128]{1,0:T(8,128)(2,1)S(1)}, u32[]{:S(2)}, u32[]{:S(2)}) collective-permute-start(bf16[48,128]{1,0:T(8,128)(2,1)S(1)} %get-tuple-element.81), channel_id=1, source_target_pairs={{0,3},{1,2},{2,5},{3,4},{4,7},{5,6},{8,11},{9,10},{10,13},{11,12},... | collective-permute-start | bytes 36872 | tf_op jit(solution)/shard_map/ppermute | solution.py:203
  22.2 7.8 %collective-permute-start.4 = (bf16[48,128]{1,0:T(8,128)(2,1)S(1)}, bf16[48,128]{1,0:T(8,128)(2,1)S(1)}, u32[]{:S(2)}, u32[]{:S(2)}) collective-permute-start(bf16[48,128]{1,0:T(8,128)(2,1)S(1)} %get-tuple-element.82), channel_id=1, source_target_pairs={{2,1},{3,0},{4,3},{5,2},{6,5},{7,4},{10,9},{11,8},{12,11},{13,10},... | collective-permute-start | bytes 36872 | tf_op jit(solution)/shard_map/ppermute | solution.py:204
  24.4 5.6 %collective-permute-start.3 = (bf16[48,512]{1,0:T(8,128)(2,1)S(1)}, bf16[48,512]{1,0:T(8,128)(2,1)S(1)}, u32[]{:S(2)}, u32[]{:S(2)}) collective-permute-start(bf16[48,512]{1,0:T(8,128)(2,1)S(1)} %reshape.44), channel_id=1, source_target_pairs={{0,1},{1,0},{2,3},{3,2},{4,5},{5,4},{6,7},{7,6},{8,9},{9,8},{10,11... | collective-permute-start | bytes 147464 | tf_op jit(solution)/shard_map/ppermute | solution.py:202
  31.0 23.4 %all-to-all-start.1 = ((bf16[16,48,512]{2,1,0:T(8,128)(2,1)}), bf16[16,48,512]{2,1,0:T(8,128)(2,1)}, u32[]{:S(2)}, u32[]{:S(2)}) async-start(bf16[16,48,512]{2,1,0:T(8,128)(2,1)} %broadcast_in_dim.17), calls=%async_computation.1 | async-start | bytes 1572864 | tf_op jit(solution)/shard_map/all_to_all | solution.py:303
  41.6 7.5 %collective-permute-start.5 = (f32[48,768]{1,0:T(8,128)S(1)}, f32[48,768]{1,0:T(8,128)S(1)}, u32[]{:S(2)}, u32[]{:S(2)}) collective-permute-start(f32[48,768]{1,0:T(8,128)S(1)} %get-tuple-element.45), channel_id=1, source_target_pairs={{0,1},{1,0},{2,3},{3,2},{4,5},{5,4},{6,7},{7,6},{8,9},{9,8},{10,11... | collective-permute-start | bytes 442376 | tf_op jit(solution)/shard_map/ppermute | solution.py:311
  54.4 5.3 %collective-permute-start.8 = (bf16[1344,384]{1,0:T(8,128)(2,1)}, bf16[1344,384]{1,0:T(8,128)(2,1)S(1)}, u32[]{:S(2)}, u32[]{:S(2)}) collective-permute-start(bf16[1344,384]{1,0:T(8,128)(2,1)} %copy-done.1), channel_id=1, source_target_pairs={{0,2},{2,0},{4,6},{6,4},{1,3},{3,1},{5,7},{7,5},{8,10},{10,8},{12,... | collective-permute-start | bytes 3096584 | tf_op jit(solution)/shard_map/ppermute | solution.py:316
  55.3 7.6 %collective-permute-start.6 = (f32[48,512]{1,0:T(8,128)S(1)}, f32[48,512]{1,0:T(8,128)S(1)}, u32[]{:S(2)}, u32[]{:S(2)}) collective-permute-start(f32[48,512]{1,0:T(8,128)S(1)} %get-tuple-element.52), channel_id=1, source_target_pairs={{0,2},{1,3},{2,4},{3,5},{4,6},{5,7},{8,10},{9,11},{10,12},{11,13},... | collective-permute-start | bytes 294920 | tf_op jit(solution)/shard_map/ppermute | solution.py:320
  57.3 5.9 %collective-permute-start.7 = (f32[48,512]{1,0:T(8,128)S(1)}, f32[48,512]{1,0:T(8,128)S(1)}, u32[]{:S(2)}, u32[]{:S(2)}) collective-permute-start(f32[48,512]{1,0:T(8,128)S(1)} %get-tuple-element.53), channel_id=1, source_target_pairs={{2,0},{3,1},{4,2},{5,3},{6,4},{7,5},{10,8},{11,9},{12,10},{13,11},... | collective-permute-start | bytes 294920 | tf_op jit(solution)/shard_map/ppermute | solution.py:321
  66.3 3.5 %collective-permute-start.9 = (bf16[1344,384]{1,0:T(8,128)(2,1)S(1)}, bf16[1344,384]{1,0:T(8,128)(2,1)S(1)}, u32[]{:S(2)}, u32[]{:S(2)}) collective-permute-start(bf16[1344,384]{1,0:T(8,128)(2,1)S(1)} %shard_map.81), channel_id=1, source_target_pairs={{0,2},{2,0},{4,6},{6,4},{1,3},{3,1},{5,7},{7,5},{8,10},{10,8},{12,... | collective-permute-start | bytes 3096584 | tf_op jit(solution)/shard_map/ppermute | solution.py:330
  66.4 15.5 %collective-permute-start.16 = (bf16[336,384]{1,0:T(8,128)(2,1)}, bf16[336,384]{1,0:T(8,128)(2,1)}, u32[]{:S(2)}, u32[]{:S(2)}) collective-permute-start(bf16[336,384]{1,0:T(8,128)(2,1)} %get-tuple-element.56), channel_id=1, source_target_pairs={{0,4},{2,6},{4,1},{6,3},{1,5},{3,7},{5,0},{7,2},{8,12},{10,14},{12... | collective-permute-start | bytes 774152 | tf_op jit(solution)/shard_map/ppermute | solution.py:239
  67.5 16.1 %collective-permute-start.18 = (bf16[336,384]{1,0:T(8,128)(2,1)}, bf16[336,384]{1,0:T(8,128)(2,1)}, u32[]{:S(2)}, u32[]{:S(2)}) collective-permute-start(bf16[336,384]{1,0:T(8,128)(2,1)} %get-tuple-element.57), channel_id=1, source_target_pairs={{0,1},{2,3},{4,5},{6,7},{1,0},{3,2},{5,4},{7,6},{8,9},{10,11},{12,... | collective-permute-start | bytes 774152 | tf_op jit(solution)/shard_map/ppermute | solution.py:239
  67.5 16.1 %collective-permute-start.17 = (bf16[336,384]{1,0:T(8,128)(2,1)S(1)}, bf16[336,384]{1,0:T(8,128)(2,1)}, u32[]{:S(2)}, u32[]{:S(2)}) collective-permute-start(bf16[336,384]{1,0:T(8,128)(2,1)S(1)} %get-tuple-element.58), channel_id=1, source_target_pairs={{0,5},{2,7},{4,0},{6,2},{1,4},{3,6},{5,1},{7,3},{8,13},{10,15},{12... | collective-permute-start | bytes 774152 | tf_op jit(solution)/shard_map/ppermute | solution.py:239
  72.4 3.1 %copy-start.4 = (bf16[336,384]{1,0:T(8,128)(2,1)}, bf16[336,384]{1,0:T(8,128)(2,1)S(1)}, u32[]{:S(2)}) copy-start(bf16[336,384]{1,0:T(8,128)(2,1)S(1)} %get-tuple-element.67) | copy-start | bytes 774148
  72.4 3.1 %copy-start.5 = (bf16[336,384]{1,0:T(8,128)(2,1)}, bf16[336,384]{1,0:T(8,128)(2,1)S(1)}, u32[]{:S(2)}) copy-start(bf16[336,384]{1,0:T(8,128)(2,1)S(1)} %get-tuple-element.66) | copy-start | bytes 774148
  72.4 11.2 %copy-start.3 = (f32[336,384]{1,0:T(8,128)S(1)}, f32[336,384]{1,0:T(8,128)}, u32[]{:S(2)}) copy-start(f32[336,384]{1,0:T(8,128)} %copy-done.2) | copy-start | bytes 1548292
  75.5 27.7 %all-to-all-start.2 = ((bf16[16,48,512]{2,1,0:T(8,128)(2,1)}), bf16[16,48,512]{2,1,0:T(8,128)(2,1)}, u32[]{:S(2)}, u32[]{:S(2)}) async-start(bf16[16,48,512]{2,1,0:T(8,128)(2,1)} %bitcast.9), calls=%async_computation.2 | async-start | bytes 1572864 | tf_op jit(solution)/shard_map/all_to_all | solution.py:339
  79.8 9.4 %collective-permute-start.10 = (bf16[336,384]{1,0:T(8,128)(2,1)}, bf16[336,384]{1,0:T(8,128)(2,1)S(1)}, u32[]{:S(2)}, u32[]{:S(2)}) collective-permute-start(bf16[336,384]{1,0:T(8,128)(2,1)} %copy-done.6), channel_id=1, source_target_pairs={{0,4},{2,6},{4,1},{6,3},{1,5},{3,7},{5,0},{7,2},{8,12},{10,14},{12... | collective-permute-start | bytes 774152 | tf_op jit(solution)/shard_map/ppermute | solution.py:239
  79.9 13.2 %collective-permute-start.12 = (bf16[336,384]{1,0:T(8,128)(2,1)}, bf16[336,384]{1,0:T(8,128)(2,1)S(1)}, u32[]{:S(2)}, u32[]{:S(2)}) collective-permute-start(bf16[336,384]{1,0:T(8,128)(2,1)} %copy-done.5), channel_id=1, source_target_pairs={{0,1},{2,3},{4,5},{6,7},{1,0},{3,2},{5,4},{7,6},{8,9},{10,11},{12,... | collective-permute-start | bytes 774152 | tf_op jit(solution)/shard_map/ppermute | solution.py:239
  81.9 12.7 %collective-permute-start.11 = (bf16[336,384]{1,0:T(8,128)(2,1)}, bf16[336,384]{1,0:T(8,128)(2,1)S(1)}, u32[]{:S(2)}, u32[]{:S(2)}) collective-permute-start(bf16[336,384]{1,0:T(8,128)(2,1)} %copy-done.4), channel_id=1, source_target_pairs={{0,5},{2,7},{4,0},{6,2},{1,4},{3,6},{5,1},{7,3},{8,13},{10,15},{12... | collective-permute-start | bytes 774152 | tf_op jit(solution)/shard_map/ppermute | solution.py:239
  84.9 16.0 %collective-permute-start.21 = (bf16[336,384]{1,0:T(8,128)(2,1)S(1)}, bf16[336,384]{1,0:T(8,128)(2,1)S(1)}, u32[]{:S(2)}, u32[]{:S(2)}) collective-permute-start(bf16[336,384]{1,0:T(8,128)(2,1)S(1)} %multiply_convert_fusion), channel_id=1, source_target_pairs={{0,5},{2,7},{4,0},{6,2},{1,4},{3,6},{5,1},{7,3},{8,13},{10,15},{12... | collective-permute-start | bytes 774152 | tf_op jit(solution)/shard_map/ppermute | solution.py:252
  86.1 14.9 %collective-permute-start.20 = (bf16[336,384]{1,0:T(8,128)(2,1)S(1)}, bf16[336,384]{1,0:T(8,128)(2,1)S(1)}, u32[]{:S(2)}, u32[]{:S(2)}) collective-permute-start(bf16[336,384]{1,0:T(8,128)(2,1)S(1)} %multiply_convert_fusion), channel_id=1, source_target_pairs={{0,1},{2,3},{4,5},{6,7},{1,0},{3,2},{5,4},{7,6},{8,9},{10,11},{12,... | collective-permute-start | bytes 774152 | tf_op jit(solution)/shard_map/ppermute | solution.py:252
  89.2 13.9 %collective-permute-start.19 = (bf16[336,384]{1,0:T(8,128)(2,1)S(1)}, bf16[336,384]{1,0:T(8,128)(2,1)}, u32[]{:S(2)}, u32[]{:S(2)}) collective-permute-start(bf16[336,384]{1,0:T(8,128)(2,1)S(1)} %multiply_convert_fusion), channel_id=1, source_target_pairs={{0,4},{2,6},{4,1},{6,3},{1,5},{3,7},{5,0},{7,2},{8,12},{10,14},{12... | collective-permute-start | bytes 774152 | tf_op jit(solution)/shard_map/ppermute | solution.py:252
  104.2 9.1 %collective-permute-start.22 = (bf16[1344,384]{1,0:T(8,128)(2,1)S(1)}, bf16[1344,384]{1,0:T(8,128)(2,1)S(1)}, u32[]{:S(2)}, u32[]{:S(2)}) collective-permute-start(bf16[1344,384]{1,0:T(8,128)(2,1)S(1)} %pad_maximum_fusion), channel_id=1, source_target_pairs={{0,2},{2,0},{4,6},{6,4},{1,3},{3,1},{5,7},{7,5},{8,10},{10,8},{12,... | collective-permute-start | bytes 3096584 | tf_op jit(solution)/shard_map/ppermute | solution.py:256
  109.8 7.8 %collective-permute-start.15 = (bf16[336,384]{1,0:T(8,128)(2,1)S(1)}, bf16[336,384]{1,0:T(8,128)(2,1)S(1)}, u32[]{:S(2)}, u32[]{:S(2)}) collective-permute-start(bf16[336,384]{1,0:T(8,128)(2,1)S(1)} %multiply_convert_fusion.1), channel_id=1, source_target_pairs={{0,5},{2,7},{4,0},{6,2},{1,4},{3,6},{5,1},{7,3},{8,13},{10,15},{12... | collective-permute-start | bytes 774152 | tf_op jit(solution)/shard_map/ppermute | solution.py:252
  110.7 9.0 %collective-permute-start.14 = (bf16[336,384]{1,0:T(8,128)(2,1)S(1)}, bf16[336,384]{1,0:T(8,128)(2,1)S(1)}, u32[]{:S(2)}, u32[]{:S(2)}) collective-permute-start(bf16[336,384]{1,0:T(8,128)(2,1)S(1)} %multiply_convert_fusion.1), channel_id=1, source_target_pairs={{0,1},{2,3},{4,5},{6,7},{1,0},{3,2},{5,4},{7,6},{8,9},{10,11},{12,... | collective-permute-start | bytes 774152 | tf_op jit(solution)/shard_map/ppermute | solution.py:252
  111.1 14.7 %collective-permute-start.13 = (bf16[336,384]{1,0:T(8,128)(2,1)S(1)}, bf16[336,384]{1,0:T(8,128)(2,1)S(1)}, u32[]{:S(2)}, u32[]{:S(2)}) collective-permute-start(bf16[336,384]{1,0:T(8,128)(2,1)S(1)} %multiply_convert_fusion.1), channel_id=1, source_target_pairs={{0,4},{2,6},{4,1},{6,3},{1,5},{3,7},{5,0},{7,2},{8,12},{10,14},{12... | collective-permute-start | bytes 774152 | tf_op jit(solution)/shard_map/ppermute | solution.py:252
  125.9 2.8 %collective-permute-start.23 = (bf16[1344,384]{1,0:T(8,128)(2,1)S(1)}, bf16[1344,384]{1,0:T(8,128)(2,1)S(1)}, u32[]{:S(2)}, u32[]{:S(2)}) collective-permute-start(bf16[1344,384]{1,0:T(8,128)(2,1)S(1)} %pad_maximum_fusion.1), channel_id=1, source_target_pairs={{0,2},{2,0},{4,6},{6,4},{1,3},{3,1},{5,7},{7,5},{8,10},{10,8},{12,... | collective-permute-start | bytes 3096584 | tf_op jit(solution)/shard_map/ppermute | solution.py:256
  (4 other events, 6.3 us)

commit v5 on v4

--- a/solution.py
+++ b/solution.py
@@ -90,9 +90,15 @@
     return lax.dot_general(left, right, (((1,), (1,)), ((), ())), preferred_element_type=F32)
 
 
-def act_grad_body(ids, w_ref, grad_ref, own_ref, over_ref, pack_ref, u_ref):
+def take(both_ref, second, field_ref):
+    for k in range(16):
+        field_ref[k * C : (k + 1) * C, :] = both_ref[k, second * C : (second + 1) * C, :]
+
+
+def act_grad_body(ids, w_ref, both_ref, own_ref, over_ref, pack_ref, field_ref, u_ref):
     sy = ids[1]
-    grad = grad_ref[...]
+    take(both_ref, 0, field_ref)
+    grad = field_ref[...]
     u_ref[...] = jnp.zeros_like(u_ref)
     for a in range(3):
         for b in range(3):
@@ -148,9 +154,10 @@
             out[:, at] = jnp.where(pre_ref[:, at].astype(F32) > 0, grad, 0.0).astype(BF)
 
 
-def send_body(act, mirror, ids, own_ref, oth_ref, full_ref, send_ref, stack_ref):
+def send_body(act, ids, own_ref, oth_ref, both_ref, send_ref, stack_ref, full_ref):
     sy, core = ids[1], ids[2]
-    fill_windows(own_ref, oth_ref, stack_ref, sy, mirror, act)
+    take(both_ref, 0 if act else 1, full_ref)
+    fill_windows(own_ref, oth_ref, stack_ref, sy, not act, act)
     other = full_ref[pl.ds(pl.multiple_of((1 - core) * HALF, HALF), HALF), :]
     for i in range(9):
         at = slice(i * 3 * C, (i + 1) * 3 * C)
@@ -158,10 +165,11 @@
     send_ref[ROWS:ROWSP, :] = jnp.zeros((ROWSP - ROWS, HALF), BF)
 
 
-def keep_body(act, mirror, ids, own_ref, oth_ref, full_ref, got_ref, keep_ref, *refs):
-    send_refs, stack_ref = refs[:3], refs[3]
+def keep_body(act, ids, own_ref, oth_ref, both_ref, got_ref, keep_ref, *refs):
+    send_refs, (stack_ref, full_ref) = refs[:3], refs[3:]
     sy, core, chip = ids[1], ids[2], ids[3]
-    fill_windows(own_ref, oth_ref, stack_ref, sy, mirror, act)
+    take(both_ref, 0 if act else 1, full_ref)
+    fill_windows(own_ref, oth_ref, stack_ref, sy, not act, act)
     stack_ref[ROWS:ROWSP, :] = jnp.zeros((ROWSP - ROWS, NXL * SLAB), BF)
     mine = full_ref[pl.ds(pl.multiple_of(core * HALF, HALF), HALF), :]
     for k in (1, 3, 2, 0):
@@ -215,21 +223,21 @@
     return [(place(x, c), place((x + shift) % 4, c)) for x in range(4) for c in range(2)]
 
 
-def filter_sums(ids, own, oth, full, act, mirror):
+def filter_sums(ids, own, oth, both, act):
     n_pos = NXL * SLAB
+    field = pltpu.VMEM((CH, n_pos), BF)
     sent = jax.ShapeDtypeStruct((ROWSP, HALF), BF)
     outs = [jax.ShapeDtypeStruct((BLOCK, HALF), F32)]
     outs += [jax.ShapeDtypeStruct((BLOCK, HALF), BF)] * 3
 
     def send():
-        stack = pltpu.VMEM((ROWS, n_pos), BF)
-        body = functools.partial(send_body, act, mirror)
-        return call(body, sent, [stack], 3)(ids, own, oth, full)
+        scratch = [pltpu.VMEM((ROWS, n_pos), BF), field]
+        return call(functools.partial(send_body, act), sent, scratch, 3)(ids, own, oth, both)
 
     def keep(got):
-        stack = pltpu.VMEM((ROWSP, n_pos), BF)
-        body = functools.partial(keep_body, act, mirror)
-        return call(body, tuple(outs), [stack], 4)(ids, own, oth, full, got)
+        scratch = [pltpu.VMEM((ROWSP, n_pos), BF), field]
+        body = functools.partial(keep_body, act)
+        return call(body, tuple(outs), scratch, 4)(ids, own, oth, both, got)
 
     return send, keep
 
@@ -293,26 +301,24 @@
     wide_b = jax.ShapeDtypeStruct((C, wide), BF)
     mid_f = jax.ShapeDtypeStruct((C, n_pos), F32)
 
-    grad = to_all(out_grad.reshape(C, n_pos), "ch", 16).reshape(CH, n_pos)
+    both = jnp.concatenate([out_grad.reshape(C, n_pos), inputs.reshape(C, n_pos)], axis=0)
+    both = to_all(both, "ch", 16)
     pre = halo(pre_act.reshape(C, n_pos))
     w_two = weight_two.reshape(ROWS, CH)
     w_one = weight_one.reshape(ROWS, CH).T
-    mine_in = inputs.reshape(C, n_pos)
-    many_in = jnp.broadcast_to(mine_in[None], (16, C, n_pos))
-    grad, w_one, many_in, pre = lax.optimization_barrier((grad, w_one, many_in, pre))
-    full_in = lax.all_to_all(many_in, "ch", 0, 0, tiled=True).reshape(CH, n_pos)
+    both, w_one, pre = lax.optimization_barrier((both, w_one, pre))
 
     own, over, pack = call(
         act_grad_body,
         (wide_f, wide_f, wide_f),
-        [pltpu.VMEM((3, 3 * C, wide), F32)],
+        [pltpu.VMEM((CH, n_pos), BF), pltpu.VMEM((3, 3 * C, wide), F32)],
         2,
-    )(ids, w_two, grad)
+    )(ids, w_two, both)
     pack = lax.ppermute(pack, LINE, to_side(0, True))
 
-    send_two, keep_two = filter_sums(ids, *pre, grad, True, False)
+    send_two, keep_two = filter_sums(ids, *pre, both, True)
     send2 = send_two()
-    pack, send2, full_in = lax.optimization_barrier((pack, send2, full_in))
+    pack, send2 = lax.optimization_barrier((pack, send2))
     got2 = lax.ppermute(send2, LINE, OTHER_CORE)
     own, oth, left, right = call(join_y_body, (wide_f, wide_f, mid_f, mid_f), [], 3)(
         ids, own, over, pack
@@ -326,7 +332,7 @@
     )
 
     arrive2 = arrive(split2)
-    send_one, keep_one = filter_sums(ids, *delta, full_in, False, True)
+    send_one, keep_one = filter_sums(ids, *delta, both, False)
     got1 = lax.ppermute(send_one(), LINE, OTHER_CORE)
     split1 = keep_one(got1)
     delta, _ = lax.optimization_barrier((delta, split1))
@@ -339,7 +345,7 @@
     got = lax.all_to_all(terms.reshape(16, C, n_pos), "ch", 0, 0, tiled=True)
     block2 = line_sum(arrive2, factor)
     block1 = line_sum(arrive(split1), factor, terms)
-    filter_two = write(ids, *line_spread(block2, (block1, got)))
+    filter_two = write(ids, *line_spread(block2, block1))
     input_grad = got.astype(F32).sum(axis=0).astype(BF).reshape(shape)
     filter_one = write(ids, *line_spread(block1, (filter_two, input_grad)))
     return input_grad, filter_one, filter_two

time: 133 us -> 132 us (level)
  waiting for transfers between devices: 37 us -> 46.4 us
  starting transfers between devices: 58.1 us -> 52.5 us
  other arithmetic: 3.99 us -> 1.81 us
  Pallas kernels: 21.5 us -> 19.9 us
    all_to_all x1, waiting for transfers between devices: 0.01 us -> 13.4 us  [shards(): got = lax.all_to_all(terms.reshape(16, C, n_pos), 'ch', 0, 0, tiled=True)]
    ppermute x6, waiting for transfers between devices: 17.9 us -> 8.33 us  [line_spread(): got = {k: lax.ppermute(block, LINE, along(k)) for k in (1, 3, 2)}]
    ppermute x6, waiting for transfers between devices: 8.04 us -> 15.5 us  [arrive(): lax.ppermute(v, LINE, along(k))]
    all_to_all x1 -> x0, starting transfers between devices: 6.98 us -> none  [shards(): full_in = lax.all_to_all(many_in, 'ch', 0, 0, tiled=True).reshape(CH, n_pos)]
    all_to_all x1 -> x0, waiting for transfers between devices: 5.28 us -> none  [shards(): full_in = lax.all_to_all(many_in, 'ch', 0, 0, tiled=True).reshape(CH, n_pos)]
    all_to_all x1, waiting for transfers between devices: 0.01 us -> 4.05 us  [to_all(): return lax.all_to_all(many, axis, 0, 0, tiled=True)]
    ppermute x2, starting transfers between devices: 6.2 us -> 2.32 us  [line_spread(): return (mine, lax.ppermute(mine, LINE, OTHER_CORE))]
    ppermute x1, starting transfers between devices: 0.39 us -> 3.69 us  [shards(): got2 = lax.ppermute(send2, LINE, OTHER_CORE)]
  transfers between devices with their start and end apart: 27 -> 26, of which waited for: 12 -> 11; matrix products, arithmetic and copies ran while one was open for 5% -> 4% of each run, Pallas kernels for 12% -> 9%
where the time goes in v5:
time: 132 us; the launch traced here: 131 us
  starting transfers between devices  52.5 us (40%)
  waiting for transfers between devices  46.4 us (35%)
  Pallas kernels  19.9 us (15%)
  local copies, waits for them, and re-layouts  9.9 us (8%)
  other arithmetic  1.81 us (1%)
    ppermute x6, waiting for transfers between devices, arrive(): lax.ppermute(v, LINE, along(k))  15.5 us
    all_to_all x1, waiting for transfers between devices, shards(): got = lax.all_to_all(terms.reshape(16, C, n_pos), 'ch', 0, 0, tiled=True)  13.4 us
    all_to_all x1, starting transfers between devices, to_all(): return lax.all_to_all(many, axis, 0, 0, tiled=True)  8.6 us
    ppermute x6, waiting for transfers between devices, line_spread(): got = {k: lax.ppermute(block, LINE, along(k)) for k in (1, 3, 2)}  8.33 us
    ppermute x2, starting transfers between devices, halo(): left = send(last, perm=to_side(1, flip))  7.15 us
    ppermute x6, starting transfers between devices, arrive(): lax.ppermute(v, LINE, along(k))  6.5 us
    pallas_call x2, Pallas kernels, write(): pl.pallas_call(write_body, out_shape=jax.ShapeDtypeStruct((OFF, C, CH), F...  6.05 us
    ppermute x6, starting transfers between devices, line_spread(): got = {k: lax.ppermute(block, LINE, along(k)) for k in (1, 3, 2)}  5.51 us
  transfers between devices with their start and end apart: 26, of which 11 were waited for; matrix products, arithmetic and copies ran while one was open for 4% of the time, Pallas kernels for 9%

profile of v5, /device:TPU:1, one launch (start us, length us, event | category | flops | bytes accessed | tf_op | source)
XLA Modules:
  0.0 131.4 jit_solution(5819391853889694008)
XLA Ops:
  4.0 8.6 %all-to-all-start = ((bf16[16,96,512]{2,1,0:T(8,128)(2,1)}), bf16[16,96,512]{2,1,0:T(8,128)(2,1)S(1)}, u32[]{:S(2)}, u32[]{:S(2)}) async-start(bf16[16,96,512]{2,1,0:T(8,128)(2,1)} %broadcast_in_dim.2), calls=%async_computation | async-start | bytes 3145728 | tf_op jit(solution)/shard_map/all_to_all | solution.py:219
  12.8 5.2 %collective-permute-start.2 = (bf16[48,128]{1,0:T(8,128)(2,1)S(1)}, bf16[48,128]{1,0:T(8,128)(2,1)S(1)}, u32[]{:S(2)}, u32[]{:S(2)}) collective-permute-start(bf16[48,128]{1,0:T(8,128)(2,1)S(1)} %get-tuple-element.77), channel_id=1, source_target_pairs={{0,3},{1,2},{2,5},{3,4},{4,7},{5,6},{8,11},{9,10},{10,13},{11,12},... | collective-permute-start | bytes 36872 | tf_op jit(solution)/shard_map/ppermute | solution.py:211
  18.0 1.9 %collective-permute-start = (bf16[48,128]{1,0:T(8,128)(2,1)S(1)}, bf16[48,128]{1,0:T(8,128)(2,1)S(1)}, u32[]{:S(2)}, u32[]{:S(2)}) collective-permute-start(bf16[48,128]{1,0:T(8,128)(2,1)S(1)} %get-tuple-element.77), channel_id=1, source_target_pairs={{0,2},{1,3},{2,4},{3,5},{4,6},{5,7},{8,10},{9,11},{10,12},{11,13},... | collective-permute-start | bytes 36872 | tf_op jit(solution)/shard_map/ppermute | solution.py:211
  19.9 2.8 %collective-permute-start.4 = (bf16[48,128]{1,0:T(8,128)(2,1)S(1)}, bf16[48,128]{1,0:T(8,128)(2,1)S(1)}, u32[]{:S(2)}, u32[]{:S(2)}) collective-permute-start(bf16[48,128]{1,0:T(8,128)(2,1)S(1)} %get-tuple-element.78), channel_id=1, source_target_pairs={{2,1},{3,0},{4,3},{5,2},{6,5},{7,4},{10,9},{11,8},{12,11},{13,10},... | collective-permute-start | bytes 36872 | tf_op jit(solution)/shard_map/ppermute | solution.py:212
  22.7 1.9 %collective-permute-start.1 = (bf16[48,128]{1,0:T(8,128)(2,1)S(1)}, bf16[48,128]{1,0:T(8,128)(2,1)S(1)}, u32[]{:S(2)}, u32[]{:S(2)}) collective-permute-start(bf16[48,128]{1,0:T(8,128)(2,1)S(1)} %get-tuple-element.78), channel_id=1, source_target_pairs={{2,0},{3,1},{4,2},{5,3},{6,4},{7,5},{10,8},{11,9},{12,10},{13,11},... | collective-permute-start | bytes 36872 | tf_op jit(solution)/shard_map/ppermute | solution.py:212
  24.7 2.5 %collective-permute-start.3 = (bf16[48,512]{1,0:T(8,128)(2,1)S(1)}, bf16[48,512]{1,0:T(8,128)(2,1)S(1)}, u32[]{:S(2)}, u32[]{:S(2)}) collective-permute-start(bf16[48,512]{1,0:T(8,128)(2,1)S(1)} %reshape.44), channel_id=1, source_target_pairs={{0,1},{1,0},{2,3},{3,2},{4,5},{5,4},{6,7},{7,6},{8,9},{9,8},{10,11... | collective-permute-start | bytes 147464 | tf_op jit(solution)/shard_map/ppermute | solution.py:210
  27.3 4.1 %copy.9 = bf16[1296,768]{0,1:T(8,128)(2,1)} copy(bf16[1296,768]{1,0:T(8,128)(2,1)} %bitcast.18) | data formatting | bytes 3981312 | tf_op jit(solution)/shard_map/reshape | solution.py:308
  31.4 4.1 %all-to-all-done.both_ref = bf16[16,96,512]{2,1,0:T(8,128)(2,1)S(1)} async-done(((bf16[16,96,512]{2,1,0:T(8,128)(2,1)}), bf16[16,96,512]{2,1,0:T(8,128)(2,1)S(1)}, u32[]{:S(2)}, u32[]{:S(2)}) %all-to-all-start) | async-done | bytes 1572896 | tf_op jit(solution)/shard_map/all_to_all | solution.py:219
  35.5 1.6 %copy-done.1 = bf16[27,48,768]{2,1,0:T(8,128)(2,1)S(1)} copy-done((bf16[27,48,768]{2,1,0:T(8,128)(2,1)S(1)}, bf16[27,48,768]{2,1,0:T(8,128)(2,1)}, u32[]{:S(2)}) %copy-start.1) | copy-done | bytes 1990680
  37.0 1.9 %shard_map.76 = (f32[48,768]{1,0:T(8,128)S(1)}, f32[48,768]{1,0:T(8,128)S(1)}, f32[48,768]{1,0:T(8,128)S(1)}) custom-call(s32[4]{0:T(128)S(1)} %pad_add_fusion.ids, bf16[1296,768]{1,0:T(8,128)(2,1)S(1)} %bitcast.15, bf16[16,96,512]{2,1,0:T(8,128)(2,1)S(1)} %all-to-all-done.both_ref), custom_call_target="tpu_custom_call" | custom-call | tf_op jit(solution)/shard_map/pallas_call | solution.py:311
  39.0 2.8 %collective-permute-start.5 = (f32[48,768]{1,0:T(8,128)S(1)}, f32[48,768]{1,0:T(8,128)S(1)}, u32[]{:S(2)}, u32[]{:S(2)}) collective-permute-start(f32[48,768]{1,0:T(8,128)S(1)} %get-tuple-element.43), channel_id=1, source_target_pairs={{0,1},{1,0},{2,3},{3,2},{4,5},{5,4},{6,7},{7,6},{8,9},{9,8},{10,11... | collective-permute-start | bytes 442376 | tf_op jit(solution)/shard_map/ppermute | solution.py:317
  41.8 1.9 %shard_map.77 = bf16[1344,384]{1,0:T(8,128)(2,1)S(1)} custom-call(s32[4]{0:T(128)S(1)} %pad_add_fusion.ids, bf16[48,768]{1,0:T(8,128)(2,1)S(1)} %pad_maximum_fusion.3.own_ref.pre_own_ref, bf16[48,768]{1,0:T(8,128)(2,1)S(1)} %pad_maximum_fusion.4.oth_ref.pre_oth_ref, bf16[16,96,512]{2,1,0:T(8,128)(2,1)S(1)} %all-to-all-done.both_ref), custom_call_target="tpu_custom_call" | custom-call | tf_op jit(solution)/shard_map/pallas_call | solution.py:235
  44.6 3.7 %collective-permute-start.8 = (bf16[1344,384]{1,0:T(8,128)(2,1)S(1)}, bf16[1344,384]{1,0:T(8,128)(2,1)S(1)}, u32[]{:S(2)}, u32[]{:S(2)}) collective-permute-start(bf16[1344,384]{1,0:T(8,128)(2,1)S(1)} %shard_map.77), channel_id=1, source_target_pairs={{0,2},{2,0},{4,6},{6,4},{1,3},{3,1},{5,7},{7,5},{8,10},{10,8},{12,... | collective-permute-start | bytes 3096584 | tf_op jit(solution)/shard_map/ppermute | solution.py:322
  48.9 3.0 %collective-permute-start.6 = (f32[48,512]{1,0:T(8,128)S(1)}, f32[48,512]{1,0:T(8,128)S(1)}, u32[]{:S(2)}, u32[]{:S(2)}) collective-permute-start(f32[48,512]{1,0:T(8,128)S(1)} %get-tuple-element.49), channel_id=1, source_target_pairs={{0,2},{1,3},{2,4},{3,5},{4,6},{5,7},{8,10},{9,11},{10,12},{11,13},... | collective-permute-start | bytes 294920 | tf_op jit(solution)/shard_map/ppermute | solution.py:326
  51.9 1.9 %collective-permute-start.7 = (f32[48,512]{1,0:T(8,128)S(1)}, f32[48,512]{1,0:T(8,128)S(1)}, u32[]{:S(2)}, u32[]{:S(2)}) collective-permute-start(f32[48,512]{1,0:T(8,128)S(1)} %get-tuple-element.50), channel_id=1, source_target_pairs={{2,0},{3,1},{4,2},{5,3},{6,4},{7,5},{10,8},{11,9},{12,10},{13,11},... | collective-permute-start | bytes 294920 | tf_op jit(solution)/shard_map/ppermute | solution.py:327
  53.8 2.0 %shard_map.79 = (f32[336,384]{1,0:T(8,128)S(1)}, bf16[336,384]{1,0:T(8,128)(2,1)S(1)}, bf16[336,384]{1,0:T(8,128)(2,1)S(1)}, bf16[336,384]{1,0:T(8,128)(2,1)S(1)}) custom-call(s32[4]{0:T(128)S(1)} %pad_add_fusion.ids, bf16[48,768]{1,0:T(8,128)(2,1)S(1)} %pad_maximum_fusion.3.own_ref.pre_own_ref, bf16[48,768]{1,0:T(8,128)(2,1)S(1)} %pad_maximum_fusion.4.oth_ref.pre_oth_ref, ...), custom_call_target="tpu_custom_call" | custom-call | tf_op jit(solution)/shard_map/pallas_call | solution.py:240
  55.8 2.0 %collective-permute-done.7.right_ref = f32[48,512]{1,0:T(8,128)S(1)} collective-permute-done((f32[48,512]{1,0:T(8,128)S(1)}, f32[48,512]{1,0:T(8,128)S(1)}, u32[]{:S(2)}, u32[]{:S(2)}) %collective-permute-start.7) | collective-permute-done | bytes 98336 | tf_op jit(solution)/shard_map/ppermute | solution.py:327
  58.4 1.9 %shard_map.81 = bf16[1344,384]{1,0:T(8,128)(2,1)S(1)} custom-call(s32[4]{0:T(128)S(1)} %pad_add_fusion.ids, bf16[48,768]{1,0:T(8,128)(2,1)S(1)} %get-tuple-element.64.own_ref.refs_0_, bf16[48,768]{1,0:T(8,128)(2,1)S(1)} %get-tuple-element.65.oth_ref.refs_1_, bf16[16,96,512]{2,1,0:T(8,128)(2,1)S(1)} %all-to-all-done.both_ref), custom_call_target="tpu_custom_call" | custom-call | tf_op jit(solution)/shard_map/pallas_call | solution.py:235
  60.5 2.5 %collective-permute-start.18 = (bf16[336,384]{1,0:T(8,128)(2,1)S(1)}, bf16[336,384]{1,0:T(8,128)(2,1)S(1)}, u32[]{:S(2)}, u32[]{:S(2)}) collective-permute-start(bf16[336,384]{1,0:T(8,128)(2,1)S(1)} %get-tuple-element.54), channel_id=1, source_target_pairs={{0,1},{2,3},{4,5},{6,7},{1,0},{3,2},{5,4},{7,6},{8,9},{10,11},{12,... | collective-permute-start | bytes 774152 | tf_op jit(solution)/shard_map/ppermute | solution.py:247
  63.1 2.0 %collective-permute-start.17 = (bf16[336,384]{1,0:T(8,128)(2,1)S(1)}, bf16[336,384]{1,0:T(8,128)(2,1)S(1)}, u32[]{:S(2)}, u32[]{:S(2)}) collective-permute-start(bf16[336,384]{1,0:T(8,128)(2,1)S(1)} %get-tuple-element.55), channel_id=1, source_target_pairs={{0,5},{2,7},{4,0},{6,2},{1,4},{3,6},{5,1},{7,3},{8,13},{10,15},{12... | collective-permute-start | bytes 774152 | tf_op jit(solution)/shard_map/ppermute | solution.py:247
  65.0 2.0 %shard_map.82 = (f32[336,384]{1,0:T(8,128)S(1)}, bf16[336,384]{1,0:T(8,128)(2,1)S(1)}, bf16[336,384]{1,0:T(8,128)(2,1)S(1)}, bf16[336,384]{1,0:T(8,128)(2,1)S(1)}) custom-call(s32[4]{0:T(128)S(1)} %pad_add_fusion.ids, bf16[48,768]{1,0:T(8,128)(2,1)S(1)} %get-tuple-element.64.own_ref.refs_0_, bf16[48,768]{1,0:T(8,128)(2,1)S(1)} %get-tuple-element.65.oth_ref.refs_1_, ...), custom_call_target="tpu_custom_call" | custom-call | tf_op jit(solution)/shard_map/pallas_call | solution.py:240
  69.8 5.0 %collective-permute-done.18 = bf16[336,384]{1,0:T(8,128)(2,1)S(1)} collective-permute-done((bf16[336,384]{1,0:T(8,128)(2,1)S(1)}, bf16[336,384]{1,0:T(8,128)(2,1)S(1)}, u32[]{:S(2)}, u32[]{:S(2)}) %collective-permute-start.18) | collective-permute-done | bytes 258080 | tf_op jit(solution)/shard_map/ppermute | solution.py:247
  75.7 4.0 %collective-permute-start.21 = (bf16[336,384]{1,0:T(8,128)(2,1)S(1)}, bf16[336,384]{1,0:T(8,128)(2,1)S(1)}, u32[]{:S(2)}, u32[]{:S(2)}) collective-permute-start(bf16[336,384]{1,0:T(8,128)(2,1)S(1)} %multiply_convert_fusion), channel_id=1, source_target_pairs={{0,5},{2,7},{4,0},{6,2},{1,4},{3,6},{5,1},{7,3},{8,13},{10,15},{12... | collective-permute-start | bytes 774152 | tf_op jit(solution)/shard_map/ppermute | solution.py:260
  79.6 3.0 %shard_map.83 = bf16[768,512]{1,0:T(8,128)(2,1)} custom-call(s32[4]{0:T(128)S(1)} %pad_add_fusion.ids, bf16[48,768]{1,0:T(8,128)(2,1)S(1)} %get-tuple-element.64.own_ref.refs_0_, bf16[48,768]{1,0:T(8,128)(2,1)S(1)} %get-tuple-element.65.oth_ref.refs_1_, bf16[768,1296]{1,0:T(8,128)(2,1)S(1)} %bitcast.12), custom_call_target="tpu_custom_call" | custom-call | tf_op jit(solution)/shard_map/pallas_call | solution.py:339
  82.7 8.9 %collective-permute-done.10 = bf16[336,384]{1,0:T(8,128)(2,1)S(1)} collective-permute-done((bf16[336,384]{1,0:T(8,128)(2,1)S(1)}, bf16[336,384]{1,0:T(8,128)(2,1)S(1)}, u32[]{:S(2)}, u32[]{:S(2)}) %collective-permute-start.10) | collective-permute-done | bytes 258080 | tf_op jit(solution)/shard_map/ppermute | solution.py:247
  92.0 8.0 %collective-permute-done.19 = bf16[336,384]{1,0:T(8,128)(2,1)S(1)} collective-permute-done((bf16[336,384]{1,0:T(8,128)(2,1)S(1)}, bf16[336,384]{1,0:T(8,128)(2,1)S(1)}, u32[]{:S(2)}, u32[]{:S(2)}) %collective-permute-start.19) | collective-permute-done | bytes 258080 | tf_op jit(solution)/shard_map/ppermute | solution.py:260
  100.1 1.4 %collective-permute-start.22 = (bf16[1344,384]{1,0:T(8,128)(2,1)S(1)}, bf16[1344,384]{1,0:T(8,128)(2,1)S(1)}, u32[]{:S(2)}, u32[]{:S(2)}) collective-permute-start(bf16[1344,384]{1,0:T(8,128)(2,1)S(1)} %pad_maximum_fusion), channel_id=1, source_target_pairs={{0,2},{2,0},{4,6},{6,4},{1,3},{3,1},{5,7},{7,5},{8,10},{10,8},{12,... | collective-permute-start | bytes 3096584 | tf_op jit(solution)/shard_map/ppermute | solution.py:264
  101.6 3.6 %all-to-all-start.1 = ((bf16[16,48,512]{2,1,0:T(8,128)(2,1)}), bf16[16,48,512]{2,1,0:T(8,128)(2,1)S(1)}, u32[]{:S(2)}, u32[]{:S(2)}) async-start(bf16[16,48,512]{2,1,0:T(8,128)(2,1)} %bitcast.7), calls=%async_computation.1 | async-start | bytes 1572864 | tf_op jit(solution)/shard_map/all_to_all | solution.py:345
  106.7 13.4 %all-to-all-done.1 = bf16[16,48,512]{2,1,0:T(8,128)(2,1)S(1)} async-done(((bf16[16,48,512]{2,1,0:T(8,128)(2,1)}), bf16[16,48,512]{2,1,0:T(8,128)(2,1)S(1)}, u32[]{:S(2)}, u32[]{:S(2)}) %all-to-all-start.1) | async-done | bytes 786464 | tf_op jit(solution)/shard_map/all_to_all | solution.py:345
  121.0 3.0 %shard_map.84 = f32[27,48,768]{2,1,0:T(8,128)} custom-call(s32[4]{0:T(128)S(1)} %pad_add_fusion.ids, bf16[4,7,48,384]{3,2,1,0:T(8,128)(2,1)S(1)} %bitcast.13, bf16[4,7,48,384]{3,2,1,0:T(8,128)(2,1)S(1)} %bitcast.16), custom_call_target="tpu_custom_call" | custom-call | tf_op jit(solution)/shard_map/pallas_call | solution.py:278
  126.1 2.3 %collective-permute-done.23 = bf16[1344,384]{1,0:T(8,128)(2,1)S(1)} collective-permute-done((bf16[1344,384]{1,0:T(8,128)(2,1)S(1)}, bf16[1344,384]{1,0:T(8,128)(2,1)S(1)}, u32[]{:S(2)}, u32[]{:S(2)}) %collective-permute-start.23) | collective-permute-done | bytes 1032224 | tf_op jit(solution)/shard_map/ppermute | solution.py:264
  128.4 3.0 %shard_map.85 = f32[27,48,768]{2,1,0:T(8,128)} custom-call(s32[4]{0:T(128)S(1)} %pad_add_fusion.ids, bf16[4,7,48,384]{3,2,1,0:T(8,128)(2,1)S(1)} %bitcast.14, bf16[4,7,48,384]{3,2,1,0:T(8,128)(2,1)S(1)} %bitcast.17), custom_call_target="tpu_custom_call" | custom-call | tf_op jit(solution)/shard_map/pallas_call | solution.py:278
  (52 shorter events, 14.5 us)
Async XLA Ops:
  2.7 9.9 %copy-start.2 = (bf16[48,4,2,64]{3,2,1,0:T(2,128)(2,1)S(1)}, bf16[48,4,2,64]{3,2,1,0:T(2,128)(2,1)}, u32[]{:S(2)}) copy-start(bf16[48,4,2,64]{3,2,1,0:T(2,128)(2,1)} %param.6) | copy-start | bytes 147460
  4.0 31.5 %all-to-all-start = ((bf16[16,96,512]{2,1,0:T(8,128)(2,1)}), bf16[16,96,512]{2,1,0:T(8,128)(2,1)S(1)}, u32[]{:S(2)}, u32[]{:S(2)}) async-start(bf16[16,96,512]{2,1,0:T(8,128)(2,1)} %broadcast_in_dim.2), calls=%async_computation | async-start | bytes 3145728 | tf_op jit(solution)/shard_map/all_to_all | solution.py:219
  12.8 18.6 %collective-permute-start.2 = (bf16[48,128]{1,0:T(8,128)(2,1)S(1)}, bf16[48,128]{1,0:T(8,128)(2,1)S(1)}, u32[]{:S(2)}, u32[]{:S(2)}) collective-permute-start(bf16[48,128]{1,0:T(8,128)(2,1)S(1)} %get-tuple-element.77), channel_id=1, source_target_pairs={{0,3},{1,2},{2,5},{3,4},{4,7},{5,6},{8,11},{9,10},{10,13},{11,12},... | collective-permute-start | bytes 36872 | tf_op jit(solution)/shard_map/ppermute | solution.py:211
  18.0 13.4 %collective-permute-start = (bf16[48,128]{1,0:T(8,128)(2,1)S(1)}, bf16[48,128]{1,0:T(8,128)(2,1)S(1)}, u32[]{:S(2)}, u32[]{:S(2)}) collective-permute-start(bf16[48,128]{1,0:T(8,128)(2,1)S(1)} %get-tuple-element.77), channel_id=1, source_target_pairs={{0,2},{1,3},{2,4},{3,5},{4,6},{5,7},{8,10},{9,11},{10,12},{11,13},... | collective-permute-start | bytes 36872 | tf_op jit(solution)/shard_map/ppermute | solution.py:211
  19.9 11.5 %collective-permute-start.4 = (bf16[48,128]{1,0:T(8,128)(2,1)S(1)}, bf16[48,128]{1,0:T(8,128)(2,1)S(1)}, u32[]{:S(2)}, u32[]{:S(2)}) collective-permute-start(bf16[48,128]{1,0:T(8,128)(2,1)S(1)} %get-tuple-element.78), channel_id=1, source_target_pairs={{2,1},{3,0},{4,3},{5,2},{6,5},{7,4},{10,9},{11,8},{12,11},{13,10},... | collective-permute-start | bytes 36872 | tf_op jit(solution)/shard_map/ppermute | solution.py:212
  22.7 8.6 %collective-permute-start.1 = (bf16[48,128]{1,0:T(8,128)(2,1)S(1)}, bf16[48,128]{1,0:T(8,128)(2,1)S(1)}, u32[]{:S(2)}, u32[]{:S(2)}) collective-permute-start(bf16[48,128]{1,0:T(8,128)(2,1)S(1)} %get-tuple-element.78), channel_id=1, source_target_pairs={{2,0},{3,1},{4,2},{5,3},{6,4},{7,5},{10,8},{11,9},{12,10},{13,11},... | collective-permute-start | bytes 36872 | tf_op jit(solution)/shard_map/ppermute | solution.py:212
  24.7 6.7 %collective-permute-start.3 = (bf16[48,512]{1,0:T(8,128)(2,1)S(1)}, bf16[48,512]{1,0:T(8,128)(2,1)S(1)}, u32[]{:S(2)}, u32[]{:S(2)}) collective-permute-start(bf16[48,512]{1,0:T(8,128)(2,1)S(1)} %reshape.44), channel_id=1, source_target_pairs={{0,1},{1,0},{2,3},{3,2},{4,5},{5,4},{6,7},{7,6},{8,9},{9,8},{10,11... | collective-permute-start | bytes 147464 | tf_op jit(solution)/shard_map/ppermute | solution.py:210
  35.5 1.6 %copy-start.1 = (bf16[27,48,768]{2,1,0:T(8,128)(2,1)S(1)}, bf16[27,48,768]{2,1,0:T(8,128)(2,1)}, u32[]{:S(2)}) copy-start(bf16[27,48,768]{2,1,0:T(8,128)(2,1)} %param.9) | copy-start | bytes 5971972
  39.0 5.6 %collective-permute-start.5 = (f32[48,768]{1,0:T(8,128)S(1)}, f32[48,768]{1,0:T(8,128)S(1)}, u32[]{:S(2)}, u32[]{:S(2)}) collective-permute-start(f32[48,768]{1,0:T(8,128)S(1)} %get-tuple-element.43), channel_id=1, source_target_pairs={{0,1},{1,0},{2,3},{3,2},{4,5},{5,4},{6,7},{7,6},{8,9},{9,8},{10,11... | collective-permute-start | bytes 442376 | tf_op jit(solution)/shard_map/ppermute | solution.py:317
  44.6 9.2 %collective-permute-start.8 = (bf16[1344,384]{1,0:T(8,128)(2,1)S(1)}, bf16[1344,384]{1,0:T(8,128)(2,1)S(1)}, u32[]{:S(2)}, u32[]{:S(2)}) collective-permute-start(bf16[1344,384]{1,0:T(8,128)(2,1)S(1)} %shard_map.77), channel_id=1, source_target_pairs={{0,2},{2,0},{4,6},{6,4},{1,3},{3,1},{5,7},{7,5},{8,10},{10,8},{12,... | collective-permute-start | bytes 3096584 | tf_op jit(solution)/shard_map/ppermute | solution.py:322
  48.9 6.9 %collective-permute-start.6 = (f32[48,512]{1,0:T(8,128)S(1)}, f32[48,512]{1,0:T(8,128)S(1)}, u32[]{:S(2)}, u32[]{:S(2)}) collective-permute-start(f32[48,512]{1,0:T(8,128)S(1)} %get-tuple-element.49), channel_id=1, source_target_pairs={{0,2},{1,3},{2,4},{3,5},{4,6},{5,7},{8,10},{9,11},{10,12},{11,13},... | collective-permute-start | bytes 294920 | tf_op jit(solution)/shard_map/ppermute | solution.py:326
  51.9 5.9 %collective-permute-start.7 = (f32[48,512]{1,0:T(8,128)S(1)}, f32[48,512]{1,0:T(8,128)S(1)}, u32[]{:S(2)}, u32[]{:S(2)}) collective-permute-start(f32[48,512]{1,0:T(8,128)S(1)} %get-tuple-element.50), channel_id=1, source_target_pairs={{2,0},{3,1},{4,2},{5,3},{6,4},{7,5},{10,8},{11,9},{12,10},{13,11},... | collective-permute-start | bytes 294920 | tf_op jit(solution)/shard_map/ppermute | solution.py:327
  60.3 19.3 %copy-start = (bf16[1296,768]{0,1:T(8,128)(2,1)S(1)}, bf16[1296,768]{0,1:T(8,128)(2,1)}, u32[]{:S(2)}) copy-start(bf16[1296,768]{0,1:T(8,128)(2,1)} %copy.9) | copy-start | bytes 5971972
  60.3 4.7 %collective-permute-start.9 = (bf16[1344,384]{1,0:T(8,128)(2,1)S(1)}, bf16[1344,384]{1,0:T(8,128)(2,1)S(1)}, u32[]{:S(2)}, u32[]{:S(2)}) collective-permute-start(bf16[1344,384]{1,0:T(8,128)(2,1)S(1)} %shard_map.81), channel_id=1, source_target_pairs={{0,2},{2,0},{4,6},{6,4},{1,3},{3,1},{5,7},{7,5},{8,10},{10,8},{12,... | collective-permute-start | bytes 3096584 | tf_op jit(solution)/shard_map/ppermute | solution.py:336
  60.4 8.6 %collective-permute-start.16 = (bf16[336,384]{1,0:T(8,128)(2,1)S(1)}, bf16[336,384]{1,0:T(8,128)(2,1)S(1)}, u32[]{:S(2)}, u32[]{:S(2)}) collective-permute-start(bf16[336,384]{1,0:T(8,128)(2,1)S(1)} %get-tuple-element.53), channel_id=1, source_target_pairs={{0,4},{2,6},{4,1},{6,3},{1,5},{3,7},{5,0},{7,2},{8,12},{10,14},{12... | collective-permute-start | bytes 774152 | tf_op jit(solution)/shard_map/ppermute | solution.py:247
  60.5 14.2 %collective-permute-start.18 = (bf16[336,384]{1,0:T(8,128)(2,1)S(1)}, bf16[336,384]{1,0:T(8,128)(2,1)S(1)}, u32[]{:S(2)}, u32[]{:S(2)}) collective-permute-start(bf16[336,384]{1,0:T(8,128)(2,1)S(1)} %get-tuple-element.54), channel_id=1, source_target_pairs={{0,1},{2,3},{4,5},{6,7},{1,0},{3,2},{5,4},{7,6},{8,9},{10,11},{12,... | collective-permute-start | bytes 774152 | tf_op jit(solution)/shard_map/ppermute | solution.py:247
  63.1 12.4 %collective-permute-start.17 = (bf16[336,384]{1,0:T(8,128)(2,1)S(1)}, bf16[336,384]{1,0:T(8,128)(2,1)S(1)}, u32[]{:S(2)}, u32[]{:S(2)}) collective-permute-start(bf16[336,384]{1,0:T(8,128)(2,1)S(1)} %get-tuple-element.55), channel_id=1, source_target_pairs={{0,5},{2,7},{4,0},{6,2},{1,4},{3,6},{5,1},{7,3},{8,13},{10,15},{12... | collective-permute-start | bytes 774152 | tf_op jit(solution)/shard_map/ppermute | solution.py:247
  67.0 24.5 %collective-permute-start.10 = (bf16[336,384]{1,0:T(8,128)(2,1)S(1)}, bf16[336,384]{1,0:T(8,128)(2,1)S(1)}, u32[]{:S(2)}, u32[]{:S(2)}) collective-permute-start(bf16[336,384]{1,0:T(8,128)(2,1)S(1)} %get-tuple-element.61), channel_id=1, source_target_pairs={{0,4},{2,6},{4,1},{6,3},{1,5},{3,7},{5,0},{7,2},{8,12},{10,14},{12... | collective-permute-start | bytes 774152 | tf_op jit(solution)/shard_map/ppermute | solution.py:247
  67.1 24.5 %collective-permute-start.12 = (bf16[336,384]{1,0:T(8,128)(2,1)S(1)}, bf16[336,384]{1,0:T(8,128)(2,1)S(1)}, u32[]{:S(2)}, u32[]{:S(2)}) collective-permute-start(bf16[336,384]{1,0:T(8,128)(2,1)S(1)} %get-tuple-element.62), channel_id=1, source_target_pairs={{0,1},{2,3},{4,5},{6,7},{1,0},{3,2},{5,4},{7,6},{8,9},{10,11},{12,... | collective-permute-start | bytes 774152 | tf_op jit(solution)/shard_map/ppermute | solution.py:247
  69.1 22.5 %collective-permute-start.11 = (bf16[336,384]{1,0:T(8,128)(2,1)S(1)}, bf16[336,384]{1,0:T(8,128)(2,1)S(1)}, u32[]{:S(2)}, u32[]{:S(2)}) collective-permute-start(bf16[336,384]{1,0:T(8,128)(2,1)S(1)} %get-tuple-element.63), channel_id=1, source_target_pairs={{0,5},{2,7},{4,0},{6,2},{1,4},{3,6},{5,1},{7,3},{8,13},{10,15},{12... | collective-permute-start | bytes 774152 | tf_op jit(solution)/shard_map/ppermute | solution.py:247
  75.7 16.4 %collective-permute-start.21 = (bf16[336,384]{1,0:T(8,128)(2,1)S(1)}, bf16[336,384]{1,0:T(8,128)(2,1)S(1)}, u32[]{:S(2)}, u32[]{:S(2)}) collective-permute-start(bf16[336,384]{1,0:T(8,128)(2,1)S(1)} %multiply_convert_fusion), channel_id=1, source_target_pairs={{0,5},{2,7},{4,0},{6,2},{1,4},{3,6},{5,1},{7,3},{8,13},{10,15},{12... | collective-permute-start | bytes 774152 | tf_op jit(solution)/shard_map/ppermute | solution.py:260
  79.6 12.4 %collective-permute-start.20 = (bf16[336,384]{1,0:T(8,128)(2,1)S(1)}, bf16[336,384]{1,0:T(8,128)(2,1)S(1)}, u32[]{:S(2)}, u32[]{:S(2)}) collective-permute-start(bf16[336,384]{1,0:T(8,128)(2,1)S(1)} %multiply_convert_fusion), channel_id=1, source_target_pairs={{0,1},{2,3},{4,5},{6,7},{1,0},{3,2},{5,4},{7,6},{8,9},{10,11},{12,... | collective-permute-start | bytes 774152 | tf_op jit(solution)/shard_map/ppermute | solution.py:260
  91.5 8.5 %collective-permute-start.19 = (bf16[336,384]{1,0:T(8,128)(2,1)S(1)}, bf16[336,384]{1,0:T(8,128)(2,1)S(1)}, u32[]{:S(2)}, u32[]{:S(2)}) collective-permute-start(bf16[336,384]{1,0:T(8,128)(2,1)S(1)} %multiply_convert_fusion), channel_id=1, source_target_pairs={{0,4},{2,6},{4,1},{6,3},{1,5},{3,7},{5,0},{7,2},{8,12},{10,14},{12... | collective-permute-start | bytes 774152 | tf_op jit(solution)/shard_map/ppermute | solution.py:260
  100.1 20.8 %collective-permute-start.22 = (bf16[1344,384]{1,0:T(8,128)(2,1)S(1)}, bf16[1344,384]{1,0:T(8,128)(2,1)S(1)}, u32[]{:S(2)}, u32[]{:S(2)}) collective-permute-start(bf16[1344,384]{1,0:T(8,128)(2,1)S(1)} %pad_maximum_fusion), channel_id=1, source_target_pairs={{0,2},{2,0},{4,6},{6,4},{1,3},{3,1},{5,7},{7,5},{8,10},{10,8},{12,... | collective-permute-start | bytes 3096584 | tf_op jit(solution)/shard_map/ppermute | solution.py:264
  101.6 18.5 %all-to-all-start.1 = ((bf16[16,48,512]{2,1,0:T(8,128)(2,1)}), bf16[16,48,512]{2,1,0:T(8,128)(2,1)S(1)}, u32[]{:S(2)}, u32[]{:S(2)}) async-start(bf16[16,48,512]{2,1,0:T(8,128)(2,1)} %bitcast.7), calls=%async_computation.1 | async-start | bytes 1572864 | tf_op jit(solution)/shard_map/all_to_all | solution.py:345
  105.2 18.8 %collective-permute-start.15 = (bf16[336,384]{1,0:T(8,128)(2,1)S(1)}, bf16[336,384]{1,0:T(8,128)(2,1)S(1)}, u32[]{:S(2)}, u32[]{:S(2)}) collective-permute-start(bf16[336,384]{1,0:T(8,128)(2,1)S(1)} %multiply_convert_fusion.1), channel_id=1, source_target_pairs={{0,5},{2,7},{4,0},{6,2},{1,4},{3,6},{5,1},{7,3},{8,13},{10,15},{12... | collective-permute-start | bytes 774152 | tf_op jit(solution)/shard_map/ppermute | solution.py:260
  105.3 18.7 %collective-permute-start.14 = (bf16[336,384]{1,0:T(8,128)(2,1)S(1)}, bf16[336,384]{1,0:T(8,128)(2,1)}, u32[]{:S(2)}, u32[]{:S(2)}) collective-permute-start(bf16[336,384]{1,0:T(8,128)(2,1)S(1)} %multiply_convert_fusion.1), channel_id=1, source_target_pairs={{0,1},{2,3},{4,5},{6,7},{1,0},{3,2},{5,4},{7,6},{8,9},{10,11},{12,... | collective-permute-start | bytes 774152 | tf_op jit(solution)/shard_map/ppermute | solution.py:260
  106.2 17.8 %collective-permute-start.13 = (bf16[336,384]{1,0:T(8,128)(2,1)S(1)}, bf16[336,384]{1,0:T(8,128)(2,1)}, u32[]{:S(2)}, u32[]{:S(2)}) collective-permute-start(bf16[336,384]{1,0:T(8,128)(2,1)S(1)} %multiply_convert_fusion.1), channel_id=1, source_target_pairs={{0,4},{2,6},{4,1},{6,3},{1,5},{3,7},{5,0},{7,2},{8,12},{10,14},{12... | collective-permute-start | bytes 774152 | tf_op jit(solution)/shard_map/ppermute | solution.py:260
  125.2 3.1 %collective-permute-start.23 = (bf16[1344,384]{1,0:T(8,128)(2,1)S(1)}, bf16[1344,384]{1,0:T(8,128)(2,1)S(1)}, u32[]{:S(2)}, u32[]{:S(2)}) collective-permute-start(bf16[1344,384]{1,0:T(8,128)(2,1)S(1)} %pad_maximum_fusion.1), channel_id=1, source_target_pairs={{0,2},{2,0},{4,6},{6,4},{1,3},{3,1},{5,7},{7,5},{8,10},{10,8},{12,... | collective-permute-start | bytes 3096584 | tf_op jit(solution)/shard_map/ppermute | solution.py:264

commit v6 on v5

--- a/solution.py
+++ b/solution.py
@@ -37,9 +37,11 @@
     return pl.BlockSpec(memory_space=pltpu.SMEM)
 
 
-def call(body, outs, scratch, n_in, limit=16):
+def call(body, outs, scratch, n_in, us=1, limit=16):
+    cost = pl.CostEstimate(flops=us * 10**9, transcendentals=0, bytes_accessed=us * 3 * 10**6)
     return pl.pallas_call(
         body,
+        cost_estimate=cost,
         out_shape=outs,
         in_specs=[smem()] + [vmem()] * n_in,
         out_specs=jax.tree.map(lambda _: vmem(), outs),
@@ -86,18 +88,47 @@
                         stack_ref[o * C : (o + 1) * C, xl * SLAB : (xl + 1) * SLAB] = part
 
 
+def line_windows(line_ref, stack_ref, first, sx, sy):
+    lane = lanes()
+    low = lane < 64
+    for xp in range(NXL + 2):
+        peer_x = sx + (-1 if xp == 0 else 1 if xp == NXL + 1 else 0)
+        inside = jnp.logical_and(peer_x >= 0, peer_x <= 3)
+        peer_x = jnp.clip(peer_x, 0, 3)
+        at = ((xp - 1) % NXL) * SLAB
+        own = line_ref[peer_x * 2 + sy, :, at : at + SLAB].astype(F32)
+        oth = line_ref[peer_x * 2 + 1 - sy, :, at : at + SLAB].astype(F32)
+        if xp in (0, NXL + 1):
+            own, oth = jnp.where(inside, own, 0.0), jnp.where(inside, oth, 0.0)
+        r_own, r_oth = pltpu.roll(own, 64, 1), pltpu.roll(oth, 64, 1)
+        rows = (
+            jnp.where(low, jnp.where(sy == 1, r_oth, 0.0), r_own),
+            own,
+            jnp.where(low, r_own, jnp.where(sy == 0, r_oth, 0.0)),
+        )
+        for b in range(3):
+            for c in range(3):
+                part = shift_z(rows[b], c, lane).astype(BF)
+                for a in range(3):
+                    xl = xp - a
+                    if 0 <= xl < NXL:
+                        o = 26 - (9 * a + 3 * b + c)
+                        to = first + xl * SLAB
+                        stack_ref[o * C : (o + 1) * C, to : to + SLAB] = part
+
+
 def nt(left, right):
     return lax.dot_general(left, right, (((1,), (1,)), ((), ())), preferred_element_type=F32)
 
 
-def take(both_ref, second, field_ref):
+def take(grad_ref, field_ref):
     for k in range(16):
-        field_ref[k * C : (k + 1) * C, :] = both_ref[k, second * C : (second + 1) * C, :]
-
-
-def act_grad_body(ids, w_ref, both_ref, own_ref, over_ref, pack_ref, field_ref, u_ref):
+        field_ref[k * C : (k + 1) * C, :] = grad_ref[k]
+
+
+def act_grad_body(ids, w_ref, grad_ref, own_ref, over_ref, pack_ref, field_ref, u_ref):
     sy = ids[1]
-    take(both_ref, 0, field_ref)
+    take(grad_ref, field_ref)
     grad = field_ref[...]
     u_ref[...] = jnp.zeros_like(u_ref)
     for a in range(3):
@@ -137,7 +168,8 @@
                 out[:, k + 2 * SLAB : k + 3 * SLAB] = oth
 
 
-def delta_body(ids, own_ref, oth_ref, left_ref, right_ref, pre_own_ref, pre_oth_ref, own_out, oth_out):
+def delta_body(ids, own_ref, oth_ref, left_ref, right_ref, pre_own_ref, pre_oth_ref, *outs):
+    own_out, oth_out, mid_out = outs
     for xp in range(NXL + 2):
         at = slice(xp * SLAB, (xp + 1) * SLAB)
         for grad_ref, pre_ref, out, half in (
@@ -151,13 +183,16 @@
             if xp >= NXL:
                 k = half + (xp - NXL) * SLAB
                 grad = grad + right_ref[:, k : k + SLAB]
-            out[:, at] = jnp.where(pre_ref[:, at].astype(F32) > 0, grad, 0.0).astype(BF)
-
-
-def send_body(act, ids, own_ref, oth_ref, both_ref, send_ref, stack_ref, full_ref):
+            delta = jnp.where(pre_ref[:, at].astype(F32) > 0, grad, 0.0).astype(BF)
+            out[:, at] = delta
+            if half == 0 and 1 <= xp <= NXL:
+                mid_out[:, (xp - 1) * SLAB : xp * SLAB] = delta
+
+
+def send_body(ids, own_ref, oth_ref, grad_ref, send_ref, stack_ref, full_ref):
     sy, core = ids[1], ids[2]
-    take(both_ref, 0 if act else 1, full_ref)
-    fill_windows(own_ref, oth_ref, stack_ref, sy, not act, act)
+    take(grad_ref, full_ref)
+    fill_windows(own_ref, oth_ref, stack_ref, sy, False, True)
     other = full_ref[pl.ds(pl.multiple_of((1 - core) * HALF, HALF), HALF), :]
     for i in range(9):
         at = slice(i * 3 * C, (i + 1) * 3 * C)
@@ -165,11 +200,11 @@
     send_ref[ROWS:ROWSP, :] = jnp.zeros((ROWSP - ROWS, HALF), BF)
 
 
-def keep_body(act, ids, own_ref, oth_ref, both_ref, got_ref, keep_ref, *refs):
+def keep_body(ids, own_ref, oth_ref, grad_ref, got_ref, keep_ref, *refs):
     send_refs, (stack_ref, full_ref) = refs[:3], refs[3:]
     sy, core, chip = ids[1], ids[2], ids[3]
-    take(both_ref, 0 if act else 1, full_ref)
-    fill_windows(own_ref, oth_ref, stack_ref, sy, not act, act)
+    take(grad_ref, full_ref)
+    fill_windows(own_ref, oth_ref, stack_ref, sy, False, True)
     stack_ref[ROWS:ROWSP, :] = jnp.zeros((ROWSP - ROWS, NXL * SLAB), BF)
     mine = full_ref[pl.ds(pl.multiple_of(core * HALF, HALF), HALF), :]
     for k in (1, 3, 2, 0):
@@ -185,6 +220,101 @@
                 send_refs[k - 1][to, :] = total.astype(BF)
 
 
+PART = 4
+CHALF = C // 2
+
+
+def whole_body(first, ids, line_ref, in_ref, *refs):
+    if first == 0:
+        out_ref, field_ref, stack_ref, full_ref = refs
+        acc_ref = out_ref
+    else:
+        before_ref, out_ref, field_ref, stack_ref, full_ref, acc_ref = refs
+    core, chip = ids[2], ids[3]
+
+    def where_is(r):
+        chip_r = (chip + 4 - r // 2) % 4
+        core_r = core if r % 2 == 0 else 1 - core
+        return (chip_r % 2) * 2 + core_r, chip_r // 2
+
+    for r in range(8):
+        sx, sy = where_is(r)
+        field_ref[sx * 2 + sy] = line_ref[r]
+    for half in range(PART // 2):
+        for j in range(2):
+            r = half * 2 + j
+            line_windows(field_ref, stack_ref, j * NXL * SLAB, *where_is(first + r))
+            at = slice(j * NXL * SLAB, (j + 1) * NXL * SLAB)
+            for k in range(8):
+                pair = [in_ref[2 * k + i, r].astype(F32) for i in range(2)]
+                full_ref[k * C : (k + 1) * C, at] = jnp.concatenate(pair, axis=0).astype(BF)
+        for i in range(9):
+            at = slice(i * 3 * C, (i + 1) * 3 * C)
+            total = nt(stack_ref[at, :], full_ref[...])
+            if half > 0:
+                total = total + acc_ref[at, :]
+            elif first > 0:
+                total = total + before_ref[at, :]
+            if first > 0 and half == PART // 2 - 1:
+                out_ref[at, :] = (total * (1.0 / 64.0)).astype(BF)
+            else:
+                acc_ref[at, :] = total
+
+
+def whole(ids, first, line, fields, before=None):
+    n = 2 * NXL * SLAB
+    scratch = [
+        pltpu.VMEM((8, C, NXL * SLAB), BF),
+        pltpu.VMEM((ROWS, n), BF),
+        pltpu.VMEM((HALF, n), BF),
+    ]
+    args = (ids, line, fields)
+    out = jax.ShapeDtypeStruct((ROWS, HALF), F32)
+    if before is not None:
+        args += (before,)
+        out = jax.ShapeDtypeStruct((ROWS, HALF), BF)
+        scratch.append(pltpu.VMEM((ROWS, HALF), F32))
+    return call(functools.partial(whole_body, first), out, scratch, len(args) - 1, 7)(*args)
+
+
+def merge_body(ids, mine_ref, other_ref, out_ref, order_ref):
+    @pl.when(pl.program_id(0) == 0)
+    def _():
+        row = lax.broadcasted_iota(jnp.int32, (HALF, CH), 0)
+        col = lax.broadcasted_iota(jnp.int32, (HALF, CH), 1)
+        at = row + CHALF * (row // CHALF)
+        for half in range(2):
+            order_ref[half] = jnp.where(col == at + CHALF * half, 1.0, 0.0).astype(BF)
+
+    core = ids[2]
+    out = jnp.dot(mine_ref[...], order_ref[core], preferred_element_type=F32)
+    out += jnp.dot(other_ref[...], order_ref[1 - core], preferred_element_type=F32)
+    for i in range(3):
+        out_ref[i] = out[i * C : (i + 1) * C, :]
+
+
+def merge(ids, mine, other):
+    spec = pl.BlockSpec((3 * C, HALF), lambda i, ids: (i, 0))
+    return pl.pallas_call(
+        merge_body,
+        out_shape=jax.ShapeDtypeStruct((OFF, C, CH), F32),
+        grid_spec=pltpu.PrefetchScalarGridSpec(
+            num_scalar_prefetch=1,
+            grid=(9,),
+            in_specs=[spec, spec],
+            out_specs=pl.BlockSpec((3, C, CH), lambda i, ids: (i, 0, 0)),
+            scratch_shapes=[pltpu.VMEM((2, HALF, CH), BF)],
+        ),
+        compiler_params=pltpu.CompilerParams(vmem_limit_bytes=16 << 20),
+    )(ids, mine, other)
+
+
+def gather_line(mine, other):
+    pair = jnp.stack([mine, other])
+    got = {k: lax.ppermute(pair, LINE, along(k)) for k in (1, 3, 2)}
+    return jnp.concatenate([pair, got[1], got[2], got[3]], axis=0)
+
+
 def data_body(ids, *refs):
     own_ref, oth_ref, w_ref, out_ref, stack_ref = refs
     fill_windows(own_ref, oth_ref, stack_ref, ids[1], True, False)
@@ -223,7 +353,7 @@
     return [(place(x, c), place((x + shift) % 4, c)) for x in range(4) for c in range(2)]
 
 
-def filter_sums(ids, own, oth, both, act):
+def filter_sums(ids, own, oth, grad):
     n_pos = NXL * SLAB
     field = pltpu.VMEM((CH, n_pos), BF)
     sent = jax.ShapeDtypeStruct((ROWSP, HALF), BF)
@@ -232,12 +362,11 @@
 
     def send():
         scratch = [pltpu.VMEM((ROWS, n_pos), BF), field]
-        return call(functools.partial(send_body, act), sent, scratch, 3)(ids, own, oth, both)
+        return call(send_body, sent, scratch, 3, 2)(ids, own, oth, grad)
 
     def keep(got):
         scratch = [pltpu.VMEM((ROWSP, n_pos), BF), field]
-        body = functools.partial(keep_body, act)
-        return call(body, tuple(outs), scratch, 4)(ids, own, oth, both, got)
+        return call(keep_body, tuple(outs), scratch, 4, 2)(ids, own, oth, grad, got)
 
     return send, keep
 
@@ -301,22 +430,27 @@
     wide_b = jax.ShapeDtypeStruct((C, wide), BF)
     mid_f = jax.ShapeDtypeStruct((C, n_pos), F32)
 
-    both = jnp.concatenate([out_grad.reshape(C, n_pos), inputs.reshape(C, n_pos)], axis=0)
-    both = to_all(both, "ch", 16)
+    grad = to_all(out_grad.reshape(C, n_pos), "ch", 16)
+    field = inputs.reshape(C, n_pos)
+    lower, upper = field[:CHALF], field[CHALF:]
+    other = lax.ppermute(jnp.where(core == 0, upper, lower), LINE, OTHER_CORE)
+    line_in = gather_line(jnp.where(core == 0, lower, upper), other)
+    pre_act, other = lax.optimization_barrier((pre_act, other))
     pre = halo(pre_act.reshape(C, n_pos))
     w_two = weight_two.reshape(ROWS, CH)
-    w_one = weight_one.reshape(ROWS, CH).T
-    both, w_one, pre = lax.optimization_barrier((both, w_one, pre))
+    grad, pre, line_in = lax.optimization_barrier((grad, pre, line_in))
+    fields = [to_all(line_in[i : i + PART], "ch", 16) for i in (0, PART)]
 
     own, over, pack = call(
         act_grad_body,
         (wide_f, wide_f, wide_f),
         [pltpu.VMEM((CH, n_pos), BF), pltpu.VMEM((3, 3 * C, wide), F32)],
         2,
-    )(ids, w_two, both)
+        2,
+    )(ids, w_two, grad)
     pack = lax.ppermute(pack, LINE, to_side(0, True))
 
-    send_two, keep_two = filter_sums(ids, *pre, both, True)
+    send_two, keep_two = filter_sums(ids, *pre, grad)
     send2 = send_two()
     pack, send2 = lax.optimization_barrier((pack, send2))
     got2 = lax.ppermute(send2, LINE, OTHER_CORE)
@@ -325,29 +459,36 @@
     )
     from_left = lax.ppermute(right, LINE, to_side(1, False))
     from_right = lax.ppermute(left, LINE, to_side(-1, False))
+    got2, _ = lax.optimization_barrier((got2, left))
     split2 = keep_two(got2)
-    from_left, from_right, _ = lax.optimization_barrier((from_left, from_right, split2))
-    delta = call(delta_body, (wide_b, wide_b), [], 6)(
+    from_left, from_right, fields[0], _ = lax.optimization_barrier(
+        (from_left, from_right, fields[0], split2)
+    )
+    mid_b = jax.ShapeDtypeStruct((C, n_pos), BF)
+    *delta, middle = call(delta_body, (wide_b, wide_b, mid_b), [], 6)(
         ids, own, oth, from_left, from_right, *pre
     )
-
+    line = gather_line(middle, lax.ppermute(middle, LINE, OTHER_CORE))
     arrive2 = arrive(split2)
-    send_one, keep_one = filter_sums(ids, *delta, both, False)
-    got1 = lax.ppermute(send_one(), LINE, OTHER_CORE)
-    split1 = keep_one(got1)
-    delta, _ = lax.optimization_barrier((delta, split1))
+    weight_one, delta = lax.optimization_barrier((weight_one, delta))
+    w_one = weight_one.reshape(ROWS, CH).T
     terms = call(
         data_body,
         jax.ShapeDtypeStruct((CH, n_pos), BF),
         [pltpu.VMEM((ROWS, n_pos), BF)],
         3,
+        3,
     )(ids, *delta, w_one)
+    part = whole(ids, 0, line, fields[0])
+    part, terms = lax.optimization_barrier((part, terms))
+    block2 = line_sum(arrive2, factor)
+    mine1 = whole(ids, PART, line, fields[1], part)
     got = lax.all_to_all(terms.reshape(16, C, n_pos), "ch", 0, 0, tiled=True)
-    block2 = line_sum(arrive2, factor)
-    block1 = line_sum(arrive(split1), factor, terms)
-    filter_two = write(ids, *line_spread(block2, block1))
+    filter_two = write(ids, *line_spread(block2))
+    other1 = lax.ppermute(mine1, LINE, OTHER_CORE)
+    other1, _, got = lax.optimization_barrier((other1, filter_two, got))
+    filter_one = merge(ids, mine1, other1)
     input_grad = got.astype(F32).sum(axis=0).astype(BF).reshape(shape)
-    filter_one = write(ids, *line_spread(block1, (filter_two, input_grad)))
     return input_grad, filter_one, filter_two
 
 

time: 132 us -> 158 us (1.20)
  Pallas kernels: 19.9 us -> 33.5 us
  starting transfers between devices: 52.5 us -> 61.5 us
  local copies, waits for them, and re-layouts: 9.9 us -> 14.3 us
  waiting for transfers between devices: 46.4 us -> 42.6 us
  other arithmetic: 1.81 us -> 3.76 us
    pallas_call x5 -> x6, Pallas kernels: 8.36 us -> 25.9 us  [the longest x2 11.2 us: whole(): call(functools.partial(whole_body, first), out, scratch, len(args) - 1, 7)]
    ppermute x1 -> x9, waiting for transfers between devices: 0.01 us -> 17.2 us  [the longest x6 16.6 us: gather_line(): got = {k: lax.ppermute(pair, LINE, along(k)) for k in (1, 3, 2)}]
    all_to_all x1 -> x3, starting transfers between devices: 8.6 us -> 19.9 us  [to_all(): return lax.all_to_all(many, axis, 0, 0, tiled=True)]
    ppermute x6 -> x3, waiting for transfers between devices: 8.33 us -> 0.01 us  [line_spread(): got = {k: lax.ppermute(block, LINE, along(k)) for k in (1, 3, 2)}]
    ppermute x6 -> x3, waiting for transfers between devices: 15.5 us -> 7.36 us  [arrive(): lax.ppermute(v, LINE, along(k))]
    ppermute x1 -> x9, starting transfers between devices: 0.09 us -> 5.09 us  [the longest x6 2.77 us: gather_line(): got = {k: lax.ppermute(pair, LINE, along(k)) for k in (1, 3, 2)}]
    ppermute x6 -> x3, starting transfers between devices: 6.5 us -> 1.86 us  [arrive(): lax.ppermute(v, LINE, along(k))]
    unnamed x6 -> x24, local copies, waits for them, and re-layouts: 1.57 us -> 5.57 us
  transfers between devices with their start and end apart: 26 -> 29, of which waited for: 11 -> 11; matrix products, arithmetic and copies ran while one was open for 4% -> 5% of each run, Pallas kernels for 9% -> 15%
where the time goes in v6:
time: 158 us; the launch traced here: 157 us
  starting transfers between devices  61.5 us (39%)
  waiting for transfers between devices  42.6 us (27%)
  Pallas kernels  33.5 us (21%)
  local copies, waits for them, and re-layouts  14.3 us (9%)
  other arithmetic  3.76 us (2%)
    all_to_all x3, starting transfers between devices, to_all(): return lax.all_to_all(many, axis, 0, 0, tiled=True)  19.9 us
    ppermute x6, waiting for transfers between devices, gather_line(): got = {k: lax.ppermute(pair, LINE, along(k)) for k in (1, 3, 2)}  16.6 us
    pallas_call x2, Pallas kernels, whole(): call(functools.partial(whole_body, first), out, scratch, len(args) - 1, 7)  11.2 us
    all_to_all x1, waiting for transfers between devices, shards(): got = lax.all_to_all(terms.reshape(16, C, n_pos), 'ch', 0, 0, tiled=True)  10.4 us
    pallas_call x1, Pallas kernels, merge(): pl.pallas_call(merge_body, out_shape=jax.ShapeDtypeStruct((OFF, C, CH), F...  8.58 us
    ppermute x2, starting transfers between devices, halo(): left = send(last, perm=to_side(1, flip))  7.37 us
    ppermute x3, waiting for transfers between devices, arrive(): lax.ppermute(v, LINE, along(k))  7.36 us
    all_to_all x1, starting transfers between devices, shards(): got = lax.all_to_all(terms.reshape(16, C, n_pos), 'ch', 0, 0, tiled=True)  6.87 us
  transfers between devices with their start and end apart: 29, of which 11 were waited for; matrix products, arithmetic and copies ran while one was open for 5% of the time, Pallas kernels for 15%

profile of v6, /device:TPU:1, one launch (start us, length us, event | category | flops | bytes accessed | tf_op | source)
XLA Modules:
  0.0 156.7 jit_solution(14404023871997729211)
XLA Ops:
  2.7 8.6 %all-to-all-start = ((bf16[16,48,512]{2,1,0:T(8,128)(2,1)}), bf16[16,48,512]{2,1,0:T(8,128)(2,1)S(1)}, u32[]{:S(2)}, u32[]{:S(2)}) async-start(bf16[16,48,512]{2,1,0:T(8,128)(2,1)} %broadcast_in_dim.9), calls=%async_computation | async-start | bytes 1572864 | tf_op jit(solution)/shard_map/all_to_all | solution.py:349
  13.5 2.3 %collective-permute-start.2 = (bf16[48,128]{1,0:T(8,128)(2,1)S(1)}, bf16[48,128]{1,0:T(8,128)(2,1)S(1)}, u32[]{:S(2)}, u32[]{:S(2)}) collective-permute-start(bf16[48,128]{1,0:T(8,128)(2,1)S(1)} %get-tuple-element.72), channel_id=1, source_target_pairs={{2,0},{3,1},{4,2},{5,3},{6,4},{7,5},{10,8},{11,9},{12,10},{13,11},... | collective-permute-start | bytes 36872 | tf_op jit(solution)/shard_map/ppermute | solution.py:342
  15.8 3.9 %collective-permute-start.5 = (bf16[48,128]{1,0:T(8,128)(2,1)S(1)}, bf16[48,128]{1,0:T(8,128)(2,1)S(1)}, u32[]{:S(2)}, u32[]{:S(2)}) collective-permute-start(bf16[48,128]{1,0:T(8,128)(2,1)S(1)} %get-tuple-element.72), channel_id=1, source_target_pairs={{2,1},{3,0},{4,3},{5,2},{6,5},{7,4},{10,9},{11,8},{12,11},{13,10},... | collective-permute-start | bytes 36872 | tf_op jit(solution)/shard_map/ppermute | solution.py:342
  20.5 3.0 %collective-permute-start.1 = (bf16[48,128]{1,0:T(8,128)(2,1)S(1)}, bf16[48,128]{1,0:T(8,128)(2,1)S(1)}, u32[]{:S(2)}, u32[]{:S(2)}) collective-permute-start(bf16[48,128]{1,0:T(8,128)(2,1)S(1)} %get-tuple-element.71), channel_id=1, source_target_pairs={{0,2},{1,3},{2,4},{3,5},{4,6},{5,7},{8,10},{9,11},{10,12},{11,13},... | collective-permute-start | bytes 36872 | tf_op jit(solution)/shard_map/ppermute | solution.py:341
  23.5 4.4 %collective-permute-start.3 = (bf16[48,128]{1,0:T(8,128)(2,1)S(1)}, bf16[48,128]{1,0:T(8,128)(2,1)S(1)}, u32[]{:S(2)}, u32[]{:S(2)}) collective-permute-start(bf16[48,128]{1,0:T(8,128)(2,1)S(1)} %get-tuple-element.71), channel_id=1, source_target_pairs={{0,3},{1,2},{2,5},{3,4},{4,7},{5,6},{8,11},{9,10},{10,13},{11,12},... | collective-permute-start | bytes 36872 | tf_op jit(solution)/shard_map/ppermute | solution.py:341
  28.4 4.3 %collective-permute-done.6 = bf16[2,24,512]{2,1,0:T(8,128)(2,1)S(1)} collective-permute-done((bf16[2,24,512]{2,1,0:T(8,128)(2,1)S(1)}, bf16[2,24,512]{2,1,0:T(8,128)(2,1)S(1)}, u32[]{:S(2)}, u32[]{:S(2)}) %collective-permute-start.6) | collective-permute-done | bytes 49184 | tf_op jit(solution)/shard_map/ppermute | solution.py:314
  32.8 2.9 %collective-permute-done.8 = bf16[2,24,512]{2,1,0:T(8,128)(2,1)S(1)} collective-permute-done((bf16[2,24,512]{2,1,0:T(8,128)(2,1)S(1)}, bf16[2,24,512]{2,1,0:T(8,128)(2,1)S(1)}, u32[]{:S(2)}, u32[]{:S(2)}) %collective-permute-start.8) | collective-permute-done | bytes 49184 | tf_op jit(solution)/shard_map/ppermute | solution.py:314
  37.3 1.9 %shard_map.76 = (f32[48,768]{1,0:T(8,128)S(1)}, f32[48,768]{1,0:T(8,128)S(1)}, f32[48,768]{1,0:T(8,128)S(1)}) custom-call(s32[4]{0:T(128)S(1)} %pad_add_fusion.ids, bf16[1296,768]{1,0:T(8,128)(2,1)S(1)} %bitcast.21, bf16[16,48,512]{2,1,0:T(8,128)(2,1)S(1)} %all-to-all-done.grad_ref), custom_call_target="tpu_custom_call" | custom-call | flops 2000000000 | bytes 6000000 | tf_op jit(solution)/shard_map/pallas_call | solution.py:444
  39.3 2.9 %shard_map.77 = bf16[1344,384]{1,0:T(8,128)(2,1)} custom-call(s32[4]{0:T(128)S(1)} %pad_add_fusion.ids, bf16[48,768]{1,0:T(8,128)(2,1)S(1)} %pad_maximum_fusion.2.own_ref.pre_own_ref, bf16[48,768]{1,0:T(8,128)(2,1)S(1)} %pad_maximum_fusion.3.oth_ref.pre_oth_ref, bf16[16,48,512]{2,1,0:T(8,128)(2,1)S(1)} %all-to-all-done.grad_ref), custom_call_target="tpu_custom_call" | custom-call | flops 2000000000 | bytes 6000000 | tf_op jit(solution)/shard_map/pallas_call | solution.py:365
  42.2 2.6 %collective-permute-done.9.pack_ref = f32[48,768]{1,0:T(8,128)S(1)} collective-permute-done((f32[48,768]{1,0:T(8,128)S(1)}, f32[48,768]{1,0:T(8,128)S(1)}, u32[]{:S(2)}, u32[]{:S(2)}) %collective-permute-start.9) | collective-permute-done | bytes 147488 | tf_op jit(solution)/shard_map/ppermute | solution.py:451
  44.8 4.1 %collective-permute-start.12 = (bf16[1344,384]{1,0:T(8,128)(2,1)}, bf16[1344,384]{1,0:T(8,128)(2,1)}, u32[]{:S(2)}, u32[]{:S(2)}) collective-permute-start(bf16[1344,384]{1,0:T(8,128)(2,1)} %shard_map.77), channel_id=1, source_target_pairs={{0,2},{2,0},{4,6},{6,4},{1,3},{3,1},{5,7},{7,5},{8,10},{10,8},{12,... | collective-permute-start | bytes 3096584 | tf_op jit(solution)/shard_map/ppermute | solution.py:456
  50.2 6.9 %all-to-all-start.1 = ((bf16[16,4,24,512]{3,2,1,0:T(8,128)(2,1)}), bf16[16,4,24,512]{3,2,1,0:T(8,128)(2,1)S(1)}, u32[]{:S(2)}, u32[]{:S(2)}) async-start(bf16[16,4,24,512]{3,2,1,0:T(8,128)(2,1)} %broadcast_in_dim.10), calls=%async_computation.1 | async-start | bytes 3145728 | tf_op jit(solution)/shard_map/all_to_all | solution.py:349
  57.7 2.6 %shard_map.79 = (f32[336,384]{1,0:T(8,128)S(1)}, bf16[336,384]{1,0:T(8,128)(2,1)S(1)}, bf16[336,384]{1,0:T(8,128)(2,1)S(1)}, bf16[336,384]{1,0:T(8,128)(2,1)S(1)}) custom-call(s32[4]{0:T(128)S(1)} %pad_add_fusion.ids, bf16[48,768]{1,0:T(8,128)(2,1)S(1)} %pad_maximum_fusion.2.own_ref.pre_own_ref, bf16[48,768]{1,0:T(8,128)(2,1)S(1)} %pad_maximum_fusion.3.oth_ref.pre_oth_ref, ...), custom_call_target="tpu_custom_call" | custom-call | flops 2000000000 | bytes 6000000 | tf_op jit(solution)/shard_map/pallas_call | solution.py:369
  60.4 1.8 %collective-permute-start.19 = (bf16[336,384]{1,0:T(8,128)(2,1)S(1)}, bf16[336,384]{1,0:T(8,128)(2,1)S(1)}, u32[]{:S(2)}, u32[]{:S(2)}) collective-permute-start(bf16[336,384]{1,0:T(8,128)(2,1)S(1)} %get-tuple-element.53), channel_id=1, source_target_pairs={{0,5},{2,7},{4,0},{6,2},{1,4},{3,6},{5,1},{7,3},{8,13},{10,15},{12... | collective-permute-start | bytes 774152 | tf_op jit(solution)/shard_map/ppermute | solution.py:376
  62.2 2.7 %collective-permute-start.11 = (f32[48,512]{1,0:T(8,128)S(1)}, f32[48,512]{1,0:T(8,128)S(1)}, u32[]{:S(2)}, u32[]{:S(2)}) collective-permute-start(f32[48,512]{1,0:T(8,128)S(1)} %get-tuple-element.46), channel_id=1, source_target_pairs={{2,0},{3,1},{4,2},{5,3},{6,4},{7,5},{10,8},{11,9},{12,10},{13,11},... | collective-permute-start | bytes 294920 | tf_op jit(solution)/shard_map/ppermute | solution.py:461
  65.0 3.3 %collective-permute-start.10 = (f32[48,512]{1,0:T(8,128)S(1)}, f32[48,512]{1,0:T(8,128)S(1)}, u32[]{:S(2)}, u32[]{:S(2)}) collective-permute-start(f32[48,512]{1,0:T(8,128)S(1)} %get-tuple-element.45), channel_id=1, source_target_pairs={{0,2},{1,3},{2,4},{3,5},{4,6},{5,7},{8,10},{9,11},{10,12},{11,13},... | collective-permute-start | bytes 294920 | tf_op jit(solution)/shard_map/ppermute | solution.py:460
  69.5 4.1 %collective-permute-done.19 = bf16[336,384]{1,0:T(8,128)(2,1)S(1)} collective-permute-done((bf16[336,384]{1,0:T(8,128)(2,1)S(1)}, bf16[336,384]{1,0:T(8,128)(2,1)S(1)}, u32[]{:S(2)}, u32[]{:S(2)}) %collective-permute-start.19) | collective-permute-done | bytes 258080 | tf_op jit(solution)/shard_map/ppermute | solution.py:376
  73.6 2.0 %collective-permute-done.18 = bf16[336,384]{1,0:T(8,128)(2,1)S(1)} collective-permute-done((bf16[336,384]{1,0:T(8,128)(2,1)S(1)}, bf16[336,384]{1,0:T(8,128)(2,1)S(1)}, u32[]{:S(2)}, u32[]{:S(2)}) %collective-permute-start.18) | collective-permute-done | bytes 258080 | tf_op jit(solution)/shard_map/ppermute | solution.py:376
  78.0 4.9 %all-to-all-done.1.in_ref = bf16[16,4,24,512]{3,2,1,0:T(8,128)(2,1)S(1)} async-done(((bf16[16,4,24,512]{3,2,1,0:T(8,128)(2,1)}), bf16[16,4,24,512]{3,2,1,0:T(8,128)(2,1)S(1)}, u32[]{:S(2)}, u32[]{:S(2)}) %all-to-all-start.1) | async-done | bytes 1572896 | tf_op jit(solution)/shard_map/all_to_all | solution.py:349
  84.5 4.4 %all-to-all-start.2 = ((bf16[16,4,24,512]{3,2,1,0:T(8,128)(2,1)}), bf16[16,4,24,512]{3,2,1,0:T(8,128)(2,1)}, u32[]{:S(2)}, u32[]{:S(2)}) async-start(bf16[16,4,24,512]{3,2,1,0:T(8,128)(2,1)} %broadcast_in_dim.22), calls=%async_computation.2 | async-start | bytes 3145728 | tf_op jit(solution)/shard_map/all_to_all | solution.py:349
  90.7 2.9 %copy.9 = bf16[1296,768]{0,1:T(8,128)(2,1)S(1)} copy(bf16[1296,768]{1,0:T(8,128)(2,1)} %bitcast.22) | data formatting | bytes 3981312 | tf_op jit(solution)/shard_map/reshape | solution.py:474
  93.6 2.1 %shard_map.82 = bf16[768,512]{1,0:T(8,128)(2,1)S(1)} custom-call(s32[4]{0:T(128)S(1)} %pad_add_fusion.ids, bf16[48,768]{1,0:T(8,128)(2,1)S(1)} %get-tuple-element.60.refs_0_, bf16[48,768]{1,0:T(8,128)(2,1)S(1)} %get-tuple-element.61.refs_1_, bf16[768,1296]{1,0:T(8,128)(2,1)S(1)} %bitcast.17), custom_call_target="tpu_custom_call" | custom-call | flops 3000000000 | bytes 9000000 | tf_op jit(solution)/shard_map/pallas_call | solution.py:475
  97.4 1.7 %collective-permute-start.15 = (bf16[2,48,512]{2,1,0:T(8,128)(2,1)S(1)}, bf16[2,48,512]{2,1,0:T(8,128)(2,1)S(1)}, u32[]{:S(2)}, u32[]{:S(2)}) collective-permute-start(bf16[2,48,512]{2,1,0:T(8,128)(2,1)S(1)} %pad_maximum_fusion.1), channel_id=1, source_target_pairs={{0,1},{2,3},{4,5},{6,7},{1,0},{3,2},{5,4},{7,6},{8,9},{10,11},{12,... | collective-permute-start | bytes 294920 | tf_op jit(solution)/shard_map/ppermute | solution.py:314
  99.1 5.7 %collective-permute-done.14 = bf16[2,48,512]{2,1,0:T(8,128)(2,1)S(1)} collective-permute-done((bf16[2,48,512]{2,1,0:T(8,128)(2,1)S(1)}, bf16[2,48,512]{2,1,0:T(8,128)(2,1)S(1)}, u32[]{:S(2)}, u32[]{:S(2)}) %collective-permute-start.14) | collective-permute-done | bytes 98336 | tf_op jit(solution)/shard_map/ppermute | solution.py:314
  104.8 3.7 %collective-permute-done.16 = bf16[2,48,512]{2,1,0:T(8,128)(2,1)S(1)} collective-permute-done((bf16[2,48,512]{2,1,0:T(8,128)(2,1)S(1)}, bf16[2,48,512]{2,1,0:T(8,128)(2,1)S(1)}, u32[]{:S(2)}, u32[]{:S(2)}) %collective-permute-start.16) | collective-permute-done | bytes 98336 | tf_op jit(solution)/shard_map/ppermute | solution.py:314
  108.5 5.2 %shard_map.81.refs_0_ = f32[1296,384]{1,0:T(8,128)S(1)} custom-call(s32[4]{0:T(128)S(1)} %pad_add_fusion.ids, bf16[8,48,512]{2,1,0:T(8,128)(2,1)S(1)} %constant_dynamic-update-slice_fusion.5.line_ref, bf16[16,4,24,512]{3,2,1,0:T(8,128)(2,1)S(1)} %copy-done.1), custom_call_target="tpu_custom_call" | custom-call | flops 7000000000 | bytes 21000000 | tf_op jit(solution)/shard_map/pallas_call | solution.py:277
  116.4 1.7 %collective-permute-start.24 = (bf16[1344,384]{1,0:T(8,128)(2,1)S(1)}, bf16[1344,384]{1,0:T(8,128)(2,1)S(1)}, u32[]{:S(2)}, u32[]{:S(2)}) collective-permute-start(bf16[1344,384]{1,0:T(8,128)(2,1)S(1)} %pad_maximum_fusion), channel_id=1, source_target_pairs={{0,2},{2,0},{4,6},{6,4},{1,3},{3,1},{5,7},{7,5},{8,10},{10,8},{12,... | collective-permute-start | bytes 3096584 | tf_op jit(solution)/shard_map/ppermute | solution.py:393
  119.7 6.0 %shard_map.83.mine_ref = bf16[1296,384]{1,0:T(8,128)(2,1)S(1)} custom-call(s32[4]{0:T(128)S(1)} %pad_add_fusion.ids, bf16[8,48,512]{2,1,0:T(8,128)(2,1)S(1)} %constant_dynamic-update-slice_fusion.5.line_ref, bf16[16,4,24,512]{3,2,1,0:T(8,128)(2,1)} %all-to-all-done.2.in_ref, f32[1296,384]{1,0:T(8,128)S(1)} %copy-done.5), custom_call_target="tpu_custom_call" | custom-call | flops 7000000000 | bytes 21000000 | tf_op jit(solution)/shard_map/pallas_call | solution.py:277
  125.8 6.9 %all-to-all-start.3 = ((bf16[16,48,512]{2,1,0:T(8,128)(2,1)}), bf16[16,48,512]{2,1,0:T(8,128)(2,1)}, u32[]{:S(2)}, u32[]{:S(2)}) async-start(bf16[16,48,512]{2,1,0:T(8,128)(2,1)} %bitcast.19), calls=%async_computation.3 | async-start | bytes 1572864 | tf_op jit(solution)/shard_map/all_to_all | solution.py:486
  132.7 3.0 %shard_map.84 = f32[27,48,768]{2,1,0:T(8,128)} custom-call(s32[4]{0:T(128)S(1)} %pad_add_fusion.ids, bf16[4,7,48,384]{3,2,1,0:T(8,128)(2,1)S(1)} %bitcast.16, bf16[4,7,48,384]{3,2,1,0:T(8,128)(2,1)S(1)} %bitcast.18), custom_call_target="tpu_custom_call" | custom-call | tf_op jit(solution)/shard_map/pallas_call | solution.py:407
  135.7 10.4 %all-to-all-done.3 = bf16[16,48,512]{2,1,0:T(8,128)(2,1)} async-done(((bf16[16,48,512]{2,1,0:T(8,128)(2,1)}), bf16[16,48,512]{2,1,0:T(8,128)(2,1)}, u32[]{:S(2)}, u32[]{:S(2)}) %all-to-all-start.3) | async-done | bytes 786464 | tf_op jit(solution)/shard_map/all_to_all | solution.py:486
  148.1 8.6 %shard_map.85 = f32[27,48,768]{2,1,0:T(8,128)} custom-call(s32[4]{0:T(128)S(1)} %pad_add_fusion.ids, bf16[1296,384]{1,0:T(8,128)(2,1)S(1)} %shard_map.83.mine_ref, bf16[1296,384]{1,0:T(8,128)(2,1)} %collective-permute-done.17.other_ref), custom_call_target="tpu_custom_call" | custom-call | tf_op jit(solution)/shard_map/pallas_call | solution.py:298
  (82 shorter events, 24.2 us)
Async XLA Ops:
  0.6 10.7 %copy-start.6 = (bf16[48,4,2,64]{3,2,1,0:T(2,128)(2,1)S(1)}, bf16[48,4,2,64]{3,2,1,0:T(2,128)(2,1)}, u32[]{:S(2)}) copy-start(bf16[48,4,2,64]{3,2,1,0:T(2,128)(2,1)} %param.5) | copy-start | bytes 147460
  0.6 12.7 %copy-start.7 = (bf16[48,4,2,64]{3,2,1,0:T(2,128)(2,1)S(1)}, bf16[48,4,2,64]{3,2,1,0:T(2,128)(2,1)}, u32[]{:S(2)}) copy-start(bf16[48,4,2,64]{3,2,1,0:T(2,128)(2,1)} %param.6) | copy-start | bytes 147460
  2.7 33.0 %all-to-all-start = ((bf16[16,48,512]{2,1,0:T(8,128)(2,1)}), bf16[16,48,512]{2,1,0:T(8,128)(2,1)S(1)}, u32[]{:S(2)}, u32[]{:S(2)}) async-start(bf16[16,48,512]{2,1,0:T(8,128)(2,1)} %broadcast_in_dim.9), calls=%async_computation | async-start | bytes 1572864 | tf_op jit(solution)/shard_map/all_to_all | solution.py:349
  11.5 1.9 %collective-permute-start = (bf16[24,512]{1,0:T(8,128)(2,1)S(1)}, bf16[24,512]{1,0:T(8,128)(2,1)S(1)}, u32[]{:S(2)}, u32[]{:S(2)}) collective-permute-start(bf16[24,512]{1,0:T(8,128)(2,1)S(1)} %select_n.40), channel_id=1, source_target_pairs={{0,2},{2,0},{4,6},{6,4},{1,3},{3,1},{5,7},{7,5},{8,10},{10,8},{12,... | collective-permute-start | bytes 73736 | tf_op jit(solution)/shard_map/ppermute | solution.py:436
  13.5 14.4 %collective-permute-start.2 = (bf16[48,128]{1,0:T(8,128)(2,1)S(1)}, bf16[48,128]{1,0:T(8,128)(2,1)S(1)}, u32[]{:S(2)}, u32[]{:S(2)}) collective-permute-start(bf16[48,128]{1,0:T(8,128)(2,1)S(1)} %get-tuple-element.72), channel_id=1, source_target_pairs={{2,0},{3,1},{4,2},{5,3},{6,4},{7,5},{10,8},{11,9},{12,10},{13,11},... | collective-permute-start | bytes 36872 | tf_op jit(solution)/shard_map/ppermute | solution.py:342
  15.8 19.9 %collective-permute-start.5 = (bf16[48,128]{1,0:T(8,128)(2,1)S(1)}, bf16[48,128]{1,0:T(8,128)(2,1)S(1)}, u32[]{:S(2)}, u32[]{:S(2)}) collective-permute-start(bf16[48,128]{1,0:T(8,128)(2,1)S(1)} %get-tuple-element.72), channel_id=1, source_target_pairs={{2,1},{3,0},{4,3},{5,2},{6,5},{7,4},{10,9},{11,8},{12,11},{13,10},... | collective-permute-start | bytes 36872 | tf_op jit(solution)/shard_map/ppermute | solution.py:342
  19.7 16.0 %collective-permute-start.4 = (bf16[48,512]{1,0:T(8,128)(2,1)S(1)}, bf16[48,512]{1,0:T(8,128)(2,1)S(1)}, u32[]{:S(2)}, u32[]{:S(2)}) collective-permute-start(bf16[48,512]{1,0:T(8,128)(2,1)S(1)} %reshape.55), channel_id=1, source_target_pairs={{0,1},{1,0},{2,3},{3,2},{4,5},{5,4},{6,7},{7,6},{8,9},{9,8},{10,11... | collective-permute-start | bytes 147464 | tf_op jit(solution)/shard_map/ppermute | solution.py:340
  20.5 7.5 %collective-permute-start.1 = (bf16[48,128]{1,0:T(8,128)(2,1)S(1)}, bf16[48,128]{1,0:T(8,128)(2,1)S(1)}, u32[]{:S(2)}, u32[]{:S(2)}) collective-permute-start(bf16[48,128]{1,0:T(8,128)(2,1)S(1)} %get-tuple-element.71), channel_id=1, source_target_pairs={{0,2},{1,3},{2,4},{3,5},{4,6},{5,7},{8,10},{9,11},{10,12},{11,13},... | collective-permute-start | bytes 36872 | tf_op jit(solution)/shard_map/ppermute | solution.py:341
  23.5 12.1 %collective-permute-start.3 = (bf16[48,128]{1,0:T(8,128)(2,1)S(1)}, bf16[48,128]{1,0:T(8,128)(2,1)S(1)}, u32[]{:S(2)}, u32[]{:S(2)}) collective-permute-start(bf16[48,128]{1,0:T(8,128)(2,1)S(1)} %get-tuple-element.71), channel_id=1, source_target_pairs={{0,3},{1,2},{2,5},{3,4},{4,7},{5,6},{8,11},{9,10},{10,13},{11,12},... | collective-permute-start | bytes 36872 | tf_op jit(solution)/shard_map/ppermute | solution.py:341
  28.0 4.7 %collective-permute-start.6 = (bf16[2,24,512]{2,1,0:T(8,128)(2,1)S(1)}, bf16[2,24,512]{2,1,0:T(8,128)(2,1)S(1)}, u32[]{:S(2)}, u32[]{:S(2)}) collective-permute-start(bf16[2,24,512]{2,1,0:T(8,128)(2,1)S(1)} %pad_maximum_fusion.4), channel_id=1, source_target_pairs={{0,4},{2,6},{4,1},{6,3},{1,5},{3,7},{5,0},{7,2},{8,12},{10,14},{12... | collective-permute-start | bytes 147464 | tf_op jit(solution)/shard_map/ppermute | solution.py:314
  28.1 4.7 %collective-permute-start.7 = (bf16[2,24,512]{2,1,0:T(8,128)(2,1)S(1)}, bf16[2,24,512]{2,1,0:T(8,128)(2,1)S(1)}, u32[]{:S(2)}, u32[]{:S(2)}) collective-permute-start(bf16[2,24,512]{2,1,0:T(8,128)(2,1)S(1)} %pad_maximum_fusion.4), channel_id=1, source_target_pairs={{0,1},{2,3},{4,5},{6,7},{1,0},{3,2},{5,4},{7,6},{8,9},{10,11},{12,... | collective-permute-start | bytes 147464 | tf_op jit(solution)/shard_map/ppermute | solution.py:314
  32.7 2.9 %collective-permute-start.8 = (bf16[2,24,512]{2,1,0:T(8,128)(2,1)S(1)}, bf16[2,24,512]{2,1,0:T(8,128)(2,1)S(1)}, u32[]{:S(2)}, u32[]{:S(2)}) collective-permute-start(bf16[2,24,512]{2,1,0:T(8,128)(2,1)S(1)} %pad_maximum_fusion.4), channel_id=1, source_target_pairs={{0,5},{2,7},{4,0},{6,2},{1,4},{3,6},{5,1},{7,3},{8,13},{10,15},{12... | collective-permute-start | bytes 147464 | tf_op jit(solution)/shard_map/ppermute | solution.py:314
  39.2 5.6 %collective-permute-start.9 = (f32[48,768]{1,0:T(8,128)S(1)}, f32[48,768]{1,0:T(8,128)S(1)}, u32[]{:S(2)}, u32[]{:S(2)}) collective-permute-start(f32[48,768]{1,0:T(8,128)S(1)} %get-tuple-element.39), channel_id=1, source_target_pairs={{0,1},{1,0},{2,3},{3,2},{4,5},{5,4},{6,7},{7,6},{8,9},{9,8},{10,11... | collective-permute-start | bytes 442376 | tf_op jit(solution)/shard_map/ppermute | solution.py:451
  44.8 12.9 %collective-permute-start.12 = (bf16[1344,384]{1,0:T(8,128)(2,1)}, bf16[1344,384]{1,0:T(8,128)(2,1)}, u32[]{:S(2)}, u32[]{:S(2)}) collective-permute-start(bf16[1344,384]{1,0:T(8,128)(2,1)} %shard_map.77), channel_id=1, source_target_pairs={{0,2},{2,0},{4,6},{6,4},{1,3},{3,1},{5,7},{7,5},{8,10},{10,8},{12,... | collective-permute-start | bytes 3096584 | tf_op jit(solution)/shard_map/ppermute | solution.py:456
  50.2 32.7 %all-to-all-start.1 = ((bf16[16,4,24,512]{3,2,1,0:T(8,128)(2,1)}), bf16[16,4,24,512]{3,2,1,0:T(8,128)(2,1)S(1)}, u32[]{:S(2)}, u32[]{:S(2)}) async-start(bf16[16,4,24,512]{3,2,1,0:T(8,128)(2,1)} %broadcast_in_dim.10), calls=%async_computation.1 | async-start | bytes 3145728 | tf_op jit(solution)/shard_map/all_to_all | solution.py:349
  60.4 9.2 %collective-permute-start.20 = (bf16[336,384]{1,0:T(8,128)(2,1)S(1)}, bf16[336,384]{1,0:T(8,128)(2,1)S(1)}, u32[]{:S(2)}, u32[]{:S(2)}) collective-permute-start(bf16[336,384]{1,0:T(8,128)(2,1)S(1)} %get-tuple-element.52), channel_id=1, source_target_pairs={{0,1},{2,3},{4,5},{6,7},{1,0},{3,2},{5,4},{7,6},{8,9},{10,11},{12,... | collective-permute-start | bytes 774152 | tf_op jit(solution)/shard_map/ppermute | solution.py:376
  60.4 13.1 %collective-permute-start.19 = (bf16[336,384]{1,0:T(8,128)(2,1)S(1)}, bf16[336,384]{1,0:T(8,128)(2,1)S(1)}, u32[]{:S(2)}, u32[]{:S(2)}) collective-permute-start(bf16[336,384]{1,0:T(8,128)(2,1)S(1)} %get-tuple-element.53), channel_id=1, source_target_pairs={{0,5},{2,7},{4,0},{6,2},{1,4},{3,6},{5,1},{7,3},{8,13},{10,15},{12... | collective-permute-start | bytes 774152 | tf_op jit(solution)/shard_map/ppermute | solution.py:376
  62.2 13.4 %collective-permute-start.18 = (bf16[336,384]{1,0:T(8,128)(2,1)S(1)}, bf16[336,384]{1,0:T(8,128)(2,1)S(1)}, u32[]{:S(2)}, u32[]{:S(2)}) collective-permute-start(bf16[336,384]{1,0:T(8,128)(2,1)S(1)} %get-tuple-element.51), channel_id=1, source_target_pairs={{0,4},{2,6},{4,1},{6,3},{1,5},{3,7},{5,0},{7,2},{8,12},{10,14},{12... | collective-permute-start | bytes 774152 | tf_op jit(solution)/shard_map/ppermute | solution.py:376
  62.2 26.7 %collective-permute-start.11 = (f32[48,512]{1,0:T(8,128)S(1)}, f32[48,512]{1,0:T(8,128)S(1)}, u32[]{:S(2)}, u32[]{:S(2)}) collective-permute-start(f32[48,512]{1,0:T(8,128)S(1)} %get-tuple-element.46), channel_id=1, source_target_pairs={{2,0},{3,1},{4,2},{5,3},{6,4},{7,5},{10,8},{11,9},{12,10},{13,11},... | collective-permute-start | bytes 294920 | tf_op jit(solution)/shard_map/ppermute | solution.py:461
  65.0 24.0 %collective-permute-start.10 = (f32[48,512]{1,0:T(8,128)S(1)}, f32[48,512]{1,0:T(8,128)S(1)}, u32[]{:S(2)}, u32[]{:S(2)}) collective-permute-start(f32[48,512]{1,0:T(8,128)S(1)} %get-tuple-element.45), channel_id=1, source_target_pairs={{0,2},{1,3},{2,4},{3,5},{4,6},{5,7},{8,10},{9,11},{10,12},{11,13},... | collective-permute-start | bytes 294920 | tf_op jit(solution)/shard_map/ppermute | solution.py:460
  76.5 38.5 %collective-permute-start.23 = (bf16[336,384]{1,0:T(8,128)(2,1)}, bf16[336,384]{1,0:T(8,128)(2,1)}, u32[]{:S(2)}, u32[]{:S(2)}) collective-permute-start(bf16[336,384]{1,0:T(8,128)(2,1)} %multiply_convert_fusion), channel_id=1, source_target_pairs={{0,5},{2,7},{4,0},{6,2},{1,4},{3,6},{5,1},{7,3},{8,13},{10,15},{12... | collective-permute-start | bytes 774152 | tf_op jit(solution)/shard_map/ppermute | solution.py:389
  77.4 37.6 %collective-permute-start.22 = (bf16[336,384]{1,0:T(8,128)(2,1)}, bf16[336,384]{1,0:T(8,128)(2,1)}, u32[]{:S(2)}, u32[]{:S(2)}) collective-permute-start(bf16[336,384]{1,0:T(8,128)(2,1)} %multiply_convert_fusion), channel_id=1, source_target_pairs={{0,1},{2,3},{4,5},{6,7},{1,0},{3,2},{5,4},{7,6},{8,9},{10,11},{12,... | collective-permute-start | bytes 774152 | tf_op jit(solution)/shard_map/ppermute | solution.py:389
  77.7 37.3 %collective-permute-start.21 = (bf16[336,384]{1,0:T(8,128)(2,1)}, bf16[336,384]{1,0:T(8,128)(2,1)}, u32[]{:S(2)}, u32[]{:S(2)}) collective-permute-start(bf16[336,384]{1,0:T(8,128)(2,1)} %multiply_convert_fusion), channel_id=1, source_target_pairs={{0,4},{2,6},{4,1},{6,3},{1,5},{3,7},{5,0},{7,2},{8,12},{10,14},{12... | collective-permute-start | bytes 774152 | tf_op jit(solution)/shard_map/ppermute | solution.py:389
  84.5 33.6 %all-to-all-start.2 = ((bf16[16,4,24,512]{3,2,1,0:T(8,128)(2,1)}), bf16[16,4,24,512]{3,2,1,0:T(8,128)(2,1)}, u32[]{:S(2)}, u32[]{:S(2)}) async-start(bf16[16,4,24,512]{3,2,1,0:T(8,128)(2,1)} %broadcast_in_dim.22), calls=%async_computation.2 | async-start | bytes 3145728 | tf_op jit(solution)/shard_map/all_to_all | solution.py:349
  89.6 7.1 %collective-permute-start.13 = (bf16[48,512]{1,0:T(8,128)(2,1)S(1)}, bf16[48,512]{1,0:T(8,128)(2,1)S(1)}, u32[]{:S(2)}, u32[]{:S(2)}) collective-permute-start(bf16[48,512]{1,0:T(8,128)(2,1)S(1)} %get-tuple-element.56), channel_id=1, source_target_pairs={{0,2},{2,0},{4,6},{6,4},{1,3},{3,1},{5,7},{7,5},{8,10},{10,8},{12,... | collective-permute-start | bytes 147464 | tf_op jit(solution)/shard_map/ppermute | solution.py:471
  93.6 14.9 %copy-start.1 = (bf16[16,4,24,512]{3,2,1,0:T(8,128)(2,1)S(1)}, bf16[16,4,24,512]{3,2,1,0:T(8,128)(2,1)}, u32[]{:S(2)}) copy-start(bf16[16,4,24,512]{3,2,1,0:T(8,128)(2,1)} %copy-done) | copy-start | bytes 4718596
  96.7 8.1 %collective-permute-start.14 = (bf16[2,48,512]{2,1,0:T(8,128)(2,1)S(1)}, bf16[2,48,512]{2,1,0:T(8,128)(2,1)S(1)}, u32[]{:S(2)}, u32[]{:S(2)}) collective-permute-start(bf16[2,48,512]{2,1,0:T(8,128)(2,1)S(1)} %pad_maximum_fusion.1), channel_id=1, source_target_pairs={{0,4},{2,6},{4,1},{6,3},{1,5},{3,7},{5,0},{7,2},{8,12},{10,14},{12... | collective-permute-start | bytes 294920 | tf_op jit(solution)/shard_map/ppermute | solution.py:314
  97.4 7.4 %collective-permute-start.15 = (bf16[2,48,512]{2,1,0:T(8,128)(2,1)S(1)}, bf16[2,48,512]{2,1,0:T(8,128)(2,1)S(1)}, u32[]{:S(2)}, u32[]{:S(2)}) collective-permute-start(bf16[2,48,512]{2,1,0:T(8,128)(2,1)S(1)} %pad_maximum_fusion.1), channel_id=1, source_target_pairs={{0,1},{2,3},{4,5},{6,7},{1,0},{3,2},{5,4},{7,6},{8,9},{10,11},{12,... | collective-permute-start | bytes 294920 | tf_op jit(solution)/shard_map/ppermute | solution.py:314
  104.8 3.7 %collective-permute-start.16 = (bf16[2,48,512]{2,1,0:T(8,128)(2,1)S(1)}, bf16[2,48,512]{2,1,0:T(8,128)(2,1)S(1)}, u32[]{:S(2)}, u32[]{:S(2)}) collective-permute-start(bf16[2,48,512]{2,1,0:T(8,128)(2,1)S(1)} %pad_maximum_fusion.1), channel_id=1, source_target_pairs={{0,5},{2,7},{4,0},{6,2},{1,4},{3,6},{5,1},{7,3},{8,13},{10,15},{12... | collective-permute-start | bytes 294920 | tf_op jit(solution)/shard_map/ppermute | solution.py:314
  116.4 16.2 %collective-permute-start.24 = (bf16[1344,384]{1,0:T(8,128)(2,1)S(1)}, bf16[1344,384]{1,0:T(8,128)(2,1)S(1)}, u32[]{:S(2)}, u32[]{:S(2)}) collective-permute-start(bf16[1344,384]{1,0:T(8,128)(2,1)S(1)} %pad_maximum_fusion), channel_id=1, source_target_pairs={{0,2},{2,0},{4,6},{6,4},{1,3},{3,1},{5,7},{7,5},{8,10},{10,8},{12,... | collective-permute-start | bytes 3096584 | tf_op jit(solution)/shard_map/ppermute | solution.py:393
  125.7 20.4 %collective-permute-start.17 = (bf16[1296,384]{1,0:T(8,128)(2,1)S(1)}, bf16[1296,384]{1,0:T(8,128)(2,1)}, u32[]{:S(2)}, u32[]{:S(2)}) collective-permute-start(bf16[1296,384]{1,0:T(8,128)(2,1)S(1)} %shard_map.83.mine_ref), channel_id=1, source_target_pairs={{0,2},{2,0},{4,6},{6,4},{1,3},{3,1},{5,7},{7,5},{8,10},{10,8},{12,... | collective-permute-start | bytes 2985992 | tf_op jit(solution)/shard_map/ppermute | solution.py:488
  125.8 20.3 %all-to-all-start.3 = ((bf16[16,48,512]{2,1,0:T(8,128)(2,1)}), bf16[16,48,512]{2,1,0:T(8,128)(2,1)}, u32[]{:S(2)}, u32[]{:S(2)}) async-start(bf16[16,48,512]{2,1,0:T(8,128)(2,1)} %bitcast.19), calls=%async_computation.3 | async-start | bytes 1572864 | tf_op jit(solution)/shard_map/all_to_all | solution.py:486
  (5 other events, 6.9 us)

commit v7 on v5

--- a/solution.py
+++ b/solution.py
@@ -256,11 +256,13 @@
     return (total * factor).astype(BF)
 
 
-def line_spread(block, after=None):
-    got = {k: lax.ppermute(block, LINE, along(k)) for k in (1, 3, 2)}
-    if after is not None:
-        got, _ = lax.optimization_barrier((got, after))
-    mine = jnp.concatenate([block, got[1], got[2], got[3]], axis=0)
+def line_send(block):
+    return [block] + [lax.ppermute(block, LINE, along(k)) for k in (1, 3, 2)]
+
+
+def line_join(parts, after):
+    (own, one, three, two), _ = lax.optimization_barrier((parts, after))
+    mine = jnp.concatenate([own, one, two, three], axis=0)
     return mine, lax.ppermute(mine, LINE, OTHER_CORE)
 
 
@@ -335,7 +337,9 @@
     send_one, keep_one = filter_sums(ids, *delta, both, False)
     got1 = lax.ppermute(send_one(), LINE, OTHER_CORE)
     split1 = keep_one(got1)
-    delta, _ = lax.optimization_barrier((delta, split1))
+    arrive2, _ = lax.optimization_barrier((arrive2, split1))
+    block2 = line_sum(arrive2, factor)
+    delta, _ = lax.optimization_barrier((delta, block2))
     terms = call(
         data_body,
         jax.ShapeDtypeStruct((CH, n_pos), BF),
@@ -343,11 +347,11 @@
         3,
     )(ids, *delta, w_one)
     got = lax.all_to_all(terms.reshape(16, C, n_pos), "ch", 0, 0, tiled=True)
-    block2 = line_sum(arrive2, factor)
-    block1 = line_sum(arrive(split1), factor, terms)
-    filter_two = write(ids, *line_spread(block2, block1))
+    block1 = line_sum(arrive(split1), factor)
+    spread2, spread1 = line_send(block2), line_send(block1)
+    filter_two = write(ids, *line_join(spread2, (spread1[1], got)))
     input_grad = got.astype(F32).sum(axis=0).astype(BF).reshape(shape)
-    filter_one = write(ids, *line_spread(block1, (filter_two, input_grad)))
+    filter_one = write(ids, *line_join(spread1, input_grad))
     return input_grad, filter_one, filter_two
 
 

time: 132 us -> 120 us (0.909)
  waiting for transfers between devices: 46.4 us -> 28.5 us
  starting transfers between devices: 52.5 us -> 58.4 us
    all_to_all x1, waiting for transfers between devices: 13.4 us -> 1.24 us  [shards(): got = lax.all_to_all(terms.reshape(16, C, n_pos), 'ch', 0, 0, tiled=True)]
    ppermute x6, waiting for transfers between devices: 15.5 us -> 6.58 us  [arrive(): lax.ppermute(v, LINE, along(k))]
    ppermute x8, starting transfers between devices: 7.83 us -> 13.5 us  [the longest x6 9.76 us: line_send(): return [block] + [lax.ppermute(block, LINE, along(k)) for k in (1, 3, 2)]]
    ppermute x8, waiting for transfers between devices: 10.6 us -> 13.7 us  [the longest x6 11.7 us: line_send(): return [block] + [lax.ppermute(block, LINE, along(k)) for k in (1, 3, 2)]]
  transfers between devices with their start and end apart: 26 -> 26, of which waited for: 11 -> 12; matrix products, arithmetic and copies ran while one was open for 4% -> 6% of each run, Pallas kernels for 9% -> 10%
where the time goes in v7:
time: 120 us
  starting transfers between devices  58.4 us (49%)
  waiting for transfers between devices  28.5 us (24%)
  Pallas kernels  20 us (17%)
  local copies, waits for them, and re-layouts  10.2 us (8%)
  other arithmetic  1.6 us (1%)
    ppermute x6, waiting for transfers between devices, line_send(): return [block] + [lax.ppermute(block, LINE, along(k)) for k in (1, 3, 2)]  11.7 us
    ppermute x6, starting transfers between devices, line_send(): return [block] + [lax.ppermute(block, LINE, along(k)) for k in (1, 3, 2)]  9.76 us
    all_to_all x1, starting transfers between devices, to_all(): return lax.all_to_all(many, axis, 0, 0, tiled=True)  8.73 us
    ppermute x2, starting transfers between devices, halo(): left = send(last, perm=to_side(1, flip))  7.15 us
    ppermute x6, waiting for transfers between devices, arrive(): lax.ppermute(v, LINE, along(k))  6.58 us
    ppermute x6, starting transfers between devices, arrive(): lax.ppermute(v, LINE, along(k))  6.51 us
    pallas_call x2, Pallas kernels, write(): pl.pallas_call(write_body, out_shape=jax.ShapeDtypeStruct((OFF, C, CH), F...  6.05 us
    ppermute x2, starting transfers between devices, halo(): right = send(first, perm=to_side(-1, flip))  4.72 us
  transfers between devices with their start and end apart: 26, of which 12 were waited for; matrix products, arithmetic and copies ran while one was open for 6% of the time, Pallas kernels for 10%

profile of v7, /device:TPU:1, one launch (start us, length us, event | category | flops | bytes accessed | tf_op | source)
XLA Modules:
  0.0 119.6 jit_solution(9582631324707342268)
XLA Ops:
  4.0 8.7 %all-to-all-start = ((bf16[16,96,512]{2,1,0:T(8,128)(2,1)}), bf16[16,96,512]{2,1,0:T(8,128)(2,1)S(1)}, u32[]{:S(2)}, u32[]{:S(2)}) async-start(bf16[16,96,512]{2,1,0:T(8,128)(2,1)} %broadcast_in_dim.2), calls=%async_computation | async-start | bytes 3145728 | tf_op jit(solution)/shard_map/all_to_all | solution.py:219
  12.9 5.2 %collective-permute-start.2 = (bf16[48,128]{1,0:T(8,128)(2,1)S(1)}, bf16[48,128]{1,0:T(8,128)(2,1)S(1)}, u32[]{:S(2)}, u32[]{:S(2)}) collective-permute-start(bf16[48,128]{1,0:T(8,128)(2,1)S(1)} %get-tuple-element.81), channel_id=1, source_target_pairs={{0,3},{1,2},{2,5},{3,4},{4,7},{5,6},{8,11},{9,10},{10,13},{11,12},... | collective-permute-start | bytes 36872 | tf_op jit(solution)/shard_map/ppermute | solution.py:211
  18.1 1.9 %collective-permute-start = (bf16[48,128]{1,0:T(8,128)(2,1)S(1)}, bf16[48,128]{1,0:T(8,128)(2,1)S(1)}, u32[]{:S(2)}, u32[]{:S(2)}) collective-permute-start(bf16[48,128]{1,0:T(8,128)(2,1)S(1)} %get-tuple-element.81), channel_id=1, source_target_pairs={{0,2},{1,3},{2,4},{3,5},{4,6},{5,7},{8,10},{9,11},{10,12},{11,13},... | collective-permute-start | bytes 36872 | tf_op jit(solution)/shard_map/ppermute | solution.py:211
  20.1 2.8 %collective-permute-start.4 = (bf16[48,128]{1,0:T(8,128)(2,1)S(1)}, bf16[48,128]{1,0:T(8,128)(2,1)S(1)}, u32[]{:S(2)}, u32[]{:S(2)}) collective-permute-start(bf16[48,128]{1,0:T(8,128)(2,1)S(1)} %get-tuple-element.82), channel_id=1, source_target_pairs={{2,1},{3,0},{4,3},{5,2},{6,5},{7,4},{10,9},{11,8},{12,11},{13,10},... | collective-permute-start | bytes 36872 | tf_op jit(solution)/shard_map/ppermute | solution.py:212
  22.9 1.9 %collective-permute-start.1 = (bf16[48,128]{1,0:T(8,128)(2,1)S(1)}, bf16[48,128]{1,0:T(8,128)(2,1)S(1)}, u32[]{:S(2)}, u32[]{:S(2)}) collective-permute-start(bf16[48,128]{1,0:T(8,128)(2,1)S(1)} %get-tuple-element.82), channel_id=1, source_target_pairs={{2,0},{3,1},{4,2},{5,3},{6,4},{7,5},{10,8},{11,9},{12,10},{13,11},... | collective-permute-start | bytes 36872 | tf_op jit(solution)/shard_map/ppermute | solution.py:212
  24.8 2.5 %collective-permute-start.3 = (bf16[48,512]{1,0:T(8,128)(2,1)S(1)}, bf16[48,512]{1,0:T(8,128)(2,1)S(1)}, u32[]{:S(2)}, u32[]{:S(2)}) collective-permute-start(bf16[48,512]{1,0:T(8,128)(2,1)S(1)} %reshape.44), channel_id=1, source_target_pairs={{0,1},{1,0},{2,3},{3,2},{4,5},{5,4},{6,7},{7,6},{8,9},{9,8},{10,11... | collective-permute-start | bytes 147464 | tf_op jit(solution)/shard_map/ppermute | solution.py:210
  27.4 4.1 %copy.9 = bf16[1296,768]{0,1:T(8,128)(2,1)} copy(bf16[1296,768]{1,0:T(8,128)(2,1)} %bitcast.18) | data formatting | bytes 3981312 | tf_op jit(solution)/shard_map/reshape | solution.py:310
  31.6 4.1 %all-to-all-done.both_ref = bf16[16,96,512]{2,1,0:T(8,128)(2,1)S(1)} async-done(((bf16[16,96,512]{2,1,0:T(8,128)(2,1)}), bf16[16,96,512]{2,1,0:T(8,128)(2,1)S(1)}, u32[]{:S(2)}, u32[]{:S(2)}) %all-to-all-start) | async-done | bytes 1572896 | tf_op jit(solution)/shard_map/all_to_all | solution.py:219
  37.2 2.0 %shard_map.76 = (f32[48,768]{1,0:T(8,128)S(1)}, f32[48,768]{1,0:T(8,128)S(1)}, f32[48,768]{1,0:T(8,128)S(1)}) custom-call(s32[4]{0:T(128)S(1)} %pad_add_fusion.ids, bf16[1296,768]{1,0:T(8,128)(2,1)S(1)} %bitcast.13, bf16[16,96,512]{2,1,0:T(8,128)(2,1)S(1)} %all-to-all-done.both_ref), custom_call_target="tpu_custom_call" | custom-call | tf_op jit(solution)/shard_map/pallas_call | solution.py:313
  39.1 2.8 %collective-permute-start.5 = (f32[48,768]{1,0:T(8,128)S(1)}, f32[48,768]{1,0:T(8,128)S(1)}, u32[]{:S(2)}, u32[]{:S(2)}) collective-permute-start(f32[48,768]{1,0:T(8,128)S(1)} %get-tuple-element.45), channel_id=1, source_target_pairs={{0,1},{1,0},{2,3},{3,2},{4,5},{5,4},{6,7},{7,6},{8,9},{9,8},{10,11... | collective-permute-start | bytes 442376 | tf_op jit(solution)/shard_map/ppermute | solution.py:319
  42.0 1.9 %shard_map.77 = bf16[1344,384]{1,0:T(8,128)(2,1)S(1)} custom-call(s32[4]{0:T(128)S(1)} %pad_add_fusion.ids, bf16[48,768]{1,0:T(8,128)(2,1)S(1)} %pad_maximum_fusion.1.own_ref.pre_own_ref, bf16[48,768]{1,0:T(8,128)(2,1)S(1)} %pad_maximum_fusion.2.oth_ref.pre_oth_ref, bf16[16,96,512]{2,1,0:T(8,128)(2,1)S(1)} %all-to-all-done.both_ref), custom_call_target="tpu_custom_call" | custom-call | tf_op jit(solution)/shard_map/pallas_call | solution.py:235
  44.7 3.7 %collective-permute-start.8 = (bf16[1344,384]{1,0:T(8,128)(2,1)S(1)}, bf16[1344,384]{1,0:T(8,128)(2,1)S(1)}, u32[]{:S(2)}, u32[]{:S(2)}) collective-permute-start(bf16[1344,384]{1,0:T(8,128)(2,1)S(1)} %shard_map.77), channel_id=1, source_target_pairs={{0,2},{2,0},{4,6},{6,4},{1,3},{3,1},{5,7},{7,5},{8,10},{10,8},{12,... | collective-permute-start | bytes 3096584 | tf_op jit(solution)/shard_map/ppermute | solution.py:324
  49.0 3.0 %collective-permute-start.6 = (f32[48,512]{1,0:T(8,128)S(1)}, f32[48,512]{1,0:T(8,128)S(1)}, u32[]{:S(2)}, u32[]{:S(2)}) collective-permute-start(f32[48,512]{1,0:T(8,128)S(1)} %get-tuple-element.51), channel_id=1, source_target_pairs={{0,2},{1,3},{2,4},{3,5},{4,6},{5,7},{8,10},{9,11},{10,12},{11,13},... | collective-permute-start | bytes 294920 | tf_op jit(solution)/shard_map/ppermute | solution.py:328
  52.0 1.9 %collective-permute-start.7 = (f32[48,512]{1,0:T(8,128)S(1)}, f32[48,512]{1,0:T(8,128)S(1)}, u32[]{:S(2)}, u32[]{:S(2)}) collective-permute-start(f32[48,512]{1,0:T(8,128)S(1)} %get-tuple-element.52), channel_id=1, source_target_pairs={{2,0},{3,1},{4,2},{5,3},{6,4},{7,5},{10,8},{11,9},{12,10},{13,11},... | collective-permute-start | bytes 294920 | tf_op jit(solution)/shard_map/ppermute | solution.py:329
  54.0 2.0 %shard_map.79 = (f32[336,384]{1,0:T(8,128)S(1)}, bf16[336,384]{1,0:T(8,128)(2,1)S(1)}, bf16[336,384]{1,0:T(8,128)(2,1)S(1)}, bf16[336,384]{1,0:T(8,128)(2,1)S(1)}) custom-call(s32[4]{0:T(128)S(1)} %pad_add_fusion.ids, bf16[48,768]{1,0:T(8,128)(2,1)S(1)} %pad_maximum_fusion.1.own_ref.pre_own_ref, bf16[48,768]{1,0:T(8,128)(2,1)S(1)} %pad_maximum_fusion.2.oth_ref.pre_oth_ref, ...), custom_call_target="tpu_custom_call" | custom-call | tf_op jit(solution)/shard_map/pallas_call | solution.py:240
  55.9 2.0 %collective-permute-done.7.right_ref = f32[48,512]{1,0:T(8,128)S(1)} collective-permute-done((f32[48,512]{1,0:T(8,128)S(1)}, f32[48,512]{1,0:T(8,128)S(1)}, u32[]{:S(2)}, u32[]{:S(2)}) %collective-permute-start.7) | collective-permute-done | bytes 98336 | tf_op jit(solution)/shard_map/ppermute | solution.py:329
  60.6 2.5 %collective-permute-start.11 = (bf16[336,384]{1,0:T(8,128)(2,1)S(1)}, bf16[336,384]{1,0:T(8,128)(2,1)S(1)}, u32[]{:S(2)}, u32[]{:S(2)}) collective-permute-start(bf16[336,384]{1,0:T(8,128)(2,1)S(1)} %get-tuple-element.56), channel_id=1, source_target_pairs={{0,1},{2,3},{4,5},{6,7},{1,0},{3,2},{5,4},{7,6},{8,9},{10,11},{12,... | collective-permute-start | bytes 774152 | tf_op jit(solution)/shard_map/ppermute | solution.py:247
  63.2 2.0 %collective-permute-start.10 = (bf16[336,384]{1,0:T(8,128)(2,1)S(1)}, bf16[336,384]{1,0:T(8,128)(2,1)S(1)}, u32[]{:S(2)}, u32[]{:S(2)}) collective-permute-start(bf16[336,384]{1,0:T(8,128)(2,1)S(1)} %get-tuple-element.57), channel_id=1, source_target_pairs={{0,5},{2,7},{4,0},{6,2},{1,4},{3,6},{5,1},{7,3},{8,13},{10,15},{12... | collective-permute-start | bytes 774152 | tf_op jit(solution)/shard_map/ppermute | solution.py:247
  65.2 2.0 %shard_map.82 = (f32[336,384]{1,0:T(8,128)S(1)}, bf16[336,384]{1,0:T(8,128)(2,1)S(1)}, bf16[336,384]{1,0:T(8,128)(2,1)S(1)}, bf16[336,384]{1,0:T(8,128)(2,1)S(1)}) custom-call(s32[4]{0:T(128)S(1)} %pad_add_fusion.ids, bf16[48,768]{1,0:T(8,128)(2,1)S(1)} %get-tuple-element.70.own_ref.refs_0_, bf16[48,768]{1,0:T(8,128)(2,1)S(1)} %get-tuple-element.71.oth_ref.refs_1_, ...), custom_call_target="tpu_custom_call" | custom-call | tf_op jit(solution)/shard_map/pallas_call | solution.py:240
  69.9 5.0 %collective-permute-done.11 = bf16[336,384]{1,0:T(8,128)(2,1)S(1)} collective-permute-done((bf16[336,384]{1,0:T(8,128)(2,1)S(1)}, bf16[336,384]{1,0:T(8,128)(2,1)S(1)}, u32[]{:S(2)}, u32[]{:S(2)}) %collective-permute-start.11) | collective-permute-done | bytes 258080 | tf_op jit(solution)/shard_map/ppermute | solution.py:247
  75.8 3.1 %shard_map.83 = bf16[768,512]{1,0:T(8,128)(2,1)} custom-call(s32[4]{0:T(128)S(1)} %pad_add_fusion.ids, bf16[48,768]{1,0:T(8,128)(2,1)S(1)} %get-tuple-element.70.own_ref.refs_0_, bf16[48,768]{1,0:T(8,128)(2,1)S(1)} %get-tuple-element.71.oth_ref.refs_1_, bf16[768,1296]{1,0:T(8,128)(2,1)S(1)} %bitcast.12), custom_call_target="tpu_custom_call" | custom-call | tf_op jit(solution)/shard_map/pallas_call | solution.py:343
  78.8 3.8 %all-to-all-start.1 = ((bf16[16,48,512]{2,1,0:T(8,128)(2,1)}), bf16[16,48,512]{2,1,0:T(8,128)(2,1)S(1)}, u32[]{:S(2)}, u32[]{:S(2)}) async-start(bf16[16,48,512]{2,1,0:T(8,128)(2,1)} %bitcast.7), calls=%async_computation.1 | async-start | bytes 1572864 | tf_op jit(solution)/shard_map/all_to_all | solution.py:349
  82.6 2.0 %collective-permute-start.22 = (bf16[336,384]{1,0:T(8,128)(2,1)S(1)}, bf16[336,384]{1,0:T(8,128)(2,1)S(1)}, u32[]{:S(2)}, u32[]{:S(2)}) collective-permute-start(bf16[336,384]{1,0:T(8,128)(2,1)S(1)} %multiply_convert_fusion.1), channel_id=1, source_target_pairs={{0,1},{2,3},{4,5},{6,7},{1,0},{3,2},{5,4},{7,6},{8,9},{10,11},{12,... | collective-permute-start | bytes 774152 | tf_op jit(solution)/shard_map/ppermute | solution.py:260
  84.6 2.1 %collective-permute-start.21 = (bf16[336,384]{1,0:T(8,128)(2,1)S(1)}, bf16[336,384]{1,0:T(8,128)(2,1)S(1)}, u32[]{:S(2)}, u32[]{:S(2)}) collective-permute-start(bf16[336,384]{1,0:T(8,128)(2,1)S(1)} %multiply_convert_fusion.1), channel_id=1, source_target_pairs={{0,5},{2,7},{4,0},{6,2},{1,4},{3,6},{5,1},{7,3},{8,13},{10,15},{12... | collective-permute-start | bytes 774152 | tf_op jit(solution)/shard_map/ppermute | solution.py:260
  90.0 2.1 %collective-permute-start.18 = (bf16[336,384]{1,0:T(8,128)(2,1)S(1)}, bf16[336,384]{1,0:T(8,128)(2,1)S(1)}, u32[]{:S(2)}, u32[]{:S(2)}) collective-permute-start(bf16[336,384]{1,0:T(8,128)(2,1)S(1)} %multiply_convert_fusion), channel_id=1, source_target_pairs={{0,1},{2,3},{4,5},{6,7},{1,0},{3,2},{5,4},{7,6},{8,9},{10,11},{12,... | collective-permute-start | bytes 774152 | tf_op jit(solution)/shard_map/ppermute | solution.py:260
  96.4 2.5 %collective-permute-done.16 = bf16[336,384]{1,0:T(8,128)(2,1)S(1)} collective-permute-done((bf16[336,384]{1,0:T(8,128)(2,1)S(1)}, bf16[336,384]{1,0:T(8,128)(2,1)S(1)}, u32[]{:S(2)}, u32[]{:S(2)}) %collective-permute-start.16) | collective-permute-done | bytes 258080 | tf_op jit(solution)/shard_map/ppermute | solution.py:260
  98.9 6.5 %collective-permute-done.18 = bf16[336,384]{1,0:T(8,128)(2,1)S(1)} collective-permute-done((bf16[336,384]{1,0:T(8,128)(2,1)S(1)}, bf16[336,384]{1,0:T(8,128)(2,1)S(1)}, u32[]{:S(2)}, u32[]{:S(2)}) %collective-permute-start.18) | collective-permute-done | bytes 258080 | tf_op jit(solution)/shard_map/ppermute | solution.py:260
  105.4 2.0 %collective-permute-done.17 = bf16[336,384]{1,0:T(8,128)(2,1)S(1)} collective-permute-done((bf16[336,384]{1,0:T(8,128)(2,1)S(1)}, bf16[336,384]{1,0:T(8,128)(2,1)S(1)}, u32[]{:S(2)}, u32[]{:S(2)}) %collective-permute-start.17) | collective-permute-done | bytes 258080 | tf_op jit(solution)/shard_map/ppermute | solution.py:260
  107.7 3.6 %collective-permute-start.19 = (bf16[1344,384]{1,0:T(8,128)(2,1)S(1)}, bf16[1344,384]{1,0:T(8,128)(2,1)S(1)}, u32[]{:S(2)}, u32[]{:S(2)}) collective-permute-start(bf16[1344,384]{1,0:T(8,128)(2,1)S(1)} %constant_dynamic-update-slice_fusion), channel_id=1, source_target_pairs={{0,2},{2,0},{4,6},{6,4},{1,3},{3,1},{5,7},{7,5},{8,10},{10,8},{12,... | collective-permute-start | bytes 3096584 | tf_op jit(solution)/shard_map/ppermute | solution.py:266
  111.5 2.0 %collective-permute-done.19 = bf16[1344,384]{1,0:T(8,128)(2,1)S(1)} collective-permute-done((bf16[1344,384]{1,0:T(8,128)(2,1)S(1)}, bf16[1344,384]{1,0:T(8,128)(2,1)S(1)}, u32[]{:S(2)}, u32[]{:S(2)}) %collective-permute-start.19) | collective-permute-done | bytes 1032224 | tf_op jit(solution)/shard_map/ppermute | solution.py:266
  113.6 3.0 %shard_map.84 = f32[27,48,768]{2,1,0:T(8,128)} custom-call(s32[4]{0:T(128)S(1)} %pad_add_fusion.ids, bf16[4,7,48,384]{3,2,1,0:T(8,128)(2,1)S(1)} %bitcast.15, bf16[4,7,48,384]{3,2,1,0:T(8,128)(2,1)S(1)} %bitcast.16), custom_call_target="tpu_custom_call" | custom-call | tf_op jit(solution)/shard_map/pallas_call | solution.py:280
  116.6 3.0 %shard_map.85 = f32[27,48,768]{2,1,0:T(8,128)} custom-call(s32[4]{0:T(128)S(1)} %pad_add_fusion.ids, bf16[4,7,48,384]{3,2,1,0:T(8,128)(2,1)S(1)} %bitcast.14, bf16[4,7,48,384]{3,2,1,0:T(8,128)(2,1)S(1)} %bitcast.17), custom_call_target="tpu_custom_call" | custom-call | tf_op jit(solution)/shard_map/pallas_call | solution.py:280
  (58 shorter events, 20.8 us)
Async XLA Ops:
  4.0 8.7 %copy-start.2 = (bf16[48,4,2,64]{3,2,1,0:T(2,128)(2,1)S(1)}, bf16[48,4,2,64]{3,2,1,0:T(2,128)(2,1)}, u32[]{:S(2)}) copy-start(bf16[48,4,2,64]{3,2,1,0:T(2,128)(2,1)} %param.6) | copy-start | bytes 147460
  4.0 31.6 %all-to-all-start = ((bf16[16,96,512]{2,1,0:T(8,128)(2,1)}), bf16[16,96,512]{2,1,0:T(8,128)(2,1)S(1)}, u32[]{:S(2)}, u32[]{:S(2)}) async-start(bf16[16,96,512]{2,1,0:T(8,128)(2,1)} %broadcast_in_dim.2), calls=%async_computation | async-start | bytes 3145728 | tf_op jit(solution)/shard_map/all_to_all | solution.py:219
  12.9 18.6 %collective-permute-start.2 = (bf16[48,128]{1,0:T(8,128)(2,1)S(1)}, bf16[48,128]{1,0:T(8,128)(2,1)S(1)}, u32[]{:S(2)}, u32[]{:S(2)}) collective-permute-start(bf16[48,128]{1,0:T(8,128)(2,1)S(1)} %get-tuple-element.81), channel_id=1, source_target_pairs={{0,3},{1,2},{2,5},{3,4},{4,7},{5,6},{8,11},{9,10},{10,13},{11,12},... | collective-permute-start | bytes 36872 | tf_op jit(solution)/shard_map/ppermute | solution.py:211
  18.1 13.4 %collective-permute-start = (bf16[48,128]{1,0:T(8,128)(2,1)S(1)}, bf16[48,128]{1,0:T(8,128)(2,1)S(1)}, u32[]{:S(2)}, u32[]{:S(2)}) collective-permute-start(bf16[48,128]{1,0:T(8,128)(2,1)S(1)} %get-tuple-element.81), channel_id=1, source_target_pairs={{0,2},{1,3},{2,4},{3,5},{4,6},{5,7},{8,10},{9,11},{10,12},{11,13},... | collective-permute-start | bytes 36872 | tf_op jit(solution)/shard_map/ppermute | solution.py:211
  20.1 11.5 %collective-permute-start.4 = (bf16[48,128]{1,0:T(8,128)(2,1)S(1)}, bf16[48,128]{1,0:T(8,128)(2,1)S(1)}, u32[]{:S(2)}, u32[]{:S(2)}) collective-permute-start(bf16[48,128]{1,0:T(8,128)(2,1)S(1)} %get-tuple-element.82), channel_id=1, source_target_pairs={{2,1},{3,0},{4,3},{5,2},{6,5},{7,4},{10,9},{11,8},{12,11},{13,10},... | collective-permute-start | bytes 36872 | tf_op jit(solution)/shard_map/ppermute | solution.py:212
  22.9 8.6 %collective-permute-start.1 = (bf16[48,128]{1,0:T(8,128)(2,1)S(1)}, bf16[48,128]{1,0:T(8,128)(2,1)S(1)}, u32[]{:S(2)}, u32[]{:S(2)}) collective-permute-start(bf16[48,128]{1,0:T(8,128)(2,1)S(1)} %get-tuple-element.82), channel_id=1, source_target_pairs={{2,0},{3,1},{4,2},{5,3},{6,4},{7,5},{10,8},{11,9},{12,10},{13,11},... | collective-permute-start | bytes 36872 | tf_op jit(solution)/shard_map/ppermute | solution.py:212
  24.8 6.7 %collective-permute-start.3 = (bf16[48,512]{1,0:T(8,128)(2,1)S(1)}, bf16[48,512]{1,0:T(8,128)(2,1)S(1)}, u32[]{:S(2)}, u32[]{:S(2)}) collective-permute-start(bf16[48,512]{1,0:T(8,128)(2,1)S(1)} %reshape.44), channel_id=1, source_target_pairs={{0,1},{1,0},{2,3},{3,2},{4,5},{5,4},{6,7},{7,6},{8,9},{9,8},{10,11... | collective-permute-start | bytes 147464 | tf_op jit(solution)/shard_map/ppermute | solution.py:210
  35.6 1.6 %copy-start.1 = (bf16[27,48,768]{2,1,0:T(8,128)(2,1)S(1)}, bf16[27,48,768]{2,1,0:T(8,128)(2,1)}, u32[]{:S(2)}) copy-start(bf16[27,48,768]{2,1,0:T(8,128)(2,1)} %param.9) | copy-start | bytes 5971972
  39.1 5.6 %collective-permute-start.5 = (f32[48,768]{1,0:T(8,128)S(1)}, f32[48,768]{1,0:T(8,128)S(1)}, u32[]{:S(2)}, u32[]{:S(2)}) collective-permute-start(f32[48,768]{1,0:T(8,128)S(1)} %get-tuple-element.45), channel_id=1, source_target_pairs={{0,1},{1,0},{2,3},{3,2},{4,5},{5,4},{6,7},{7,6},{8,9},{9,8},{10,11... | collective-permute-start | bytes 442376 | tf_op jit(solution)/shard_map/ppermute | solution.py:319
  44.7 9.2 %collective-permute-start.8 = (bf16[1344,384]{1,0:T(8,128)(2,1)S(1)}, bf16[1344,384]{1,0:T(8,128)(2,1)S(1)}, u32[]{:S(2)}, u32[]{:S(2)}) collective-permute-start(bf16[1344,384]{1,0:T(8,128)(2,1)S(1)} %shard_map.77), channel_id=1, source_target_pairs={{0,2},{2,0},{4,6},{6,4},{1,3},{3,1},{5,7},{7,5},{8,10},{10,8},{12,... | collective-permute-start | bytes 3096584 | tf_op jit(solution)/shard_map/ppermute | solution.py:324
  49.0 6.9 %collective-permute-start.6 = (f32[48,512]{1,0:T(8,128)S(1)}, f32[48,512]{1,0:T(8,128)S(1)}, u32[]{:S(2)}, u32[]{:S(2)}) collective-permute-start(f32[48,512]{1,0:T(8,128)S(1)} %get-tuple-element.51), channel_id=1, source_target_pairs={{0,2},{1,3},{2,4},{3,5},{4,6},{5,7},{8,10},{9,11},{10,12},{11,13},... | collective-permute-start | bytes 294920 | tf_op jit(solution)/shard_map/ppermute | solution.py:328
  52.0 5.9 %collective-permute-start.7 = (f32[48,512]{1,0:T(8,128)S(1)}, f32[48,512]{1,0:T(8,128)S(1)}, u32[]{:S(2)}, u32[]{:S(2)}) collective-permute-start(f32[48,512]{1,0:T(8,128)S(1)} %get-tuple-element.52), channel_id=1, source_target_pairs={{2,0},{3,1},{4,2},{5,3},{6,4},{7,5},{10,8},{11,9},{12,10},{13,11},... | collective-permute-start | bytes 294920 | tf_op jit(solution)/shard_map/ppermute | solution.py:329
  60.5 15.3 %copy-start = (bf16[1296,768]{0,1:T(8,128)(2,1)S(1)}, bf16[1296,768]{0,1:T(8,128)(2,1)}, u32[]{:S(2)}) copy-start(bf16[1296,768]{0,1:T(8,128)(2,1)} %copy.9) | copy-start | bytes 5971972
  60.5 4.7 %collective-permute-start.12 = (bf16[1344,384]{1,0:T(8,128)(2,1)S(1)}, bf16[1344,384]{1,0:T(8,128)(2,1)S(1)}, u32[]{:S(2)}, u32[]{:S(2)}) collective-permute-start(bf16[1344,384]{1,0:T(8,128)(2,1)S(1)} %shard_map.81), channel_id=1, source_target_pairs={{0,2},{2,0},{4,6},{6,4},{1,3},{3,1},{5,7},{7,5},{8,10},{10,8},{12,... | collective-permute-start | bytes 3096584 | tf_op jit(solution)/shard_map/ppermute | solution.py:338
  60.6 8.6 %collective-permute-start.9 = (bf16[336,384]{1,0:T(8,128)(2,1)S(1)}, bf16[336,384]{1,0:T(8,128)(2,1)S(1)}, u32[]{:S(2)}, u32[]{:S(2)}) collective-permute-start(bf16[336,384]{1,0:T(8,128)(2,1)S(1)} %get-tuple-element.55), channel_id=1, source_target_pairs={{0,4},{2,6},{4,1},{6,3},{1,5},{3,7},{5,0},{7,2},{8,12},{10,14},{12... | collective-permute-start | bytes 774152 | tf_op jit(solution)/shard_map/ppermute | solution.py:247
  60.6 14.3 %collective-permute-start.11 = (bf16[336,384]{1,0:T(8,128)(2,1)S(1)}, bf16[336,384]{1,0:T(8,128)(2,1)S(1)}, u32[]{:S(2)}, u32[]{:S(2)}) collective-permute-start(bf16[336,384]{1,0:T(8,128)(2,1)S(1)} %get-tuple-element.56), channel_id=1, source_target_pairs={{0,1},{2,3},{4,5},{6,7},{1,0},{3,2},{5,4},{7,6},{8,9},{10,11},{12,... | collective-permute-start | bytes 774152 | tf_op jit(solution)/shard_map/ppermute | solution.py:247
  63.2 12.4 %collective-permute-start.10 = (bf16[336,384]{1,0:T(8,128)(2,1)S(1)}, bf16[336,384]{1,0:T(8,128)(2,1)S(1)}, u32[]{:S(2)}, u32[]{:S(2)}) collective-permute-start(bf16[336,384]{1,0:T(8,128)(2,1)S(1)} %get-tuple-element.57), channel_id=1, source_target_pairs={{0,5},{2,7},{4,0},{6,2},{1,4},{3,6},{5,1},{7,3},{8,13},{10,15},{12... | collective-permute-start | bytes 774152 | tf_op jit(solution)/shard_map/ppermute | solution.py:247
  67.1 19.6 %collective-permute-start.13 = (bf16[336,384]{1,0:T(8,128)(2,1)S(1)}, bf16[336,384]{1,0:T(8,128)(2,1)S(1)}, u32[]{:S(2)}, u32[]{:S(2)}) collective-permute-start(bf16[336,384]{1,0:T(8,128)(2,1)S(1)} %get-tuple-element.63), channel_id=1, source_target_pairs={{0,4},{2,6},{4,1},{6,3},{1,5},{3,7},{5,0},{7,2},{8,12},{10,14},{12... | collective-permute-start | bytes 774152 | tf_op jit(solution)/shard_map/ppermute | solution.py:247
  67.2 20.0 %collective-permute-start.15 = (bf16[336,384]{1,0:T(8,128)(2,1)S(1)}, bf16[336,384]{1,0:T(8,128)(2,1)}, u32[]{:S(2)}, u32[]{:S(2)}) collective-permute-start(bf16[336,384]{1,0:T(8,128)(2,1)S(1)} %get-tuple-element.64), channel_id=1, source_target_pairs={{0,1},{2,3},{4,5},{6,7},{1,0},{3,2},{5,4},{7,6},{8,9},{10,11},{12,... | collective-permute-start | bytes 774152 | tf_op jit(solution)/shard_map/ppermute | solution.py:247
  69.2 18.0 %collective-permute-start.14 = (bf16[336,384]{1,0:T(8,128)(2,1)S(1)}, bf16[336,384]{1,0:T(8,128)(2,1)}, u32[]{:S(2)}, u32[]{:S(2)}) collective-permute-start(bf16[336,384]{1,0:T(8,128)(2,1)S(1)} %get-tuple-element.65), channel_id=1, source_target_pairs={{0,5},{2,7},{4,0},{6,2},{1,4},{3,6},{5,1},{7,3},{8,13},{10,15},{12... | collective-permute-start | bytes 774152 | tf_op jit(solution)/shard_map/ppermute | solution.py:247
  78.8 16.1 %all-to-all-start.1 = ((bf16[16,48,512]{2,1,0:T(8,128)(2,1)}), bf16[16,48,512]{2,1,0:T(8,128)(2,1)S(1)}, u32[]{:S(2)}, u32[]{:S(2)}) async-start(bf16[16,48,512]{2,1,0:T(8,128)(2,1)} %bitcast.7), calls=%async_computation.1 | async-start | bytes 1572864 | tf_op jit(solution)/shard_map/all_to_all | solution.py:349
  82.6 9.5 %collective-permute-start.22 = (bf16[336,384]{1,0:T(8,128)(2,1)S(1)}, bf16[336,384]{1,0:T(8,128)(2,1)S(1)}, u32[]{:S(2)}, u32[]{:S(2)}) collective-permute-start(bf16[336,384]{1,0:T(8,128)(2,1)S(1)} %multiply_convert_fusion.1), channel_id=1, source_target_pairs={{0,1},{2,3},{4,5},{6,7},{1,0},{3,2},{5,4},{7,6},{8,9},{10,11},{12,... | collective-permute-start | bytes 774152 | tf_op jit(solution)/shard_map/ppermute | solution.py:260
  84.6 11.8 %collective-permute-start.21 = (bf16[336,384]{1,0:T(8,128)(2,1)S(1)}, bf16[336,384]{1,0:T(8,128)(2,1)S(1)}, u32[]{:S(2)}, u32[]{:S(2)}) collective-permute-start(bf16[336,384]{1,0:T(8,128)(2,1)S(1)} %multiply_convert_fusion.1), channel_id=1, source_target_pairs={{0,5},{2,7},{4,0},{6,2},{1,4},{3,6},{5,1},{7,3},{8,13},{10,15},{12... | collective-permute-start | bytes 774152 | tf_op jit(solution)/shard_map/ppermute | solution.py:260
  86.8 9.7 %collective-permute-start.20 = (bf16[336,384]{1,0:T(8,128)(2,1)S(1)}, bf16[336,384]{1,0:T(8,128)(2,1)S(1)}, u32[]{:S(2)}, u32[]{:S(2)}) collective-permute-start(bf16[336,384]{1,0:T(8,128)(2,1)S(1)} %multiply_convert_fusion.1), channel_id=1, source_target_pairs={{0,4},{2,6},{4,1},{6,3},{1,5},{3,7},{5,0},{7,2},{8,12},{10,14},{12... | collective-permute-start | bytes 774152 | tf_op jit(solution)/shard_map/ppermute | solution.py:260
  88.5 10.5 %collective-permute-start.16 = (bf16[336,384]{1,0:T(8,128)(2,1)S(1)}, bf16[336,384]{1,0:T(8,128)(2,1)S(1)}, u32[]{:S(2)}, u32[]{:S(2)}) collective-permute-start(bf16[336,384]{1,0:T(8,128)(2,1)S(1)} %multiply_convert_fusion), channel_id=1, source_target_pairs={{0,4},{2,6},{4,1},{6,3},{1,5},{3,7},{5,0},{7,2},{8,12},{10,14},{12... | collective-permute-start | bytes 774152 | tf_op jit(solution)/shard_map/ppermute | solution.py:260
  90.0 15.5 %collective-permute-start.18 = (bf16[336,384]{1,0:T(8,128)(2,1)S(1)}, bf16[336,384]{1,0:T(8,128)(2,1)S(1)}, u32[]{:S(2)}, u32[]{:S(2)}) collective-permute-start(bf16[336,384]{1,0:T(8,128)(2,1)S(1)} %multiply_convert_fusion), channel_id=1, source_target_pairs={{0,1},{2,3},{4,5},{6,7},{1,0},{3,2},{5,4},{7,6},{8,9},{10,11},{12,... | collective-permute-start | bytes 774152 | tf_op jit(solution)/shard_map/ppermute | solution.py:260
  92.1 15.3 %collective-permute-start.17 = (bf16[336,384]{1,0:T(8,128)(2,1)S(1)}, bf16[336,384]{1,0:T(8,128)(2,1)S(1)}, u32[]{:S(2)}, u32[]{:S(2)}) collective-permute-start(bf16[336,384]{1,0:T(8,128)(2,1)S(1)} %multiply_convert_fusion), channel_id=1, source_target_pairs={{0,5},{2,7},{4,0},{6,2},{1,4},{3,6},{5,1},{7,3},{8,13},{10,15},{12... | collective-permute-start | bytes 774152 | tf_op jit(solution)/shard_map/ppermute | solution.py:260
  107.7 5.9 %collective-permute-start.19 = (bf16[1344,384]{1,0:T(8,128)(2,1)S(1)}, bf16[1344,384]{1,0:T(8,128)(2,1)S(1)}, u32[]{:S(2)}, u32[]{:S(2)}) collective-permute-start(bf16[1344,384]{1,0:T(8,128)(2,1)S(1)} %constant_dynamic-update-slice_fusion), channel_id=1, source_target_pairs={{0,2},{2,0},{4,6},{6,4},{1,3},{3,1},{5,7},{7,5},{8,10},{10,8},{12,... | collective-permute-start | bytes 3096584 | tf_op jit(solution)/shard_map/ppermute | solution.py:266
  111.5 5.1 %collective-permute-start.23 = (bf16[1344,384]{1,0:T(8,128)(2,1)S(1)}, bf16[1344,384]{1,0:T(8,128)(2,1)S(1)}, u32[]{:S(2)}, u32[]{:S(2)}) collective-permute-start(bf16[1344,384]{1,0:T(8,128)(2,1)S(1)} %constant_dynamic-update-slice_fusion.4), channel_id=1, source_target_pairs={{0,2},{2,0},{4,6},{6,4},{1,3},{3,1},{5,7},{7,5},{8,10},{10,8},{12,... | collective-permute-start | bytes 3096584 | tf_op jit(solution)/shard_map/ppermute | solution.py:266

commit v8 on v7

--- a/solution.py
+++ b/solution.py
@@ -268,10 +268,9 @@
 
 def write_body(ids, mine_ref, other_ref, out_ref):
     core = ids[2]
-    mine = mine_ref[0].astype(F32)
-    other = other_ref[0].astype(F32)
-    out_ref[:, :, :HALF] = jnp.where(core == 0, mine, other)
-    out_ref[:, :, HALF:] = jnp.where(core == 0, other, mine)
+    for ref, half in ((mine_ref, core), (other_ref, 1 - core)):
+        at = pl.ds(pl.multiple_of(half * HALF, HALF), HALF)
+        out_ref[:, :, at] = ref[0].astype(F32)
 
 
 def write(ids, mine, other):
@@ -303,7 +302,7 @@
     wide_b = jax.ShapeDtypeStruct((C, wide), BF)
     mid_f = jax.ShapeDtypeStruct((C, n_pos), F32)
 
-    both = jnp.concatenate([out_grad.reshape(C, n_pos), inputs.reshape(C, n_pos)], axis=0)
+    both = jnp.concatenate([out_grad, inputs], axis=0).reshape(2 * C, n_pos)
     both = to_all(both, "ch", 16)
     pre = halo(pre_act.reshape(C, n_pos))
     w_two = weight_two.reshape(ROWS, CH)

time: 120 us -> 119 us (level)
  local copies, waits for them, and re-layouts: 10.2 us -> 8.42 us
  other arithmetic: 1.6 us -> 2.85 us
    reshape x2 -> x0, local copies, waits for them, and re-layouts: 2.05 us -> none  [the longest x1 1.03 us: shards(): out_grad.reshape(C, n_pos)]
    concatenate x1, other arithmetic: 0.01 us -> 1.25 us  [shards(): both = jnp.concatenate([out_grad, inputs], axis=0).reshape(2 * C, n_pos)]
where the time goes in v8:
time: 119 us
  starting transfers between devices  58.1 us (49%)
  waiting for transfers between devices  28.5 us (24%)
  Pallas kernels  19.8 us (17%)
  local copies, waits for them, and re-layouts  8.42 us (7%)
  other arithmetic  2.85 us (2%)
    ppermute x6, waiting for transfers between devices, line_send(): return [block] + [lax.ppermute(block, LINE, along(k)) for k in (1, 3, 2)]  11.7 us
    ppermute x6, starting transfers between devices, line_send(): return [block] + [lax.ppermute(block, LINE, along(k)) for k in (1, 3, 2)]  9.73 us
    all_to_all x1, starting transfers between devices, to_all(): return lax.all_to_all(many, axis, 0, 0, tiled=True)  8.6 us
    ppermute x2, starting transfers between devices, halo(): left = send(last, perm=to_side(1, flip))  7.15 us
    ppermute x6, waiting for transfers between devices, arrive(): lax.ppermute(v, LINE, along(k))  6.62 us
    ppermute x6, starting transfers between devices, arrive(): lax.ppermute(v, LINE, along(k))  6.49 us
    pallas_call x2, Pallas kernels, write(): pl.pallas_call(write_body, out_shape=jax.ShapeDtypeStruct((OFF, C, CH), F...  5.85 us
    ppermute x2, starting transfers between devices, halo(): right = send(first, perm=to_side(-1, flip))  4.72 us
  transfers between devices with their start and end apart: 26, of which 12 were waited for; matrix products, arithmetic and copies ran while one was open for 6% of the time, Pallas kernels for 10%

profile of v8, /device:TPU:1, one launch (start us, length us, event | category | flops | bytes accessed | tf_op | source)
XLA Modules:
  0.0 118.6 jit_solution(863174511874413402)
XLA Ops:
  3.5 8.6 %all-to-all-start = ((bf16[16,96,512]{2,1,0:T(8,128)(2,1)}), bf16[16,96,512]{2,1,0:T(8,128)(2,1)S(1)}, u32[]{:S(2)}, u32[]{:S(2)}) async-start(bf16[16,96,512]{2,1,0:T(8,128)(2,1)} %broadcast_in_dim.8), calls=%async_computation | async-start | bytes 3145728 | tf_op jit(solution)/shard_map/all_to_all | solution.py:219
  12.2 5.2 %collective-permute-start.2 = (bf16[48,128]{1,0:T(8,128)(2,1)S(1)}, bf16[48,128]{1,0:T(8,128)(2,1)S(1)}, u32[]{:S(2)}, u32[]{:S(2)}) collective-permute-start(bf16[48,128]{1,0:T(8,128)(2,1)S(1)} %get-tuple-element.81), channel_id=1, source_target_pairs={{0,3},{1,2},{2,5},{3,4},{4,7},{5,6},{8,11},{9,10},{10,13},{11,12},... | collective-permute-start | bytes 36872 | tf_op jit(solution)/shard_map/ppermute | solution.py:211
  17.5 1.9 %collective-permute-start = (bf16[48,128]{1,0:T(8,128)(2,1)S(1)}, bf16[48,128]{1,0:T(8,128)(2,1)S(1)}, u32[]{:S(2)}, u32[]{:S(2)}) collective-permute-start(bf16[48,128]{1,0:T(8,128)(2,1)S(1)} %get-tuple-element.81), channel_id=1, source_target_pairs={{0,2},{1,3},{2,4},{3,5},{4,6},{5,7},{8,10},{9,11},{10,12},{11,13},... | collective-permute-start | bytes 36872 | tf_op jit(solution)/shard_map/ppermute | solution.py:211
  19.4 2.8 %collective-permute-start.4 = (bf16[48,128]{1,0:T(8,128)(2,1)S(1)}, bf16[48,128]{1,0:T(8,128)(2,1)S(1)}, u32[]{:S(2)}, u32[]{:S(2)}) collective-permute-start(bf16[48,128]{1,0:T(8,128)(2,1)S(1)} %get-tuple-element.82), channel_id=1, source_target_pairs={{2,1},{3,0},{4,3},{5,2},{6,5},{7,4},{10,9},{11,8},{12,11},{13,10},... | collective-permute-start | bytes 36872 | tf_op jit(solution)/shard_map/ppermute | solution.py:212
  22.2 1.9 %collective-permute-start.1 = (bf16[48,128]{1,0:T(8,128)(2,1)S(1)}, bf16[48,128]{1,0:T(8,128)(2,1)S(1)}, u32[]{:S(2)}, u32[]{:S(2)}) collective-permute-start(bf16[48,128]{1,0:T(8,128)(2,1)S(1)} %get-tuple-element.82), channel_id=1, source_target_pairs={{2,0},{3,1},{4,2},{5,3},{6,4},{7,5},{10,8},{11,9},{12,10},{13,11},... | collective-permute-start | bytes 36872 | tf_op jit(solution)/shard_map/ppermute | solution.py:212
  24.1 2.5 %collective-permute-start.3 = (bf16[48,512]{1,0:T(8,128)(2,1)S(1)}, bf16[48,512]{1,0:T(8,128)(2,1)S(1)}, u32[]{:S(2)}, u32[]{:S(2)}) collective-permute-start(bf16[48,512]{1,0:T(8,128)(2,1)S(1)} %reshape.36), channel_id=1, source_target_pairs={{0,1},{1,0},{2,3},{3,2},{4,5},{5,4},{6,7},{7,6},{8,9},{9,8},{10,11... | collective-permute-start | bytes 147464 | tf_op jit(solution)/shard_map/ppermute | solution.py:210
  26.7 4.1 %copy.11 = bf16[1296,768]{0,1:T(8,128)(2,1)} copy(bf16[1296,768]{1,0:T(8,128)(2,1)} %bitcast.19) | data formatting | bytes 3981312 | tf_op jit(solution)/shard_map/reshape | solution.py:309
  30.9 4.1 %all-to-all-done.both_ref = bf16[16,96,512]{2,1,0:T(8,128)(2,1)S(1)} async-done(((bf16[16,96,512]{2,1,0:T(8,128)(2,1)}), bf16[16,96,512]{2,1,0:T(8,128)(2,1)S(1)}, u32[]{:S(2)}, u32[]{:S(2)}) %all-to-all-start) | async-done | bytes 1572896 | tf_op jit(solution)/shard_map/all_to_all | solution.py:219
  36.5 2.0 %shard_map.76 = (f32[48,768]{1,0:T(8,128)S(1)}, f32[48,768]{1,0:T(8,128)S(1)}, f32[48,768]{1,0:T(8,128)S(1)}) custom-call(s32[4]{0:T(128)S(1)} %pad_add_fusion.ids, bf16[1296,768]{1,0:T(8,128)(2,1)S(1)} %bitcast.14, bf16[16,96,512]{2,1,0:T(8,128)(2,1)S(1)} %all-to-all-done.both_ref), custom_call_target="tpu_custom_call" | custom-call | tf_op jit(solution)/shard_map/pallas_call | solution.py:312
  38.5 2.8 %collective-permute-start.5 = (f32[48,768]{1,0:T(8,128)S(1)}, f32[48,768]{1,0:T(8,128)S(1)}, u32[]{:S(2)}, u32[]{:S(2)}) collective-permute-start(f32[48,768]{1,0:T(8,128)S(1)} %get-tuple-element.45), channel_id=1, source_target_pairs={{0,1},{1,0},{2,3},{3,2},{4,5},{5,4},{6,7},{7,6},{8,9},{9,8},{10,11... | collective-permute-start | bytes 442376 | tf_op jit(solution)/shard_map/ppermute | solution.py:318
  41.3 1.9 %shard_map.77 = bf16[1344,384]{1,0:T(8,128)(2,1)S(1)} custom-call(s32[4]{0:T(128)S(1)} %pad_add_fusion.ids, bf16[48,768]{1,0:T(8,128)(2,1)S(1)} %pad_maximum_fusion.1.own_ref.pre_own_ref, bf16[48,768]{1,0:T(8,128)(2,1)S(1)} %pad_maximum_fusion.2.oth_ref.pre_oth_ref, bf16[16,96,512]{2,1,0:T(8,128)(2,1)S(1)} %all-to-all-done.both_ref), custom_call_target="tpu_custom_call" | custom-call | tf_op jit(solution)/shard_map/pallas_call | solution.py:235
  44.0 3.7 %collective-permute-start.8 = (bf16[1344,384]{1,0:T(8,128)(2,1)S(1)}, bf16[1344,384]{1,0:T(8,128)(2,1)S(1)}, u32[]{:S(2)}, u32[]{:S(2)}) collective-permute-start(bf16[1344,384]{1,0:T(8,128)(2,1)S(1)} %shard_map.77), channel_id=1, source_target_pairs={{0,2},{2,0},{4,6},{6,4},{1,3},{3,1},{5,7},{7,5},{8,10},{10,8},{12,... | collective-permute-start | bytes 3096584 | tf_op jit(solution)/shard_map/ppermute | solution.py:323
  48.3 3.0 %collective-permute-start.6 = (f32[48,512]{1,0:T(8,128)S(1)}, f32[48,512]{1,0:T(8,128)S(1)}, u32[]{:S(2)}, u32[]{:S(2)}) collective-permute-start(f32[48,512]{1,0:T(8,128)S(1)} %get-tuple-element.51), channel_id=1, source_target_pairs={{0,2},{1,3},{2,4},{3,5},{4,6},{5,7},{8,10},{9,11},{10,12},{11,13},... | collective-permute-start | bytes 294920 | tf_op jit(solution)/shard_map/ppermute | solution.py:327
  51.3 1.9 %collective-permute-start.7 = (f32[48,512]{1,0:T(8,128)S(1)}, f32[48,512]{1,0:T(8,128)S(1)}, u32[]{:S(2)}, u32[]{:S(2)}) collective-permute-start(f32[48,512]{1,0:T(8,128)S(1)} %get-tuple-element.52), channel_id=1, source_target_pairs={{2,0},{3,1},{4,2},{5,3},{6,4},{7,5},{10,8},{11,9},{12,10},{13,11},... | collective-permute-start | bytes 294920 | tf_op jit(solution)/shard_map/ppermute | solution.py:328
  53.3 2.0 %shard_map.79 = (f32[336,384]{1,0:T(8,128)S(1)}, bf16[336,384]{1,0:T(8,128)(2,1)S(1)}, bf16[336,384]{1,0:T(8,128)(2,1)S(1)}, bf16[336,384]{1,0:T(8,128)(2,1)S(1)}) custom-call(s32[4]{0:T(128)S(1)} %pad_add_fusion.ids, bf16[48,768]{1,0:T(8,128)(2,1)S(1)} %pad_maximum_fusion.1.own_ref.pre_own_ref, bf16[48,768]{1,0:T(8,128)(2,1)S(1)} %pad_maximum_fusion.2.oth_ref.pre_oth_ref, ...), custom_call_target="tpu_custom_call" | custom-call | tf_op jit(solution)/shard_map/pallas_call | solution.py:240
  55.3 2.0 %collective-permute-done.7.right_ref = f32[48,512]{1,0:T(8,128)S(1)} collective-permute-done((f32[48,512]{1,0:T(8,128)S(1)}, f32[48,512]{1,0:T(8,128)S(1)}, u32[]{:S(2)}, u32[]{:S(2)}) %collective-permute-start.7) | collective-permute-done | bytes 98336 | tf_op jit(solution)/shard_map/ppermute | solution.py:328
  60.0 2.5 %collective-permute-start.11 = (bf16[336,384]{1,0:T(8,128)(2,1)S(1)}, bf16[336,384]{1,0:T(8,128)(2,1)S(1)}, u32[]{:S(2)}, u32[]{:S(2)}) collective-permute-start(bf16[336,384]{1,0:T(8,128)(2,1)S(1)} %get-tuple-element.56), channel_id=1, source_target_pairs={{0,1},{2,3},{4,5},{6,7},{1,0},{3,2},{5,4},{7,6},{8,9},{10,11},{12,... | collective-permute-start | bytes 774152 | tf_op jit(solution)/shard_map/ppermute | solution.py:247
  62.5 2.0 %collective-permute-start.10 = (bf16[336,384]{1,0:T(8,128)(2,1)S(1)}, bf16[336,384]{1,0:T(8,128)(2,1)S(1)}, u32[]{:S(2)}, u32[]{:S(2)}) collective-permute-start(bf16[336,384]{1,0:T(8,128)(2,1)S(1)} %get-tuple-element.57), channel_id=1, source_target_pairs={{0,5},{2,7},{4,0},{6,2},{1,4},{3,6},{5,1},{7,3},{8,13},{10,15},{12... | collective-permute-start | bytes 774152 | tf_op jit(solution)/shard_map/ppermute | solution.py:247
  64.5 2.0 %shard_map.82 = (f32[336,384]{1,0:T(8,128)S(1)}, bf16[336,384]{1,0:T(8,128)(2,1)S(1)}, bf16[336,384]{1,0:T(8,128)(2,1)S(1)}, bf16[336,384]{1,0:T(8,128)(2,1)S(1)}) custom-call(s32[4]{0:T(128)S(1)} %pad_add_fusion.ids, bf16[48,768]{1,0:T(8,128)(2,1)S(1)} %get-tuple-element.70.own_ref.refs_0_, bf16[48,768]{1,0:T(8,128)(2,1)S(1)} %get-tuple-element.71.oth_ref.refs_1_, ...), custom_call_target="tpu_custom_call" | custom-call | tf_op jit(solution)/shard_map/pallas_call | solution.py:240
  69.2 5.0 %collective-permute-done.11 = bf16[336,384]{1,0:T(8,128)(2,1)S(1)} collective-permute-done((bf16[336,384]{1,0:T(8,128)(2,1)S(1)}, bf16[336,384]{1,0:T(8,128)(2,1)S(1)}, u32[]{:S(2)}, u32[]{:S(2)}) %collective-permute-start.11) | collective-permute-done | bytes 258080 | tf_op jit(solution)/shard_map/ppermute | solution.py:247
  75.1 3.1 %shard_map.83 = bf16[768,512]{1,0:T(8,128)(2,1)} custom-call(s32[4]{0:T(128)S(1)} %pad_add_fusion.ids, bf16[48,768]{1,0:T(8,128)(2,1)S(1)} %get-tuple-element.70.own_ref.refs_0_, bf16[48,768]{1,0:T(8,128)(2,1)S(1)} %get-tuple-element.71.oth_ref.refs_1_, bf16[768,1296]{1,0:T(8,128)(2,1)S(1)} %bitcast.13), custom_call_target="tpu_custom_call" | custom-call | tf_op jit(solution)/shard_map/pallas_call | solution.py:342
  78.2 3.6 %all-to-all-start.1 = ((bf16[16,48,512]{2,1,0:T(8,128)(2,1)}), bf16[16,48,512]{2,1,0:T(8,128)(2,1)S(1)}, u32[]{:S(2)}, u32[]{:S(2)}) async-start(bf16[16,48,512]{2,1,0:T(8,128)(2,1)} %bitcast.8), calls=%async_computation.1 | async-start | bytes 1572864 | tf_op jit(solution)/shard_map/all_to_all | solution.py:348
  81.8 2.0 %collective-permute-start.22 = (bf16[336,384]{1,0:T(8,128)(2,1)S(1)}, bf16[336,384]{1,0:T(8,128)(2,1)S(1)}, u32[]{:S(2)}, u32[]{:S(2)}) collective-permute-start(bf16[336,384]{1,0:T(8,128)(2,1)S(1)} %multiply_convert_fusion.1), channel_id=1, source_target_pairs={{0,1},{2,3},{4,5},{6,7},{1,0},{3,2},{5,4},{7,6},{8,9},{10,11},{12,... | collective-permute-start | bytes 774152 | tf_op jit(solution)/shard_map/ppermute | solution.py:260
  83.8 2.2 %collective-permute-start.21 = (bf16[336,384]{1,0:T(8,128)(2,1)S(1)}, bf16[336,384]{1,0:T(8,128)(2,1)S(1)}, u32[]{:S(2)}, u32[]{:S(2)}) collective-permute-start(bf16[336,384]{1,0:T(8,128)(2,1)S(1)} %multiply_convert_fusion.1), channel_id=1, source_target_pairs={{0,5},{2,7},{4,0},{6,2},{1,4},{3,6},{5,1},{7,3},{8,13},{10,15},{12... | collective-permute-start | bytes 774152 | tf_op jit(solution)/shard_map/ppermute | solution.py:260
  89.1 2.3 %collective-permute-start.18 = (bf16[336,384]{1,0:T(8,128)(2,1)S(1)}, bf16[336,384]{1,0:T(8,128)(2,1)S(1)}, u32[]{:S(2)}, u32[]{:S(2)}) collective-permute-start(bf16[336,384]{1,0:T(8,128)(2,1)S(1)} %multiply_convert_fusion), channel_id=1, source_target_pairs={{0,1},{2,3},{4,5},{6,7},{1,0},{3,2},{5,4},{7,6},{8,9},{10,11},{12,... | collective-permute-start | bytes 774152 | tf_op jit(solution)/shard_map/ppermute | solution.py:260
  95.6 2.6 %collective-permute-done.16 = bf16[336,384]{1,0:T(8,128)(2,1)S(1)} collective-permute-done((bf16[336,384]{1,0:T(8,128)(2,1)S(1)}, bf16[336,384]{1,0:T(8,128)(2,1)S(1)}, u32[]{:S(2)}, u32[]{:S(2)}) %collective-permute-start.16) | collective-permute-done | bytes 258080 | tf_op jit(solution)/shard_map/ppermute | solution.py:260
  98.2 6.5 %collective-permute-done.18 = bf16[336,384]{1,0:T(8,128)(2,1)S(1)} collective-permute-done((bf16[336,384]{1,0:T(8,128)(2,1)S(1)}, bf16[336,384]{1,0:T(8,128)(2,1)S(1)}, u32[]{:S(2)}, u32[]{:S(2)}) %collective-permute-start.18) | collective-permute-done | bytes 258080 | tf_op jit(solution)/shard_map/ppermute | solution.py:260
  104.6 2.0 %collective-permute-done.17 = bf16[336,384]{1,0:T(8,128)(2,1)S(1)} collective-permute-done((bf16[336,384]{1,0:T(8,128)(2,1)S(1)}, bf16[336,384]{1,0:T(8,128)(2,1)S(1)}, u32[]{:S(2)}, u32[]{:S(2)}) %collective-permute-start.17) | collective-permute-done | bytes 258080 | tf_op jit(solution)/shard_map/ppermute | solution.py:260
  106.8 3.6 %collective-permute-start.19 = (bf16[1344,384]{1,0:T(8,128)(2,1)S(1)}, bf16[1344,384]{1,0:T(8,128)(2,1)S(1)}, u32[]{:S(2)}, u32[]{:S(2)}) collective-permute-start(bf16[1344,384]{1,0:T(8,128)(2,1)S(1)} %constant_dynamic-update-slice_fusion), channel_id=1, source_target_pairs={{0,2},{2,0},{4,6},{6,4},{1,3},{3,1},{5,7},{7,5},{8,10},{10,8},{12,... | collective-permute-start | bytes 3096584 | tf_op jit(solution)/shard_map/ppermute | solution.py:266
  110.7 2.0 %collective-permute-done.19 = bf16[1344,384]{1,0:T(8,128)(2,1)S(1)} collective-permute-done((bf16[1344,384]{1,0:T(8,128)(2,1)S(1)}, bf16[1344,384]{1,0:T(8,128)(2,1)S(1)}, u32[]{:S(2)}, u32[]{:S(2)}) %collective-permute-start.19) | collective-permute-done | bytes 1032224 | tf_op jit(solution)/shard_map/ppermute | solution.py:266
  112.7 2.9 %shard_map.84 = f32[27,48,768]{2,1,0:T(8,128)} custom-call(s32[4]{0:T(128)S(1)} %pad_add_fusion.ids, bf16[4,7,48,384]{3,2,1,0:T(8,128)(2,1)S(1)} %bitcast.16, bf16[4,7,48,384]{3,2,1,0:T(8,128)(2,1)S(1)} %bitcast.17), custom_call_target="tpu_custom_call" | custom-call | tf_op jit(solution)/shard_map/pallas_call | solution.py:279
  115.6 2.9 %shard_map.85 = f32[27,48,768]{2,1,0:T(8,128)} custom-call(s32[4]{0:T(128)S(1)} %pad_add_fusion.ids, bf16[4,7,48,384]{3,2,1,0:T(8,128)(2,1)S(1)} %bitcast.15, bf16[4,7,48,384]{3,2,1,0:T(8,128)(2,1)S(1)} %bitcast.18), custom_call_target="tpu_custom_call" | custom-call | tf_op jit(solution)/shard_map/pallas_call | solution.py:279
  (58 shorter events, 20.1 us)
Async XLA Ops:
  2.2 9.9 %copy-start.2 = (bf16[48,4,2,64]{3,2,1,0:T(2,128)(2,1)S(1)}, bf16[48,4,2,64]{3,2,1,0:T(2,128)(2,1)}, u32[]{:S(2)}) copy-start(bf16[48,4,2,64]{3,2,1,0:T(2,128)(2,1)} %param.6) | copy-start | bytes 147460
  3.5 31.5 %all-to-all-start = ((bf16[16,96,512]{2,1,0:T(8,128)(2,1)}), bf16[16,96,512]{2,1,0:T(8,128)(2,1)S(1)}, u32[]{:S(2)}, u32[]{:S(2)}) async-start(bf16[16,96,512]{2,1,0:T(8,128)(2,1)} %broadcast_in_dim.8), calls=%async_computation | async-start | bytes 3145728 | tf_op jit(solution)/shard_map/all_to_all | solution.py:219
  12.2 18.6 %collective-permute-start.2 = (bf16[48,128]{1,0:T(8,128)(2,1)S(1)}, bf16[48,128]{1,0:T(8,128)(2,1)S(1)}, u32[]{:S(2)}, u32[]{:S(2)}) collective-permute-start(bf16[48,128]{1,0:T(8,128)(2,1)S(1)} %get-tuple-element.81), channel_id=1, source_target_pairs={{0,3},{1,2},{2,5},{3,4},{4,7},{5,6},{8,11},{9,10},{10,13},{11,12},... | collective-permute-start | bytes 36872 | tf_op jit(solution)/shard_map/ppermute | solution.py:211
  17.5 13.4 %collective-permute-start = (bf16[48,128]{1,0:T(8,128)(2,1)S(1)}, bf16[48,128]{1,0:T(8,128)(2,1)S(1)}, u32[]{:S(2)}, u32[]{:S(2)}) collective-permute-start(bf16[48,128]{1,0:T(8,128)(2,1)S(1)} %get-tuple-element.81), channel_id=1, source_target_pairs={{0,2},{1,3},{2,4},{3,5},{4,6},{5,7},{8,10},{9,11},{10,12},{11,13},... | collective-permute-start | bytes 36872 | tf_op jit(solution)/shard_map/ppermute | solution.py:211
  19.4 11.5 %collective-permute-start.4 = (bf16[48,128]{1,0:T(8,128)(2,1)S(1)}, bf16[48,128]{1,0:T(8,128)(2,1)S(1)}, u32[]{:S(2)}, u32[]{:S(2)}) collective-permute-start(bf16[48,128]{1,0:T(8,128)(2,1)S(1)} %get-tuple-element.82), channel_id=1, source_target_pairs={{2,1},{3,0},{4,3},{5,2},{6,5},{7,4},{10,9},{11,8},{12,11},{13,10},... | collective-permute-start | bytes 36872 | tf_op jit(solution)/shard_map/ppermute | solution.py:212
  22.2 8.6 %collective-permute-start.1 = (bf16[48,128]{1,0:T(8,128)(2,1)S(1)}, bf16[48,128]{1,0:T(8,128)(2,1)S(1)}, u32[]{:S(2)}, u32[]{:S(2)}) collective-permute-start(bf16[48,128]{1,0:T(8,128)(2,1)S(1)} %get-tuple-element.82), channel_id=1, source_target_pairs={{2,0},{3,1},{4,2},{5,3},{6,4},{7,5},{10,8},{11,9},{12,10},{13,11},... | collective-permute-start | bytes 36872 | tf_op jit(solution)/shard_map/ppermute | solution.py:212
  24.1 6.7 %collective-permute-start.3 = (bf16[48,512]{1,0:T(8,128)(2,1)S(1)}, bf16[48,512]{1,0:T(8,128)(2,1)S(1)}, u32[]{:S(2)}, u32[]{:S(2)}) collective-permute-start(bf16[48,512]{1,0:T(8,128)(2,1)S(1)} %reshape.36), channel_id=1, source_target_pairs={{0,1},{1,0},{2,3},{3,2},{4,5},{5,4},{6,7},{7,6},{8,9},{9,8},{10,11... | collective-permute-start | bytes 147464 | tf_op jit(solution)/shard_map/ppermute | solution.py:210
  34.9 1.6 %copy-start.1 = (bf16[27,48,768]{2,1,0:T(8,128)(2,1)S(1)}, bf16[27,48,768]{2,1,0:T(8,128)(2,1)}, u32[]{:S(2)}) copy-start(bf16[27,48,768]{2,1,0:T(8,128)(2,1)} %param.9) | copy-start | bytes 5971972
  38.5 5.6 %collective-permute-start.5 = (f32[48,768]{1,0:T(8,128)S(1)}, f32[48,768]{1,0:T(8,128)S(1)}, u32[]{:S(2)}, u32[]{:S(2)}) collective-permute-start(f32[48,768]{1,0:T(8,128)S(1)} %get-tuple-element.45), channel_id=1, source_target_pairs={{0,1},{1,0},{2,3},{3,2},{4,5},{5,4},{6,7},{7,6},{8,9},{9,8},{10,11... | collective-permute-start | bytes 442376 | tf_op jit(solution)/shard_map/ppermute | solution.py:318
  44.0 9.2 %collective-permute-start.8 = (bf16[1344,384]{1,0:T(8,128)(2,1)S(1)}, bf16[1344,384]{1,0:T(8,128)(2,1)S(1)}, u32[]{:S(2)}, u32[]{:S(2)}) collective-permute-start(bf16[1344,384]{1,0:T(8,128)(2,1)S(1)} %shard_map.77), channel_id=1, source_target_pairs={{0,2},{2,0},{4,6},{6,4},{1,3},{3,1},{5,7},{7,5},{8,10},{10,8},{12,... | collective-permute-start | bytes 3096584 | tf_op jit(solution)/shard_map/ppermute | solution.py:323
  48.3 6.9 %collective-permute-start.6 = (f32[48,512]{1,0:T(8,128)S(1)}, f32[48,512]{1,0:T(8,128)S(1)}, u32[]{:S(2)}, u32[]{:S(2)}) collective-permute-start(f32[48,512]{1,0:T(8,128)S(1)} %get-tuple-element.51), channel_id=1, source_target_pairs={{0,2},{1,3},{2,4},{3,5},{4,6},{5,7},{8,10},{9,11},{10,12},{11,13},... | collective-permute-start | bytes 294920 | tf_op jit(solution)/shard_map/ppermute | solution.py:327
  51.3 5.9 %collective-permute-start.7 = (f32[48,512]{1,0:T(8,128)S(1)}, f32[48,512]{1,0:T(8,128)S(1)}, u32[]{:S(2)}, u32[]{:S(2)}) collective-permute-start(f32[48,512]{1,0:T(8,128)S(1)} %get-tuple-element.52), channel_id=1, source_target_pairs={{2,0},{3,1},{4,2},{5,3},{6,4},{7,5},{10,8},{11,9},{12,10},{13,11},... | collective-permute-start | bytes 294920 | tf_op jit(solution)/shard_map/ppermute | solution.py:328
  59.8 15.3 %copy-start = (bf16[1296,768]{0,1:T(8,128)(2,1)S(1)}, bf16[1296,768]{0,1:T(8,128)(2,1)}, u32[]{:S(2)}) copy-start(bf16[1296,768]{0,1:T(8,128)(2,1)} %copy.11) | copy-start | bytes 5971972
  59.8 4.7 %collective-permute-start.12 = (bf16[1344,384]{1,0:T(8,128)(2,1)S(1)}, bf16[1344,384]{1,0:T(8,128)(2,1)S(1)}, u32[]{:S(2)}, u32[]{:S(2)}) collective-permute-start(bf16[1344,384]{1,0:T(8,128)(2,1)S(1)} %shard_map.81), channel_id=1, source_target_pairs={{0,2},{2,0},{4,6},{6,4},{1,3},{3,1},{5,7},{7,5},{8,10},{10,8},{12,... | collective-permute-start | bytes 3096584 | tf_op jit(solution)/shard_map/ppermute | solution.py:337
  59.9 8.6 %collective-permute-start.9 = (bf16[336,384]{1,0:T(8,128)(2,1)S(1)}, bf16[336,384]{1,0:T(8,128)(2,1)S(1)}, u32[]{:S(2)}, u32[]{:S(2)}) collective-permute-start(bf16[336,384]{1,0:T(8,128)(2,1)S(1)} %get-tuple-element.55), channel_id=1, source_target_pairs={{0,4},{2,6},{4,1},{6,3},{1,5},{3,7},{5,0},{7,2},{8,12},{10,14},{12... | collective-permute-start | bytes 774152 | tf_op jit(solution)/shard_map/ppermute | solution.py:247
  60.0 14.2 %collective-permute-start.11 = (bf16[336,384]{1,0:T(8,128)(2,1)S(1)}, bf16[336,384]{1,0:T(8,128)(2,1)S(1)}, u32[]{:S(2)}, u32[]{:S(2)}) collective-permute-start(bf16[336,384]{1,0:T(8,128)(2,1)S(1)} %get-tuple-element.56), channel_id=1, source_target_pairs={{0,1},{2,3},{4,5},{6,7},{1,0},{3,2},{5,4},{7,6},{8,9},{10,11},{12,... | collective-permute-start | bytes 774152 | tf_op jit(solution)/shard_map/ppermute | solution.py:247
  62.5 12.5 %collective-permute-start.10 = (bf16[336,384]{1,0:T(8,128)(2,1)S(1)}, bf16[336,384]{1,0:T(8,128)(2,1)S(1)}, u32[]{:S(2)}, u32[]{:S(2)}) collective-permute-start(bf16[336,384]{1,0:T(8,128)(2,1)S(1)} %get-tuple-element.57), channel_id=1, source_target_pairs={{0,5},{2,7},{4,0},{6,2},{1,4},{3,6},{5,1},{7,3},{8,13},{10,15},{12... | collective-permute-start | bytes 774152 | tf_op jit(solution)/shard_map/ppermute | solution.py:247
  66.4 19.5 %collective-permute-start.13 = (bf16[336,384]{1,0:T(8,128)(2,1)S(1)}, bf16[336,384]{1,0:T(8,128)(2,1)S(1)}, u32[]{:S(2)}, u32[]{:S(2)}) collective-permute-start(bf16[336,384]{1,0:T(8,128)(2,1)S(1)} %get-tuple-element.63), channel_id=1, source_target_pairs={{0,4},{2,6},{4,1},{6,3},{1,5},{3,7},{5,0},{7,2},{8,12},{10,14},{12... | collective-permute-start | bytes 774152 | tf_op jit(solution)/shard_map/ppermute | solution.py:247
  66.5 19.8 %collective-permute-start.15 = (bf16[336,384]{1,0:T(8,128)(2,1)S(1)}, bf16[336,384]{1,0:T(8,128)(2,1)}, u32[]{:S(2)}, u32[]{:S(2)}) collective-permute-start(bf16[336,384]{1,0:T(8,128)(2,1)S(1)} %get-tuple-element.64), channel_id=1, source_target_pairs={{0,1},{2,3},{4,5},{6,7},{1,0},{3,2},{5,4},{7,6},{8,9},{10,11},{12,... | collective-permute-start | bytes 774152 | tf_op jit(solution)/shard_map/ppermute | solution.py:247
  68.5 17.8 %collective-permute-start.14 = (bf16[336,384]{1,0:T(8,128)(2,1)S(1)}, bf16[336,384]{1,0:T(8,128)(2,1)}, u32[]{:S(2)}, u32[]{:S(2)}) collective-permute-start(bf16[336,384]{1,0:T(8,128)(2,1)S(1)} %get-tuple-element.65), channel_id=1, source_target_pairs={{0,5},{2,7},{4,0},{6,2},{1,4},{3,6},{5,1},{7,3},{8,13},{10,15},{12... | collective-permute-start | bytes 774152 | tf_op jit(solution)/shard_map/ppermute | solution.py:247
  78.2 15.9 %all-to-all-start.1 = ((bf16[16,48,512]{2,1,0:T(8,128)(2,1)}), bf16[16,48,512]{2,1,0:T(8,128)(2,1)S(1)}, u32[]{:S(2)}, u32[]{:S(2)}) async-start(bf16[16,48,512]{2,1,0:T(8,128)(2,1)} %bitcast.8), calls=%async_computation.1 | async-start | bytes 1572864 | tf_op jit(solution)/shard_map/all_to_all | solution.py:348
  81.8 9.7 %collective-permute-start.22 = (bf16[336,384]{1,0:T(8,128)(2,1)S(1)}, bf16[336,384]{1,0:T(8,128)(2,1)S(1)}, u32[]{:S(2)}, u32[]{:S(2)}) collective-permute-start(bf16[336,384]{1,0:T(8,128)(2,1)S(1)} %multiply_convert_fusion.1), channel_id=1, source_target_pairs={{0,1},{2,3},{4,5},{6,7},{1,0},{3,2},{5,4},{7,6},{8,9},{10,11},{12,... | collective-permute-start | bytes 774152 | tf_op jit(solution)/shard_map/ppermute | solution.py:260
  83.8 11.8 %collective-permute-start.21 = (bf16[336,384]{1,0:T(8,128)(2,1)S(1)}, bf16[336,384]{1,0:T(8,128)(2,1)S(1)}, u32[]{:S(2)}, u32[]{:S(2)}) collective-permute-start(bf16[336,384]{1,0:T(8,128)(2,1)S(1)} %multiply_convert_fusion.1), channel_id=1, source_target_pairs={{0,5},{2,7},{4,0},{6,2},{1,4},{3,6},{5,1},{7,3},{8,13},{10,15},{12... | collective-permute-start | bytes 774152 | tf_op jit(solution)/shard_map/ppermute | solution.py:260
  86.0 9.6 %collective-permute-start.20 = (bf16[336,384]{1,0:T(8,128)(2,1)S(1)}, bf16[336,384]{1,0:T(8,128)(2,1)S(1)}, u32[]{:S(2)}, u32[]{:S(2)}) collective-permute-start(bf16[336,384]{1,0:T(8,128)(2,1)S(1)} %multiply_convert_fusion.1), channel_id=1, source_target_pairs={{0,4},{2,6},{4,1},{6,3},{1,5},{3,7},{5,0},{7,2},{8,12},{10,14},{12... | collective-permute-start | bytes 774152 | tf_op jit(solution)/shard_map/ppermute | solution.py:260
  87.6 10.6 %collective-permute-start.16 = (bf16[336,384]{1,0:T(8,128)(2,1)S(1)}, bf16[336,384]{1,0:T(8,128)(2,1)S(1)}, u32[]{:S(2)}, u32[]{:S(2)}) collective-permute-start(bf16[336,384]{1,0:T(8,128)(2,1)S(1)} %multiply_convert_fusion), channel_id=1, source_target_pairs={{0,4},{2,6},{4,1},{6,3},{1,5},{3,7},{5,0},{7,2},{8,12},{10,14},{12... | collective-permute-start | bytes 774152 | tf_op jit(solution)/shard_map/ppermute | solution.py:260
  89.1 15.5 %collective-permute-start.18 = (bf16[336,384]{1,0:T(8,128)(2,1)S(1)}, bf16[336,384]{1,0:T(8,128)(2,1)S(1)}, u32[]{:S(2)}, u32[]{:S(2)}) collective-permute-start(bf16[336,384]{1,0:T(8,128)(2,1)S(1)} %multiply_convert_fusion), channel_id=1, source_target_pairs={{0,1},{2,3},{4,5},{6,7},{1,0},{3,2},{5,4},{7,6},{8,9},{10,11},{12,... | collective-permute-start | bytes 774152 | tf_op jit(solution)/shard_map/ppermute | solution.py:260
  91.5 15.2 %collective-permute-start.17 = (bf16[336,384]{1,0:T(8,128)(2,1)S(1)}, bf16[336,384]{1,0:T(8,128)(2,1)S(1)}, u32[]{:S(2)}, u32[]{:S(2)}) collective-permute-start(bf16[336,384]{1,0:T(8,128)(2,1)S(1)} %multiply_convert_fusion), channel_id=1, source_target_pairs={{0,5},{2,7},{4,0},{6,2},{1,4},{3,6},{5,1},{7,3},{8,13},{10,15},{12... | collective-permute-start | bytes 774152 | tf_op jit(solution)/shard_map/ppermute | solution.py:260
  106.8 5.9 %collective-permute-start.19 = (bf16[1344,384]{1,0:T(8,128)(2,1)S(1)}, bf16[1344,384]{1,0:T(8,128)(2,1)S(1)}, u32[]{:S(2)}, u32[]{:S(2)}) collective-permute-start(bf16[1344,384]{1,0:T(8,128)(2,1)S(1)} %constant_dynamic-update-slice_fusion), channel_id=1, source_target_pairs={{0,2},{2,0},{4,6},{6,4},{1,3},{3,1},{5,7},{7,5},{8,10},{10,8},{12,... | collective-permute-start | bytes 3096584 | tf_op jit(solution)/shard_map/ppermute | solution.py:266
  110.6 5.0 %collective-permute-start.23 = (bf16[1344,384]{1,0:T(8,128)(2,1)S(1)}, bf16[1344,384]{1,0:T(8,128)(2,1)S(1)}, u32[]{:S(2)}, u32[]{:S(2)}) collective-permute-start(bf16[1344,384]{1,0:T(8,128)(2,1)S(1)} %constant_dynamic-update-slice_fusion.4), channel_id=1, source_target_pairs={{0,2},{2,0},{4,6},{6,4},{1,3},{3,1},{5,7},{7,5},{8,10},{10,8},{12,... | collective-permute-start | bytes 3096584 | tf_op jit(solution)/shard_map/ppermute | solution.py:266

commit v9 on v8

--- a/solution.py
+++ b/solution.py
@@ -336,15 +336,15 @@
     send_one, keep_one = filter_sums(ids, *delta, both, False)
     got1 = lax.ppermute(send_one(), LINE, OTHER_CORE)
     split1 = keep_one(got1)
-    arrive2, _ = lax.optimization_barrier((arrive2, split1))
-    block2 = line_sum(arrive2, factor)
-    delta, _ = lax.optimization_barrier((delta, block2))
+    delta, _ = lax.optimization_barrier((delta, split1))
     terms = call(
         data_body,
         jax.ShapeDtypeStruct((CH, n_pos), BF),
         [pltpu.VMEM((ROWS, n_pos), BF)],
         3,
     )(ids, *delta, w_one)
+    arrive2, _ = lax.optimization_barrier((arrive2, (split1, terms)))
+    block2 = line_sum(arrive2, factor)
     got = lax.all_to_all(terms.reshape(16, C, n_pos), "ch", 0, 0, tiled=True)
     block1 = line_sum(arrive(split1), factor)
     spread2, spread1 = line_send(block2), line_send(block1)

time: 119 us -> 120 us (level)
  other arithmetic: 2.85 us -> 4.16 us
    ppermute x6, starting transfers between devices: 9.73 us -> 8.16 us  [line_send(): return [block] + [lax.ppermute(block, LINE, along(k)) for k in (1, 3, 2)]]
    convert_element_type x2, other arithmetic: 1.38 us -> 2.7 us  [line_sum(): return (total * factor).astype(BF)]
    all_to_all x1, waiting for transfers between devices: 1.25 us -> 0.01 us  [shards(): got = lax.all_to_all(terms.reshape(16, C, n_pos), 'ch', 0, 0, tiled=True)]
    unnamed x12 -> x16, local copies, waits for them, and re-layouts: 1.79 us -> 2.5 us
  transfers between devices with their start and end apart: 26 -> 26, of which waited for: 12 -> 10; matrix products, arithmetic and copies ran while one was open for 6% -> 7% of each run, Pallas kernels for 10% -> 10%
where the time goes in v9:
time: 120 us; the launch traced here: 119 us
  starting transfers between devices  57 us (48%)
  waiting for transfers between devices  28.2 us (24%)
  Pallas kernels  19.7 us (16%)
  local copies, waits for them, and re-layouts  9.13 us (8%)
  other arithmetic  4.16 us (3%)
    ppermute x6, waiting for transfers between devices, line_send(): return [block] + [lax.ppermute(block, LINE, along(k)) for k in (1, 3, 2)]  11.5 us
    all_to_all x1, starting transfers between devices, to_all(): return lax.all_to_all(many, axis, 0, 0, tiled=True)  8.6 us
    ppermute x6, starting transfers between devices, line_send(): return [block] + [lax.ppermute(block, LINE, along(k)) for k in (1, 3, 2)]  8.16 us
    ppermute x6, waiting for transfers between devices, arrive(): lax.ppermute(v, LINE, along(k))  7.7 us
    ppermute x6, starting transfers between devices, arrive(): lax.ppermute(v, LINE, along(k))  7.33 us
    ppermute x2, starting transfers between devices, halo(): left = send(last, perm=to_side(1, flip))  7.15 us
    pallas_call x2, Pallas kernels, write(): pl.pallas_call(write_body, out_shape=jax.ShapeDtypeStruct((OFF, C, CH), F...  5.85 us
    ppermute x2, starting transfers between devices, halo(): right = send(first, perm=to_side(-1, flip))  4.72 us
  transfers between devices with their start and end apart: 26, of which 10 were waited for; matrix products, arithmetic and copies ran while one was open for 7% of the time, Pallas kernels for 10%

profile of v9, /device:TPU:1, one launch (start us, length us, event | category | flops | bytes accessed | tf_op | source)
XLA Modules:
  0.0 119.2 jit_solution(14530006387662233558)
XLA Ops:
  3.5 8.6 %all-to-all-start = ((bf16[16,96,512]{2,1,0:T(8,128)(2,1)}), bf16[16,96,512]{2,1,0:T(8,128)(2,1)S(1)}, u32[]{:S(2)}, u32[]{:S(2)}) async-start(bf16[16,96,512]{2,1,0:T(8,128)(2,1)} %broadcast_in_dim.8), calls=%async_computation | async-start | bytes 3145728 | tf_op jit(solution)/shard_map/all_to_all | solution.py:219
  12.2 5.2 %collective-permute-start.2 = (bf16[48,128]{1,0:T(8,128)(2,1)S(1)}, bf16[48,128]{1,0:T(8,128)(2,1)S(1)}, u32[]{:S(2)}, u32[]{:S(2)}) collective-permute-start(bf16[48,128]{1,0:T(8,128)(2,1)S(1)} %get-tuple-element.81), channel_id=1, source_target_pairs={{0,3},{1,2},{2,5},{3,4},{4,7},{5,6},{8,11},{9,10},{10,13},{11,12},... | collective-permute-start | bytes 36872 | tf_op jit(solution)/shard_map/ppermute | solution.py:211
  17.5 1.9 %collective-permute-start = (bf16[48,128]{1,0:T(8,128)(2,1)S(1)}, bf16[48,128]{1,0:T(8,128)(2,1)S(1)}, u32[]{:S(2)}, u32[]{:S(2)}) collective-permute-start(bf16[48,128]{1,0:T(8,128)(2,1)S(1)} %get-tuple-element.81), channel_id=1, source_target_pairs={{0,2},{1,3},{2,4},{3,5},{4,6},{5,7},{8,10},{9,11},{10,12},{11,13},... | collective-permute-start | bytes 36872 | tf_op jit(solution)/shard_map/ppermute | solution.py:211
  19.4 2.8 %collective-permute-start.4 = (bf16[48,128]{1,0:T(8,128)(2,1)S(1)}, bf16[48,128]{1,0:T(8,128)(2,1)S(1)}, u32[]{:S(2)}, u32[]{:S(2)}) collective-permute-start(bf16[48,128]{1,0:T(8,128)(2,1)S(1)} %get-tuple-element.82), channel_id=1, source_target_pairs={{2,1},{3,0},{4,3},{5,2},{6,5},{7,4},{10,9},{11,8},{12,11},{13,10},... | collective-permute-start | bytes 36872 | tf_op jit(solution)/shard_map/ppermute | solution.py:212
  22.2 1.9 %collective-permute-start.1 = (bf16[48,128]{1,0:T(8,128)(2,1)S(1)}, bf16[48,128]{1,0:T(8,128)(2,1)S(1)}, u32[]{:S(2)}, u32[]{:S(2)}) collective-permute-start(bf16[48,128]{1,0:T(8,128)(2,1)S(1)} %get-tuple-element.82), channel_id=1, source_target_pairs={{2,0},{3,1},{4,2},{5,3},{6,4},{7,5},{10,8},{11,9},{12,10},{13,11},... | collective-permute-start | bytes 36872 | tf_op jit(solution)/shard_map/ppermute | solution.py:212
  24.1 2.5 %collective-permute-start.3 = (bf16[48,512]{1,0:T(8,128)(2,1)S(1)}, bf16[48,512]{1,0:T(8,128)(2,1)S(1)}, u32[]{:S(2)}, u32[]{:S(2)}) collective-permute-start(bf16[48,512]{1,0:T(8,128)(2,1)S(1)} %reshape.36), channel_id=1, source_target_pairs={{0,1},{1,0},{2,3},{3,2},{4,5},{5,4},{6,7},{7,6},{8,9},{9,8},{10,11... | collective-permute-start | bytes 147464 | tf_op jit(solution)/shard_map/ppermute | solution.py:210
  26.7 4.1 %copy.11 = bf16[1296,768]{0,1:T(8,128)(2,1)} copy(bf16[1296,768]{1,0:T(8,128)(2,1)} %bitcast.19) | data formatting | bytes 3981312 | tf_op jit(solution)/shard_map/reshape | solution.py:309
  30.9 4.1 %all-to-all-done.both_ref = bf16[16,96,512]{2,1,0:T(8,128)(2,1)S(1)} async-done(((bf16[16,96,512]{2,1,0:T(8,128)(2,1)}), bf16[16,96,512]{2,1,0:T(8,128)(2,1)S(1)}, u32[]{:S(2)}, u32[]{:S(2)}) %all-to-all-start) | async-done | bytes 1572896 | tf_op jit(solution)/shard_map/all_to_all | solution.py:219
  36.5 2.0 %shard_map.76 = (f32[48,768]{1,0:T(8,128)S(1)}, f32[48,768]{1,0:T(8,128)S(1)}, f32[48,768]{1,0:T(8,128)S(1)}) custom-call(s32[4]{0:T(128)S(1)} %pad_add_fusion.ids, bf16[1296,768]{1,0:T(8,128)(2,1)S(1)} %bitcast.14, bf16[16,96,512]{2,1,0:T(8,128)(2,1)S(1)} %all-to-all-done.both_ref), custom_call_target="tpu_custom_call" | custom-call | tf_op jit(solution)/shard_map/pallas_call | solution.py:312
  38.5 2.8 %collective-permute-start.5 = (f32[48,768]{1,0:T(8,128)S(1)}, f32[48,768]{1,0:T(8,128)S(1)}, u32[]{:S(2)}, u32[]{:S(2)}) collective-permute-start(f32[48,768]{1,0:T(8,128)S(1)} %get-tuple-element.45), channel_id=1, source_target_pairs={{0,1},{1,0},{2,3},{3,2},{4,5},{5,4},{6,7},{7,6},{8,9},{9,8},{10,11... | collective-permute-start | bytes 442376 | tf_op jit(solution)/shard_map/ppermute | solution.py:318
  41.3 1.9 %shard_map.77 = bf16[1344,384]{1,0:T(8,128)(2,1)S(1)} custom-call(s32[4]{0:T(128)S(1)} %pad_add_fusion.ids, bf16[48,768]{1,0:T(8,128)(2,1)S(1)} %pad_maximum_fusion.1.own_ref.pre_own_ref, bf16[48,768]{1,0:T(8,128)(2,1)S(1)} %pad_maximum_fusion.2.oth_ref.pre_oth_ref, bf16[16,96,512]{2,1,0:T(8,128)(2,1)S(1)} %all-to-all-done.both_ref), custom_call_target="tpu_custom_call" | custom-call | tf_op jit(solution)/shard_map/pallas_call | solution.py:235
  44.0 3.7 %collective-permute-start.8 = (bf16[1344,384]{1,0:T(8,128)(2,1)S(1)}, bf16[1344,384]{1,0:T(8,128)(2,1)S(1)}, u32[]{:S(2)}, u32[]{:S(2)}) collective-permute-start(bf16[1344,384]{1,0:T(8,128)(2,1)S(1)} %shard_map.77), channel_id=1, source_target_pairs={{0,2},{2,0},{4,6},{6,4},{1,3},{3,1},{5,7},{7,5},{8,10},{10,8},{12,... | collective-permute-start | bytes 3096584 | tf_op jit(solution)/shard_map/ppermute | solution.py:323
  48.3 3.0 %collective-permute-start.6 = (f32[48,512]{1,0:T(8,128)S(1)}, f32[48,512]{1,0:T(8,128)S(1)}, u32[]{:S(2)}, u32[]{:S(2)}) collective-permute-start(f32[48,512]{1,0:T(8,128)S(1)} %get-tuple-element.51), channel_id=1, source_target_pairs={{0,2},{1,3},{2,4},{3,5},{4,6},{5,7},{8,10},{9,11},{10,12},{11,13},... | collective-permute-start | bytes 294920 | tf_op jit(solution)/shard_map/ppermute | solution.py:327
  51.3 1.9 %collective-permute-start.7 = (f32[48,512]{1,0:T(8,128)S(1)}, f32[48,512]{1,0:T(8,128)S(1)}, u32[]{:S(2)}, u32[]{:S(2)}) collective-permute-start(f32[48,512]{1,0:T(8,128)S(1)} %get-tuple-element.52), channel_id=1, source_target_pairs={{2,0},{3,1},{4,2},{5,3},{6,4},{7,5},{10,8},{11,9},{12,10},{13,11},... | collective-permute-start | bytes 294920 | tf_op jit(solution)/shard_map/ppermute | solution.py:328
  53.3 2.0 %shard_map.79 = (f32[336,384]{1,0:T(8,128)S(1)}, bf16[336,384]{1,0:T(8,128)(2,1)S(1)}, bf16[336,384]{1,0:T(8,128)(2,1)S(1)}, bf16[336,384]{1,0:T(8,128)(2,1)S(1)}) custom-call(s32[4]{0:T(128)S(1)} %pad_add_fusion.ids, bf16[48,768]{1,0:T(8,128)(2,1)S(1)} %pad_maximum_fusion.1.own_ref.pre_own_ref, bf16[48,768]{1,0:T(8,128)(2,1)S(1)} %pad_maximum_fusion.2.oth_ref.pre_oth_ref, ...), custom_call_target="tpu_custom_call" | custom-call | tf_op jit(solution)/shard_map/pallas_call | solution.py:240
  55.2 2.0 %collective-permute-done.7.right_ref = f32[48,512]{1,0:T(8,128)S(1)} collective-permute-done((f32[48,512]{1,0:T(8,128)S(1)}, f32[48,512]{1,0:T(8,128)S(1)}, u32[]{:S(2)}, u32[]{:S(2)}) %collective-permute-start.7) | collective-permute-done | bytes 98336 | tf_op jit(solution)/shard_map/ppermute | solution.py:328
  60.0 2.5 %collective-permute-start.19 = (bf16[336,384]{1,0:T(8,128)(2,1)S(1)}, bf16[336,384]{1,0:T(8,128)(2,1)S(1)}, u32[]{:S(2)}, u32[]{:S(2)}) collective-permute-start(bf16[336,384]{1,0:T(8,128)(2,1)S(1)} %get-tuple-element.56), channel_id=1, source_target_pairs={{0,1},{2,3},{4,5},{6,7},{1,0},{3,2},{5,4},{7,6},{8,9},{10,11},{12,... | collective-permute-start | bytes 774152 | tf_op jit(solution)/shard_map/ppermute | solution.py:247
  62.5 2.0 %collective-permute-start.18 = (bf16[336,384]{1,0:T(8,128)(2,1)S(1)}, bf16[336,384]{1,0:T(8,128)(2,1)S(1)}, u32[]{:S(2)}, u32[]{:S(2)}) collective-permute-start(bf16[336,384]{1,0:T(8,128)(2,1)S(1)} %get-tuple-element.57), channel_id=1, source_target_pairs={{0,5},{2,7},{4,0},{6,2},{1,4},{3,6},{5,1},{7,3},{8,13},{10,15},{12... | collective-permute-start | bytes 774152 | tf_op jit(solution)/shard_map/ppermute | solution.py:247
  64.5 2.0 %shard_map.82 = (f32[336,384]{1,0:T(8,128)S(1)}, bf16[336,384]{1,0:T(8,128)(2,1)S(1)}, bf16[336,384]{1,0:T(8,128)(2,1)S(1)}, bf16[336,384]{1,0:T(8,128)(2,1)S(1)}) custom-call(s32[4]{0:T(128)S(1)} %pad_add_fusion.ids, bf16[48,768]{1,0:T(8,128)(2,1)S(1)} %get-tuple-element.66.own_ref.refs_0_, bf16[48,768]{1,0:T(8,128)(2,1)S(1)} %get-tuple-element.67.oth_ref.refs_1_, ...), custom_call_target="tpu_custom_call" | custom-call | tf_op jit(solution)/shard_map/pallas_call | solution.py:240
  67.7 3.1 %shard_map.83 = bf16[768,512]{1,0:T(8,128)(2,1)} custom-call(s32[4]{0:T(128)S(1)} %pad_add_fusion.ids, bf16[48,768]{1,0:T(8,128)(2,1)S(1)} %get-tuple-element.66.own_ref.refs_0_, bf16[48,768]{1,0:T(8,128)(2,1)S(1)} %get-tuple-element.67.oth_ref.refs_1_, bf16[768,1296]{1,0:T(8,128)(2,1)S(1)} %bitcast.13), custom_call_target="tpu_custom_call" | custom-call | tf_op jit(solution)/shard_map/pallas_call | solution.py:340
  72.3 2.0 %collective-permute-done.19 = bf16[336,384]{1,0:T(8,128)(2,1)S(1)} collective-permute-done((bf16[336,384]{1,0:T(8,128)(2,1)S(1)}, bf16[336,384]{1,0:T(8,128)(2,1)S(1)}, u32[]{:S(2)}, u32[]{:S(2)}) %collective-permute-start.19) | collective-permute-done | bytes 258080 | tf_op jit(solution)/shard_map/ppermute | solution.py:247
  75.6 3.6 %all-to-all-start.1 = ((bf16[16,48,512]{2,1,0:T(8,128)(2,1)}), bf16[16,48,512]{2,1,0:T(8,128)(2,1)S(1)}, u32[]{:S(2)}, u32[]{:S(2)}) async-start(bf16[16,48,512]{2,1,0:T(8,128)(2,1)} %bitcast.8), calls=%async_computation.1 | async-start | bytes 1572864 | tf_op jit(solution)/shard_map/all_to_all | solution.py:348
  80.6 2.1 %collective-permute-start.22 = (bf16[336,384]{1,0:T(8,128)(2,1)S(1)}, bf16[336,384]{1,0:T(8,128)(2,1)S(1)}, u32[]{:S(2)}, u32[]{:S(2)}) collective-permute-start(bf16[336,384]{1,0:T(8,128)(2,1)S(1)} %multiply_convert_fusion), channel_id=1, source_target_pairs={{0,1},{2,3},{4,5},{6,7},{1,0},{3,2},{5,4},{7,6},{8,9},{10,11},{12,... | collective-permute-start | bytes 774152 | tf_op jit(solution)/shard_map/ppermute | solution.py:260
  82.7 2.1 %collective-permute-start.21 = (bf16[336,384]{1,0:T(8,128)(2,1)S(1)}, bf16[336,384]{1,0:T(8,128)(2,1)S(1)}, u32[]{:S(2)}, u32[]{:S(2)}) collective-permute-start(bf16[336,384]{1,0:T(8,128)(2,1)S(1)} %multiply_convert_fusion), channel_id=1, source_target_pairs={{0,5},{2,7},{4,0},{6,2},{1,4},{3,6},{5,1},{7,3},{8,13},{10,15},{12... | collective-permute-start | bytes 774152 | tf_op jit(solution)/shard_map/ppermute | solution.py:260
  84.9 5.0 %collective-permute-done.10 = bf16[336,384]{1,0:T(8,128)(2,1)} collective-permute-done((bf16[336,384]{1,0:T(8,128)(2,1)S(1)}, bf16[336,384]{1,0:T(8,128)(2,1)}, u32[]{:S(2)}, u32[]{:S(2)}) %collective-permute-start.10) | collective-permute-done | bytes 258080 | tf_op jit(solution)/shard_map/ppermute | solution.py:247
  91.3 3.8 %collective-permute-start.15 = (bf16[336,384]{1,0:T(8,128)(2,1)S(1)}, bf16[336,384]{1,0:T(8,128)(2,1)S(1)}, u32[]{:S(2)}, u32[]{:S(2)}) collective-permute-start(bf16[336,384]{1,0:T(8,128)(2,1)S(1)} %multiply_convert_fusion.1), channel_id=1, source_target_pairs={{0,1},{2,3},{4,5},{6,7},{1,0},{3,2},{5,4},{7,6},{8,9},{10,11},{12,... | collective-permute-start | bytes 774152 | tf_op jit(solution)/shard_map/ppermute | solution.py:260
  97.6 6.7 %collective-permute-done.13 = bf16[336,384]{1,0:T(8,128)(2,1)S(1)} collective-permute-done((bf16[336,384]{1,0:T(8,128)(2,1)S(1)}, bf16[336,384]{1,0:T(8,128)(2,1)S(1)}, u32[]{:S(2)}, u32[]{:S(2)}) %collective-permute-start.13) | collective-permute-done | bytes 258080 | tf_op jit(solution)/shard_map/ppermute | solution.py:260
  104.3 3.3 %collective-permute-done.15 = bf16[336,384]{1,0:T(8,128)(2,1)S(1)} collective-permute-done((bf16[336,384]{1,0:T(8,128)(2,1)S(1)}, bf16[336,384]{1,0:T(8,128)(2,1)S(1)}, u32[]{:S(2)}, u32[]{:S(2)}) %collective-permute-start.15) | collective-permute-done | bytes 258080 | tf_op jit(solution)/shard_map/ppermute | solution.py:260
  107.8 3.3 %collective-permute-start.16 = (bf16[1344,384]{1,0:T(8,128)(2,1)S(1)}, bf16[1344,384]{1,0:T(8,128)(2,1)S(1)}, u32[]{:S(2)}, u32[]{:S(2)}) collective-permute-start(bf16[1344,384]{1,0:T(8,128)(2,1)S(1)} %constant_dynamic-update-slice_fusion), channel_id=1, source_target_pairs={{0,2},{2,0},{4,6},{6,4},{1,3},{3,1},{5,7},{7,5},{8,10},{10,8},{12,... | collective-permute-start | bytes 3096584 | tf_op jit(solution)/shard_map/ppermute | solution.py:266
  111.3 2.0 %collective-permute-done.16 = bf16[1344,384]{1,0:T(8,128)(2,1)S(1)} collective-permute-done((bf16[1344,384]{1,0:T(8,128)(2,1)S(1)}, bf16[1344,384]{1,0:T(8,128)(2,1)S(1)}, u32[]{:S(2)}, u32[]{:S(2)}) %collective-permute-start.16) | collective-permute-done | bytes 1032224 | tf_op jit(solution)/shard_map/ppermute | solution.py:266
  113.3 2.9 %shard_map.84 = f32[27,48,768]{2,1,0:T(8,128)} custom-call(s32[4]{0:T(128)S(1)} %pad_add_fusion.ids, bf16[4,7,48,384]{3,2,1,0:T(8,128)(2,1)S(1)} %bitcast.16, bf16[4,7,48,384]{3,2,1,0:T(8,128)(2,1)S(1)} %bitcast.17), custom_call_target="tpu_custom_call" | custom-call | tf_op jit(solution)/shard_map/pallas_call | solution.py:279
  116.3 2.9 %shard_map.85 = f32[27,48,768]{2,1,0:T(8,128)} custom-call(s32[4]{0:T(128)S(1)} %pad_add_fusion.ids, bf16[4,7,48,384]{3,2,1,0:T(8,128)(2,1)S(1)} %bitcast.15, bf16[4,7,48,384]{3,2,1,0:T(8,128)(2,1)S(1)} %bitcast.18), custom_call_target="tpu_custom_call" | custom-call | tf_op jit(solution)/shard_map/pallas_call | solution.py:279
  (62 shorter events, 18.5 us)
Async XLA Ops:
  2.2 9.9 %copy-start.4 = (bf16[48,4,2,64]{3,2,1,0:T(2,128)(2,1)S(1)}, bf16[48,4,2,64]{3,2,1,0:T(2,128)(2,1)}, u32[]{:S(2)}) copy-start(bf16[48,4,2,64]{3,2,1,0:T(2,128)(2,1)} %param.6) | copy-start | bytes 147460
  3.5 31.5 %all-to-all-start = ((bf16[16,96,512]{2,1,0:T(8,128)(2,1)}), bf16[16,96,512]{2,1,0:T(8,128)(2,1)S(1)}, u32[]{:S(2)}, u32[]{:S(2)}) async-start(bf16[16,96,512]{2,1,0:T(8,128)(2,1)} %broadcast_in_dim.8), calls=%async_computation | async-start | bytes 3145728 | tf_op jit(solution)/shard_map/all_to_all | solution.py:219
  12.2 18.6 %collective-permute-start.2 = (bf16[48,128]{1,0:T(8,128)(2,1)S(1)}, bf16[48,128]{1,0:T(8,128)(2,1)S(1)}, u32[]{:S(2)}, u32[]{:S(2)}) collective-permute-start(bf16[48,128]{1,0:T(8,128)(2,1)S(1)} %get-tuple-element.81), channel_id=1, source_target_pairs={{0,3},{1,2},{2,5},{3,4},{4,7},{5,6},{8,11},{9,10},{10,13},{11,12},... | collective-permute-start | bytes 36872 | tf_op jit(solution)/shard_map/ppermute | solution.py:211
  17.5 13.4 %collective-permute-start = (bf16[48,128]{1,0:T(8,128)(2,1)S(1)}, bf16[48,128]{1,0:T(8,128)(2,1)S(1)}, u32[]{:S(2)}, u32[]{:S(2)}) collective-permute-start(bf16[48,128]{1,0:T(8,128)(2,1)S(1)} %get-tuple-element.81), channel_id=1, source_target_pairs={{0,2},{1,3},{2,4},{3,5},{4,6},{5,7},{8,10},{9,11},{10,12},{11,13},... | collective-permute-start | bytes 36872 | tf_op jit(solution)/shard_map/ppermute | solution.py:211
  19.4 11.5 %collective-permute-start.4 = (bf16[48,128]{1,0:T(8,128)(2,1)S(1)}, bf16[48,128]{1,0:T(8,128)(2,1)S(1)}, u32[]{:S(2)}, u32[]{:S(2)}) collective-permute-start(bf16[48,128]{1,0:T(8,128)(2,1)S(1)} %get-tuple-element.82), channel_id=1, source_target_pairs={{2,1},{3,0},{4,3},{5,2},{6,5},{7,4},{10,9},{11,8},{12,11},{13,10},... | collective-permute-start | bytes 36872 | tf_op jit(solution)/shard_map/ppermute | solution.py:212
  22.2 8.6 %collective-permute-start.1 = (bf16[48,128]{1,0:T(8,128)(2,1)S(1)}, bf16[48,128]{1,0:T(8,128)(2,1)S(1)}, u32[]{:S(2)}, u32[]{:S(2)}) collective-permute-start(bf16[48,128]{1,0:T(8,128)(2,1)S(1)} %get-tuple-element.82), channel_id=1, source_target_pairs={{2,0},{3,1},{4,2},{5,3},{6,4},{7,5},{10,8},{11,9},{12,10},{13,11},... | collective-permute-start | bytes 36872 | tf_op jit(solution)/shard_map/ppermute | solution.py:212
  24.1 6.7 %collective-permute-start.3 = (bf16[48,512]{1,0:T(8,128)(2,1)S(1)}, bf16[48,512]{1,0:T(8,128)(2,1)S(1)}, u32[]{:S(2)}, u32[]{:S(2)}) collective-permute-start(bf16[48,512]{1,0:T(8,128)(2,1)S(1)} %reshape.36), channel_id=1, source_target_pairs={{0,1},{1,0},{2,3},{3,2},{4,5},{5,4},{6,7},{7,6},{8,9},{9,8},{10,11... | collective-permute-start | bytes 147464 | tf_op jit(solution)/shard_map/ppermute | solution.py:210
  34.9 1.6 %copy-start.1 = (bf16[27,48,768]{2,1,0:T(8,128)(2,1)S(1)}, bf16[27,48,768]{2,1,0:T(8,128)(2,1)}, u32[]{:S(2)}) copy-start(bf16[27,48,768]{2,1,0:T(8,128)(2,1)} %param.9) | copy-start | bytes 5971972
  38.5 5.6 %collective-permute-start.5 = (f32[48,768]{1,0:T(8,128)S(1)}, f32[48,768]{1,0:T(8,128)S(1)}, u32[]{:S(2)}, u32[]{:S(2)}) collective-permute-start(f32[48,768]{1,0:T(8,128)S(1)} %get-tuple-element.45), channel_id=1, source_target_pairs={{0,1},{1,0},{2,3},{3,2},{4,5},{5,4},{6,7},{7,6},{8,9},{9,8},{10,11... | collective-permute-start | bytes 442376 | tf_op jit(solution)/shard_map/ppermute | solution.py:318
  44.0 9.2 %collective-permute-start.8 = (bf16[1344,384]{1,0:T(8,128)(2,1)S(1)}, bf16[1344,384]{1,0:T(8,128)(2,1)S(1)}, u32[]{:S(2)}, u32[]{:S(2)}) collective-permute-start(bf16[1344,384]{1,0:T(8,128)(2,1)S(1)} %shard_map.77), channel_id=1, source_target_pairs={{0,2},{2,0},{4,6},{6,4},{1,3},{3,1},{5,7},{7,5},{8,10},{10,8},{12,... | collective-permute-start | bytes 3096584 | tf_op jit(solution)/shard_map/ppermute | solution.py:323
  48.3 6.9 %collective-permute-start.6 = (f32[48,512]{1,0:T(8,128)S(1)}, f32[48,512]{1,0:T(8,128)S(1)}, u32[]{:S(2)}, u32[]{:S(2)}) collective-permute-start(f32[48,512]{1,0:T(8,128)S(1)} %get-tuple-element.51), channel_id=1, source_target_pairs={{0,2},{1,3},{2,4},{3,5},{4,6},{5,7},{8,10},{9,11},{10,12},{11,13},... | collective-permute-start | bytes 294920 | tf_op jit(solution)/shard_map/ppermute | solution.py:327
  51.3 5.9 %collective-permute-start.7 = (f32[48,512]{1,0:T(8,128)S(1)}, f32[48,512]{1,0:T(8,128)S(1)}, u32[]{:S(2)}, u32[]{:S(2)}) collective-permute-start(f32[48,512]{1,0:T(8,128)S(1)} %get-tuple-element.52), channel_id=1, source_target_pairs={{2,0},{3,1},{4,2},{5,3},{6,4},{7,5},{10,8},{11,9},{12,10},{13,11},... | collective-permute-start | bytes 294920 | tf_op jit(solution)/shard_map/ppermute | solution.py:328
  59.8 7.9 %copy-start = (bf16[1296,768]{0,1:T(8,128)(2,1)S(1)}, bf16[1296,768]{0,1:T(8,128)(2,1)}, u32[]{:S(2)}) copy-start(bf16[1296,768]{0,1:T(8,128)(2,1)} %copy.11) | copy-start | bytes 5971972
  59.8 4.7 %collective-permute-start.9 = (bf16[1344,384]{1,0:T(8,128)(2,1)S(1)}, bf16[1344,384]{1,0:T(8,128)(2,1)S(1)}, u32[]{:S(2)}, u32[]{:S(2)}) collective-permute-start(bf16[1344,384]{1,0:T(8,128)(2,1)S(1)} %shard_map.81), channel_id=1, source_target_pairs={{0,2},{2,0},{4,6},{6,4},{1,3},{3,1},{5,7},{7,5},{8,10},{10,8},{12,... | collective-permute-start | bytes 3096584 | tf_op jit(solution)/shard_map/ppermute | solution.py:337
  59.9 10.9 %collective-permute-start.17 = (bf16[336,384]{1,0:T(8,128)(2,1)S(1)}, bf16[336,384]{1,0:T(8,128)(2,1)}, u32[]{:S(2)}, u32[]{:S(2)}) collective-permute-start(bf16[336,384]{1,0:T(8,128)(2,1)S(1)} %get-tuple-element.55), channel_id=1, source_target_pairs={{0,4},{2,6},{4,1},{6,3},{1,5},{3,7},{5,0},{7,2},{8,12},{10,14},{12... | collective-permute-start | bytes 774152 | tf_op jit(solution)/shard_map/ppermute | solution.py:247
  60.0 14.2 %collective-permute-start.19 = (bf16[336,384]{1,0:T(8,128)(2,1)S(1)}, bf16[336,384]{1,0:T(8,128)(2,1)S(1)}, u32[]{:S(2)}, u32[]{:S(2)}) collective-permute-start(bf16[336,384]{1,0:T(8,128)(2,1)S(1)} %get-tuple-element.56), channel_id=1, source_target_pairs={{0,1},{2,3},{4,5},{6,7},{1,0},{3,2},{5,4},{7,6},{8,9},{10,11},{12,... | collective-permute-start | bytes 774152 | tf_op jit(solution)/shard_map/ppermute | solution.py:247
  62.5 12.4 %collective-permute-start.18 = (bf16[336,384]{1,0:T(8,128)(2,1)S(1)}, bf16[336,384]{1,0:T(8,128)(2,1)S(1)}, u32[]{:S(2)}, u32[]{:S(2)}) collective-permute-start(bf16[336,384]{1,0:T(8,128)(2,1)S(1)} %get-tuple-element.57), channel_id=1, source_target_pairs={{0,5},{2,7},{4,0},{6,2},{1,4},{3,6},{5,1},{7,3},{8,13},{10,15},{12... | collective-permute-start | bytes 774152 | tf_op jit(solution)/shard_map/ppermute | solution.py:247
  66.4 23.4 %collective-permute-start.10 = (bf16[336,384]{1,0:T(8,128)(2,1)S(1)}, bf16[336,384]{1,0:T(8,128)(2,1)}, u32[]{:S(2)}, u32[]{:S(2)}) collective-permute-start(bf16[336,384]{1,0:T(8,128)(2,1)S(1)} %get-tuple-element.63), channel_id=1, source_target_pairs={{0,4},{2,6},{4,1},{6,3},{1,5},{3,7},{5,0},{7,2},{8,12},{10,14},{12... | collective-permute-start | bytes 774152 | tf_op jit(solution)/shard_map/ppermute | solution.py:247
  66.5 23.4 %collective-permute-start.12 = (bf16[336,384]{1,0:T(8,128)(2,1)S(1)}, bf16[336,384]{1,0:T(8,128)(2,1)}, u32[]{:S(2)}, u32[]{:S(2)}) collective-permute-start(bf16[336,384]{1,0:T(8,128)(2,1)S(1)} %get-tuple-element.64), channel_id=1, source_target_pairs={{0,1},{2,3},{4,5},{6,7},{1,0},{3,2},{5,4},{7,6},{8,9},{10,11},{12,... | collective-permute-start | bytes 774152 | tf_op jit(solution)/shard_map/ppermute | solution.py:247
  70.8 19.1 %collective-permute-start.11 = (bf16[336,384]{1,0:T(8,128)(2,1)S(1)}, bf16[336,384]{1,0:T(8,128)(2,1)}, u32[]{:S(2)}, u32[]{:S(2)}) collective-permute-start(bf16[336,384]{1,0:T(8,128)(2,1)S(1)} %get-tuple-element.65), channel_id=1, source_target_pairs={{0,5},{2,7},{4,0},{6,2},{1,4},{3,6},{5,1},{7,3},{8,13},{10,15},{12... | collective-permute-start | bytes 774152 | tf_op jit(solution)/shard_map/ppermute | solution.py:247
  74.2 0.7 copy-start.2
  74.9 0.7 copy-start.3
  75.6 19.5 %all-to-all-start.1 = ((bf16[16,48,512]{2,1,0:T(8,128)(2,1)}), bf16[16,48,512]{2,1,0:T(8,128)(2,1)S(1)}, u32[]{:S(2)}, u32[]{:S(2)}) async-start(bf16[16,48,512]{2,1,0:T(8,128)(2,1)} %bitcast.8), calls=%async_computation.1 | async-start | bytes 1572864 | tf_op jit(solution)/shard_map/all_to_all | solution.py:348
  80.6 14.5 %collective-permute-start.22 = (bf16[336,384]{1,0:T(8,128)(2,1)S(1)}, bf16[336,384]{1,0:T(8,128)(2,1)S(1)}, u32[]{:S(2)}, u32[]{:S(2)}) collective-permute-start(bf16[336,384]{1,0:T(8,128)(2,1)S(1)} %multiply_convert_fusion), channel_id=1, source_target_pairs={{0,1},{2,3},{4,5},{6,7},{1,0},{3,2},{5,4},{7,6},{8,9},{10,11},{12,... | collective-permute-start | bytes 774152 | tf_op jit(solution)/shard_map/ppermute | solution.py:260
  82.7 13.3 %collective-permute-start.21 = (bf16[336,384]{1,0:T(8,128)(2,1)S(1)}, bf16[336,384]{1,0:T(8,128)(2,1)S(1)}, u32[]{:S(2)}, u32[]{:S(2)}) collective-permute-start(bf16[336,384]{1,0:T(8,128)(2,1)S(1)} %multiply_convert_fusion), channel_id=1, source_target_pairs={{0,5},{2,7},{4,0},{6,2},{1,4},{3,6},{5,1},{7,3},{8,13},{10,15},{12... | collective-permute-start | bytes 774152 | tf_op jit(solution)/shard_map/ppermute | solution.py:260
  89.9 7.7 %collective-permute-start.20 = (bf16[336,384]{1,0:T(8,128)(2,1)S(1)}, bf16[336,384]{1,0:T(8,128)(2,1)S(1)}, u32[]{:S(2)}, u32[]{:S(2)}) collective-permute-start(bf16[336,384]{1,0:T(8,128)(2,1)S(1)} %multiply_convert_fusion), channel_id=1, source_target_pairs={{0,4},{2,6},{4,1},{6,3},{1,5},{3,7},{5,0},{7,2},{8,12},{10,14},{12... | collective-permute-start | bytes 774152 | tf_op jit(solution)/shard_map/ppermute | solution.py:260
  91.2 13.0 %collective-permute-start.13 = (bf16[336,384]{1,0:T(8,128)(2,1)S(1)}, bf16[336,384]{1,0:T(8,128)(2,1)S(1)}, u32[]{:S(2)}, u32[]{:S(2)}) collective-permute-start(bf16[336,384]{1,0:T(8,128)(2,1)S(1)} %multiply_convert_fusion.1), channel_id=1, source_target_pairs={{0,4},{2,6},{4,1},{6,3},{1,5},{3,7},{5,0},{7,2},{8,12},{10,14},{12... | collective-permute-start | bytes 774152 | tf_op jit(solution)/shard_map/ppermute | solution.py:260
  91.3 16.2 %collective-permute-start.15 = (bf16[336,384]{1,0:T(8,128)(2,1)S(1)}, bf16[336,384]{1,0:T(8,128)(2,1)S(1)}, u32[]{:S(2)}, u32[]{:S(2)}) collective-permute-start(bf16[336,384]{1,0:T(8,128)(2,1)S(1)} %multiply_convert_fusion.1), channel_id=1, source_target_pairs={{0,1},{2,3},{4,5},{6,7},{1,0},{3,2},{5,4},{7,6},{8,9},{10,11},{12,... | collective-permute-start | bytes 774152 | tf_op jit(solution)/shard_map/ppermute | solution.py:260
  95.2 12.4 %collective-permute-start.14 = (bf16[336,384]{1,0:T(8,128)(2,1)S(1)}, bf16[336,384]{1,0:T(8,128)(2,1)S(1)}, u32[]{:S(2)}, u32[]{:S(2)}) collective-permute-start(bf16[336,384]{1,0:T(8,128)(2,1)S(1)} %multiply_convert_fusion.1), channel_id=1, source_target_pairs={{0,5},{2,7},{4,0},{6,2},{1,4},{3,6},{5,1},{7,3},{8,13},{10,15},{12... | collective-permute-start | bytes 774152 | tf_op jit(solution)/shard_map/ppermute | solution.py:260
  107.8 5.6 %collective-permute-start.16 = (bf16[1344,384]{1,0:T(8,128)(2,1)S(1)}, bf16[1344,384]{1,0:T(8,128)(2,1)S(1)}, u32[]{:S(2)}, u32[]{:S(2)}) collective-permute-start(bf16[1344,384]{1,0:T(8,128)(2,1)S(1)} %constant_dynamic-update-slice_fusion), channel_id=1, source_target_pairs={{0,2},{2,0},{4,6},{6,4},{1,3},{3,1},{5,7},{7,5},{8,10},{10,8},{12,... | collective-permute-start | bytes 3096584 | tf_op jit(solution)/shard_map/ppermute | solution.py:266
  111.2 5.0 %collective-permute-start.23 = (bf16[1344,384]{1,0:T(8,128)(2,1)S(1)}, bf16[1344,384]{1,0:T(8,128)(2,1)S(1)}, u32[]{:S(2)}, u32[]{:S(2)}) collective-permute-start(bf16[1344,384]{1,0:T(8,128)(2,1)S(1)} %constant_dynamic-update-slice_fusion.4), channel_id=1, source_target_pairs={{0,2},{2,0},{4,6},{6,4},{1,3},{3,1},{5,7},{7,5},{8,10},{10,8},{12,... | collective-permute-start | bytes 3096584 | tf_op jit(solution)/shard_map/ppermute | solution.py:266
